TPU v7x, 32 devices: a whole 2x2x4 slice. The times are simulated.
32 devices in a mesh: fsdp: 8 (over z, y), seq: 4 (over x, core).
Axes of the slice: x: 2, y: 2, z: 4, core: 2. Of those that a mesh axis runs over, the one named last changes fastest.
Arguments:
- inputs: bfloat16 [16, 2048, 1024], P('fsdp', 'seq'), may hold values from -6 to 6
- first_values: bfloat16 [16, 2048, 1024], P('fsdp', 'seq'), may hold values from -6 to 6
- out_grad: bfloat16 [16, 2048, 1024], P('fsdp', 'seq'), may hold values from -6 to 6
- attn_gain: bfloat16 [1024], P('fsdp'), may hold values from 0.099609375 to 1.8984375
- query_weight: bfloat16 [1024, 1024], P('fsdp'), may hold values from -0.25 to 0.25
- key_weight: bfloat16 [1024, 1024], P('fsdp'), may hold values from -0.25 to 0.25
- value_weight: bfloat16 [1024, 1024], P('fsdp'), may hold values from -0.1875 to 0.1875
- output_weight: bfloat16 [1024, 1024], P('fsdp'), may hold values from -1 to 1
- mlp_gain: bfloat16 [1024], P('fsdp'), may hold values from 0.099609375 to 1.8984375
- gate_weight: bfloat16 [1024, 2816], P('fsdp'), may hold values from -0.1875 to 0.1875
- up_weight: bfloat16 [1024, 2816], P('fsdp'), may hold values from -0.1875 to 0.1875
- down_weight: bfloat16 [2816, 1024], P('fsdp'), may hold values from -0.21875 to 0.21875
Outputs:
- outputs: float32 [16, 2048, 1024], P('fsdp', 'seq')
- input_grad: float32 [16, 2048, 1024], P('fsdp', 'seq')
- first_values_grad: float32 [16, 2048, 1024], P('fsdp', 'seq')
- attn_gain_grad: float32 [1024], P('fsdp')
- mlp_gain_grad: float32 [1024], P('fsdp')
- query_weight_grad: float32 [1024, 1024], P('fsdp')
- key_weight_grad: float32 [1024, 1024], P('fsdp')
- value_weight_grad: float32 [1024, 1024], P('fsdp')
- output_weight_grad: float32 [1024, 1024], P('fsdp')
- gate_weight_grad: float32 [1024, 2816], P('fsdp')
- up_weight_grad: float32 [1024, 2816], P('fsdp')
- down_weight_grad: float32 [2816, 1024], P('fsdp')
All inputs are finite; a program needn't handle non-finite values.
Results may differ from a plain program's by a relative error of at most 0.023.
Values may be sent and summed in bfloat16 or wider, within the bound.
A program may use at most 384 MiB of HBM per device.

v0:
```python
import jax
import jax.numpy as jnp
from jax import lax
from jax.sharding import PartitionSpec as P

D = 1024
HEADS = 16
HEAD_DIM = 64


epsilon = 1e-06
rope_base = 10000.0


def shortened(value):

    def short(part):
        return part.astype(jnp.bfloat16) if part.dtype == jnp.float32 else part

    return jax.tree.map(short, value)


def rope_tables(positions, head_dim):
    half = head_dim // 2
    freqs = rope_base ** (-(jnp.arange(half, dtype=jnp.float32) * 2.0 / head_dim))
    angles = positions.astype(jnp.float32)[:, None] * freqs[None, :]
    return (jnp.cos(angles), jnp.sin(angles))


def rotate(values, cosine, sine):
    half = values.shape[-1] // 2
    first = values[..., :half]
    second = values[..., half:]
    return jnp.concatenate(
        [first * cosine - second * sine, first * sine + second * cosine], axis=-1
    )


def unrotate(values, cosine, sine):
    half = values.shape[-1] // 2
    first = values[..., :half]
    second = values[..., half:]
    return jnp.concatenate(
        [first * cosine + second * sine, second * cosine - first * sine], axis=-1
    )


def norm_forward(values, gain):
    scale = lax.rsqrt(jnp.mean(values * values, axis=-1, keepdims=True) + epsilon)
    return (scale, values * scale * gain)


def norm_backward(values, scale, gain, grad_normed):
    weighted = grad_normed * gain
    inner = jnp.mean(weighted * values, axis=-1, keepdims=True)
    grad_values = scale * weighted - values * (scale * scale * scale) * inner
    grad_gain = jnp.sum(grad_normed * values * scale, axis=0)
    return (grad_values, grad_gain)


def attend(items):
    queries, keys, values = items
    length = queries.shape[-2]
    width = queries.shape[-1]
    block = min(512, length)
    scale = width ** (-0.5)
    mixed_parts = []
    total_parts = []
    for number in range(length // block):
        start = number * block
        finish = start + block
        rows = queries[..., start:finish, :]
        near_keys = keys[..., :finish, :]
        near_values = values[..., :finish, :]
        scores = (
            jnp.einsum("...qe,...ke->...qk", rows, near_keys, preferred_element_type=jnp.float32)
            * scale
        )
        query_pos = start + jnp.arange(block, dtype=jnp.int32)
        allowed = jnp.arange(finish, dtype=jnp.int32)[None, :] <= query_pos[:, None]
        scores = jnp.where(allowed, scores, -1e30)
        peak = jnp.max(scores, axis=-1, keepdims=True)
        weights = jnp.exp(scores - peak)
        total = jnp.sum(weights, axis=-1, keepdims=True)
        probs = (weights / total).astype(jnp.bfloat16)
        mixed = jnp.einsum(
            "...qk,...ke->...qe", probs, near_values, preferred_element_type=jnp.float32
        )
        mixed_parts.append(mixed.astype(jnp.bfloat16))
        total_parts.append((peak + jnp.log(total))[..., 0])
    mixed = jnp.concatenate(mixed_parts, axis=-2)
    log_total = jnp.concatenate(total_parts, axis=-1)
    return (mixed, log_total, queries, keys, values)


def attend_back(queries, keys, values, log_total, grad_mixed):
    count, length, width = queries.shape
    block = min(512, length)
    scale = width ** (-0.5)
    grad_keys = jnp.zeros((count, length, width), jnp.float32)
    grad_values = jnp.zeros((count, length, width), jnp.float32)
    query_parts = []
    for number in range(length // block):
        start = number * block
        finish = start + block
        rows = queries[:, start:finish]
        grad_rows = grad_mixed[:, start:finish]
        totals = log_total[:, start:finish]
        near_keys = keys[:, :finish]
        near_values = values[:, :finish]
        scores = (
            jnp.einsum("hqe,hke->hqk", rows, near_keys, preferred_element_type=jnp.float32) * scale
        )
        query_pos = start + jnp.arange(block, dtype=jnp.int32)
        allowed = jnp.arange(finish, dtype=jnp.int32)[None, :] <= query_pos[:, None]
        scores = jnp.where(allowed[None], scores, -1e30)
        probs = jnp.exp(scores - totals[..., None])
        low_probs = probs.astype(jnp.bfloat16)
        grad_probs = jnp.einsum(
            "hqe,hke->hqk", grad_rows, near_values, preferred_element_type=jnp.float32
        )
        inner = jnp.sum(grad_probs * probs, axis=-1, keepdims=True)
        grad_scores = (probs * (grad_probs - inner)).astype(jnp.bfloat16)
        query_parts.append(
            jnp.einsum("hqk,hke->hqe", grad_scores, near_keys, preferred_element_type=jnp.float32)
            * scale
        )
        grad_keys = grad_keys.at[:, :finish].add(
            jnp.einsum("hqk,hqe->hke", grad_scores, rows, preferred_element_type=jnp.float32)
            * scale
        )
        grad_values = grad_values.at[:, :finish].add(
            jnp.einsum("hqk,hqe->hke", low_probs, grad_rows, preferred_element_type=jnp.float32)
        )
    grad_queries = jnp.concatenate(query_parts, axis=1)
    return (grad_queries, grad_keys, grad_values)


def shards(
    inputs,
    first_values,
    out_grad,
    attn_gain,
    query_weight,
    key_weight,
    value_weight,
    output_weight,
    mlp_gain,
    gate_weight,
    up_weight,
    down_weight,
):
    tok_len = inputs.shape[1]
    groups = lax.axis_size("seq")
    local_heads = HEADS // groups
    length = tok_len * groups
    positions = lax.axis_index("seq") * tok_len + jnp.arange(tok_len, dtype=jnp.int32)
    cosine, sine = rope_tables(positions, HEAD_DIM)
    full_cos, full_sin = rope_tables(jnp.arange(length, dtype=jnp.int32), HEAD_DIM)

    def split_heads(values):
        return values.reshape(groups, local_heads, tok_len, HEAD_DIM)

    def layer_step(gain_totals, batch):
        seq_in, seq_first, seq_grad = batch
        gathered = (
            lax.all_gather(attn_gain, "fsdp", axis=0, tiled=True),
            lax.all_gather(query_weight, "fsdp", axis=0, tiled=True),
            lax.all_gather(key_weight, "fsdp", axis=0, tiled=True),
            lax.all_gather(value_weight, "fsdp", axis=0, tiled=True),
            lax.all_gather(output_weight, "fsdp", axis=0, tiled=True),
            lax.all_gather(mlp_gain, "fsdp", axis=0, tiled=True),
            lax.all_gather(gate_weight, "fsdp", axis=0, tiled=True),
            lax.all_gather(up_weight, "fsdp", axis=0, tiled=True),
            lax.all_gather(down_weight, "fsdp", axis=0, tiled=True),
        )
        (
            gain_attn,
            query_full,
            key_full,
            value_full,
            output_full,
            gain_mlp,
            gate_full,
            up_full,
            down_full,
        ) = gathered
        query_three = query_full.reshape(D, HEADS, HEAD_DIM)
        key_three = key_full.reshape(D, HEADS, HEAD_DIM)
        value_three = value_full.reshape(D, HEADS, HEAD_DIM)
        output_three = output_full.reshape(HEADS, HEAD_DIM, D)
        resid = seq_in.astype(jnp.float32)
        attn_scale, normed = norm_forward(resid, gain_attn.astype(jnp.float32))
        normed_low = normed.astype(jnp.bfloat16)
        raw_queries = jnp.einsum(
            "td,dhe->hte", normed_low, query_three, preferred_element_type=jnp.float32
        )
        raw_keys = jnp.einsum(
            "td,dhe->hte", normed_low, key_three, preferred_element_type=jnp.float32
        )
        raw_values = jnp.einsum(
            "td,dhe->hte", normed_low, value_three, preferred_element_type=jnp.float32
        )
        queries = rotate(raw_queries, cosine, sine).astype(jnp.bfloat16)
        keys = rotate(raw_keys, cosine, sine).astype(jnp.bfloat16)
        first_heads = (
            seq_first.reshape(tok_len, HEADS, HEAD_DIM).transpose(1, 0, 2).astype(jnp.float32)
        )
        mixed_values = (0.5 * raw_values + 0.5 * first_heads).astype(jnp.bfloat16)
        mixed, log_total, head_queries, head_keys, head_values = attend(
            (
                lax.all_to_all(
                    split_heads(queries), "seq", split_axis=0, concat_axis=2, tiled=True
                ),
                lax.all_to_all(split_heads(keys), "seq", split_axis=0, concat_axis=2, tiled=True),
                lax.all_to_all(
                    split_heads(mixed_values), "seq", split_axis=0, concat_axis=2, tiled=True
                ),
            )
        )
        attended = (
            lax.all_to_all(shortened(mixed), "seq", split_axis=2, concat_axis=0, tiled=True)
            .astype(mixed.dtype)
            .reshape(HEADS, tok_len, HEAD_DIM)
        )
        middle = resid + jnp.einsum(
            "hte,heo->to", attended, output_three, preferred_element_type=jnp.float32
        )
        mlp_scale, normed2 = norm_forward(middle, gain_mlp.astype(jnp.float32))
        normed2_low = normed2.astype(jnp.bfloat16)
        gate = jnp.dot(normed2_low, gate_full, preferred_element_type=jnp.float32)
        up_proj = jnp.dot(normed2_low, up_full, preferred_element_type=jnp.float32)
        sigma = jax.nn.sigmoid(gate)
        silu_gate = gate * sigma
        active = (silu_gate * up_proj).astype(jnp.bfloat16)
        result = middle + jnp.dot(active, down_full, preferred_element_type=jnp.float32)
        grad_active = jnp.einsum(
            "td,fd->tf", seq_grad, down_full, preferred_element_type=jnp.float32
        )
        grad_gate = (grad_active * up_proj * sigma * (1.0 + gate * (1.0 - sigma))).astype(
            jnp.bfloat16
        )
        grad_up = (grad_active * silu_gate).astype(jnp.bfloat16)
        grad_normed2 = jnp.einsum(
            "tf,df->td", grad_gate, gate_full, preferred_element_type=jnp.float32
        )
        grad_normed2 = grad_normed2 + jnp.einsum(
            "tf,df->td", grad_up, up_full, preferred_element_type=jnp.float32
        )
        grad_middle, mlp_gain_grad = norm_backward(
            middle, mlp_scale, gain_mlp.astype(jnp.float32), grad_normed2
        )
        grad_middle = grad_middle + seq_grad.astype(jnp.float32)
        low_grad_middle = grad_middle.astype(jnp.bfloat16)
        grad_attended = jnp.einsum(
            "to,heo->hte", low_grad_middle, output_three, preferred_element_type=jnp.float32
        ).astype(jnp.bfloat16)
        grad_heads = lax.all_to_all(
            split_heads(grad_attended), "seq", split_axis=0, concat_axis=2, tiled=True
        )
        grad_queries, grad_keys, grad_mixed = attend_back(
            head_queries[0], head_keys[0], head_values[0], log_total[0], grad_heads[0]
        )
        grad_queries = unrotate(grad_queries, full_cos, full_sin).astype(jnp.bfloat16)
        grad_keys = unrotate(grad_keys, full_cos, full_sin).astype(jnp.bfloat16)
        grad_mixed = grad_mixed.astype(jnp.bfloat16)
        tok_queries, tok_keys, tok_mixed = (
            lax.all_to_all(grad_queries[None], "seq", split_axis=2, concat_axis=0, tiled=True),
            lax.all_to_all(grad_keys[None], "seq", split_axis=2, concat_axis=0, tiled=True),
            lax.all_to_all(grad_mixed[None], "seq", split_axis=2, concat_axis=0, tiled=True),
        )
        tok_queries = tok_queries.reshape(HEADS, tok_len, HEAD_DIM)
        tok_keys = tok_keys.reshape(HEADS, tok_len, HEAD_DIM)
        tok_mixed = tok_mixed.reshape(HEADS, tok_len, HEAD_DIM)
        half_mixed = 0.5 * tok_mixed.astype(jnp.float32)
        half_low = half_mixed.astype(jnp.bfloat16)
        first_grad = half_mixed.transpose(1, 0, 2).reshape(tok_len, D)
        grad_normed = jnp.einsum(
            "hte,dhe->td", tok_queries, query_three, preferred_element_type=jnp.float32
        )
        grad_normed = grad_normed + jnp.einsum(
            "hte,dhe->td", tok_keys, key_three, preferred_element_type=jnp.float32
        )
        grad_normed = grad_normed + jnp.einsum(
            "hte,dhe->td", half_low, value_three, preferred_element_type=jnp.float32
        )
        grad_resid, attn_gain_grad = norm_backward(
            resid, attn_scale, gain_attn.astype(jnp.float32), grad_normed
        )
        input_grad = grad_resid + grad_middle
        updated = (gain_totals[0] + attn_gain_grad, gain_totals[1] + mlp_gain_grad)
        kept = (
            normed_low,
            tok_queries,
            tok_keys,
            half_low,
            attended,
            low_grad_middle,
            normed2_low,
            grad_gate,
            grad_up,
            active,
        )
        return (updated, (result, input_grad, first_grad, kept))

    gain_zeros = (jnp.zeros((D,), jnp.float32), jnp.zeros((D,), jnp.float32))
    gain_totals, stacked = lax.scan(layer_step, gain_zeros, (inputs, first_values, out_grad))
    outputs, input_grad, first_grad, kept = stacked
    (
        normed_all,
        queries_all,
        keys_all,
        half_all,
        attended_all,
        middle_all,
        normed2_all,
        gate_all,
        up_all,
        active_all,
    ) = kept
    query_grad = jnp.einsum(
        "mtd,mhte->dhe", normed_all, queries_all, preferred_element_type=jnp.float32
    ).reshape(D, D)
    key_grad = jnp.einsum(
        "mtd,mhte->dhe", normed_all, keys_all, preferred_element_type=jnp.float32
    ).reshape(D, D)
    value_grad = jnp.einsum(
        "mtd,mhte->dhe", normed_all, half_all, preferred_element_type=jnp.float32
    ).reshape(D, D)
    output_grad = jnp.einsum(
        "mhte,mto->heo", attended_all, middle_all, preferred_element_type=jnp.float32
    ).reshape(D, D)
    gate_grad = jnp.einsum("mtd,mtf->df", normed2_all, gate_all, preferred_element_type=jnp.float32)
    up_grad = jnp.einsum("mtd,mtf->df", normed2_all, up_all, preferred_element_type=jnp.float32)
    down_grad = jnp.einsum("mtf,mtd->fd", active_all, out_grad, preferred_element_type=jnp.float32)
    totals = (
        gain_totals[0],
        query_grad,
        key_grad,
        value_grad,
        output_grad,
        gain_totals[1],
        gate_grad,
        up_grad,
        down_grad,
    )
    rows = (
        lax.psum_scatter(
            totals[0].astype(jnp.bfloat16), "fsdp", scatter_dimension=0, tiled=True
        ).astype(jnp.float32),
        lax.psum_scatter(
            totals[1].astype(jnp.bfloat16), "fsdp", scatter_dimension=0, tiled=True
        ).astype(jnp.float32),
        lax.psum_scatter(
            totals[2].astype(jnp.bfloat16), "fsdp", scatter_dimension=0, tiled=True
        ).astype(jnp.float32),
        lax.psum_scatter(
            totals[3].astype(jnp.bfloat16), "fsdp", scatter_dimension=0, tiled=True
        ).astype(jnp.float32),
        lax.psum_scatter(
            totals[4].astype(jnp.bfloat16), "fsdp", scatter_dimension=0, tiled=True
        ).astype(jnp.float32),
        lax.psum_scatter(
            totals[5].astype(jnp.bfloat16), "fsdp", scatter_dimension=0, tiled=True
        ).astype(jnp.float32),
        lax.psum_scatter(
            totals[6].astype(jnp.bfloat16), "fsdp", scatter_dimension=0, tiled=True
        ).astype(jnp.float32),
        lax.psum_scatter(
            totals[7].astype(jnp.bfloat16), "fsdp", scatter_dimension=0, tiled=True
        ).astype(jnp.float32),
        lax.psum_scatter(
            totals[8].astype(jnp.bfloat16), "fsdp", scatter_dimension=0, tiled=True
        ).astype(jnp.float32),
    )
    final = (
        lax.psum(rows[0].astype(jnp.bfloat16), "seq").astype(jnp.float32),
        lax.psum(rows[1].astype(jnp.bfloat16), "seq").astype(jnp.float32),
        lax.psum(rows[2].astype(jnp.bfloat16), "seq").astype(jnp.float32),
        lax.psum(rows[3].astype(jnp.bfloat16), "seq").astype(jnp.float32),
        lax.psum(rows[4].astype(jnp.bfloat16), "seq").astype(jnp.float32),
        lax.psum(rows[5].astype(jnp.bfloat16), "seq").astype(jnp.float32),
        lax.psum(rows[6].astype(jnp.bfloat16), "seq").astype(jnp.float32),
        lax.psum(rows[7].astype(jnp.bfloat16), "seq").astype(jnp.float32),
        lax.psum(rows[8].astype(jnp.bfloat16), "seq").astype(jnp.float32),
    )
    return (
        outputs,
        input_grad,
        first_grad,
        final[0],
        final[5],
        final[1],
        final[2],
        final[3],
        final[4],
        final[6],
        final[7],
        final[8],
    )


def solution(mesh):
    return jax.shard_map(
        shards,
        mesh=mesh,
        in_specs=(
            P("fsdp", "seq", None),
            P("fsdp", "seq", None),
            P("fsdp", "seq", None),
            P("fsdp"),
            P("fsdp", None),
            P("fsdp", None),
            P("fsdp", None),
            P("fsdp", None),
            P("fsdp"),
            P("fsdp", None),
            P("fsdp", None),
            P("fsdp", None),
        ),
        out_specs=(
            P("fsdp", "seq", None),
            P("fsdp", "seq", None),
            P("fsdp", "seq", None),
            P("fsdp"),
            P("fsdp"),
            P("fsdp", None),
            P("fsdp", None),
            P("fsdp", None),
            P("fsdp", None),
            P("fsdp", None),
            P("fsdp", None),
            P("fsdp", None),
        ),
        check_vma=False,
    )
```

profile of v0, /device:TPU:25, one launch (start us, length us, event | category | flops | bytes accessed | tf_op | source)
XLA Modules:
  0.0 2199.6 jit_solution(1069465024235674960)
XLA Ops:
  11.6 1471.6 %while.55 = (s32[]{:T(128)}, f32[1024]{0:T(1024)}, f32[1024]{0:T(1024)}, f32[2,512,1024]{2,1,0:T(8,128)}, f32[2,512,1024]{2,1,0:T(8,128)}, /*index=5*/f32[2,512,...) while((s32[]{:T(128)}, f32[1024]{0:T(1024)}, ...), condition=%wide.region_19.20_spmd.clone.clone.clone.clone, body=%wide.region_0.19_spmd.clone.clone.clone.clone.sunk | while | flops 36053942272 | bytes 1585558656 | solution.py:307
  18.9 12.6 all-gather.10
  33.6 31.9 %all-gather.24.cloned.1.call-done = bf16[1024,1024]{0,1:T(8,128)(2,1)} async-done(((bf16[128,1024]{0,1:T(8,128)(2,1)}), bf16[1024,1024]{0,1:T(8,128)(2,1)}) %all-gather.24.cloned.1.call-update) | async-done | bytes 2097168 | tf_op jit(solution)/shard_map/while/body/eval_jaxpr/all_gather | solution.py:169
  69.8 47.2 %all-gather.22.cloned.1.call-done = bf16[1024,1024]{0,1:T(8,128)(2,1)} async-done(((bf16[128,1024]{0,1:T(8,128)(2,1)}), bf16[1024,1024]{0,1:T(8,128)(2,1)}) %all-gather.22.cloned.1.call-update) | async-done | bytes 2097168 | tf_op jit(solution)/shard_map/while/body/eval_jaxpr/all_gather | solution.py:168
  144.6 12.2 all-gather.11
  283.8 28.3 %all-gather.30.cloned.1.call-done = bf16[2816,1024]{1,0:T(8,128)(2,1)} async-done(((bf16[352,1024]{1,0:T(8,128)(2,1)}), bf16[2816,1024]{1,0:T(8,128)(2,1)}) %all-gather.30.cloned.1.call-update) | async-done | bytes 5767184 | tf_op jit(solution)/shard_map/while/body/eval_jaxpr/all_gather | solution.py:175
  320.8 84.4 %all-gather.28.cloned.1.call-done = bf16[1024,2816]{1,0:T(8,128)(2,1)} async-done(((bf16[128,2816]{1,0:T(8,128)(2,1)}), bf16[1024,2816]{1,0:T(8,128)(2,1)}) %all-gather.28.cloned.1.call-update) | async-done | bytes 5767184 | tf_op jit(solution)/shard_map/while/body/eval_jaxpr/all_gather | solution.py:173
  413.8 84.7 %all-gather.32.cloned.1.call-done = bf16[1024,2816]{1,0:T(8,128)(2,1)} async-done(((bf16[128,2816]{1,0:T(8,128)(2,1)}), bf16[1024,2816]{1,0:T(8,128)(2,1)}) %all-gather.32.cloned.1.call-update) | async-done | bytes 5767184 | tf_op jit(solution)/shard_map/while/body/eval_jaxpr/all_gather | solution.py:174
  498.5 13.0 bitcast_dynamic-update-slice_fusion.11
  764.9 31.9 %all-gather.24.cloned.1.call-done = bf16[1024,1024]{0,1:T(8,128)(2,1)} async-done(((bf16[128,1024]{0,1:T(8,128)(2,1)}), bf16[1024,1024]{0,1:T(8,128)(2,1)}) %all-gather.24.cloned.1.call-update) | async-done | bytes 2097168 | tf_op jit(solution)/shard_map/while/body/eval_jaxpr/all_gather | solution.py:169
  801.1 47.2 %all-gather.22.cloned.1.call-done = bf16[1024,1024]{0,1:T(8,128)(2,1)} async-done(((bf16[128,1024]{0,1:T(8,128)(2,1)}), bf16[1024,1024]{0,1:T(8,128)(2,1)}) %all-gather.22.cloned.1.call-update) | async-done | bytes 2097168 | tf_op jit(solution)/shard_map/while/body/eval_jaxpr/all_gather | solution.py:168
  875.8 12.2 all-gather.11
  1014.9 28.6 %all-gather.30.cloned.1.call-done = bf16[2816,1024]{1,0:T(8,128)(2,1)} async-done(((bf16[352,1024]{1,0:T(8,128)(2,1)}), bf16[2816,1024]{1,0:T(8,128)(2,1)}) %all-gather.30.cloned.1.call-update) | async-done | bytes 5767184 | tf_op jit(solution)/shard_map/while/body/eval_jaxpr/all_gather | solution.py:175
  1052.2 84.6 %all-gather.28.cloned.1.call-done = bf16[1024,2816]{1,0:T(8,128)(2,1)} async-done(((bf16[128,2816]{1,0:T(8,128)(2,1)}), bf16[1024,2816]{1,0:T(8,128)(2,1)}) %all-gather.28.cloned.1.call-update) | async-done | bytes 5767184 | tf_op jit(solution)/shard_map/while/body/eval_jaxpr/all_gather | solution.py:173
  1145.3 84.5 %all-gather.32.cloned.1.call-done = bf16[1024,2816]{1,0:T(8,128)(2,1)} async-done(((bf16[128,2816]{1,0:T(8,128)(2,1)}), bf16[1024,2816]{1,0:T(8,128)(2,1)}) %all-gather.32.cloned.1.call-update) | async-done | bytes 5767184 | tf_op jit(solution)/shard_map/while/body/eval_jaxpr/all_gather | solution.py:174
  1229.9 13.1 bitcast_dynamic-update-slice_fusion.11
  1555.4 70.2 %reduce-scatter.10.cloned.1.call-done = bf16[128,1024]{1,0:T(8,128)(2,1)} async-done(((bf16[1024,1024]{1,0:T(8,128)(2,1)}), bf16[128,1024]{1,0:T(8,128)(2,1)}) %reduce-scatter.10.cloned.1.call-update) | async-done | bytes 262160 | tf_op jit(solution)/shard_map/reduce_scatter | solution.py:354
  1625.6 70.1 %reduce-scatter.12.cloned.1.call-done = bf16[128,1024]{1,0:T(8,128)(2,1)} async-done(((bf16[1024,1024]{1,0:T(8,128)(2,1)}), bf16[128,1024]{1,0:T(8,128)(2,1)}) %reduce-scatter.12.cloned.1.call-update) | async-done | bytes 262160 | tf_op jit(solution)/shard_map/reduce_scatter | solution.py:357
  1695.8 70.4 %reduce-scatter.14.cloned.1.call-done = bf16[128,1024]{1,0:T(8,128)(2,1)} async-done(((bf16[1024,1024]{1,0:T(8,128)(2,1)}), bf16[128,1024]{1,0:T(8,128)(2,1)}) %reduce-scatter.14.cloned.1.call-update) | async-done | bytes 262160 | tf_op jit(solution)/shard_map/reduce_scatter | solution.py:360
  1766.1 114.1 %reduce-scatter.20.cloned.1.call-done = bf16[352,1024]{1,0:T(8,128)(2,1)} async-done(((bf16[2816,1024]{1,0:T(8,128)(2,1)}), bf16[352,1024]{1,0:T(8,128)(2,1)}) %reduce-scatter.20.cloned.1.call-update) | async-done | bytes 720912 | tf_op jit(solution)/shard_map/reduce_scatter | solution.py:372
  1880.2 113.1 %reduce-scatter.18.cloned.1.call-done = bf16[128,2816]{1,0:T(8,128)(2,1)} async-done(((bf16[1024,2816]{1,0:T(8,128)(2,1)}), bf16[128,2816]{1,0:T(8,128)(2,1)}) %reduce-scatter.18.cloned.1.call-update) | async-done | bytes 720912 | tf_op jit(solution)/shard_map/reduce_scatter | solution.py:369
  1993.3 113.0 %reduce-scatter.16.cloned.1.call-done = bf16[128,2816]{1,0:T(8,128)(2,1)} async-done(((bf16[1024,2816]{1,0:T(8,128)(2,1)}), bf16[128,2816]{1,0:T(8,128)(2,1)}) %reduce-scatter.16.cloned.1.call-update) | async-done | bytes 720912 | tf_op jit(solution)/shard_map/reduce_scatter | solution.py:366
  2107.7 13.3 all-reduce.4
  2131.6 48.5 %all-reduce.9.cloned.1.call-done = (bf16[128,1024]{1,0:T(8,128)(2,1)}, bf16[128,1024]{1,0:T(8,128)(2,1)}, bf16[128,1024]{1,0:T(8,128)(2,1)}, bf16[128,1024]{1,0:...) async-done(((bf16[128,1024]{1,0:T(8,128)(2,1)}, bf16[128,1024]{1,0:T(8,128)(2,1)}, bf16[128,1024]{1,0:T(8,128)(2,1)}, ...) | async-done | bytes 3211280 | tf_op jit(solution)/shard_map/psum | solution.py:378
  (790 shorter events, 943.0 us)
Async XLA Ops:
  12.0 53.5 %all-gather.24.cloned.1.call-start = ((), (), s32[]{:S(2)}) async-start(), calls=%async_computation.25 | async-start | bytes 2359296 | tf_op jit(solution)/shard_map/while/body/eval_jaxpr/all_gather | solution.py:169
  12.8 104.2 %all-gather.22.cloned.1.call-start = ((), (), s32[]{:S(2)}) async-start(), calls=%async_computation.24 | async-start | bytes 2359296 | tf_op jit(solution)/shard_map/while/body/eval_jaxpr/all_gather | solution.py:168
  13.5 155.5 %all-gather.20.cloned.1.call-start = ((), (), s32[]{:S(2)}) async-start(), calls=%async_computation.23 | async-start | bytes 2359296 | tf_op jit(solution)/shard_map/while/body/eval_jaxpr/all_gather | solution.py:170
  14.3 264.1 %all-gather.26.cloned.1.call-start = ((), (), s32[]{:S(2)}) async-start(), calls=%async_computation.26 | async-start | bytes 2359296 | tf_op jit(solution)/shard_map/while/body/eval_jaxpr/all_gather | solution.py:171
  14.8 297.3 %all-gather.30.cloned.1.call-start = ((), (), s32[]{:S(2)}) async-start(), calls=%async_computation.28 | async-start | bytes 6488064 | tf_op jit(solution)/shard_map/while/body/eval_jaxpr/all_gather | solution.py:175
  15.4 389.8 %all-gather.28.cloned.1.call-start = ((), (), s32[]{:S(2)}) async-start(), calls=%async_computation.27 | async-start | bytes 6488064 | tf_op jit(solution)/shard_map/while/body/eval_jaxpr/all_gather | solution.py:173
  16.0 482.5 %all-gather.32.cloned.1.call-start = ((), (), s32[]{:S(2)}) async-start(), calls=%async_computation.29 | async-start | bytes 6488064 | tf_op jit(solution)/shard_map/while/body/eval_jaxpr/all_gather | solution.py:174
  682.4 34.8 %all-to-all-start.7 = ((bf16[4,2,65536]{2,1,0:T(2,128)(2,1)}), bf16[4,2,65536]{2,1,0:T(2,128)(2,1)}, u32[]{:S(2)}, u32[]{:S(2)}) async-start(bf16[4,2,65536]{2,1,0:T(2,128)(2,1)} %reshape.1169), calls=%async_computation.7 | async-start | bytes 2097152 | tf_op jit(solution)/shard_map/while/body/eval_jaxpr/all_to_all | solution.py:268
  744.3 52.4 %all-gather.24.cloned.1.call-start = ((), (), s32[]{:S(2)}) async-start(), calls=%async_computation.25 | async-start | bytes 2359296 | tf_op jit(solution)/shard_map/while/body/eval_jaxpr/all_gather | solution.py:169
  745.0 103.2 %all-gather.22.cloned.1.call-start = ((), (), s32[]{:S(2)}) async-start(), calls=%async_computation.24 | async-start | bytes 2359296 | tf_op jit(solution)/shard_map/while/body/eval_jaxpr/all_gather | solution.py:168
  745.8 154.3 %all-gather.20.cloned.1.call-start = ((), (), s32[]{:S(2)}) async-start(), calls=%async_computation.23 | async-start | bytes 2359296 | tf_op jit(solution)/shard_map/while/body/eval_jaxpr/all_gather | solution.py:170
  746.4 263.1 %all-gather.26.cloned.1.call-start = ((), (), s32[]{:S(2)}) async-start(), calls=%async_computation.26 | async-start | bytes 2359296 | tf_op jit(solution)/shard_map/while/body/eval_jaxpr/all_gather | solution.py:171
  747.1 296.4 %all-gather.30.cloned.1.call-start = ((), (), s32[]{:S(2)}) async-start(), calls=%async_computation.28 | async-start | bytes 6488064 | tf_op jit(solution)/shard_map/while/body/eval_jaxpr/all_gather | solution.py:175
  747.7 389.1 %all-gather.28.cloned.1.call-start = ((), (), s32[]{:S(2)}) async-start(), calls=%async_computation.27 | async-start | bytes 6488064 | tf_op jit(solution)/shard_map/while/body/eval_jaxpr/all_gather | solution.py:173
  748.4 481.5 %all-gather.32.cloned.1.call-start = ((), (), s32[]{:S(2)}) async-start(), calls=%async_computation.29 | async-start | bytes 6488064 | tf_op jit(solution)/shard_map/while/body/eval_jaxpr/all_gather | solution.py:174
  1413.9 34.8 %all-to-all-start.7 = ((bf16[4,2,65536]{2,1,0:T(2,128)(2,1)}), bf16[4,2,65536]{2,1,0:T(2,128)(2,1)}, u32[]{:S(2)}, u32[]{:S(2)}) async-start(bf16[4,2,65536]{2,1,0:T(2,128)(2,1)} %reshape.1169), calls=%async_computation.7 | async-start | bytes 2097152 | tf_op jit(solution)/shard_map/while/body/eval_jaxpr/all_to_all | solution.py:268
  1483.2 72.2 %reduce-scatter.8.cloned.1.call-start = ((), (), s32[]{:S(2)}) async-start(), calls=%async_computation.15 | async-start | bytes 2359296 | tf_op jit(solution)/shard_map/reduce_scatter | solution.py:351
  1490.5 135.2 %reduce-scatter.10.cloned.1.call-start = ((), (), s32[]{:S(2)}) async-start(), calls=%async_computation.16 | async-start | bytes 2359296 | tf_op jit(solution)/shard_map/reduce_scatter | solution.py:354
  1497.7 198.1 %reduce-scatter.12.cloned.1.call-start = ((), (), s32[]{:S(2)}) async-start(), calls=%async_computation.17 | async-start | bytes 2359296 | tf_op jit(solution)/shard_map/reduce_scatter | solution.py:357
  1505.7 260.5 %reduce-scatter.14.cloned.1.call-start = ((), (), s32[]{:S(2)}) async-start(), calls=%async_computation.18 | async-start | bytes 2359296 | tf_op jit(solution)/shard_map/reduce_scatter | solution.py:360
  1511.9 368.4 %reduce-scatter.20.cloned.1.call-start = ((), (), s32[]{:S(2)}) async-start(), calls=%async_computation.21 | async-start | bytes 6488064 | tf_op jit(solution)/shard_map/reduce_scatter | solution.py:372
  1523.0 470.4 %reduce-scatter.18.cloned.1.call-start = ((), (), s32[]{:S(2)}) async-start(), calls=%async_computation.20 | async-start | bytes 6488064 | tf_op jit(solution)/shard_map/reduce_scatter | solution.py:369
  1534.2 572.2 %reduce-scatter.16.cloned.1.call-start = ((), (), s32[]{:S(2)}) async-start(), calls=%async_computation.19 | async-start | bytes 6488064 | tf_op jit(solution)/shard_map/reduce_scatter | solution.py:366
  1545.2 634.9 %all-reduce.9.cloned.1.call-start = ((), (), s32[]{:S(2)}) async-start(), calls=%async_computation.22 | async-start | bytes 6422528 | tf_op jit(solution)/shard_map/psum | solution.py:378
  (218 other events, 4883.8 us)
Sparse Core Ops, SparseCore 0:
  15.1 50.3 all-gather.23
  67.7 49.2 all-gather.21
  119.8 49.0 all-gather.19
  171.2 47.5 all-gather.25
  221.1 90.9 all-gather.29
  314.4 90.8 all-gather.27
  407.6 90.8 all-gather.31
  747.4 49.2 all-gather.23
  799.0 49.2 all-gather.21
  850.9 49.1 all-gather.19
  902.4 47.7 all-gather.25
  952.5 90.9 all-gather.29
  1045.9 90.8 all-gather.27
  1139.0 90.8 all-gather.31
Sparse Core Ops, SparseCore 1:
  1490.5 64.8 reduce-scatter.7
  1558.8 66.7 reduce-scatter.9
  1629.1 66.7 reduce-scatter.11
  1699.3 66.7 reduce-scatter.13
  1769.8 110.3 reduce-scatter.19
  1883.9 109.4 reduce-scatter.17
  1996.9 109.4 reduce-scatter.15
  2109.1 71.0 all-reduce.8
where the time goes:
time: 2210 us; the launch traced here: 2200 us
  waiting for transfers between devices  1230 us (56%)
  matrix products  433 us (20%)
  local copies, waits for them, and re-layouts  218 us (10%)
  other arithmetic  143 us (6%)
  starting transfers between devices  74.7 us (3%)
  blocking collectives  71.3 us (3%)
    all_gather x2, waiting for transfers between devices, layer_step(): lax.all_gather(up_weight, 'fsdp', axis=0, tiled=True)  169 us
    all_gather x2, waiting for transfers between devices, layer_step(): lax.all_gather(gate_weight, 'fsdp', axis=0, tiled=True)  169 us
    reduce_scatter x1, waiting for transfers between devices, shards(): lax.psum_scatter(totals[8].astype(jnp.bfloat16), 'fsdp', scatter_dimensio...  114 us
    reduce_scatter x1, waiting for transfers between devices, shards(): lax.psum_scatter(totals[7].astype(jnp.bfloat16), 'fsdp', scatter_dimensio...  113 us
    reduce_scatter x1, waiting for transfers between devices, shards(): lax.psum_scatter(totals[6].astype(jnp.bfloat16), 'fsdp', scatter_dimensio...  113 us
    all_gather x2, waiting for transfers between devices, layer_step(): lax.all_gather(query_weight, 'fsdp', axis=0, tiled=True)  94.4 us
    while x412, local copies, waits for them, and re-layouts  90.3 us
    reduce_scatter x1, waiting for transfers between devices, shards(): lax.psum_scatter(totals[4].astype(jnp.bfloat16), 'fsdp', scatter_dimensio...  70.4 us
  transfers between devices with their start and end apart: 38, of which 30 were waited for; matrix products, arithmetic and copies ran while one was open for 22% of the time, Pallas kernels for 0%

commit v1 on v0

v1 whole, which is shorter than its diff:
```python
import functools

import jax
import jax.numpy as jnp
from jax import lax
from jax.experimental import pallas as pl
from jax.experimental.pallas import tpu as pltpu
from jax.sharding import PartitionSpec as P

D = 1024
HEADS = 16
HEAD_DIM = 64
HALF = HEAD_DIM // 2
PAIR = 2 * HEAD_DIM
F32 = jnp.float32
BF16 = jnp.bfloat16
NEG = -1e30
MIB = 1024 * 1024
epsilon = 1e-06
rope_base = 10000.0


def dot(a, b):
    return lax.dot_general(a, b, (((1,), (0,)), ((), ())), preferred_element_type=F32)


def head_rows(value, head):
    row = lax.broadcasted_iota(jnp.int32, value.shape, 0)
    return jnp.where((row // HEAD_DIM) == head, value, jnp.zeros_like(value))


def head_lanes(value, head):
    lane = lax.broadcasted_iota(jnp.int32, value.shape, 1)
    return jnp.where((lane // HEAD_DIM) == head, value, jnp.zeros_like(value))


def causal(scores):
    side = scores.shape[0]
    square = scores[:, :side]
    key = lax.broadcasted_iota(jnp.int32, square.shape, 0)
    query = lax.broadcasted_iota(jnp.int32, square.shape, 1)
    square = jnp.where(key <= query, square, NEG)
    if scores.shape[1] == side:
        return square
    return jnp.concatenate([square, scores[:, side:]], axis=1)


def attend_kernel(count, slots, tok, tile_k, order, *refs):
    pieces = refs[:count]
    outs = refs[count : 2 * count]
    lse_ref = refs[2 * count]
    qz, kn, vt, ot = refs[2 * count + 1 :]
    for source in range(count):
        for slot in range(slots):
            cols = pl.ds(pl.multiple_of(order[source * slots + slot] * tok, tok), tok)
            take = slice(slot * tok, (slot + 1) * tok)
            query = pieces[source][0, :, take] * jnp.asarray(HEAD_DIM**-0.5, BF16)
            for head in range(2):
                qz[head, :, cols] = head_rows(query, head)
            kn[cols, :] = pieces[source][1, :, take].T
            vt[:, cols] = pieces[source][2, :, take]
    length = count * slots * tok


    def score(sub, head):
        start = sub * tile_k
        return causal(dot(kn[start : start + tile_k, :], qz[head, :, start:]))

    def absorb(sub, head, carry, scores):
        peak, total, mixed = carry
        start = sub * tile_k
        new_peak = jnp.maximum(peak, jnp.max(scores, axis=0, keepdims=True))
        weights = jnp.exp(scores - new_peak)
        fade = jnp.exp(peak - new_peak)
        total = total * fade + jnp.sum(weights, axis=0, keepdims=True)
        values = vt[head * HEAD_DIM : (head + 1) * HEAD_DIM, start : start + tile_k]
        mixed = mixed * fade + dot(values, weights.astype(BF16))
        return (new_peak, total, mixed)

    tiles = [(sub, head) for sub in range(length // tile_k) for head in range(2)]
    carries = [
        (
            jnp.full((1, length), NEG, F32),
            jnp.zeros((1, length), F32),
            jnp.zeros((HEAD_DIM, length), F32),
        )
        for _ in range(2)
    ]
    ahead = score(*tiles[0])
    for number, (sub, head) in enumerate(tiles):
        scores = ahead
        if number + 1 < len(tiles):
            ahead = score(*tiles[number + 1])
        peak, total, mixed = absorb(sub, head, carries[head], scores)
        done = slice(sub * tile_k, (sub + 1) * tile_k)
        rows = slice(head * HEAD_DIM, (head + 1) * HEAD_DIM)
        ot[rows, done] = (mixed[:, :tile_k] / total[:, :tile_k]).astype(BF16)
        lse_ref[0, head : head + 1, done] = peak[:, :tile_k] + jnp.log(total[:, :tile_k])
        carries[head] = (peak[:, tile_k:], total[:, tile_k:], mixed[:, tile_k:])
    for source in range(count):
        for slot in range(slots):
            cols = pl.ds(pl.multiple_of(order[source * slots + slot] * tok, tok), tok)
            outs[source][:, slot * tok : (slot + 1) * tok] = ot[:, cols]


def attend(pieces, order, slots):
    count = len(pieces)
    width, span = pieces[0].shape[1:]
    tok = span // slots
    length = count * span
    pairs = width // PAIR
    tile_k = min(256, length)
    grid_spec = pltpu.PrefetchScalarGridSpec(
        num_scalar_prefetch=1,
        grid=(pairs,),
        in_specs=[pl.BlockSpec((3, PAIR, span), lambda p, o: (0, p, 0))] * count,
        out_specs=[pl.BlockSpec((PAIR, span), lambda p, o: (p, 0))] * count
        + [pl.BlockSpec((1, 8, length), lambda p, o: (p, 0, 0))],
        scratch_shapes=[
            pltpu.VMEM((2, PAIR, length), BF16),
            pltpu.VMEM((length, PAIR), BF16),
            pltpu.VMEM((PAIR, length), BF16),
            pltpu.VMEM((PAIR, length), BF16),
        ],
    )
    area = pairs * 2 * length * length // 2
    results = pl.pallas_call(
        functools.partial(attend_kernel, count, slots, tok, tile_k),
        out_shape=[jax.ShapeDtypeStruct((width, span), BF16)] * count
        + [jax.ShapeDtypeStruct((pairs, 8, length), F32)],
        grid_spec=grid_spec,
        compiler_params=pltpu.CompilerParams(
            dimension_semantics=("arbitrary",), vmem_limit_bytes=48 * MIB
        ),
        cost_estimate=pl.CostEstimate(
            flops=area * 1024, bytes_accessed=8 * width * length, transcendentals=area
        ),
        name="attend",
    )(order, *pieces)
    return (results[:count], results[count])


def attend_back_kernel(count, slots, tok, tile_q, tile_k, order, *refs):
    pieces = refs[:count]
    mixes = refs[count : 2 * count]
    grads = refs[2 * count : 3 * count]
    lse_ref, cos_ref, sin_ref = refs[3 * count : 3 * count + 3]
    outs = refs[3 * count + 3 : 4 * count + 3]
    qz, gz, qn, gn, kn, vn, kt, inner, dq, dk, dv = refs[4 * count + 3 :]
    length = count * slots * tok
    for source in range(count):
        for slot in range(slots):
            cols = pl.ds(pl.multiple_of(order[source * slots + slot] * tok, tok), tok)
            take = slice(slot * tok, (slot + 1) * tok)
            query = pieces[source][0, :, take] * jnp.asarray(HEAD_DIM**-0.5, BF16)
            grad = grads[source][:, take]
            query_rows = query.T
            grad_rows = grad.T
            for head in range(2):
                qz[head, :, cols] = head_rows(query, head)
                gz[head, :, cols] = head_rows(grad, head)
                qn[head, cols, :] = head_lanes(query_rows, head)
                gn[head, cols, :] = head_lanes(grad_rows, head)
            key = pieces[source][1, :, take]
            kt[:, cols] = key
            kn[cols, :] = key.T
            vn[cols, :] = pieces[source][2, :, take].T
            both = grad.astype(F32) * mixes[source][:, take].astype(F32)
            for head in range(2):
                inner[head : head + 1, cols] = jnp.sum(
                    both[head * HEAD_DIM : (head + 1) * HEAD_DIM], axis=0, keepdims=True
                )
    dq[...] = jnp.zeros_like(dq)
    steps = tile_q // tile_k

    def tile(key_start, query_start, width, masked, carry):
        grad_keys, grad_values = carry
        keys = kn[pl.ds(key_start, tile_k), :]
        values = vn[pl.ds(key_start, tile_k), :]
        cols = pl.ds(query_start, width)
        for head in range(2):
            rows = slice(head * HEAD_DIM, (head + 1) * HEAD_DIM)
            scores = dot(keys, qz[head, :, cols])
            if masked:
                scores = causal(scores)
            probs = jnp.exp(scores - lse_ref[0, head : head + 1, cols])
            grad_probs = dot(values, gz[head, :, cols])
            grad_scores = (probs * (grad_probs - inner[head : head + 1, cols])).astype(BF16)
            grad_values = grad_values + dot(probs.astype(BF16), gn[head, cols, :])
            grad_keys = grad_keys + dot(grad_scores, qn[head, cols, :])
            dq[rows, cols] += dot(kt[rows, pl.ds(key_start, tile_k)], grad_scores)
        return (grad_keys, grad_values)

    def one(number, _):
        base = pl.multiple_of(number * tile_q, tile_q)
        for sub in range(steps):
            skip = sub * tile_k
            key_start = pl.multiple_of(base + skip, tile_k)
            carry = (jnp.zeros((tile_k, PAIR), F32), jnp.zeros((tile_k, PAIR), F32))
            carry = tile(key_start, key_start, tile_q - skip, True, carry)

            def body(step, carry):
                return tile(
                    key_start, pl.multiple_of(step * tile_q, tile_q), tile_q, False, carry
                )

            carry = lax.fori_loop(number + 1, length // tile_q, body, carry)
            dk[pl.ds(key_start, tile_k), :] = carry[0]
            dv[pl.ds(key_start, tile_k), :] = carry[1]
        return 0

    lax.fori_loop(0, length // tile_q, one, 0)
    half = HEAD_DIM // 2
    for source in range(count):
        for slot in range(slots):
            cols = pl.ds(pl.multiple_of(order[source * slots + slot] * tok, tok), tok)
            take = slice(slot * tok, (slot + 1) * tok)
            cosine = cos_ref[:, cols]
            sine = sin_ref[:, cols]
            for which, grad in enumerate((dq[:, cols] * (HEAD_DIM**-0.5), dk[cols, :].T)):
                for head in range(2):
                    low = head * HEAD_DIM
                    first = grad[low : low + half]
                    second = grad[low + half : low + 2 * half]
                    outs[source][which, low : low + half, take] = (
                        first * cosine + second * sine
                    ).astype(BF16)
                    outs[source][which, low + half : low + 2 * half, take] = (
                        second * cosine - first * sine
                    ).astype(BF16)
            outs[source][2, :, take] = dv[cols, :].T.astype(BF16)


def attend_back(pieces, mixes, grads, lse, cosine, sine, order, slots):
    count = len(pieces)
    width, span = pieces[0].shape[1:]
    tok = span // slots
    length = count * span
    pairs = width // PAIR
    tile_q = min(512, length)
    tile_k = min(256, length)
    triple = pl.BlockSpec((3, PAIR, span), lambda p, o: (0, p, 0))
    single = pl.BlockSpec((PAIR, span), lambda p, o: (p, 0))
    table = pl.BlockSpec((HEAD_DIM // 2, length), lambda p, o: (0, 0))
    grid_spec = pltpu.PrefetchScalarGridSpec(
        num_scalar_prefetch=1,
        grid=(pairs,),
        in_specs=[triple] * count
        + [single] * (2 * count)
        + [pl.BlockSpec((1, 8, length), lambda p, o: (p, 0, 0)), table, table],
        out_specs=[triple] * count,
        scratch_shapes=[
            pltpu.VMEM((2, PAIR, length), BF16),
            pltpu.VMEM((2, PAIR, length), BF16),
            pltpu.VMEM((2, length, PAIR), BF16),
            pltpu.VMEM((2, length, PAIR), BF16),
            pltpu.VMEM((length, PAIR), BF16),
            pltpu.VMEM((length, PAIR), BF16),
            pltpu.VMEM((PAIR, length), BF16),
            pltpu.VMEM((8, length), F32),
            pltpu.VMEM((PAIR, length), F32),
            pltpu.VMEM((length, PAIR), F32),
            pltpu.VMEM((length, PAIR), F32),
        ],
    )
    area = pairs * 2 * length * length // 2
    return pl.pallas_call(
        functools.partial(attend_back_kernel, count, slots, tok, tile_q, tile_k),
        out_shape=[jax.ShapeDtypeStruct((3, width, span), BF16)] * count,
        grid_spec=grid_spec,
        compiler_params=pltpu.CompilerParams(
            dimension_semantics=("arbitrary",), vmem_limit_bytes=56 * MIB
        ),
        cost_estimate=pl.CostEstimate(
            flops=area * 2560, bytes_accessed=16 * width * length, transcendentals=area
        ),
        name="attend_back",
    )(order, *pieces, *mixes, *grads, lse, cosine, sine)


def project_kernel(count, per, wide, place, x_ref, gain_ref, w_ref, first_ref, cos_ref, sin_ref, *refs):
    outs = refs[:count]
    normed_ref = refs[count]
    step = pl.program_id(0)
    kind = (step // per) % 3
    target = step // (3 * per)

    @pl.when(step == 0)
    def _():
        values = x_ref[...].astype(F32)
        scale = lax.rsqrt(jnp.mean(values * values, axis=1, keepdims=True) + epsilon)
        normed_ref[...] = (values * scale * gain_ref[...].astype(F32)).astype(BF16)

    raw = lax.dot_general(
        w_ref[...].T, normed_ref[...], (((1,), (1,)), ((), ())), preferred_element_type=F32
    )

    def store(value):
        for number in range(count):

            @pl.when(target == number)
            def _(number=number):
                outs[number][0] = value

    @pl.when(kind < 2)
    def _():
        parts = raw.reshape(wide // HEAD_DIM, 2, HALF, raw.shape[1])
        first, second = parts[:, 0], parts[:, 1]
        cosine, sine = cos_ref[...][None], sin_ref[...][None]
        turned = jnp.stack(
            [first * cosine - second * sine, first * sine + second * cosine], axis=1
        )
        store(turned.reshape(raw.shape).astype(BF16))

    @pl.when(kind == 2)
    def _():
        store((0.5 * raw + 0.5 * first_ref[...].T.astype(F32)).astype(BF16))


def project(x, gain, weight, first, cosine, sine, rank, count):
    span, depth = x.shape
    width = depth // count
    wide = min(width, 512)
    per = width // wide
    stride = depth // wide

    def column(step, place):
        return ((place[0] + 1 + step // (3 * per)) % count) * per + step % per

    def out_map(number):
        def index(step, place):
            local = jnp.clip(step - number * 3 * per, 0, 3 * per - 1)
            return (local // per, local % per, 0)

        return index

    grid_spec = pltpu.PrefetchScalarGridSpec(
        num_scalar_prefetch=1,
        grid=(count * 3 * per,),
        in_specs=[
            pl.BlockSpec((span, depth), lambda s, p: (0, 0)),
            pl.BlockSpec((1, depth), lambda s, p: (0, 0)),
            pl.BlockSpec((depth, wide), lambda s, p: (0, ((s // per) % 3) * stride + column(s, p))),
            pl.BlockSpec((span, wide), lambda s, p: (0, column(s, p))),
            pl.BlockSpec((HALF, span), lambda s, p: (0, 0)),
            pl.BlockSpec((HALF, span), lambda s, p: (0, 0)),
        ],
        out_specs=[pl.BlockSpec((1, wide, span), out_map(number)) for number in range(count)]
        + [pl.BlockSpec((span, depth), lambda s, p: (0, 0))],
    )
    results = pl.pallas_call(
        functools.partial(project_kernel, count, per, wide),
        out_shape=[jax.ShapeDtypeStruct((3, width, span), BF16)] * count
        + [jax.ShapeDtypeStruct((span, depth), BF16)],
        grid_spec=grid_spec,
        compiler_params=pltpu.CompilerParams(
            dimension_semantics=("arbitrary",), vmem_limit_bytes=48 * MIB
        ),
        cost_estimate=pl.CostEstimate(
            flops=6 * span * depth * depth,
            bytes_accessed=2 * (5 * span * depth + 3 * depth * depth),
            transcendentals=0,
        ),
        name="project",
    )(rank, x, gain, weight, first, cosine, sine)
    return (results[:count], results[count])


def norm_backward(values, scale, gain, grad_normed):
    weighted = grad_normed * gain
    inner = jnp.mean(weighted * values, axis=-1, keepdims=True)
    grad_values = scale * weighted - values * (scale * scale * scale) * inner
    grad_gain = jnp.sum(grad_normed * values * scale, axis=0)
    return (grad_values, grad_gain)


def inverse_rms(values):
    return lax.rsqrt(jnp.mean(values * values, axis=-1, keepdims=True) + epsilon)


def mm(subscripts, a, b):
    return jnp.einsum(subscripts, a, b, preferred_element_type=F32)


def shards(
    inputs,
    first_values,
    out_grad,
    attn_gain,
    query_weight,
    key_weight,
    value_weight,
    output_weight,
    mlp_gain,
    gate_weight,
    up_weight,
    down_weight,
):
    slots, tok, _ = inputs.shape
    groups = lax.axis_size("seq")
    count = groups // slots
    length = tok * groups
    span = slots * tok
    seat = lax.axis_index("seq")
    side = seat // count
    rank = seat % count
    width = D // count
    both = ("fsdp", "seq")

    def to_sequence(values):
        taken = [lax.dynamic_index_in_dim(values, side, 0, keepdims=False)]
        for jump in range(1, slots):
            sent = lax.dynamic_index_in_dim(values, (side + jump) % slots, 0, keepdims=False)
            pairs = [(i, (i + jump * count) % groups) for i in range(groups)]
            taken.append(lax.ppermute(sent, "seq", pairs))
        return jnp.concatenate(taken, axis=0)

    def to_home(values):
        rows = [values[:tok].astype(F32)]
        for jump in range(1, slots):
            sent = values[jump * tok : (jump + 1) * tok].astype(BF16)
            pairs = [((i + jump * count) % groups, i) for i in range(groups)]
            rows.append(lax.ppermute(sent, "seq", pairs).astype(F32))
        if slots == 2:
            swap = side == 1
            return jnp.stack([jnp.where(swap, rows[1], rows[0]), jnp.where(swap, rows[0], rows[1])])
        stacked = jnp.zeros((slots, tok, D), F32)
        for jump in range(slots):
            stacked = lax.dynamic_update_index_in_dim(
                stacked, rows[jump], (side + jump) % slots, 0
            )
        return stacked

    def exchange(pieces):
        received = []
        for jump in range(1, count):
            pairs = [
                (i, (i // count) * count + (i % count + jump) % count) for i in range(groups)
            ]
            received.append(lax.ppermute(pieces[jump - 1], "seq", pairs))
        return received + [pieces[count - 1]]

    def exchange_back(pieces):
        received = []
        for jump in range(1, count):
            pairs = [
                ((i // count) * count + (i % count + jump) % count, i) for i in range(groups)
            ]
            received.append(lax.ppermute(pieces[jump - 1], "seq", pairs))
        return received + [pieces[count - 1]]

    def join(pieces, axis):
        if count == 2:
            odd = rank == 1
            return jnp.concatenate(
                [
                    jnp.where(odd, pieces[0], pieces[1]),
                    jnp.where(odd, pieces[1], pieces[0]),
                ],
                axis=axis,
            )
        size = pieces[0].shape[axis]
        shape = list(pieces[0].shape)
        shape[axis] = size * count
        whole = jnp.zeros(shape, pieces[0].dtype)
        for number in range(count):
            whole = lax.dynamic_update_slice_in_dim(
                whole, pieces[number], ((rank + 1 + number) % count) * size, axis
            )
        return whole

    def gather(shard):
        part = shard.shape[0] // groups
        own = lax.dynamic_slice_in_dim(shard, seat * part, part, 0)
        return lax.all_gather(own, both, axis=0, tiled=True)

    def scatter(total):
        part = lax.psum_scatter(total.astype(BF16), both, scatter_dimension=0, tiled=True)
        return lax.all_gather(part, "seq", axis=0, tiled=True).astype(F32)

    steps = jnp.arange(slots, dtype=jnp.int32)
    starts = ((side - steps) % slots) * (count * tok) + rank * tok
    positions = (starts[:, None] + jnp.arange(tok, dtype=jnp.int32)[None]).reshape(span)
    freqs = rope_base ** (-(jnp.arange(HALF, dtype=F32) * 2.0 / HEAD_DIM))

    def tables(positions):
        angles = freqs[:, None] * positions.astype(F32)[None, :]
        return (jnp.cos(angles), jnp.sin(angles))

    cosine, sine = tables(positions)
    full_cos, full_sin = tables(jnp.arange(length, dtype=jnp.int32))
    sources = jnp.concatenate(
        [(rank - 1 - jnp.arange(count - 1, dtype=jnp.int32)) % count, rank[None]]
    ).astype(jnp.int32)
    order = (((side - steps) % slots)[None, :] * count + sources[:, None]).reshape(-1)
    order = order.astype(jnp.int32)

    qkv_weight = gather(jnp.concatenate([query_weight, key_weight, value_weight], axis=1))
    gains = lax.all_gather(
        jnp.stack([attn_gain, mlp_gain]), "fsdp", axis=1, tiled=True
    ).astype(F32)
    gain_attn, gain_mlp = gains[0:1], gains[1:2]
    tokens = to_sequence(inputs)
    firsts = to_sequence(first_values)
    grads = to_sequence(out_grad)
    output_full = gather(output_weight)
    gate_full = gather(gate_weight)
    up_full = gather(up_weight)
    down_full = gather(down_weight)

    resid = tokens.astype(F32)
    heads, normed_low = project(
        tokens, gain_attn.astype(BF16), qkv_weight, firsts, cosine, sine, rank[None], count
    )
    pieces = exchange(heads)
    mixes, lse = attend(pieces, order, slots)
    attended = join(exchange_back(mixes), 0)
    middle = resid + mm("ht,ho->to", attended, output_full)
    mlp_scale = inverse_rms(middle)
    normed2_low = (middle * mlp_scale * gain_mlp).astype(BF16)
    gate = mm("td,df->tf", normed2_low, gate_full)
    up_proj = mm("td,df->tf", normed2_low, up_full)
    sigma = jax.nn.sigmoid(gate)
    silu_gate = gate * sigma
    active = (silu_gate * up_proj).astype(BF16)
    outputs = middle + mm("tf,fd->td", active, down_full)
    grad_active = mm("td,fd->tf", grads, down_full)
    grad_gate = (grad_active * up_proj * sigma * (1.0 + gate * (1.0 - sigma))).astype(BF16)
    grad_up = (grad_active * silu_gate).astype(BF16)
    down_grad = mm("tf,td->fd", active, grads)
    gate_grad = mm("td,tf->df", normed2_low, grad_gate)
    up_grad = mm("td,tf->df", normed2_low, grad_up)
    grad_normed2 = mm("tf,df->td", grad_gate, gate_full) + mm("tf,df->td", grad_up, up_full)
    grad_middle, mlp_gain_grad = norm_backward(middle, mlp_scale, gain_mlp, grad_normed2)
    grad_middle = grad_middle + grads.astype(F32)
    low_grad_middle = grad_middle.astype(BF16)
    output_grad = mm("ht,to->ho", attended, low_grad_middle)
    grad_attended = mm("to,ho->ht", low_grad_middle, output_full).astype(BF16)
    grad_pieces = [
        lax.dynamic_slice_in_dim(grad_attended, ((rank + 1 + d) % count) * width, width, 0)
        for d in range(count)
    ]
    grad_heads = exchange(grad_pieces)
    back = attend_back(pieces, mixes, grad_heads, lse, full_cos, full_sin, order, slots)
    grad_qkv = join(exchange_back(back), 1)
    grad_query, grad_key, grad_mixed = grad_qkv[0], grad_qkv[1], grad_qkv[2]
    half_mixed = 0.5 * grad_mixed.astype(F32)
    half_low = half_mixed.astype(BF16)
    first_grad = half_mixed.T
    query_grad = mm("td,ct->dc", normed_low, grad_query)
    key_grad = mm("td,ct->dc", normed_low, grad_key)
    value_grad = mm("td,ct->dc", normed_low, half_low)
    grad_normed = mm("ct,dc->td", grad_query, qkv_weight[:, :D])
    grad_normed = grad_normed + mm("ct,dc->td", grad_key, qkv_weight[:, D : 2 * D])
    grad_normed = grad_normed + mm("ct,dc->td", half_low, qkv_weight[:, 2 * D :])
    grad_resid, attn_gain_grad = norm_backward(resid, inverse_rms(resid), gain_attn, grad_normed)
    input_grad = grad_resid + grad_middle
    gain_grads = lax.psum(jnp.stack([attn_gain_grad, mlp_gain_grad]), both)
    part = attn_gain.shape[0]
    gain_grads = lax.dynamic_slice_in_dim(gain_grads, lax.axis_index("fsdp") * part, part, 1)
    qkv_grad = scatter(jnp.concatenate([query_grad, key_grad, value_grad], axis=1))
    return (
        to_home(outputs),
        to_home(input_grad),
        to_home(first_grad),
        gain_grads[0],
        gain_grads[1],
        qkv_grad[:, :D],
        qkv_grad[:, D : 2 * D],
        qkv_grad[:, 2 * D :],
        scatter(output_grad),
        scatter(gate_grad),
        scatter(up_grad),
        scatter(down_grad),
    )


def solution(mesh):
    token_spec = P("fsdp", "seq", None)
    weight_spec = P("fsdp", None)
    gain_spec = P("fsdp")
    return jax.shard_map(
        shards,
        mesh=mesh,
        in_specs=(token_spec,) * 3
        + (gain_spec,)
        + (weight_spec,) * 4
        + (gain_spec,)
        + (weight_spec,) * 3,
        out_specs=(token_spec,) * 3 + (gain_spec,) * 2 + (weight_spec,) * 7,
        check_vma=False,
    )
```

time: 2210 us -> 1120 us (0.51)
  waiting for transfers between devices: 1230 us -> 538 us
  matrix products: 433 us -> 139 us
  local copies, waits for them, and re-layouts: 218 us -> 70 us
  Pallas kernels: 0 us -> 113 us
  blocking collectives: 71.3 us -> 166 us
  other arithmetic: 143 us -> 57.7 us
  starting transfers between devices: 74.7 us -> 10.4 us
    all_gather x14 -> x5, waiting for transfers between devices: 575 us -> 189 us  [gather(): return lax.all_gather(own, both, axis=0, tiled=True)]
    reduce_scatter x7 -> x5, waiting for transfers between devices: 561 us -> 265 us  [scatter(): lax.psum_scatter(total.astype(BF16), both, scatter_dimension=0, tiled=True)]
    dot_general x85 -> x18, matrix products: 412 us -> 139 us  [mm(): return jnp.einsum(subscripts, a, b, preferred_element_type=F32)]
    pallas_call x0 -> x3, Pallas kernels: none -> 113 us  [the longest x1 69.7 us: attend_back(): pl.pallas_call(functools.partial(attend_back_kernel, count, slots, tok, t...]
    while x412 -> x0, local copies, waits for them, and re-layouts: 90.3 us -> none
    ppermute x0 -> x10, waiting for transfers between devices: none -> 84.3 us  [the longest x3 39.1 us: to_home(): rows.append(lax.ppermute(sent, 'seq', pairs).astype(F32))]
    all_to_all x16 -> x0, starting transfers between devices: 73.8 us -> none  [the longest x2 10.2 us: layer_step(): lax.all_to_all(grad_mixed[None], 'seq', split_axis=2, concat_axis=0, tile...]
    convert_element_type x29 -> x6, other arithmetic: 73.1 us -> 4.89 us  [the longest x4 4.49 us: scatter(): return lax.all_gather(part, 'seq', axis=0, tiled=True).astype(F32)]
  transfers between devices with their start and end apart: 38 -> 20, of which waited for: 30 -> 13; matrix products, arithmetic and copies ran while one was open for 22% -> 18% of each run, Pallas kernels for 0% -> 10%
where the time goes in v1:
time: 1120 us; the launch traced here: 1110 us
  waiting for transfers between devices  538 us (48%)
  blocking collectives  166 us (15%)
  matrix products  139 us (12%)
  Pallas kernels  113 us (10%)
  local copies, waits for them, and re-layouts  70 us (6%)
  other arithmetic  57.7 us (5%)
  between operations  15.2 us (1%)
    reduce_scatter x5, waiting for transfers between devices, scatter(): lax.psum_scatter(total.astype(BF16), both, scatter_dimension=0, tiled=True)  265 us
    all_gather x5, waiting for transfers between devices, gather(): return lax.all_gather(own, both, axis=0, tiled=True)  189 us
    dot_general x18, matrix products, mm(): return jnp.einsum(subscripts, a, b, preferred_element_type=F32)  139 us
    all_gather x5, blocking collectives, scatter(): return lax.all_gather(part, 'seq', axis=0, tiled=True).astype(F32)  77.3 us
    psum x1, blocking collectives, shards(): gain_grads = lax.psum(jnp.stack([attn_gain_grad, mlp_gain_grad]), both)  76.5 us
    pallas_call x1, Pallas kernels, attend_back(): pl.pallas_call(functools.partial(attend_back_kernel, count, slots, tok, t...  69.7 us
    ppermute x3, waiting for transfers between devices, to_home(): rows.append(lax.ppermute(sent, 'seq', pairs).astype(F32))  39.1 us
    unnamed x81, local copies, waits for them, and re-layouts  39.1 us
  transfers between devices with their start and end apart: 20, of which 13 were waited for; matrix products, arithmetic and copies ran while one was open for 18% of the time, Pallas kernels for 10%

profile of v1, /device:TPU:25, one launch (start us, length us, event | category | flops | bytes accessed | tf_op | source)
XLA Modules:
  0.0 1110.4 jit_solution(16053604947612963369)
XLA Ops:
  26.1 12.4 %all_gather.33 = bf16[2,1024]{1,0:T(2,128)(2,1)S(1)} all-gather(bf16[2,128]{1,0:T(2,128)(2,1)S(1)} %pad_maximum_fusion.14), channel_id=1, replica_groups=mesh['fsdp'=8,'seq'=4] {'fsdp'}, dimensions={1}, use_global_device_ids=true | all-gather | bytes 4608 | tf_op jit(solution)/shard_map/all_gather | solution.py:499
  51.6 26.6 %collective-permute-done.1 = bf16[512,1024]{1,0:T(8,128)(2,1)} collective-permute-done((bf16[512,1024]{1,0:T(8,128)(2,1)}, bf16[512,1024]{1,0:T(8,128)(2,1)}, u32[]{:S(2)}, u32[]{:S(2)}) %collective-permute-start.1) | collective-permute-done | bytes 1048608 | tf_op jit(solution)/shard_map/ppermute | solution.py:415
  81.3 12.8 %all-gather.6.cloned.1.call-done.w_ref = bf16[1024,3072]{1,0:T(8,128)(2,1)} async-done(((bf16[32,3072]{1,0:T(8,128)(2,1)}), bf16[1024,3072]{1,0:T(8,128)(2,1)}) %all-gather.6.cloned.1.call-update) | async-done | bytes 6291472 | tf_op jit(solution)/shard_map/all_gather | solution.py:475
  94.0 15.1 %project.1 = (bf16[3,512,1024]{2,1,0:T(8,128)(2,1)}, bf16[3,512,1024]{2,1,0:T(8,128)(2,1)}, bf16[1024,1024]{1,0:T(8,128)(2,1)S(1)}) custom-call(s32[1]{0:T(128)} %bitcast.3.place, bf16[1024,1024]{1,0:T(8,128)(2,1)S(1)} %copy.43.x_ref, bf16[1,1024]{1,0:T(2,128)(2,1)S(1)} %bitcast.77, bf16[1024,3072]{1,0:T(8,128)(2,1)} %all-gather.6.cloned.1.call-done.w_ref, ...), custom_call_target="tpu_custom_call" | custom-call | flops 6442450944 | bytes 16777216 | tf_op jit(solution)/shard_map/project/pallas_call | solution.py:351
  116.5 28.6 %attend.1 = (bf16[512,1024]{1,0:T(8,128)(2,1)S(1)}, bf16[512,1024]{1,0:T(8,128)(2,1)S(1)}, f32[4,8,2048]{2,1,0:T(8,128)S(1)}) custom-call(s32[4]{0:T(128)S(1)} %add.199.order, bf16[3,512,1024]{2,1,0:T(8,128)(2,1)} %collective-permute-done.2.refs_0_, bf16[3,512,1024]{2,1,0:T(8,128)(2,1)} %get-tuple-element.21.refs_1_), custom_call_target="tpu_custom_call" | custom-call | flops 17179869184 | bytes 8388608 | tf_op jit(solution)/shard_map/attend/pallas_call | solution.py:127
  163.6 60.3 %all-gather.12.cloned.1.call-done = bf16[1024,2816]{1,0:T(8,128)(2,1)} async-done(((bf16[32,2816]{1,0:T(8,128)(2,1)}), bf16[1024,2816]{1,0:T(8,128)(2,1)}) %all-gather.12.cloned.1.call-update) | async-done | bytes 5767184 | tf_op jit(solution)/shard_map/all_gather | solution.py:475
  223.9 11.6 %fusion.46 = f32[1024,2816]{1,0:T(8,128)} fusion(bf16[1024,1024]{0,1:T(8,128)(2,1)S(1)} %multiply_convert_fusion.3, bf16[1024,2816]{1,0:T(8,128)(2,1)} %all-gather.12.cloned.1.call-done), kind=kOutput, calls=%fused_computation.134 | convolution fusion | flops 5905580032 | bytes 19398656 | tf_op jit(solution)/shard_map/td,df->tf/dot_general | solution.py:382
  235.5 58.0 %all-gather.10.cloned.1.call-done = bf16[1024,2816]{1,0:T(8,128)(2,1)} async-done(((bf16[32,2816]{1,0:T(8,128)(2,1)}), bf16[1024,2816]{1,0:T(8,128)(2,1)}) %all-gather.10.cloned.1.call-update) | async-done | bytes 5767184 | tf_op jit(solution)/shard_map/all_gather | solution.py:475
  293.4 11.8 %fusion.45 = f32[1024,2816]{1,0:T(8,128)} fusion(bf16[1024,1024]{0,1:T(8,128)(2,1)} %copy-done.22, bf16[1024,2816]{1,0:T(8,128)(2,1)} %all-gather.10.cloned.1.call-done), kind=kOutput, calls=%fused_computation.133 | convolution fusion | flops 5905580032 | bytes 19398656 | tf_op jit(solution)/shard_map/td,df->tf/dot_general | solution.py:382
  305.2 57.7 %all-gather.14.cloned.1.call-done = bf16[2816,1024]{1,0:T(8,128)(2,1)} async-done(((bf16[88,1024]{1,0:T(8,128)(2,1)}), bf16[2816,1024]{1,0:T(8,128)(2,1)}) %all-gather.14.cloned.1.call-update) | async-done | bytes 5767184 | tf_op jit(solution)/shard_map/all_gather | solution.py:475
  363.0 20.1 %multiply_convert_fusion = (bf16[1024,2816]{1,0:T(8,128)(2,1)}, bf16[1024,2816]{1,0:T(8,128)(2,1)}, bf16[1024,2816]{1,0:T(8,128)(2,1)}) fusion(f32[1024,2816]{1,0:T(8,128)} %fusion.45, f32[1024,2816]{1,0:T(8,128)} %fusion.46, bf16[2816,1024]{1,0:T(8,128)(2,1)} %all-gather.14.cloned.1.call-done, bf16[512,1024]{0,1:T(8,128)(2,1)} %collective-permute-done.5, ...), kind=kOutput, calls=%fused_computation | convolution fusion | flops 5953028096 | bytes 48234496 | tf_op jit(solution)/shard_map/td,fd->tf/dot_general | solution.py:382
  411.6 10.9 convolution_convert_fusion.2
  422.5 10.9 convolution_convert_fusion.1
  433.5 10.9 convolution_convert_fusion
  455.3 69.7 %attend_back.1 = (bf16[3,512,1024]{2,1,0:T(8,128)(2,1)}, bf16[3,512,1024]{2,1,0:T(8,128)(2,1)}) custom-call(s32[4]{0:T(128)} %copy-done.4, bf16[3,512,1024]{2,1,0:T(8,128)(2,1)} %collective-permute-done.2.refs_0_, bf16[3,512,1024]{2,1,0:T(8,128)(2,1)} %get-tuple-element.21.refs_1_, bf16[512,1024]{1,0:T(8,128)(2,1)} %copy-done.3, ...), custom_call_target="tpu_custom_call" | custom-call | flops 42949672960 | bytes 16777216 | tf_op jit(solution)/shard_map/attend_back/pallas_call | solution.py:267
  543.4 13.5 %pad_maximum_fusion = bf16[1024,3072]{0,1:T(8,128)(2,1)} fusion(bf16[1024,1024]{0,1:T(8,128)(2,1)S(1)} %convolution_convert_fusion.3, bf16[1024,1024]{0,1:T(8,128)(2,1)S(1)} %convolution_convert_fusion.4, bf16[1024,1024]{0,1:T(8,128)(2,1)S(1)} %convolution_convert_fusion.5), kind=kLoop, calls=%fused_computation.14 | loop fusion | flops 18874368 | bytes 12582912 | tf_op jit(solution)/shard_map/concatenate | solution.py:561
  581.0 39.1 %collective-permute-done.4 = bf16[512,1024]{0,1:T(8,128)(2,1)} collective-permute-done((bf16[512,1024]{0,1:T(8,128)(2,1)}, bf16[512,1024]{0,1:T(8,128)(2,1)}, u32[]{:S(2)}, u32[]{:S(2)}) %collective-permute-start.4) | collective-permute-done | bytes 1048608 | tf_op jit(solution)/shard_map/ppermute | solution.py:423
  648.0 30.5 %all_gather.40 = bf16[128,1024]{1,0:T(8,128)(2,1)S(1)} all-gather(bf16[32,1024]{1,0:T(8,128)(2,1)} %reduce-scatter.8.cloned.1.call-done), channel_id=1, replica_groups=mesh['fsdp'=8,'seq'=4] {'seq'}, dimensions={0}, use_global_device_ids=true | all-gather | bytes 327680 | tf_op jit(solution)/shard_map/all_gather | solution.py:479
  688.9 76.5 %psum.7 = f32[2,1024]{1,0:T(2,128)S(1)} all-reduce(f32[2,1024]{1,0:T(2,128)S(1)} %pad_maximum_fusion.13), channel_id=1, replica_groups=mesh['fsdp'=8,'seq'=4] {'fsdp','seq'}, use_global_device_ids=true, to_apply=%region_6.7 | all-reduce | flops 2048 | bytes 16384 | tf_op jit(solution)/shard_map/psum | solution.py:558
  797.9 19.0 %reduce-scatter.12.cloned.1.call-done = bf16[32,2816]{1,0:T(8,128)(2,1)} async-done(((bf16[1024,2816]{1,0:T(8,128)(2,1)}), bf16[32,2816]{1,0:T(8,128)(2,1)}) %reduce-scatter.12.cloned.1.call-update) | async-done | bytes 180240 | tf_op jit(solution)/shard_map/reduce_scatter | solution.py:478
  816.9 13.4 %all_gather.42 = bf16[128,2816]{1,0:T(8,128)(2,1)S(1)} all-gather(bf16[32,2816]{1,0:T(8,128)(2,1)} %reduce-scatter.12.cloned.1.call-done), channel_id=1, replica_groups=mesh['fsdp'=8,'seq'=4] {'seq'}, dimensions={0}, use_global_device_ids=true | all-gather | bytes 901120 | tf_op jit(solution)/shard_map/all_gather | solution.py:479
  831.5 128.5 %reduce-scatter.14.cloned.1.call-done = bf16[88,1024]{1,0:T(8,128)(2,1)} async-done(((bf16[2816,1024]{1,0:T(8,128)(2,1)}), bf16[88,1024]{1,0:T(8,128)(2,1)}) %reduce-scatter.14.cloned.1.call-update) | async-done | bytes 180240 | tf_op jit(solution)/shard_map/reduce_scatter | solution.py:478
  960.0 12.3 %all_gather.43 = bf16[352,1024]{1,0:T(8,128)(2,1)S(1)} all-gather(bf16[88,1024]{1,0:T(8,128)(2,1)} %reduce-scatter.14.cloned.1.call-done), channel_id=1, replica_groups=mesh['fsdp'=8,'seq'=4] {'seq'}, dimensions={0}, use_global_device_ids=true | all-gather | bytes 901120 | tf_op jit(solution)/shard_map/all_gather | solution.py:479
  973.6 117.5 %reduce-scatter.16.cloned.1.call-done = bf16[32,3072]{1,0:T(8,128)(2,1)} async-done(((bf16[1024,3072]{1,0:T(8,128)(2,1)}), bf16[32,3072]{1,0:T(8,128)(2,1)}) %reduce-scatter.16.cloned.1.call-update) | async-done | bytes 196624 | tf_op jit(solution)/shard_map/reduce_scatter | solution.py:478
  (191 shorter events, 227.6 us)
Async XLA Ops:
  7.2 86.8 %all-gather.6.cloned.1.call-start = ((), (), s32[]{:S(2)}) async-start(), calls=%async_computation.5 | async-start | bytes 6488064 | tf_op jit(solution)/shard_map/all_gather | solution.py:475
  8.9 146.9 %all-gather.8.cloned.1.call-start = ((), (), s32[]{:S(2)}) async-start(), calls=%async_computation.6 | async-start | bytes 2162688 | tf_op jit(solution)/shard_map/all_gather | solution.py:475
  10.5 213.4 %all-gather.12.cloned.1.call-start = ((), (), s32[]{:S(2)}) async-start(), calls=%async_computation.8 | async-start | bytes 5947392 | tf_op jit(solution)/shard_map/all_gather | solution.py:475
  11.3 282.2 %all-gather.10.cloned.1.call-start = ((), (), s32[]{:S(2)}) async-start(), calls=%async_computation.7 | async-start | bytes 5947392 | tf_op jit(solution)/shard_map/all_gather | solution.py:475
  12.9 350.0 %all-gather.14.cloned.1.call-start = ((), (), s32[]{:S(2)}) async-start(), calls=%async_computation.9 | async-start | bytes 5947392 | tf_op jit(solution)/shard_map/all_gather | solution.py:475
  18.3 27.8 %collective-permute-start = (bf16[512,1024]{0,1:T(8,128)(2,1)}, bf16[512,1024]{0,1:T(8,128)(2,1)S(1)}, u32[]{:S(2)}, u32[]{:S(2)}) collective-permute-start(bf16[512,1024]{0,1:T(8,128)(2,1)} %bitcast.86), channel_id=1, source_target_pairs={{0,2},{1,3},{2,0},{3,1},{4,6},{5,7},{6,4},{7,5},{8,10},{9,11},{10,... | collective-permute-start | bytes 3145736 | tf_op jit(solution)/shard_map/ppermute | solution.py:415
  22.6 55.6 %collective-permute-start.1 = (bf16[512,1024]{1,0:T(8,128)(2,1)}, bf16[512,1024]{1,0:T(8,128)(2,1)}, u32[]{:S(2)}, u32[]{:S(2)}) collective-permute-start(bf16[512,1024]{1,0:T(8,128)(2,1)} %get-tuple-element.76), channel_id=1, source_target_pairs={{0,2},{1,3},{2,0},{3,1},{4,6},{5,7},{6,4},{7,5},{8,10},{9,11},{10,... | collective-permute-start | bytes 3145736 | tf_op jit(solution)/shard_map/ppermute | solution.py:415
  24.4 623.6 %reduce-scatter.8.cloned.1.call-start = ((), (), s32[]{:S(2)}) async-start(), calls=%async_computation.10 | async-start | bytes 2162688 | tf_op jit(solution)/shard_map/reduce_scatter | solution.py:478
  110.5 6.0 collective-permute-start.2
  111.0 34.2 %copy-start.4 = (s32[4]{0:T(128)}, s32[4]{0:T(128)S(1)}, u32[]{:S(2)}) copy-start(s32[4]{0:T(128)S(1)} %add.199.order) | copy-start | bytes 52
  145.8 7.3 collective-permute-start.3
  148.8 156.5 %collective-permute-start.5 = (bf16[512,1024]{0,1:T(8,128)(2,1)}, bf16[512,1024]{0,1:T(8,128)(2,1)}, u32[]{:S(2)}, u32[]{:S(2)}) collective-permute-start(bf16[512,1024]{0,1:T(8,128)(2,1)} %bitcast.87), channel_id=1, source_target_pairs={{0,2},{1,3},{2,0},{3,1},{4,6},{5,7},{6,4},{7,5},{8,10},{9,11},{10,... | collective-permute-start | bytes 3145736 | tf_op jit(solution)/shard_map/ppermute | solution.py:415
  163.6 60.3 %copy-start.22 = (bf16[1024,1024]{0,1:T(8,128)(2,1)}, bf16[1024,1024]{0,1:T(8,128)(2,1)S(1)}, u32[]{:S(2)}) copy-start(bf16[1024,1024]{0,1:T(8,128)(2,1)S(1)} %multiply_convert_fusion.3) | copy-start | bytes 6291460
  235.5 127.5 %copy-start.20 = (bf16[1,512,1024]{1,2,0:T(8,128)(2,1)S(1)}, bf16[1,512,1024]{1,2,0:T(8,128)(2,1)}, u32[]{:S(2)}) copy-start(bf16[1,512,1024]{1,2,0:T(8,128)(2,1)} %copy.45) | copy-start | bytes 3145732
  411.5 375.0 %reduce-scatter.10.cloned.1.call-start = ((), (), s32[]{:S(2)}) async-start(), calls=%async_computation.11 | async-start | bytes 5947392 | tf_op jit(solution)/shard_map/reduce_scatter | solution.py:478
  422.5 394.4 %reduce-scatter.12.cloned.1.call-start = ((), (), s32[]{:S(2)}) async-start(), calls=%async_computation.12 | async-start | bytes 5947392 | tf_op jit(solution)/shard_map/reduce_scatter | solution.py:478
  433.4 526.6 %reduce-scatter.14.cloned.1.call-start = ((), (), s32[]{:S(2)}) async-start(), calls=%async_computation.13 | async-start | bytes 5947392 | tf_op jit(solution)/shard_map/reduce_scatter | solution.py:478
  444.4 646.6 %reduce-scatter.16.cloned.1.call-start = ((), (), s32[]{:S(2)}) async-start(), calls=%async_computation.14 | async-start | bytes 6488064 | tf_op jit(solution)/shard_map/reduce_scatter | solution.py:478
  451.7 2.7 collective-permute-start.6
  525.0 5.9 collective-permute-start.7
  579.6 40.6 %collective-permute-start.4 = (bf16[512,1024]{0,1:T(8,128)(2,1)}, bf16[512,1024]{0,1:T(8,128)(2,1)}, u32[]{:S(2)}, u32[]{:S(2)}) collective-permute-start(bf16[512,1024]{0,1:T(8,128)(2,1)} %slice.143), channel_id=1, source_target_pairs={{2,0},{3,1},{0,2},{1,3},{6,4},{7,5},{4,6},{5,7},{10,8},{11,9},{8,1... | collective-permute-start | bytes 3145736 | tf_op jit(solution)/shard_map/ppermute | solution.py:423
  633.6 132.3 %collective-permute-start.9 = (bf16[512,1024]{0,1:T(8,128)(2,1)}, bf16[512,1024]{0,1:T(8,128)(2,1)}, u32[]{:S(2)}, u32[]{:S(2)}) collective-permute-start(bf16[512,1024]{0,1:T(8,128)(2,1)} %slice.141), channel_id=1, source_target_pairs={{2,0},{3,1},{0,2},{1,3},{6,4},{7,5},{4,6},{5,7},{10,8},{11,9},{8,1... | collective-permute-start | bytes 3145736 | tf_op jit(solution)/shard_map/ppermute | solution.py:423
  685.7 90.7 %collective-permute-start.8 = (bf16[512,1024]{0,1:T(8,128)(2,1)S(1)}, bf16[512,1024]{0,1:T(8,128)(2,1)S(1)}, u32[]{:S(2)}, u32[]{:S(2)}) collective-permute-start(bf16[512,1024]{0,1:T(8,128)(2,1)S(1)} %slice.142), channel_id=1, source_target_pairs={{2,0},{3,1},{0,2},{1,3},{6,4},{7,5},{4,6},{5,7},{10,8},{11,9},{8,1... | collective-permute-start | bytes 3145736 | tf_op jit(solution)/shard_map/ppermute | solution.py:423
  816.9 286.3 %copy-start.1 = (bf16[128,2816]{1,0:T(8,128)(2,1)S(1)}, bf16[128,2816]{1,0:T(8,128)(2,1)}, u32[]{:S(2)}) copy-start(bf16[128,2816]{1,0:T(8,128)(2,1)} %param.22) | copy-start | bytes 2162692
  (34 other events, 214.5 us)
Sparse Core Ops, SparseCore 0:
  11.5 82.5 all-gather.5
  96.9 56.3 all-gather.7
  156.7 67.1 all-gather.11
  227.2 66.2 all-gather.9
  296.7 66.2 all-gather.13
  411.6 120.6 reduce-scatter.7
  534.8 144.1 reduce-scatter.9
  681.3 135.5 reduce-scatter.11
  819.3 140.6 reduce-scatter.13
  966.4 124.6 reduce-scatter.15

commit v2 on v1

--- a/solution.py
+++ b/solution.py
@@ -278,29 +278,57 @@
     )(order, *pieces, *mixes, *grads, lse, cosine, sine)
 
 
-def project_kernel(count, per, wide, place, x_ref, gain_ref, w_ref, first_ref, cos_ref, sin_ref, *refs):
-    outs = refs[:count]
-    normed_ref = refs[count]
+def nt(a, b):
+    return lax.dot_general(a, b, (((1,), (1,)), ((), ())), preferred_element_type=F32)
+
+
+def whole_block(shape):
+    zeros = (0,) * len(shape)
+    return pl.BlockSpec(shape, lambda *_: zeros)
+
+
+def parameters(mib):
+    return pltpu.CompilerParams(dimension_semantics=("arbitrary",), vmem_limit_bytes=mib * MIB)
+
+
+def project_kernel(slots, tok, count, rows, place, *refs):
+    xs, firsts = refs[:slots], refs[slots : 2 * slots]
+    own = refs[2 * slots : 2 * slots + count]
+    other = refs[2 * slots + count : 2 * slots + 2 * count]
+    cos_ref, sin_ref = refs[2 * slots + 2 * count : 2 * slots + 2 * count + 2]
+    other_ref, own_ref, normed_ref, full_ref, gains_ref, column = refs[2 * slots + 2 * count + 2 :]
     step = pl.program_id(0)
-    kind = (step // per) % 3
-    target = step // (3 * per)
+    target, kind = step // 3, step % 3
+    core = place[1]
+    half = jnp.where(target == 0, 1 - core, core)
+    depth = normed_ref.shape[1]
+    wide = own_ref.shape[1]
 
     @pl.when(step == 0)
     def _():
-        values = x_ref[...].astype(F32)
-        scale = lax.rsqrt(jnp.mean(values * values, axis=1, keepdims=True) + epsilon)
-        normed_ref[...] = (values * scale * gain_ref[...].astype(F32)).astype(BF16)
-
-    raw = lax.dot_general(
-        w_ref[...].T, normed_ref[...], (((1,), (1,)), ((), ())), preferred_element_type=F32
-    )
+        for number in range(count):
+            at = pl.ds(pl.multiple_of(place[2 + number] * rows, rows), rows)
+            full_ref[core, at, :] = own[number][:, : 3 * wide]
+            full_ref[1 - core, at, :] = other[number][:, : 3 * wide]
+            column[at, :] = own[number][:, 3 * wide :]
+        gains_ref[...] = column[...].T[:8].astype(F32)
+        gain = gains_ref[0:1, :]
+        for slot in range(slots):
+            values = xs[slot][...].reshape(tok, depth).astype(F32)
+            scale = lax.rsqrt(jnp.mean(values * values, axis=1, keepdims=True) + epsilon)
+            normed_ref[slot * tok : (slot + 1) * tok, :] = (values * scale * gain).astype(BF16)
+
+    weight = full_ref[half, :, pl.ds(pl.multiple_of(kind * wide, wide), wide)]
+    raw = nt(weight.T, normed_ref[...])
 
     def store(value):
-        for number in range(count):
-
-            @pl.when(target == number)
-            def _(number=number):
-                outs[number][0] = value
+        @pl.when(target == 0)
+        def _():
+            other_ref[0] = value
+
+        @pl.when(target == 1)
+        def _():
+            own_ref[0] = value
 
     @pl.when(kind < 2)
     def _():
@@ -314,72 +342,555 @@
 
     @pl.when(kind == 2)
     def _():
-        store((0.5 * raw + 0.5 * first_ref[...].T.astype(F32)).astype(BF16))
-
-
-def project(x, gain, weight, first, cosine, sine, rank, count):
-    span, depth = x.shape
-    width = depth // count
-    wide = min(width, 512)
-    per = width // wide
-    stride = depth // wide
-
-    def column(step, place):
-        return ((place[0] + 1 + step // (3 * per)) % count) * per + step % per
-
-    def out_map(number):
-        def index(step, place):
-            local = jnp.clip(step - number * 3 * per, 0, 3 * per - 1)
-            return (local // per, local % per, 0)
-
-        return index
-
+        first = jnp.concatenate(
+            [ref[...].reshape(tok, wide).T.astype(F32) for ref in firsts], axis=1
+        )
+        store((0.5 * raw + 0.5 * first).astype(BF16))
+
+
+def project(inputs, received, firsts, firsts_received, own, other, cosine, sine, place):
+    slots, tok, depth = inputs.shape
+    count, rows = len(own), own[0].shape[0]
+    wide = depth // 2
+    span = slots * tok
+
+    def half(s, p):
+        return jnp.where(s < 3, 1 - p[1], p[1])
+
+    x_specs = [pl.BlockSpec((1, tok, depth), lambda s, p: (p[0], 0, 0))]
+    x_specs += [whole_block((tok, depth))] * (slots - 1)
+    first_specs = [pl.BlockSpec((1, tok, wide), lambda s, p: (p[0], 0, half(s, p)))]
+    first_specs += [pl.BlockSpec((tok, wide), lambda s, p: (0, half(s, p)))] * (slots - 1)
     grid_spec = pltpu.PrefetchScalarGridSpec(
         num_scalar_prefetch=1,
-        grid=(count * 3 * per,),
-        in_specs=[
-            pl.BlockSpec((span, depth), lambda s, p: (0, 0)),
-            pl.BlockSpec((1, depth), lambda s, p: (0, 0)),
-            pl.BlockSpec((depth, wide), lambda s, p: (0, ((s // per) % 3) * stride + column(s, p))),
-            pl.BlockSpec((span, wide), lambda s, p: (0, column(s, p))),
-            pl.BlockSpec((HALF, span), lambda s, p: (0, 0)),
-            pl.BlockSpec((HALF, span), lambda s, p: (0, 0)),
-        ],
-        out_specs=[pl.BlockSpec((1, wide, span), out_map(number)) for number in range(count)]
-        + [pl.BlockSpec((span, depth), lambda s, p: (0, 0))],
-    )
-    results = pl.pallas_call(
-        functools.partial(project_kernel, count, per, wide),
-        out_shape=[jax.ShapeDtypeStruct((3, width, span), BF16)] * count
-        + [jax.ShapeDtypeStruct((span, depth), BF16)],
+        grid=(6,),
+        in_specs=x_specs
+        + first_specs
+        + [whole_block(own[0].shape)] * (2 * count)
+        + [whole_block((HALF, span))] * 2,
+        out_specs=[
+            pl.BlockSpec((1, wide, span), lambda s, p: (jnp.minimum(s, 2), 0, 0)),
+            pl.BlockSpec((1, wide, span), lambda s, p: (jnp.maximum(s - 3, 0), 0, 0)),
+            whole_block((span, depth)),
+            whole_block((2, depth, 3 * wide)),
+            whole_block((8, depth)),
+        ],
+        scratch_shapes=[pltpu.VMEM((depth, 128), BF16)],
+    )
+    return pl.pallas_call(
+        functools.partial(project_kernel, slots, tok, count, rows),
+        out_shape=[
+            jax.ShapeDtypeStruct((3, wide, span), BF16),
+            jax.ShapeDtypeStruct((3, wide, span), BF16),
+            jax.ShapeDtypeStruct((span, depth), BF16),
+            jax.ShapeDtypeStruct((2, depth, 3 * wide), BF16),
+            jax.ShapeDtypeStruct((8, depth), F32),
+        ],
         grid_spec=grid_spec,
-        compiler_params=pltpu.CompilerParams(
-            dimension_semantics=("arbitrary",), vmem_limit_bytes=48 * MIB
-        ),
+        compiler_params=parameters(56),
         cost_estimate=pl.CostEstimate(
             flops=6 * span * depth * depth,
-            bytes_accessed=2 * (5 * span * depth + 3 * depth * depth),
+            bytes_accessed=2 * (8 * span * depth + 6 * depth * depth),
             transcendentals=0,
         ),
         name="project",
-    )(rank, x, gain, weight, first, cosine, sine)
-    return (results[:count], results[count])
-
-
-def norm_backward(values, scale, gain, grad_normed):
-    weighted = grad_normed * gain
-    inner = jnp.mean(weighted * values, axis=-1, keepdims=True)
-    grad_values = scale * weighted - values * (scale * scale * scale) * inner
-    grad_gain = jnp.sum(grad_normed * values * scale, axis=0)
-    return (grad_values, grad_gain)
-
-
-def inverse_rms(values):
-    return lax.rsqrt(jnp.mean(values * values, axis=-1, keepdims=True) + epsilon)
-
-
-def mm(subscripts, a, b):
-    return jnp.einsum(subscripts, a, b, preferred_element_type=F32)
+    )(place, inputs, *received, firsts, *firsts_received, *own, *other, cosine, sine)
+
+
+def output_kernel(slots, tok, count, rows, place, *refs):
+    xs = refs[:slots]
+    own = refs[slots : slots + count]
+    other = refs[slots + count : slots + 2 * count]
+    att_other, att_own, gains_ref = refs[slots + 2 * count : slots + 2 * count + 3]
+    middle_ref, normed_ref, full_ref = refs[slots + 2 * count + 3 :]
+    step = pl.program_id(0)
+    core = place[1]
+    wide = att_own.shape[0]
+    depth = 2 * wide
+    mine = pl.ds(pl.multiple_of(core * wide, wide), wide)
+    others = pl.ds(pl.multiple_of((1 - core) * wide, wide), wide)
+
+    @pl.when(step == 0)
+    def _():
+        for number in range(count):
+            at = pl.ds(pl.multiple_of(place[2 + number] * rows, rows), rows)
+            full_ref[at, mine] = own[number][...]
+            full_ref[at, others] = other[number][...]
+
+    total = dot(att_own[...].T, full_ref[mine, :]) + dot(att_other[...].T, full_ref[others, :])
+    for slot in range(slots):
+
+        @pl.when(step == slot)
+        def _(slot=slot):
+            middle_ref[...] = xs[slot][...].reshape(tok, depth).astype(F32) + total
+
+    middle = middle_ref[...]
+    scale = lax.rsqrt(jnp.mean(middle * middle, axis=1, keepdims=True) + epsilon)
+    normed_ref[...] = (middle * scale * gains_ref[1:2, :]).astype(BF16)
+
+
+def output_projection(inputs, received, own, other, att_other, att_own, gains, place):
+    slots, tok, depth = inputs.shape
+    count, rows = len(own), own[0].shape[0]
+    wide = depth // 2
+    span = slots * tok
+    x_specs = [pl.BlockSpec((1, tok, depth), lambda s, p: (p[0], 0, 0))]
+    x_specs += [whole_block((tok, depth))] * (slots - 1)
+    grid_spec = pltpu.PrefetchScalarGridSpec(
+        num_scalar_prefetch=1,
+        grid=(slots,),
+        in_specs=x_specs
+        + [whole_block(own[0].shape)] * (2 * count)
+        + [pl.BlockSpec((wide, tok), lambda s, p: (0, s))] * 2
+        + [whole_block((8, depth))],
+        out_specs=[
+            pl.BlockSpec((tok, depth), lambda s, p: (s, 0)),
+            pl.BlockSpec((tok, depth), lambda s, p: (s, 0)),
+            whole_block((depth, depth)),
+        ],
+    )
+    return pl.pallas_call(
+        functools.partial(output_kernel, slots, tok, count, rows),
+        out_shape=[
+            jax.ShapeDtypeStruct((span, depth), F32),
+            jax.ShapeDtypeStruct((span, depth), BF16),
+            jax.ShapeDtypeStruct((depth, depth), BF16),
+        ],
+        grid_spec=grid_spec,
+        compiler_params=parameters(56),
+        cost_estimate=pl.CostEstimate(
+            flops=2 * span * depth * depth,
+            bytes_accessed=12 * span * depth + 4 * depth * depth,
+            transcendentals=0,
+        ),
+        name="output_projection",
+    )(place, inputs, *received, *own, *other, att_other, att_own, gains)
+
+
+def mlp_kernel(slots, tok, count, rows, down_rows, blocks, place, *refs):
+    grads = refs[:slots]
+    middle_ref, normed_ref, gains_ref = refs[slots : slots + 3]
+    base = slots + 3
+    own_gu, other_gu = refs[base : base + count], refs[base + count : base + 2 * count]
+    own_d, other_d = refs[base + 2 * count : base + 3 * count], refs[base + 3 * count : base + 4 * count]
+    (
+        out_ref,
+        send_ref,
+        grad_ref,
+        low_ref,
+        gain_ref,
+        gu_send,
+        gu_keep,
+        d_send,
+        d_keep,
+        wgu,
+        wd,
+        og,
+        normed_t,
+        acc,
+        back,
+        sems,
+    ) = refs[base + 4 * count :]
+    step = pl.program_id(0)
+    core = place[1]
+    depth = og.shape[1]
+    wide = depth // 2
+    strip = 128
+    mine = pl.ds(pl.multiple_of(core * wide, wide), wide)
+    others = pl.ds(pl.multiple_of((1 - core) * wide, wide), wide)
+
+    def loads():
+        copies = []
+        for number in range(count):
+            at = pl.ds(pl.multiple_of(place[2 + number] * rows, rows), rows)
+            copies.append((own_gu[number], wgu.at[0, at, :], 0))
+            copies.append((other_gu[number], wgu.at[1, at, :], 0))
+        for number in range(count):
+            at = pl.ds(pl.multiple_of(place[2 + number] * down_rows, down_rows), down_rows)
+            copies.append((own_d[number], wd.at[at, mine], 1))
+            copies.append((other_d[number], wd.at[at, others], 1))
+        return [
+            pltpu.make_async_copy(source, target, sems.at[number])
+            for number, (source, target, _) in enumerate(copies)
+        ]
+
+    @pl.when(step == 0)
+    def _():
+        copies = loads()
+        for copy in copies:
+            copy.start()
+        for slot in range(slots):
+            og[slot * tok : (slot + 1) * tok, :] = grads[slot][...].reshape(tok, depth)
+        normed_t[...] = normed_ref[...].T
+        acc[...] = jnp.zeros_like(acc)
+        back[...] = jnp.zeros_like(back)
+        for copy in copies:
+            copy.wait()
+
+    half_width = blocks * strip
+    at = pl.ds(pl.multiple_of(step * strip, strip), strip)
+    up_at = pl.ds(pl.multiple_of(half_width + step * strip, strip), strip)
+    gate_w = jnp.concatenate([wgu[0, :, at], wgu[1, :, at]], axis=1)
+    up_w = jnp.concatenate([wgu[0, :, up_at], wgu[1, :, up_at]], axis=1)
+    own_rows = pl.ds(pl.multiple_of(core * half_width + step * strip, strip), strip)
+    other_rows = pl.ds(pl.multiple_of((1 - core) * half_width + step * strip, strip), strip)
+    down_w = jnp.concatenate([wd[own_rows, :], wd[other_rows, :]], axis=0)
+    normed = normed_ref[...]
+    gate = dot(normed, gate_w)
+    up = dot(normed, up_w)
+    grad_active = nt(og[...], down_w)
+    sigma = jax.nn.sigmoid(gate)
+    silu = gate * sigma
+    active = (silu * up).astype(BF16)
+    grad_up = (grad_active * silu).astype(BF16)
+    grad_gate = (grad_active * up * sigma * (1.0 + gate * (1.0 - sigma))).astype(BF16)
+    acc[...] += dot(active, down_w)
+    back[...] += nt(grad_gate, gate_w) + nt(grad_up, up_w)
+    grad_gate_w = dot(normed_t[...], grad_gate).astype(BF16)
+    gu_keep[0] = grad_gate_w[:, :strip]
+    gu_send[0] = grad_gate_w[:, strip:]
+    grad_up_w = dot(normed_t[...], grad_up).astype(BF16)
+    gu_keep[1] = grad_up_w[:, :strip]
+    gu_send[1] = grad_up_w[:, strip:]
+    active_t = active.T
+    kept = dot(active_t, og[:, mine]).astype(BF16)
+    sent = dot(active_t, og[:, others]).astype(BF16)
+    d_keep[core] = kept[:strip]
+    d_keep[1 - core] = kept[strip:]
+    d_send[core] = sent[:strip]
+    d_send[1 - core] = sent[strip:]
+
+    @pl.when(step == blocks - 1)
+    def _():
+        gain = gains_ref[1:2, :]
+        chunk = min(128, tok)
+        gain_ref[...] = jnp.zeros_like(gain_ref)
+        for slot in range(slots):
+
+            def finish(number, _, slot=slot):
+                local = pl.ds(pl.multiple_of(number * chunk, chunk), chunk)
+                some = pl.ds(pl.multiple_of(slot * tok + number * chunk, chunk), chunk)
+                middle = middle_ref[some, :]
+                scale = lax.rsqrt(jnp.mean(middle * middle, axis=1, keepdims=True) + epsilon)
+                result = middle + acc[some, :]
+                if slot == 0:
+                    out_ref[0, local, :] = result
+                else:
+                    send_ref[pl.ds(pl.multiple_of((slot - 1) * tok + number * chunk, chunk), chunk), :] = (
+                        result.astype(BF16)
+                    )
+                grad = back[some, :]
+                gain_ref[0:1, :] += jnp.sum(grad * middle * scale, axis=0, keepdims=True)
+                weighted = grad * gain
+                inner = jnp.mean(weighted * middle, axis=1, keepdims=True)
+                grad_middle = (
+                    scale * weighted
+                    - middle * (scale * scale * scale) * inner
+                    + og[some, :].astype(F32)
+                )
+                grad_ref[some, :] = grad_middle
+                low_ref[some, :] = grad_middle.astype(BF16)
+                return 0
+
+            lax.fori_loop(0, tok // chunk, finish, 0)
+
+
+def mlp(grads, grads_received, middle, normed, gains, gate_up, down, place):
+    slots, tok, depth = grads.shape
+    own_gu, other_gu = gate_up
+    own_d, other_d = down
+    count, rows = len(own_gu), own_gu[0].shape[0]
+    down_rows = own_d[0].shape[0]
+    half_width = own_gu[0].shape[1] // 2
+    wide = depth // 2
+    span = slots * tok
+    blocks = half_width // 128
+    once = pl.Buffered(1)
+    g_specs = [pl.BlockSpec((1, tok, depth), lambda s, p: (p[0], 0, 0), pipeline_mode=once)]
+    g_specs += [pl.BlockSpec((tok, depth), lambda s, p: (0, 0), pipeline_mode=once)] * (slots - 1)
+    gu_spec = pl.BlockSpec((2, depth, 128), lambda s, p: (0, 0, s))
+    d_spec = pl.BlockSpec((2, 128, wide), lambda s, p: (0, s, 0))
+    grid_spec = pltpu.PrefetchScalarGridSpec(
+        num_scalar_prefetch=1,
+        grid=(blocks,),
+        in_specs=g_specs
+        + [
+            pl.BlockSpec((span, depth), lambda s, p: (0, 0), pipeline_mode=once),
+            pl.BlockSpec((span, depth), lambda s, p: (0, 0), pipeline_mode=once),
+            whole_block((8, depth)),
+        ]
+        + [pl.BlockSpec(memory_space=pl.ANY)] * (4 * count),
+        out_specs=[
+            pl.BlockSpec((1, tok, depth), lambda s, p: (p[0], 0, 0), pipeline_mode=once),
+            pl.BlockSpec(((slots - 1) * tok, depth), lambda s, p: (0, 0), pipeline_mode=once),
+            pl.BlockSpec((span, depth), lambda s, p: (0, 0), pipeline_mode=once),
+            pl.BlockSpec((span, depth), lambda s, p: (0, 0), pipeline_mode=once),
+            whole_block((8, depth)),
+            gu_spec,
+            gu_spec,
+            d_spec,
+            d_spec,
+        ],
+        scratch_shapes=[
+            pltpu.VMEM((2, depth, 2 * half_width), BF16),
+            pltpu.VMEM((2 * half_width, depth), BF16),
+            pltpu.VMEM((span, depth), BF16),
+            pltpu.VMEM((depth, span), BF16),
+            pltpu.VMEM((span, depth), F32),
+            pltpu.VMEM((span, depth), F32),
+            pltpu.SemaphoreType.DMA((4 * count,)),
+        ],
+    )
+    return pl.pallas_call(
+        functools.partial(mlp_kernel, slots, tok, count, rows, down_rows, blocks),
+        out_shape=[
+            jax.ShapeDtypeStruct((slots, tok, depth), F32),
+            jax.ShapeDtypeStruct(((slots - 1) * tok, depth), BF16),
+            jax.ShapeDtypeStruct((span, depth), F32),
+            jax.ShapeDtypeStruct((span, depth), BF16),
+            jax.ShapeDtypeStruct((8, depth), F32),
+            jax.ShapeDtypeStruct((2, depth, half_width), BF16),
+            jax.ShapeDtypeStruct((2, depth, half_width), BF16),
+            jax.ShapeDtypeStruct((2, half_width, wide), BF16),
+            jax.ShapeDtypeStruct((2, half_width, wide), BF16),
+        ],
+        grid_spec=grid_spec,
+        compiler_params=parameters(63),
+        cost_estimate=pl.CostEstimate(
+            flops=16 * span * depth * 2 * half_width,
+            bytes_accessed=24 * depth * half_width + 20 * span * depth,
+            transcendentals=2 * span * half_width,
+        ),
+        name="mlp",
+    )(place, grads, *grads_received, middle, normed, gains, *own_gu, *other_gu, *own_d, *other_d)
+
+
+def grad_attended_kernel(place, low_ref, full_ref, att_other, att_own, ga_other, ga_own, sent, kept):
+    step = pl.program_id(0)
+    core = place[1]
+    wide = att_own.shape[0]
+    mine = pl.ds(pl.multiple_of(core * wide, wide), wide)
+    others = pl.ds(pl.multiple_of((1 - core) * wide, wide), wide)
+    for number, (att, result) in enumerate(((att_other, ga_other), (att_own, ga_own))):
+
+        @pl.when(step == number)
+        def _(att=att, result=result):
+            result[...] = nt(full_ref[...], low_ref[...]).astype(BF16)
+            kept[...] = dot(att[...], low_ref[:, mine]).astype(BF16)
+            sent[...] = dot(att[...], low_ref[:, others]).astype(BF16)
+
+
+def grad_attended(low, full, att_other, att_own, place):
+    span, depth = low.shape
+    wide = depth // 2
+
+    def half(s, p):
+        return jnp.where(s == 0, 1 - p[1], p[1])
+
+    row_spec = pl.BlockSpec((wide, wide), lambda s, p: (half(s, p), 0))
+    grid_spec = pltpu.PrefetchScalarGridSpec(
+        num_scalar_prefetch=1,
+        grid=(2,),
+        in_specs=[
+            whole_block((span, depth)),
+            pl.BlockSpec((wide, depth), lambda s, p: (half(s, p), 0)),
+            whole_block((wide, span)),
+            whole_block((wide, span)),
+        ],
+        out_specs=[whole_block((wide, span)), whole_block((wide, span)), row_spec, row_spec],
+    )
+    return pl.pallas_call(
+        grad_attended_kernel,
+        out_shape=[
+            jax.ShapeDtypeStruct((wide, span), BF16),
+            jax.ShapeDtypeStruct((wide, span), BF16),
+            jax.ShapeDtypeStruct((depth, wide), BF16),
+            jax.ShapeDtypeStruct((depth, wide), BF16),
+        ],
+        grid_spec=grid_spec,
+        compiler_params=parameters(48),
+        cost_estimate=pl.CostEstimate(
+            flops=4 * span * depth * depth,
+            bytes_accessed=6 * span * depth + 4 * depth * depth,
+            transcendentals=0,
+        ),
+        name="grad_attended",
+    )(place, low, full, att_other, att_own)
+
+
+def tail_kernel(slots, tok, place, *refs):
+    xs = refs[:slots]
+    (
+        back_other,
+        back_own,
+        full_ref,
+        normed_ref,
+        grad_ref,
+        gains_ref,
+        mlp_gain_ref,
+        out_ref,
+        send_ref,
+        first_ref,
+        first_send,
+        gain_ref,
+        sent,
+        kept,
+        normed_t,
+        acc,
+    ) = refs[slots:]
+    step = pl.program_id(0)
+    target, kind = step // 3, step % 3
+    depth = acc.shape[1]
+
+    @pl.when(step == 0)
+    def _():
+        normed_t[...] = normed_ref[...].T
+        acc[...] = jnp.zeros_like(acc)
+
+    def part(back, result):
+        grad = back[0]
+
+        @pl.when(kind == 2)
+        def _():
+            rows = 0.5 * grad.astype(F32).T
+            first_ref[0] = rows[:tok]
+            first_send[...] = rows[tok:].astype(BF16)
+
+        grad = grad * jnp.where(kind == 2, 0.5, 1.0).astype(BF16)
+        acc[...] += nt(grad.T, full_ref[0])
+        result[0] = nt(normed_t[...], grad).astype(BF16)
+
+    @pl.when(target == 0)
+    def _():
+        part(back_other, sent)
+
+    @pl.when(target == 1)
+    def _():
+        part(back_own, kept)
+
+    @pl.when(step == 5)
+    def _():
+        gain = gains_ref[0:1, :]
+        chunk = min(128, tok)
+        gain_ref[...] = jnp.zeros_like(gain_ref)
+        gain_ref[1:2, :] = mlp_gain_ref[0:1, :]
+        for slot in range(slots):
+
+            def finish(number, _, slot=slot):
+                local = pl.ds(pl.multiple_of(number * chunk, chunk), chunk)
+                some = pl.ds(pl.multiple_of(slot * tok + number * chunk, chunk), chunk)
+                if slot == 0:
+                    values = xs[slot][0, local, :].astype(F32)
+                else:
+                    values = xs[slot][local, :].astype(F32)
+                scale = lax.rsqrt(jnp.mean(values * values, axis=1, keepdims=True) + epsilon)
+                grad = acc[some, :]
+                gain_ref[0:1, :] += jnp.sum(grad * values * scale, axis=0, keepdims=True)
+                weighted = grad * gain
+                inner = jnp.mean(weighted * values, axis=1, keepdims=True)
+                result = (
+                    scale * weighted
+                    - values * (scale * scale * scale) * inner
+                    + grad_ref[some, :]
+                )
+                if slot == 0:
+                    out_ref[0, local, :] = result
+                else:
+                    send_ref[pl.ds(pl.multiple_of((slot - 1) * tok + number * chunk, chunk), chunk), :] = (
+                        result.astype(BF16)
+                    )
+                return 0
+
+            lax.fori_loop(0, tok // chunk, finish, 0)
+
+
+def tail(inputs, received, back_other, back_own, full, normed, grad_middle, gains, mlp_gain, place):
+    slots, tok, depth = inputs.shape
+    wide = depth // 2
+    span = slots * tok
+    rest = (slots - 1) * tok
+    once = pl.Buffered(1)
+
+    def half(s, p):
+        return jnp.where(s < 3, 1 - p[1], p[1])
+
+    x_specs = [pl.BlockSpec((1, tok, depth), lambda s, p: (p[0], 0, 0))]
+    x_specs += [whole_block((tok, depth))] * (slots - 1)
+    grid_spec = pltpu.PrefetchScalarGridSpec(
+        num_scalar_prefetch=1,
+        grid=(6,),
+        in_specs=x_specs
+        + [
+            pl.BlockSpec((1, wide, span), lambda s, p: (jnp.minimum(s, 2), 0, 0)),
+            pl.BlockSpec((1, wide, span), lambda s, p: (jnp.maximum(s - 3, 0), 0, 0)),
+            pl.BlockSpec((1, depth, wide), lambda s, p: (half(s, p), 0, s % 3)),
+            whole_block((span, depth)),
+            pl.BlockSpec((span, depth), lambda s, p: (0, 0), pipeline_mode=once),
+            whole_block((8, depth)),
+            whole_block((8, depth)),
+        ],
+        out_specs=[
+            pl.BlockSpec((1, tok, depth), lambda s, p: (p[0], 0, 0)),
+            whole_block((rest, depth)),
+            pl.BlockSpec((1, tok, wide), lambda s, p: (p[0], 0, half(s, p))),
+            pl.BlockSpec((rest, wide), lambda s, p: (0, half(s, p))),
+            whole_block((8, depth)),
+            pl.BlockSpec((1, depth, wide), lambda s, p: (jnp.minimum(s, 2), 0, 0)),
+            pl.BlockSpec((1, depth, wide), lambda s, p: (jnp.maximum(s - 3, 0), 0, 0)),
+        ],
+        scratch_shapes=[pltpu.VMEM((depth, span), BF16), pltpu.VMEM((span, depth), F32)],
+    )
+    return pl.pallas_call(
+        functools.partial(tail_kernel, slots, tok),
+        out_shape=[
+            jax.ShapeDtypeStruct((slots, tok, depth), F32),
+            jax.ShapeDtypeStruct((rest, depth), BF16),
+            jax.ShapeDtypeStruct((slots, tok, depth), F32),
+            jax.ShapeDtypeStruct((rest, depth), BF16),
+            jax.ShapeDtypeStruct((8, depth), F32),
+            jax.ShapeDtypeStruct((3, depth, wide), BF16),
+            jax.ShapeDtypeStruct((3, depth, wide), BF16),
+        ],
+        grid_spec=grid_spec,
+        compiler_params=parameters(60),
+        cost_estimate=pl.CostEstimate(
+            flops=12 * span * depth * depth,
+            bytes_accessed=24 * span * depth + 12 * depth * depth,
+            transcendentals=0,
+        ),
+        name="tail",
+    )(
+        place, inputs, *received, back_other, back_own, full, normed, grad_middle, gains, mlp_gain
+    )
+
+
+def land_kernel(place, whole_ref, part_ref, out_ref):
+    out_ref[0] = part_ref[...].astype(F32)
+
+
+def land(whole, part, slot):
+    _, tok, depth = whole.shape
+    tile = min(256, tok)
+    grid_spec = pltpu.PrefetchScalarGridSpec(
+        num_scalar_prefetch=1,
+        grid=(tok // tile,),
+        in_specs=[
+            pl.BlockSpec(memory_space=pl.ANY),
+            pl.BlockSpec((tile, depth), lambda s, p: (s, 0)),
+        ],
+        out_specs=pl.BlockSpec((1, tile, depth), lambda s, p: (p[0], s, 0)),
+    )
+    return pl.pallas_call(
+        land_kernel,
+        out_shape=jax.ShapeDtypeStruct(whole.shape, F32),
+        grid_spec=grid_spec,
+        input_output_aliases={1: 0},
+        compiler_params=parameters(16),
+        cost_estimate=pl.CostEstimate(
+            flops=tok * depth, bytes_accessed=6 * tok * depth, transcendentals=0
+        ),
+        name="land",
+    )(slot, whole, part)
 
 
 def shards(
@@ -398,85 +909,172 @@
 ):
     slots, tok, _ = inputs.shape
     groups = lax.axis_size("seq")
+    parts = lax.axis_size("fsdp")
+    line = parts // 2
     count = groups // slots
     length = tok * groups
     span = slots * tok
     seat = lax.axis_index("seq")
+    shard = lax.axis_index("fsdp")
     side = seat // count
     rank = seat % count
+    core = seat % 2
+    z, y = shard // 2, shard % 2
+    wide = D // 2
     width = D // count
-    both = ("fsdp", "seq")
+
+    def along_seq(value, partner):
+        return lax.ppermute(value, "seq", [(i, partner(i)) for i in range(groups)])
+
+    def along_fsdp(value, partner):
+        return lax.ppermute(value, "fsdp", [(i, partner(i)) for i in range(parts)])
+
+    def to_core(value):
+        return along_seq(value, lambda i: i ^ 1)
+
+    def to_y(value):
+        return along_fsdp(value, lambda i: i ^ 1)
+
+    def to_z(value, jump):
+        return along_fsdp(value, lambda i: (i + 2 * jump) % parts)
+
+    def after(value, *others):
+        return lax.optimization_barrier((value,) + others)[0]
 
     def to_sequence(values):
-        taken = [lax.dynamic_index_in_dim(values, side, 0, keepdims=False)]
+        taken = []
         for jump in range(1, slots):
             sent = lax.dynamic_index_in_dim(values, (side + jump) % slots, 0, keepdims=False)
-            pairs = [(i, (i + jump * count) % groups) for i in range(groups)]
-            taken.append(lax.ppermute(sent, "seq", pairs))
-        return jnp.concatenate(taken, axis=0)
-
-    def to_home(values):
-        rows = [values[:tok].astype(F32)]
+            taken.append(along_seq(sent, lambda i: (i + jump * count) % groups))
+        return taken
+
+    def to_home(whole, sent):
         for jump in range(1, slots):
-            sent = values[jump * tok : (jump + 1) * tok].astype(BF16)
-            pairs = [((i + jump * count) % groups, i) for i in range(groups)]
-            rows.append(lax.ppermute(sent, "seq", pairs).astype(F32))
-        if slots == 2:
-            swap = side == 1
-            return jnp.stack([jnp.where(swap, rows[1], rows[0]), jnp.where(swap, rows[0], rows[1])])
-        stacked = jnp.zeros((slots, tok, D), F32)
-        for jump in range(slots):
-            stacked = lax.dynamic_update_index_in_dim(
-                stacked, rows[jump], (side + jump) % slots, 0
+            part = sent[(jump - 1) * tok : jump * tok]
+            part = along_seq(part, lambda i: (i - jump * count) % groups)
+            whole = land(whole, part, ((side + jump) % slots)[None])
+        return whole
+
+    def rank_up(i, jump):
+        return (i // count) * count + (i % count + jump) % count
+
+    def rank_down(i, jump):
+        return (i // count) * count + (i % count - jump) % count
+
+    def halves_to_ranks(other, own, axis):
+        if count == 2:
+            return [other, own]
+        return [
+            lax.dynamic_slice_in_dim(
+                join(other, own, axis), ((rank + 1 + number) % count) * width, width, axis
             )
-        return stacked
-
-    def exchange(pieces):
-        received = []
-        for jump in range(1, count):
-            pairs = [
-                (i, (i // count) * count + (i % count + jump) % count) for i in range(groups)
-            ]
-            received.append(lax.ppermute(pieces[jump - 1], "seq", pairs))
-        return received + [pieces[count - 1]]
-
-    def exchange_back(pieces):
-        received = []
-        for jump in range(1, count):
-            pairs = [
-                ((i // count) * count + (i % count + jump) % count, i) for i in range(groups)
-            ]
-            received.append(lax.ppermute(pieces[jump - 1], "seq", pairs))
-        return received + [pieces[count - 1]]
-
-    def join(pieces, axis):
+            for number in range(count)
+        ]
+
+    def join(other, own, axis):
+        first = jnp.where(core == 0, own, other)
+        second = jnp.where(core == 0, other, own)
+        return jnp.concatenate([first, second], axis=axis)
+
+    def ranks_to_halves(pieces, axis):
         if count == 2:
-            odd = rank == 1
-            return jnp.concatenate(
-                [
-                    jnp.where(odd, pieces[0], pieces[1]),
-                    jnp.where(odd, pieces[1], pieces[0]),
-                ],
-                axis=axis,
-            )
-        size = pieces[0].shape[axis]
+            return pieces
         shape = list(pieces[0].shape)
-        shape[axis] = size * count
+        shape[axis] = D
         whole = jnp.zeros(shape, pieces[0].dtype)
         for number in range(count):
             whole = lax.dynamic_update_slice_in_dim(
-                whole, pieces[number], ((rank + 1 + number) % count) * size, axis
+                whole, pieces[number], ((rank + 1 + number) % count) * width, axis
             )
-        return whole
-
-    def gather(shard):
-        part = shard.shape[0] // groups
-        own = lax.dynamic_slice_in_dim(shard, seat * part, part, 0)
-        return lax.all_gather(own, both, axis=0, tiled=True)
-
-    def scatter(total):
-        part = lax.psum_scatter(total.astype(BF16), both, scatter_dimension=0, tiled=True)
-        return lax.all_gather(part, "seq", axis=0, tiled=True).astype(F32)
+        return [
+            lax.dynamic_slice_in_dim(whole, which * wide, wide, axis)
+            for which in (1 - core, core)
+        ]
+
+    def exchange(pieces):
+        received = [
+            along_seq(pieces[jump - 1], lambda i: rank_up(i, jump)) for jump in range(1, count)
+        ]
+        return received + [pieces[count - 1]]
+
+    def exchange_back(pieces):
+        received = [
+            along_seq(pieces[jump - 1], lambda i: rank_down(i, jump)) for jump in range(1, count)
+        ]
+        return received + [pieces[count - 1]]
+
+    def split(*weights):
+        results = []
+        for which in (core, 1 - core):
+            columns = []
+            for weight in weights:
+                size = weight.shape[1] // 2
+                columns.append(lax.dynamic_slice_in_dim(weight, which * size, size, 1))
+            results.append(columns)
+        return results
+
+    def gather_z(half):
+        return [half] + [to_z(half, jump) for jump in range(1, line)]
+
+    def gather_rest(along_z, other):
+        along_y = [to_y(piece) for piece in along_z]
+        own = [piece for pair in zip(along_z, along_y) for piece in pair]
+        return (own, [other] + [to_core(piece) for piece in own[1:]])
+
+    numbers = []
+    for jump in range(line):
+        for flip in range(2):
+            numbers.append(((z - jump) % line) * 2 + (y ^ flip))
+    place = jnp.stack([side, core] + numbers).astype(jnp.int32)
+
+    def low(value):
+        return value.astype(BF16)
+
+    def add(a, b):
+        return low(a.astype(F32) + b.astype(F32))
+
+    def pick(value, index, axis):
+        return lax.dynamic_index_in_dim(value, index, axis, keepdims=False)
+
+    def scatter(sent, kept, rows_axis):
+        shape = kept.shape
+        rows = shape[rows_axis] // parts
+        cut = shape[:rows_axis] + (line, 2, rows) + shape[rows_axis + 1 :]
+        received = to_core(sent).reshape(cut)
+        kept = kept.reshape(cut)
+        axis = rows_axis + 1
+        received_y = to_y(add(pick(kept, 1 - y, axis), pick(received, 1 - y, axis)))
+        kept_y = pick(kept, y, axis), pick(received, y, axis)
+
+        def partial(index):
+            total = pick(kept_y[0], index, rows_axis).astype(F32)
+            total = total + pick(kept_y[1], index, rows_axis).astype(F32)
+            return total + pick(received_y, index, rows_axis).astype(F32)
+
+        total = partial(z)
+        for jump in range(1, line):
+            total = total + to_z(low(partial((z + jump) % line)), jump).astype(F32)
+        mine = low(total)
+        for jump in range(1, groups // 2):
+            total = total + along_seq(mine, lambda i: (i + 2 * jump) % groups).astype(F32)
+        mine = low(total)
+        return (mine, to_core(mine))
+
+    def columns(mine, others):
+        first = jnp.where(core == 0, mine, others)
+        second = jnp.where(core == 0, others, mine)
+        return jnp.concatenate([first, second], axis=-1).astype(F32)
+
+    def everywhere(value):
+        value = value + to_core(value)
+        value = value + to_y(value)
+        total = value
+        for jump in range(1, line):
+            total = total + to_z(value, jump)
+        value = total
+        for jump in range(1, groups // 2):
+            total = total + along_seq(value, lambda i: (i + 2 * jump) % groups)
+        return total
 
     steps = jnp.arange(slots, dtype=jnp.int32)
     starts = ((side - steps) % slots) * (count * tok) + rank * tok
@@ -495,83 +1093,87 @@
     order = (((side - steps) % slots)[None, :] * count + sources[:, None]).reshape(-1)
     order = order.astype(jnp.int32)
 
-    qkv_weight = gather(jnp.concatenate([query_weight, key_weight, value_weight], axis=1))
-    gains = lax.all_gather(
-        jnp.stack([attn_gain, mlp_gain]), "fsdp", axis=1, tiled=True
-    ).astype(F32)
-    gain_attn, gain_mlp = gains[0:1], gains[1:2]
+    gains = jnp.pad(jnp.stack([attn_gain, mlp_gain], axis=1), ((0, 0), (0, 126)))
+    qkv = [
+        jnp.concatenate(half + [gains], axis=1)
+        for half in split(query_weight, key_weight, value_weight)
+    ]
+    gate_up = [jnp.concatenate(half, axis=1) for half in split(gate_weight, up_weight)]
+    out_halves = [half[0] for half in split(output_weight)]
+    down_halves = [half[0] for half in split(down_weight)]
+
     tokens = to_sequence(inputs)
-    firsts = to_sequence(first_values)
-    grads = to_sequence(out_grad)
-    output_full = gather(output_weight)
-    gate_full = gather(gate_weight)
-    up_full = gather(up_weight)
-    down_full = gather(down_weight)
-
-    resid = tokens.astype(F32)
-    heads, normed_low = project(
-        tokens, gain_attn.astype(BF16), qkv_weight, firsts, cosine, sine, rank[None], count
-    )
-    pieces = exchange(heads)
+    qkv_z = gather_z(qkv[0])
+    firsts = to_sequence(after(first_values, *tokens))
+    qkv_own, qkv_other = gather_rest(qkv_z, qkv[1])
+    out_z = gather_z(after(out_halves[0], *qkv_z))
+    gate_up_z = gather_z(after(gate_up[0], *qkv_z))
+    down_z = gather_z(after(down_halves[0], *qkv_z))
+    grads = to_sequence(after(out_grad, *firsts))
+    out_own, out_other = gather_rest(out_z, out_halves[1])
+    gate_up_pieces = gather_rest(gate_up_z, gate_up[1])
+    down_pieces = gather_rest(down_z, down_halves[1])
+
+    heads_other, heads_own, normed, qkv_full, gains_full = project(
+        inputs, tokens, first_values, firsts, qkv_own, qkv_other, cosine, sine, place
+    )
+    pieces = exchange(halves_to_ranks(heads_other, heads_own, 1))
     mixes, lse = attend(pieces, order, slots)
-    attended = join(exchange_back(mixes), 0)
-    middle = resid + mm("ht,ho->to", attended, output_full)
-    mlp_scale = inverse_rms(middle)
-    normed2_low = (middle * mlp_scale * gain_mlp).astype(BF16)
-    gate = mm("td,df->tf", normed2_low, gate_full)
-    up_proj = mm("td,df->tf", normed2_low, up_full)
-    sigma = jax.nn.sigmoid(gate)
-    silu_gate = gate * sigma
-    active = (silu_gate * up_proj).astype(BF16)
-    outputs = middle + mm("tf,fd->td", active, down_full)
-    grad_active = mm("td,fd->tf", grads, down_full)
-    grad_gate = (grad_active * up_proj * sigma * (1.0 + gate * (1.0 - sigma))).astype(BF16)
-    grad_up = (grad_active * silu_gate).astype(BF16)
-    down_grad = mm("tf,td->fd", active, grads)
-    gate_grad = mm("td,tf->df", normed2_low, grad_gate)
-    up_grad = mm("td,tf->df", normed2_low, grad_up)
-    grad_normed2 = mm("tf,df->td", grad_gate, gate_full) + mm("tf,df->td", grad_up, up_full)
-    grad_middle, mlp_gain_grad = norm_backward(middle, mlp_scale, gain_mlp, grad_normed2)
-    grad_middle = grad_middle + grads.astype(F32)
-    low_grad_middle = grad_middle.astype(BF16)
-    output_grad = mm("ht,to->ho", attended, low_grad_middle)
-    grad_attended = mm("to,ho->ht", low_grad_middle, output_full).astype(BF16)
-    grad_pieces = [
-        lax.dynamic_slice_in_dim(grad_attended, ((rank + 1 + d) % count) * width, width, 0)
-        for d in range(count)
-    ]
-    grad_heads = exchange(grad_pieces)
+    att_other, att_own = ranks_to_halves(exchange_back(mixes), 0)
+    middle, normed2, out_full = output_projection(
+        inputs, tokens, out_own, out_other, att_other, att_own, gains_full, place
+    )
+    (
+        outputs,
+        outputs_sent,
+        grad_middle,
+        low_grad,
+        mlp_gain_grad,
+        gu_sent,
+        gu_kept,
+        down_sent,
+        down_kept,
+    ) = mlp(out_grad, grads, middle, normed2, gains_full, gate_up_pieces, down_pieces, place)
+    ga_other, ga_own, out_sent, out_kept = grad_attended(
+        low_grad, out_full, att_other, att_own, place
+    )
+    gate_up_grad = scatter(gu_sent, gu_kept, 1)
+    down_grad = scatter(
+        down_sent.reshape(-1, wide), down_kept.reshape(-1, wide), 0
+    )
+    output_grad = scatter(out_sent, out_kept, 0)
+    grad_heads = exchange(halves_to_ranks(ga_other, ga_own, 0))
     back = attend_back(pieces, mixes, grad_heads, lse, full_cos, full_sin, order, slots)
-    grad_qkv = join(exchange_back(back), 1)
-    grad_query, grad_key, grad_mixed = grad_qkv[0], grad_qkv[1], grad_qkv[2]
-    half_mixed = 0.5 * grad_mixed.astype(F32)
-    half_low = half_mixed.astype(BF16)
-    first_grad = half_mixed.T
-    query_grad = mm("td,ct->dc", normed_low, grad_query)
-    key_grad = mm("td,ct->dc", normed_low, grad_key)
-    value_grad = mm("td,ct->dc", normed_low, half_low)
-    grad_normed = mm("ct,dc->td", grad_query, qkv_weight[:, :D])
-    grad_normed = grad_normed + mm("ct,dc->td", grad_key, qkv_weight[:, D : 2 * D])
-    grad_normed = grad_normed + mm("ct,dc->td", half_low, qkv_weight[:, 2 * D :])
-    grad_resid, attn_gain_grad = norm_backward(resid, inverse_rms(resid), gain_attn, grad_normed)
-    input_grad = grad_resid + grad_middle
-    gain_grads = lax.psum(jnp.stack([attn_gain_grad, mlp_gain_grad]), both)
-    part = attn_gain.shape[0]
-    gain_grads = lax.dynamic_slice_in_dim(gain_grads, lax.axis_index("fsdp") * part, part, 1)
-    qkv_grad = scatter(jnp.concatenate([query_grad, key_grad, value_grad], axis=1))
+    back_other, back_own = ranks_to_halves(exchange_back(back), 1)
+    input_grad, input_sent, first_grad, first_sent, gain_grads, qkv_sent, qkv_kept = tail(
+        inputs,
+        tokens,
+        back_other,
+        back_own,
+        qkv_full,
+        normed,
+        grad_middle,
+        gains_full,
+        mlp_gain_grad,
+        place,
+    )
+    qkv_grad = columns(*scatter(qkv_sent, qkv_kept, 1))
+    gate_up_grad = columns(*gate_up_grad)
+    gain_grads = everywhere(gain_grads)
+    gain_grads = lax.dynamic_slice_in_dim(gain_grads, shard * (D // parts), D // parts, 1)
     return (
-        to_home(outputs),
-        to_home(input_grad),
-        to_home(first_grad),
+        to_home(outputs, outputs_sent),
+        to_home(input_grad, input_sent),
+        to_home(first_grad, first_sent),
         gain_grads[0],
         gain_grads[1],
-        qkv_grad[:, :D],
-        qkv_grad[:, D : 2 * D],
-        qkv_grad[:, 2 * D :],
-        scatter(output_grad),
-        scatter(gate_grad),
-        scatter(up_grad),
-        scatter(down_grad),
+        qkv_grad[0],
+        qkv_grad[1],
+        qkv_grad[2],
+        columns(*output_grad),
+        gate_up_grad[0],
+        gate_up_grad[1],
+        columns(*down_grad),
     )
 
 

time: 1120 us -> 843 us (0.75)
  blocking collectives: 166 us -> 0 us
  matrix products: 139 us -> 0 us
  Pallas kernels: 113 us -> 246 us
  waiting for transfers between devices: 538 us -> 431 us
  starting transfers between devices: 10.4 us -> 98.5 us
  local copies, waits for them, and re-layouts: 70 us -> 19.5 us
  other arithmetic: 57.7 us -> 38.6 us
  between operations: 15.2 us -> 1.86 us
    ppermute x10 -> x100, waiting for transfers between devices: 84.3 us -> 431 us  [the longest x48 359 us: along_fsdp(): return lax.ppermute(value, 'fsdp', [(i, partner(i)) for i in range(parts)])]
    reduce_scatter x5 -> x0, waiting for transfers between devices: 265 us -> none  [scatter(): lax.psum_scatter(total.astype(BF16), both, scatter_dimension=0, tiled=True)]
    all_gather x5 -> x0, waiting for transfers between devices: 189 us -> none  [gather(): return lax.all_gather(own, both, axis=0, tiled=True)]
    dot_general x18 -> x0, matrix products: 139 us -> none  [mm(): return jnp.einsum(subscripts, a, b, preferred_element_type=F32)]
    pallas_call x1 -> x8, Pallas kernels: 15.1 us -> 146 us  [the longest x1 75.9 us: mlp(): pl.pallas_call(functools.partial(mlp_kernel, slots, tok, count, rows, dow...]
    all_gather x6 -> x0, blocking collectives: 89.7 us -> none  [the longest x5 77.3 us: scatter(): return lax.all_gather(part, 'seq', axis=0, tiled=True).astype(F32)]
    ppermute x10 -> x100, starting transfers between devices: 9.96 us -> 98.5 us  [the longest x52 63.4 us: along_seq(): return lax.ppermute(value, 'seq', [(i, partner(i)) for i in range(groups)])]
    psum x1 -> x0, blocking collectives: 76.5 us -> none  [shards(): gain_grads = lax.psum(jnp.stack([attn_gain_grad, mlp_gain_grad]), both)]
  transfers between devices with their start and end apart: 20 -> 100, of which waited for: 13 -> 35; matrix products, arithmetic and copies ran while one was open for 18% -> 6% of each run, Pallas kernels for 10% -> 8%
where the time goes in v2:
time: 843 us; the launch traced here: 835 us
  waiting for transfers between devices  431 us (51%)
  Pallas kernels  246 us (29%)
  starting transfers between devices  98.5 us (12%)
  other arithmetic  38.6 us (5%)
  local copies, waits for them, and re-layouts  19.5 us (2%)
    ppermute x48, waiting for transfers between devices, along_fsdp(): return lax.ppermute(value, 'fsdp', [(i, partner(i)) for i in range(parts)])  359 us
    pallas_call x1, Pallas kernels, mlp(): pl.pallas_call(functools.partial(mlp_kernel, slots, tok, count, rows, dow...  75.9 us
    ppermute x52, waiting for transfers between devices, along_seq(): return lax.ppermute(value, 'seq', [(i, partner(i)) for i in range(groups)])  71.4 us
    pallas_call x1, Pallas kernels, attend_back(): pl.pallas_call(functools.partial(attend_back_kernel, count, slots, tok, t...  69.9 us
    ppermute x52, starting transfers between devices, along_seq(): return lax.ppermute(value, 'seq', [(i, partner(i)) for i in range(groups)])  63.4 us
    ppermute x48, starting transfers between devices, along_fsdp(): return lax.ppermute(value, 'fsdp', [(i, partner(i)) for i in range(parts)])  35 us
    convert_element_type x16, other arithmetic, low(): return value.astype(BF16)  29.9 us
    pallas_call x1, Pallas kernels, attend(): pl.pallas_call(functools.partial(attend_kernel, count, slots, tok, tile_k...  29.5 us
  transfers between devices with their start and end apart: 100, of which 35 were waited for; matrix products, arithmetic and copies ran while one was open for 6% of the time, Pallas kernels for 8%

profile of v2, /device:TPU:25, one launch (start us, length us, event | category | flops | bytes accessed | tf_op | source)
XLA Modules:
  0.0 834.6 jit_solution(11680583168132687098)
XLA Ops:
  9.2 7.7 collective-permute-done.3.refs_6_
  18.1 26.0 %collective-permute-done.4.refs_8_ = bf16[128,1664]{1,0:T(8,128)(2,1)} collective-permute-done((bf16[128,1664]{1,0:T(8,128)(2,1)S(1)}, bf16[128,1664]{1,0:T(8,128)(2,1)}, u32[]{:S(2)}, u32[]{:S(2)}) %collective-permute-start.4) | collective-permute-done | bytes 426016 | tf_op jit(solution)/shard_map/ppermute | solution.py:930
  70.3 21.9 %project.1 = (bf16[3,512,1024]{2,1,0:T(8,128)(2,1)}, bf16[3,512,1024]{2,1,0:T(8,128)(2,1)}, bf16[1024,1024]{1,0:T(8,128)(2,1)}, bf16[2,1024,1536]{2,1,0:T(8,128)(2,1)}, f32[8,1024]{1,0:T(8,128)}) custom-call(s32[10]{0:T(128)} %stack.52.place, bf16[2,512,1024]{2,1,0:T(8,128)(2,1)} %refs_0_.7, bf16[512,1024]{1,0:T(8,128)(2,1)} %collective-permute-done.refs_1_, ...), custom_call_target="tpu_custom_call" | custom-call | flops 6442450944 | bytes 29360128 | tf_op jit(solution)/shard_map/project/pallas_call | solution.py:380
  121.4 7.0 collective-permute-done.48.refs_23_
  129.3 20.4 %collective-permute-done.50.refs_25_ = bf16[352,512]{1,0:T(8,128)(2,1)} collective-permute-done((bf16[352,512]{1,0:T(8,128)(2,1)}, bf16[352,512]{1,0:T(8,128)(2,1)}, u32[]{:S(2)}, u32[]{:S(2)}) %collective-permute-start.50) | collective-permute-done | bytes 360480 | tf_op jit(solution)/shard_map/ppermute | solution.py:930
  156.5 11.5 %collective-permute-done.34.refs_7_ = bf16[128,2816]{1,0:T(8,128)(2,1)S(1)} collective-permute-done((bf16[128,2816]{1,0:T(8,128)(2,1)S(1)}, bf16[128,2816]{1,0:T(8,128)(2,1)S(1)}, u32[]{:S(2)}, u32[]{:S(2)}) %collective-permute-start.34) | collective-permute-done | bytes 720928 | tf_op jit(solution)/shard_map/ppermute | solution.py:930
  168.2 43.0 %collective-permute-done.36.refs_9_ = bf16[128,2816]{1,0:T(8,128)(2,1)S(1)} collective-permute-done((bf16[128,2816]{1,0:T(8,128)(2,1)S(1)}, bf16[128,2816]{1,0:T(8,128)(2,1)S(1)}, u32[]{:S(2)}, u32[]{:S(2)}) %collective-permute-start.36) | collective-permute-done | bytes 720928 | tf_op jit(solution)/shard_map/ppermute | solution.py:930
  233.6 29.5 %attend.1 = (bf16[512,1024]{1,0:T(8,128)(2,1)S(1)}, bf16[512,1024]{1,0:T(8,128)(2,1)S(1)}, f32[4,8,2048]{2,1,0:T(8,128)S(1)}) custom-call(s32[4]{0:T(128)S(1)} %add.686.order, bf16[3,512,1024]{2,1,0:T(8,128)(2,1)S(1)} %collective-permute-done.31.refs_0_, bf16[3,512,1024]{2,1,0:T(8,128)(2,1)} %get-tuple-element.54.refs_1_), custom_call_target="tpu_custom_call" | custom-call | flops 17179869184 | bytes 8388608 | tf_op jit(solution)/shard_map/attend/pallas_call | solution.py:127
  266.2 16.5 %collective-permute-done.39.refs_12_ = bf16[128,2816]{1,0:T(8,128)(2,1)S(1)} collective-permute-done((bf16[128,2816]{1,0:T(8,128)(2,1)}, bf16[128,2816]{1,0:T(8,128)(2,1)S(1)}, u32[]{:S(2)}, u32[]{:S(2)}) %collective-permute-start.39) | collective-permute-done | bytes 720928 | tf_op jit(solution)/shard_map/ppermute | solution.py:930
  286.2 9.1 %output_projection.1 = (f32[1024,1024]{1,0:T(8,128)}, bf16[1024,1024]{1,0:T(8,128)(2,1)}, bf16[1024,1024]{1,0:T(8,128)(2,1)}) custom-call(s32[10]{0:T(128)} %stack.52.place, bf16[2,512,1024]{2,1,0:T(8,128)(2,1)} %refs_0_.7, bf16[512,1024]{1,0:T(8,128)(2,1)} %collective-permute-done.refs_1_, bf16[128,512]{1,0:T(8,128)(2,1)} %copy-done.19, ...), custom_call_target="tpu_custom_call" | custom-call | flops 2147483648 | bytes 16777216 | tf_op jit(solution)/shard_map/output_projection/pallas_call | solution.py:452
  295.3 11.2 %collective-permute-done.2.refs_1_ = bf16[512,1024]{1,0:T(8,128)(2,1)S(1)} collective-permute-done((bf16[512,1024]{1,0:T(8,128)(2,1)S(1)}, bf16[512,1024]{1,0:T(8,128)(2,1)S(1)}, u32[]{:S(2)}, u32[]{:S(2)}) %collective-permute-start.2) | collective-permute-done | bytes 1048608 | tf_op jit(solution)/shard_map/ppermute | solution.py:927
  307.5 75.9 %mlp.1 = (f32[2,512,1024]{2,1,0:T(8,128)}, bf16[512,1024]{1,0:T(8,128)(2,1)}, f32[1024,1024]{1,0:T(8,128)}, bf16[1024,1024]{1,0:T(8,128)(2,1)}, f32[8,1024]{1,0:...) custom-call(s32[10]{0:T(128)} %stack.52.place, ...), custom_call_target="tpu_custom_call" | custom-call | flops 47244640256 | bytes 55574528 | tf_op jit(solution)/shard_map/mlp/pallas_call | solution.py:644
  384.6 7.5 grad_attended.1
  398.1 69.9 %attend_back.1 = (bf16[3,512,1024]{2,1,0:T(8,128)(2,1)}, bf16[3,512,1024]{2,1,0:T(8,128)(2,1)}) custom-call(s32[4]{0:T(128)} %copy-done.5, bf16[3,512,1024]{2,1,0:T(8,128)(2,1)} %copy-done.1, bf16[3,512,1024]{2,1,0:T(8,128)(2,1)} %get-tuple-element.54.refs_1_, bf16[512,1024]{1,0:T(8,128)(2,1)} %copy-done.2, bf16[512,1024]{1,0:T(8,128)(2,1)} %copy-done.6, ...), custom_call_target="tpu_custom_call" | custom-call | flops 42949672960 | bytes 16777216 | tf_op jit(solution)/shard_map/attend_back/pallas_call | solution.py:267
  474.0 27.6 %tail.1 = (f32[2,512,1024]{2,1,0:T(8,128)}, bf16[512,1024]{1,0:T(8,128)(2,1)}, f32[2,512,1024]{2,1,0:T(8,128)}, bf16[512,1024]{1,0:T(8,128)(2,1)}, f32[8,1024]{1...) custom-call(s32[10]{0:T(128)} %stack.52.place, bf16[2,512,1024]{2,1,0:T(8,128)(2,1)} %refs_0_.7, ...), custom_call_target="tpu_custom_call" | custom-call | flops 12884901888 | bytes 37748736 | tf_op jit(solution)/shard_map/tail/pallas_call | solution.py:843
  514.8 67.8 %collective-permute-done.80 = bf16[4,128,512]{2,1,0:T(8,128)(2,1)} collective-permute-done((bf16[4,128,512]{2,1,0:T(8,128)(2,1)}, bf16[4,128,512]{2,1,0:T(8,128)(2,1)}, u32[]{:S(2)}, u32[]{:S(2)}) %collective-permute-start.80) | collective-permute-done | bytes 524320 | tf_op jit(solution)/shard_map/ppermute | solution.py:930
  594.6 6.4 collective-permute-done.83
  616.5 31.4 %collective-permute-done.67 = f32[8,1024]{1,0:T(8,128)S(1)} collective-permute-done((f32[8,1024]{1,0:T(8,128)S(1)}, f32[8,1024]{1,0:T(8,128)S(1)}, u32[]{:S(2)}, u32[]{:S(2)}) %collective-permute-start.67) | collective-permute-done | bytes 32800 | tf_op jit(solution)/shard_map/ppermute | solution.py:930
  676.0 81.1 %collective-permute-done.75 = bf16[3,128,512]{2,1,0:T(8,128)(2,1)S(1)} collective-permute-done((bf16[3,128,512]{2,1,0:T(8,128)(2,1)S(1)}, bf16[3,128,512]{2,1,0:T(8,128)(2,1)S(1)}, u32[]{:S(2)}, u32[]{:S(2)}) %collective-permute-start.75) | collective-permute-done | bytes 393248 | tf_op jit(solution)/shard_map/ppermute | solution.py:930
  768.2 10.4 %collective-permute-done.65.part_ref = bf16[512,1024]{1,0:T(8,128)(2,1)S(1)} collective-permute-done((bf16[512,1024]{1,0:T(8,128)(2,1)S(1)}, bf16[512,1024]{1,0:T(8,128)(2,1)S(1)}, u32[]{:S(2)}, u32[]{:S(2)}) %collective-permute-start.65) | collective-permute-done | bytes 1048608 | tf_op jit(solution)/shard_map/ppermute | solution.py:927
  779.9 21.1 %collective-permute-done.64.part_ref = bf16[512,1024]{1,0:T(8,128)(2,1)S(1)} collective-permute-done((bf16[512,1024]{1,0:T(8,128)(2,1)S(1)}, bf16[512,1024]{1,0:T(8,128)(2,1)S(1)}, u32[]{:S(2)}, u32[]{:S(2)}) %collective-permute-start.64) | collective-permute-done | bytes 1048608 | tf_op jit(solution)/shard_map/ppermute | solution.py:927
  802.4 7.0 collective-permute-done.77
  809.6 8.1 collective-permute-start.78
  817.6 7.3 collective-permute-done.91
  (359 shorter events, 207.5 us)
Async XLA Ops:
  2.0 43.4 %collective-permute-start = (bf16[512,1024]{1,0:T(8,128)(2,1)S(1)}, bf16[512,1024]{1,0:T(8,128)(2,1)}, u32[]{:S(2)}, u32[]{:S(2)}) collective-permute-start(bf16[512,1024]{1,0:T(8,128)(2,1)S(1)} %dynamic-slice_bitcast_fusion.2), channel_id=1, source_target_pairs={{0,2},{1,3},{2,0},{3,1},{4,6},{5,7},{6,4},{7,5},{8,10},{9,11},{10,... | collective-permute-start | bytes 3145736 | tf_op jit(solution)/shard_map/ppermute | solution.py:927
  7.8 38.3 %collective-permute-start.5 = (bf16[128,1664]{1,0:T(8,128)(2,1)S(1)}, bf16[128,1664]{1,0:T(8,128)(2,1)}, u32[]{:S(2)}, u32[]{:S(2)}) collective-permute-start(bf16[128,1664]{1,0:T(8,128)(2,1)S(1)} %get-tuple-element.136.refs_4_), channel_id=1, source_target_pairs={{0,24},{4,28},{8,0},{12,4},{16,8},{20,12},{24,16},{28,20},{1,25},{... | collective-permute-start | bytes 1277960 | tf_op jit(solution)/shard_map/ppermute | solution.py:930
  7.9 38.4 %collective-permute-start.20 = (bf16[128,1664]{1,0:T(8,128)(2,1)S(1)}, bf16[128,1664]{1,0:T(8,128)(2,1)}, u32[]{:S(2)}, u32[]{:S(2)}) collective-permute-start(bf16[128,1664]{1,0:T(8,128)(2,1)S(1)} %get-tuple-element.136.refs_4_), channel_id=1, source_target_pairs={{0,4},{4,0},{8,12},{12,8},{16,20},{20,16},{24,28},{28,24},{1,5},{5... | collective-permute-start | bytes 1277960 | tf_op jit(solution)/shard_map/ppermute | solution.py:930
  92.2 140.9 %collective-permute-start.31 = (bf16[3,512,1024]{2,1,0:T(8,128)(2,1)}, bf16[3,512,1024]{2,1,0:T(8,128)(2,1)S(1)}, u32[]{:S(2)}, u32[]{:S(2)}) collective-permute-start(bf16[3,512,1024]{2,1,0:T(8,128)(2,1)} %get-tuple-element.53), channel_id=1, source_target_pairs={{0,1},{1,0},{2,3},{3,2},{4,5},{5,4},{6,7},{7,6},{8,9},{9,8},{10,11... | collective-permute-start | bytes 9437192 | tf_op jit(solution)/shard_map/ppermute | solution.py:927
  149.7 61.6 %collective-permute-start.36 = (bf16[128,2816]{1,0:T(8,128)(2,1)S(1)}, bf16[128,2816]{1,0:T(8,128)(2,1)S(1)}, u32[]{:S(2)}, u32[]{:S(2)}) collective-permute-start(bf16[128,2816]{1,0:T(8,128)(2,1)S(1)} %pad_maximum_fusion.refs_5_), channel_id=1, source_target_pairs={{0,16},{4,20},{8,24},{12,28},{16,0},{20,4},{24,8},{28,12},{1,17},{... | collective-permute-start | bytes 2162696 | tf_op jit(solution)/shard_map/ppermute | solution.py:930
  152.3 59.2 %collective-permute-start.38 = (bf16[128,2816]{1,0:T(8,128)(2,1)S(1)}, bf16[128,2816]{1,0:T(8,128)(2,1)}, u32[]{:S(2)}, u32[]{:S(2)}) collective-permute-start(bf16[128,2816]{1,0:T(8,128)(2,1)S(1)} %pad_maximum_fusion.refs_5_), channel_id=1, source_target_pairs={{0,24},{4,28},{8,0},{12,4},{16,8},{20,12},{24,16},{28,20},{1,25},{... | collective-permute-start | bytes 2162696 | tf_op jit(solution)/shard_map/ppermute | solution.py:930
  156.2 56.5 %collective-permute-start.33 = (bf16[128,2816]{1,0:T(8,128)(2,1)S(1)}, bf16[128,2816]{1,0:T(8,128)(2,1)S(1)}, u32[]{:S(2)}, u32[]{:S(2)}) collective-permute-start(bf16[128,2816]{1,0:T(8,128)(2,1)S(1)} %pad_maximum_fusion.refs_5_), channel_id=1, source_target_pairs={{0,4},{4,0},{8,12},{12,8},{16,20},{20,16},{24,28},{28,24},{1,5},{5... | collective-permute-start | bytes 2162696 | tf_op jit(solution)/shard_map/ppermute | solution.py:930
  168.0 46.4 %collective-permute-start.49 = (bf16[352,512]{1,0:T(8,128)(2,1)}, bf16[352,512]{1,0:T(8,128)(2,1)S(1)}, u32[]{:S(2)}, u32[]{:S(2)}) collective-permute-start(bf16[352,512]{1,0:T(8,128)(2,1)} %collective-permute-done.48.refs_23_), channel_id=1, source_target_pairs={{0,4},{4,0},{8,12},{12,8},{16,20},{20,16},{24,28},{28,24},{1,5},{5... | collective-permute-start | bytes 1081352 | tf_op jit(solution)/shard_map/ppermute | solution.py:930
  468.5 41.6 %collective-permute-start.93 = (bf16[2816,512]{1,0:T(8,128)(2,1)}, bf16[2816,512]{1,0:T(8,128)(2,1)}, u32[]{:S(2)}, u32[]{:S(2)}) collective-permute-start(bf16[2816,512]{1,0:T(8,128)(2,1)} %bitcast.58), channel_id=1, source_target_pairs={{0,1},{1,0},{2,3},{3,2},{4,5},{5,4},{6,7},{7,6},{8,9},{9,8},{10,11... | collective-permute-start | bytes 8650760 | tf_op jit(solution)/shard_map/ppermute | solution.py:927
  501.6 83.0 %collective-permute-start.72 = (bf16[3,1024,512]{2,1,0:T(8,128)(2,1)}, bf16[3,1024,512]{2,1,0:T(8,128)(2,1)}, u32[]{:S(2)}, u32[]{:S(2)}) collective-permute-start(bf16[3,1024,512]{2,1,0:T(8,128)(2,1)} %get-tuple-element.81), channel_id=1, source_target_pairs={{0,1},{1,0},{2,3},{3,2},{4,5},{5,4},{6,7},{7,6},{8,9},{9,8},{10,11... | collective-permute-start | bytes 9437192 | tf_op jit(solution)/shard_map/ppermute | solution.py:927
  507.3 160.2 %collective-permute-start.87 = (bf16[2,4,128,1408]{3,2,0,1:T(8,128)(2,1)}, bf16[2,4,128,1408]{3,2,0,1:T(8,128)(2,1)}, u32[]{:S(2)}, u32[]{:S(2)}) collective-permute-start(bf16[2,4,128,1408]{3,2,0,1:T(8,128)(2,1)} %fusion), channel_id=1, source_target_pairs={{0,4},{4,0},{8,12},{12,8},{16,20},{20,16},{24,28},{28,24},{1,5},{5... | collective-permute-start | bytes 8650760 | tf_op jit(solution)/shard_map/ppermute | solution.py:930
  509.8 72.7 %collective-permute-start.80 = (bf16[4,128,512]{2,1,0:T(8,128)(2,1)}, bf16[4,128,512]{2,1,0:T(8,128)(2,1)}, u32[]{:S(2)}, u32[]{:S(2)}) collective-permute-start(bf16[4,128,512]{2,1,0:T(8,128)(2,1)} %fusion.22), channel_id=1, source_target_pairs={{0,4},{4,0},{8,12},{12,8},{16,20},{20,16},{24,28},{28,24},{1,5},{5... | collective-permute-start | bytes 1572872 | tf_op jit(solution)/shard_map/ppermute | solution.py:930
  513.0 100.4 %collective-permute-start.94 = (bf16[4,352,512]{2,1,0:T(8,128)(2,1)}, bf16[4,352,512]{2,1,0:T(8,128)(2,1)S(1)}, u32[]{:S(2)}, u32[]{:S(2)}) collective-permute-start(bf16[4,352,512]{2,1,0:T(8,128)(2,1)} %fusion.2), channel_id=1, source_target_pairs={{0,4},{4,0},{8,12},{12,8},{16,20},{20,16},{24,28},{28,24},{1,5},{5... | collective-permute-start | bytes 4325384 | tf_op jit(solution)/shard_map/ppermute | solution.py:930
  514.2 102.2 %collective-permute-start.61 = (bf16[512,1024]{1,0:T(8,128)(2,1)}, bf16[512,1024]{1,0:T(8,128)(2,1)S(1)}, u32[]{:S(2)}, u32[]{:S(2)}) collective-permute-start(bf16[512,1024]{1,0:T(8,128)(2,1)} %get-tuple-element.63), channel_id=1, source_target_pairs={{0,2},{1,3},{2,0},{3,1},{4,6},{5,7},{6,4},{7,5},{8,10},{9,11},{10,... | collective-permute-start | bytes 3145736 | tf_op jit(solution)/shard_map/ppermute | solution.py:927
  589.0 71.4 %collective-permute-start.73 = (bf16[3,4,128,512]{3,2,0,1:T(8,128)(2,1)}, bf16[3,4,128,512]{3,2,0,1:T(8,128)(2,1)}, u32[]{:S(2)}, u32[]{:S(2)}) collective-permute-start(bf16[3,4,128,512]{3,2,0,1:T(8,128)(2,1)} %fusion.1), channel_id=1, source_target_pairs={{0,4},{4,0},{8,12},{12,8},{16,20},{20,16},{24,28},{28,24},{1,5},{5... | collective-permute-start | bytes 4718600 | tf_op jit(solution)/shard_map/ppermute | solution.py:930
  671.1 89.0 %collective-permute-start.88 = (bf16[2,128,1408]{2,1,0:T(8,128)(2,1)S(1)}, bf16[2,128,1408]{2,1,0:T(8,128)(2,1)S(1)}, u32[]{:S(2)}, u32[]{:S(2)}) collective-permute-start(bf16[2,128,1408]{2,1,0:T(8,128)(2,1)S(1)} %get-tuple-element.96), channel_id=1, source_target_pairs={{0,8},{4,12},{8,16},{12,20},{16,24},{20,28},{24,0},{28,4},{1,9},{5... | collective-permute-start | bytes 2162696 | tf_op jit(solution)/shard_map/ppermute | solution.py:930
  671.2 92.8 %collective-permute-start.89 = (bf16[2,128,1408]{2,1,0:T(8,128)(2,1)S(1)}, bf16[2,128,1408]{2,1,0:T(8,128)(2,1)S(1)}, u32[]{:S(2)}, u32[]{:S(2)}) collective-permute-start(bf16[2,128,1408]{2,1,0:T(8,128)(2,1)S(1)} %get-tuple-element.98), channel_id=1, source_target_pairs={{0,16},{4,20},{8,24},{12,28},{16,0},{20,4},{24,8},{28,12},{1,17},{... | collective-permute-start | bytes 2162696 | tf_op jit(solution)/shard_map/ppermute | solution.py:930
  671.3 93.6 %collective-permute-start.90 = (bf16[2,128,1408]{2,1,0:T(8,128)(2,1)S(1)}, bf16[2,128,1408]{2,1,0:T(8,128)(2,1)S(1)}, u32[]{:S(2)}, u32[]{:S(2)}) collective-permute-start(bf16[2,128,1408]{2,1,0:T(8,128)(2,1)S(1)} %get-tuple-element.97), channel_id=1, source_target_pairs={{0,24},{4,28},{8,0},{12,4},{16,8},{20,12},{24,16},{28,20},{1,25},{... | collective-permute-start | bytes 2162696 | tf_op jit(solution)/shard_map/ppermute | solution.py:930
  672.6 84.5 %collective-permute-start.75 = (bf16[3,128,512]{2,1,0:T(8,128)(2,1)S(1)}, bf16[3,128,512]{2,1,0:T(8,128)(2,1)S(1)}, u32[]{:S(2)}, u32[]{:S(2)}) collective-permute-start(bf16[3,128,512]{2,1,0:T(8,128)(2,1)S(1)} %get-tuple-element.101), channel_id=1, source_target_pairs={{0,16},{4,20},{8,24},{12,28},{16,0},{20,4},{24,8},{28,12},{1,17},{... | collective-permute-start | bytes 1179656 | tf_op jit(solution)/shard_map/ppermute | solution.py:930
  675.0 83.2 %collective-permute-start.76 = (bf16[3,128,512]{2,1,0:T(8,128)(2,1)S(1)}, bf16[3,128,512]{2,1,0:T(8,128)(2,1)S(1)}, u32[]{:S(2)}, u32[]{:S(2)}) collective-permute-start(bf16[3,128,512]{2,1,0:T(8,128)(2,1)S(1)} %get-tuple-element.100), channel_id=1, source_target_pairs={{0,24},{4,28},{8,0},{12,4},{16,8},{20,12},{24,16},{28,20},{1,25},{... | collective-permute-start | bytes 1179656 | tf_op jit(solution)/shard_map/ppermute | solution.py:930
  758.2 42.8 %collective-permute-start.64 = (bf16[512,1024]{1,0:T(8,128)(2,1)S(1)}, bf16[512,1024]{1,0:T(8,128)(2,1)S(1)}, u32[]{:S(2)}, u32[]{:S(2)}) collective-permute-start(bf16[512,1024]{1,0:T(8,128)(2,1)S(1)} %copy-done.20), channel_id=1, source_target_pairs={{0,2},{1,3},{2,0},{3,1},{4,6},{5,7},{6,4},{7,5},{8,10},{9,11},{10,... | collective-permute-start | bytes 3145736 | tf_op jit(solution)/shard_map/ppermute | solution.py:927
  760.1 42.3 %collective-permute-start.99 = (bf16[352,512]{1,0:T(8,128)(2,1)S(1)}, bf16[352,512]{1,0:T(8,128)(2,1)S(1)}, u32[]{:S(2)}, u32[]{:S(2)}) collective-permute-start(bf16[352,512]{1,0:T(8,128)(2,1)S(1)} %add_convert_fusion.6), channel_id=1, source_target_pairs={{0,1},{1,0},{2,3},{3,2},{4,5},{5,4},{6,7},{7,6},{8,9},{9,8},{10,11... | collective-permute-start | bytes 1081352 | tf_op jit(solution)/shard_map/ppermute | solution.py:927
  764.0 45.4 %collective-permute-start.77 = (bf16[3,128,512]{2,1,0:T(8,128)(2,1)S(1)}, bf16[3,128,512]{2,1,0:T(8,128)(2,1)S(1)}, u32[]{:S(2)}, u32[]{:S(2)}) collective-permute-start(bf16[3,128,512]{2,1,0:T(8,128)(2,1)S(1)} %get-tuple-element.94), channel_id=1, source_target_pairs={{0,2},{1,3},{2,0},{3,1},{4,6},{5,7},{6,4},{7,5},{8,10},{9,11},{10,... | collective-permute-start | bytes 1179656 | tf_op jit(solution)/shard_map/ppermute | solution.py:927
  766.9 57.9 %collective-permute-start.91 = (bf16[2,128,1408]{2,1,0:T(8,128)(2,1)S(1)}, bf16[2,128,1408]{2,1,0:T(8,128)(2,1)S(1)}, u32[]{:S(2)}, u32[]{:S(2)}) collective-permute-start(bf16[2,128,1408]{2,1,0:T(8,128)(2,1)S(1)} %get-tuple-element.90), channel_id=1, source_target_pairs={{0,2},{1,3},{2,0},{3,1},{4,6},{5,7},{6,4},{7,5},{8,10},{9,11},{10,... | collective-permute-start | bytes 2162696 | tf_op jit(solution)/shard_map/ppermute | solution.py:927
  (135 other events, 2557.6 us)

commit v3 on v2

--- a/solution.py
+++ b/solution.py
@@ -45,23 +45,7 @@
     return jnp.concatenate([square, scores[:, side:]], axis=1)
 
 
-def attend_kernel(count, slots, tok, tile_k, order, *refs):
-    pieces = refs[:count]
-    outs = refs[count : 2 * count]
-    lse_ref = refs[2 * count]
-    qz, kn, vt, ot = refs[2 * count + 1 :]
-    for source in range(count):
-        for slot in range(slots):
-            cols = pl.ds(pl.multiple_of(order[source * slots + slot] * tok, tok), tok)
-            take = slice(slot * tok, (slot + 1) * tok)
-            query = pieces[source][0, :, take] * jnp.asarray(HEAD_DIM**-0.5, BF16)
-            for head in range(2):
-                qz[head, :, cols] = head_rows(query, head)
-            kn[cols, :] = pieces[source][1, :, take].T
-            vt[:, cols] = pieces[source][2, :, take]
-    length = count * slots * tok
-
-
+def attend_body(length, tile_k, qz, kn, vt, ot, lse_ref):
     def score(sub, head):
         start = sub * tile_k
         return causal(dot(kn[start : start + tile_k, :], qz[head, :, start:]))
@@ -97,6 +81,24 @@
         ot[rows, done] = (mixed[:, :tile_k] / total[:, :tile_k]).astype(BF16)
         lse_ref[0, head : head + 1, done] = peak[:, :tile_k] + jnp.log(total[:, :tile_k])
         carries[head] = (peak[:, tile_k:], total[:, tile_k:], mixed[:, tile_k:])
+
+
+def attend_kernel(count, slots, tok, tile_k, order, *refs):
+    pieces = refs[:count]
+    outs = refs[count : 2 * count]
+    lse_ref = refs[2 * count]
+    qz, kn, vt, ot = refs[2 * count + 1 :]
+    for source in range(count):
+        for slot in range(slots):
+            cols = pl.ds(pl.multiple_of(order[source * slots + slot] * tok, tok), tok)
+            take = slice(slot * tok, (slot + 1) * tok)
+            query = pieces[source][0, :, take] * jnp.asarray(HEAD_DIM**-0.5, BF16)
+            for head in range(2):
+                qz[head, :, cols] = head_rows(query, head)
+            kn[cols, :] = pieces[source][1, :, take].T
+            vt[:, cols] = pieces[source][2, :, take]
+    length = count * slots * tok
+    attend_body(length, tile_k, qz, kn, vt, ot, lse_ref)
     for source in range(count):
         for slot in range(slots):
             cols = pl.ds(pl.multiple_of(order[source * slots + slot] * tok, tok), tok)
@@ -308,8 +310,10 @@
     def _():
         for number in range(count):
             at = pl.ds(pl.multiple_of(place[2 + number] * rows, rows), rows)
-            full_ref[core, at, :] = own[number][:, : 3 * wide]
-            full_ref[1 - core, at, :] = other[number][:, : 3 * wide]
+            for which in range(3):
+                columns = slice(which * wide, (which + 1) * wide)
+                full_ref[core, which, at, :] = own[number][:, columns]
+                full_ref[1 - core, which, at, :] = other[number][:, columns]
             column[at, :] = own[number][:, 3 * wide :]
         gains_ref[...] = column[...].T[:8].astype(F32)
         gain = gains_ref[0:1, :]
@@ -318,7 +322,7 @@
             scale = lax.rsqrt(jnp.mean(values * values, axis=1, keepdims=True) + epsilon)
             normed_ref[slot * tok : (slot + 1) * tok, :] = (values * scale * gain).astype(BF16)
 
-    weight = full_ref[half, :, pl.ds(pl.multiple_of(kind * wide, wide), wide)]
+    weight = full_ref[half, kind]
     raw = nt(weight.T, normed_ref[...])
 
     def store(value):
@@ -372,7 +376,7 @@
             pl.BlockSpec((1, wide, span), lambda s, p: (jnp.minimum(s, 2), 0, 0)),
             pl.BlockSpec((1, wide, span), lambda s, p: (jnp.maximum(s - 3, 0), 0, 0)),
             whole_block((span, depth)),
-            whole_block((2, depth, 3 * wide)),
+            whole_block((2, 3, depth, wide)),
             whole_block((8, depth)),
         ],
         scratch_shapes=[pltpu.VMEM((depth, 128), BF16)],
@@ -383,7 +387,7 @@
             jax.ShapeDtypeStruct((3, wide, span), BF16),
             jax.ShapeDtypeStruct((3, wide, span), BF16),
             jax.ShapeDtypeStruct((span, depth), BF16),
-            jax.ShapeDtypeStruct((2, depth, 3 * wide), BF16),
+            jax.ShapeDtypeStruct((2, 3, depth, wide), BF16),
             jax.ShapeDtypeStruct((8, depth), F32),
         ],
         grid_spec=grid_spec,
@@ -471,8 +475,9 @@
     grads = refs[:slots]
     middle_ref, normed_ref, gains_ref = refs[slots : slots + 3]
     base = slots + 3
-    own_gu, other_gu = refs[base : base + count], refs[base + count : base + 2 * count]
-    own_d, other_d = refs[base + 2 * count : base + 3 * count], refs[base + 3 * count : base + 4 * count]
+    own_g, other_g, own_u, other_u, own_d, other_d = (
+        refs[base + number * count : base + (number + 1) * count] for number in range(6)
+    )
     (
         out_ref,
         send_ref,
@@ -490,12 +495,13 @@
         acc,
         back,
         sems,
-    ) = refs[base + 4 * count :]
+    ) = refs[base + 6 * count :]
     step = pl.program_id(0)
     core = place[1]
     depth = og.shape[1]
     wide = depth // 2
     strip = 128
+    half_width = blocks * strip
     mine = pl.ds(pl.multiple_of(core * wide, wide), wide)
     others = pl.ds(pl.multiple_of((1 - core) * wide, wide), wide)
 
@@ -503,15 +509,16 @@
         copies = []
         for number in range(count):
             at = pl.ds(pl.multiple_of(place[2 + number] * rows, rows), rows)
-            copies.append((own_gu[number], wgu.at[0, at, :], 0))
-            copies.append((other_gu[number], wgu.at[1, at, :], 0))
+            for which, (gate, up) in enumerate(((own_g, own_u), (other_g, other_u))):
+                copies.append((gate[number], wgu.at[which, at, pl.ds(0, half_width)]))
+                copies.append((up[number], wgu.at[which, at, pl.ds(half_width, half_width)]))
         for number in range(count):
             at = pl.ds(pl.multiple_of(place[2 + number] * down_rows, down_rows), down_rows)
-            copies.append((own_d[number], wd.at[at, mine], 1))
-            copies.append((other_d[number], wd.at[at, others], 1))
+            copies.append((own_d[number], wd.at[at, mine]))
+            copies.append((other_d[number], wd.at[at, others]))
         return [
             pltpu.make_async_copy(source, target, sems.at[number])
-            for number, (source, target, _) in enumerate(copies)
+            for number, (source, target) in enumerate(copies)
         ]
 
     @pl.when(step == 0)
@@ -527,7 +534,6 @@
         for copy in copies:
             copy.wait()
 
-    half_width = blocks * strip
     at = pl.ds(pl.multiple_of(step * strip, strip), strip)
     up_at = pl.ds(pl.multiple_of(half_width + step * strip, strip), strip)
     gate_w = jnp.concatenate([wgu[0, :, at], wgu[1, :, at]], axis=1)
@@ -595,13 +601,12 @@
             lax.fori_loop(0, tok // chunk, finish, 0)
 
 
-def mlp(grads, grads_received, middle, normed, gains, gate_up, down, place):
+def mlp(grads, grads_received, middle, normed, gains, gate, up, down, place):
     slots, tok, depth = grads.shape
-    own_gu, other_gu = gate_up
     own_d, other_d = down
-    count, rows = len(own_gu), own_gu[0].shape[0]
+    count, rows = len(own_d), gate[0][0].shape[0]
     down_rows = own_d[0].shape[0]
-    half_width = own_gu[0].shape[1] // 2
+    half_width = gate[0][0].shape[1]
     wide = depth // 2
     span = slots * tok
     blocks = half_width // 128
@@ -619,7 +624,7 @@
             pl.BlockSpec((span, depth), lambda s, p: (0, 0), pipeline_mode=once),
             whole_block((8, depth)),
         ]
-        + [pl.BlockSpec(memory_space=pl.ANY)] * (4 * count),
+        + [pl.BlockSpec(memory_space=pl.ANY)] * (6 * count),
         out_specs=[
             pl.BlockSpec((1, tok, depth), lambda s, p: (p[0], 0, 0), pipeline_mode=once),
             pl.BlockSpec(((slots - 1) * tok, depth), lambda s, p: (0, 0), pipeline_mode=once),
@@ -638,7 +643,7 @@
             pltpu.VMEM((depth, span), BF16),
             pltpu.VMEM((span, depth), F32),
             pltpu.VMEM((span, depth), F32),
-            pltpu.SemaphoreType.DMA((4 * count,)),
+            pltpu.SemaphoreType.DMA((6 * count,)),
         ],
     )
     return pl.pallas_call(
@@ -662,7 +667,20 @@
             transcendentals=2 * span * half_width,
         ),
         name="mlp",
-    )(place, grads, *grads_received, middle, normed, gains, *own_gu, *other_gu, *own_d, *other_d)
+    )(
+        place,
+        grads,
+        *grads_received,
+        middle,
+        normed,
+        gains,
+        *gate[0],
+        *gate[1],
+        *up[0],
+        *up[1],
+        *own_d,
+        *other_d,
+    )
 
 
 def grad_attended_kernel(place, low_ref, full_ref, att_other, att_own, ga_other, ga_own, sent, kept):
@@ -757,7 +775,7 @@
             first_send[...] = rows[tok:].astype(BF16)
 
         grad = grad * jnp.where(kind == 2, 0.5, 1.0).astype(BF16)
-        acc[...] += nt(grad.T, full_ref[0])
+        acc[...] += nt(grad.T, full_ref[0, 0])
         result[0] = nt(normed_t[...], grad).astype(BF16)
 
     @pl.when(target == 0)
@@ -823,7 +841,7 @@
         + [
             pl.BlockSpec((1, wide, span), lambda s, p: (jnp.minimum(s, 2), 0, 0)),
             pl.BlockSpec((1, wide, span), lambda s, p: (jnp.maximum(s - 3, 0), 0, 0)),
-            pl.BlockSpec((1, depth, wide), lambda s, p: (half(s, p), 0, s % 3)),
+            pl.BlockSpec((1, 1, depth, wide), lambda s, p: (half(s, p), s % 3, 0, 0)),
             whole_block((span, depth)),
             pl.BlockSpec((span, depth), lambda s, p: (0, 0), pipeline_mode=once),
             whole_block((8, depth)),
@@ -893,6 +911,545 @@
     )(slot, whole, part)
 
 
+MESH = pl.DeviceIdType.MESH
+
+
+def seats():
+    shard = lax.axis_index("fsdp")
+    seat = lax.axis_index("seq")
+    return (shard // 2, shard % 2, seat // 2, seat % 2)
+
+
+def meet(line, keys):
+    shard = lax.axis_index("fsdp")
+    seat = lax.axis_index("seq")
+    partners = []
+    if "z" in keys:
+        partners += [{"fsdp": lax.rem(shard + 2 * jump, 2 * line)} for jump in range(1, line)]
+    if "y" in keys:
+        partners.append({"fsdp": shard + 1 - 2 * (shard % 2)})
+    if "x" in keys:
+        partners.append({"seq": lax.rem(seat + 2, 4)})
+    if "core" in keys:
+        partners.append({"seq": seat + 1 - 2 * (seat % 2)})
+    barrier = pltpu.get_barrier_semaphore()
+    for partner in partners:
+        pl.semaphore_signal(barrier, inc=1, device_id=partner, device_id_type=MESH)
+    pl.semaphore_wait(barrier, len(partners))
+
+
+def send(source, target, sems, number, partner):
+    return pltpu.make_async_remote_copy(
+        src_ref=source,
+        dst_ref=target,
+        send_sem=sems.at[0, number],
+        recv_sem=sems.at[1, number],
+        device_id=partner,
+        device_id_type=MESH,
+    )
+
+
+def to_core_partner():
+    seat = lax.axis_index("seq")
+    return {"seq": seat + 1 - 2 * (seat % 2)}
+
+
+def to_x_partner():
+    return {"seq": lax.rem(lax.axis_index("seq") + 2, 4)}
+
+
+def to_y_partner():
+    shard = lax.axis_index("fsdp")
+    return {"fsdp": shard + 1 - 2 * (shard % 2)}
+
+
+def to_z_partner(line, jump):
+    return {"fsdp": lax.rem(lax.axis_index("fsdp") + 2 * jump, 2 * line)}
+
+
+class Gather:
+    def __init__(self, line, shard, own, other, sems, split=False):
+        self.line, self.shard, self.own, self.other = line, shard, own, other
+        self.sems = sems
+        z, y, x, _ = seats()
+        self.z, self.y = z, y
+        rows = own.shape[2]
+        if split:
+            self.rows = pl.ds(pl.multiple_of(x * (rows // 2), rows // 2), rows // 2)
+        else:
+            self.rows = pl.ds(0, rows)
+
+    def here(self):
+        return pltpu.make_async_copy(
+            self.shard.at[self.rows, :],
+            self.own.at[self.z, self.y, self.rows, :],
+            self.sems.at[0, self.line + 2],
+        )
+
+    def along_z(self):
+        return [
+            send(
+                self.shard.at[self.rows, :],
+                self.own.at[self.z, self.y, self.rows, :],
+                self.sems,
+                jump - 1,
+                to_z_partner(self.line, jump),
+            )
+            for jump in range(1, self.line)
+        ]
+
+    def along_y(self):
+        part = self.own.at[:, self.y, self.rows, :]
+        return send(part, part, self.sems, self.line - 1, to_y_partner())
+
+    def along_x(self):
+        part = self.own.at[:, :, self.rows, :]
+        return send(part, part, self.sems, self.line, to_x_partner())
+
+    def along_core(self):
+        return send(self.own, self.other, self.sems, self.line + 1, to_core_partner())
+
+    def start_z(self):
+        self.here().start()
+        for copy in self.along_z():
+            copy.start()
+
+    def wait_z(self):
+        self.here().wait()
+        for copy in self.along_z():
+            copy.wait()
+
+
+def gather_sems(line):
+    return pltpu.SemaphoreType.DMA((2, line + 3))
+
+
+def front_kernel(line, tok, *refs):
+    (
+        inputs,
+        firsts,
+        q_shard,
+        k_shard,
+        v_shard,
+        o_shard,
+        d_shard,
+        cos_ref,
+        sin_ref,
+        x_received,
+        f_received,
+        heads_own,
+        heads_received,
+        normed_ref,
+        full_ref,
+        gains_ref,
+        o_own,
+        o_other,
+        d_own,
+        xs,
+        fs,
+        q_own,
+        q_other,
+        k_own,
+        k_other,
+        v_own,
+        v_other,
+        outgoing,
+        q_sems,
+        k_sems,
+        v_sems,
+        o_sems,
+        d_sems,
+        swap_sems,
+        head_sems,
+        local_sems,
+    ) = refs
+    step = pl.program_id(0)
+    _, _, side, core = seats()
+    wide = outgoing.shape[1]
+    depth = 2 * wide
+    gathers = [
+        Gather(line, q_shard, q_own, q_other, q_sems),
+        Gather(line, k_shard, k_own, k_other, k_sems),
+        Gather(line, v_shard, v_own, v_other, v_sems),
+    ]
+    query, key, value = gathers
+    out = Gather(line, o_shard, o_own, o_other, o_sems)
+    down = Gather(line, d_shard, d_own, d_own, d_sems, split=True)
+    swap_x = send(inputs.at[1 - side], x_received, swap_sems, 0, to_x_partner())
+    swap_f = send(firsts.at[1 - side], f_received, swap_sems, 1, to_x_partner())
+    load_x = pltpu.make_async_copy(inputs.at[side], xs.at[pl.ds(0, tok), :], local_sems.at[0])
+    load_f = pltpu.make_async_copy(firsts.at[side], fs.at[pl.ds(0, tok), :], local_sems.at[1])
+    more_x = pltpu.make_async_copy(x_received, xs.at[pl.ds(tok, tok), :], local_sems.at[2])
+    more_f = pltpu.make_async_copy(f_received, fs.at[pl.ds(tok, tok), :], local_sems.at[3])
+
+    def weight(halves, columns):
+        return halves[:, :, :, columns].reshape(depth, wide)
+
+    def heads(number):
+        return send(
+            outgoing.at[number], heads_received.at[number], head_sems, number, to_core_partner()
+        )
+
+    saves = []
+    for number, (mine, others) in enumerate(((q_own, q_other), (k_own, k_other), (v_own, v_other))):
+        for which, ref in ((0, mine), (1, others)):
+            half = core if which == 0 else 1 - core
+            saves.append(
+                pltpu.make_async_copy(
+                    ref.at[:, :, :, pl.ds(0, wide)],
+                    full_ref.at[half, number],
+                    local_sems.at[4 + 2 * number + which],
+                )
+            )
+
+    @pl.when(step == 0)
+    def _():
+        meet(line, ("z", "y", "x", "core"))
+        swap_x.start()
+        load_x.start()
+        load_f.start()
+        query.start_z()
+        query.wait_z()
+        query.along_y().start()
+        key.start_z()
+        key.wait_z()
+        key.along_y().start()
+        value.start_z()
+        query.along_y().wait()
+        query.along_core().start()
+        swap_x.wait()
+        more_x.start()
+        swap_f.start()
+        value.wait_z()
+        value.along_y().start()
+        out.start_z()
+        key.along_y().wait()
+        key.along_core().start()
+        load_x.wait()
+        more_x.wait()
+        value.along_y().wait()
+        value.along_core().start()
+        columns = v_own[:, :, :, wide:].reshape(depth, 128)
+        gains_ref[...] = columns.astype(F32).T[:8]
+        gain = gains_ref[0:1, :]
+        chunk = min(256, 2 * tok)
+
+        def norm(number, _):
+            at = pl.ds(pl.multiple_of(number * chunk, chunk), chunk)
+            values = xs[at, :].astype(F32)
+            scale = lax.rsqrt(jnp.mean(values * values, axis=1, keepdims=True) + epsilon)
+            normed_ref[at, :] = (values * scale * gain).astype(BF16)
+            return 0
+
+        lax.fori_loop(0, 2 * tok // chunk, norm, 0)
+
+    @pl.when(step == 2)
+    def _():
+        out.wait_z()
+        out.along_y().start()
+        down.start_z()
+        swap_f.wait()
+        more_f.start()
+        load_f.wait()
+        more_f.wait()
+
+    @pl.when(step == 3)
+    def _():
+        query.along_core().wait()
+        key.along_core().wait()
+        value.along_core().wait()
+        for save in saves:
+            save.start()
+
+    @pl.when(step == 5)
+    def _():
+        out.along_y().wait()
+        out.along_core().start()
+
+    def project_one(halves, kind, mine):
+        raw = nt(weight(halves, slice(0, wide)).T, normed_ref[...])
+        if kind < 2:
+            parts = raw.reshape(wide // HEAD_DIM, 2, HALF, raw.shape[1])
+            first, second = parts[:, 0], parts[:, 1]
+            cosine, sine = cos_ref[...][None], sin_ref[...][None]
+            turned = jnp.stack(
+                [first * cosine - second * sine, first * sine + second * cosine], axis=1
+            )
+            result = turned.reshape(raw.shape).astype(BF16)
+        else:
+            half = core if mine else 1 - core
+            first = fs[:, pl.ds(pl.multiple_of(half * wide, wide), wide)]
+            result = (0.5 * raw + 0.5 * first.astype(F32).T).astype(BF16)
+        if mine:
+            heads_own[0] = result
+        else:
+            outgoing[kind] = result
+            heads(kind).start()
+
+    for number, (halves, kind, mine) in enumerate(
+        (
+            (q_own, 0, True),
+            (k_own, 1, True),
+            (v_own, 2, True),
+            (q_other, 0, False),
+            (k_other, 1, False),
+            (v_other, 2, False),
+        )
+    ):
+
+        @pl.when(step == number)
+        def _(halves=halves, kind=kind, mine=mine):
+            project_one(halves, kind, mine)
+
+    @pl.when(step == 5)
+    def _():
+        for number in range(3):
+            heads(number).wait()
+        for save in saves:
+            save.wait()
+        out.along_core().wait()
+        down.wait_z()
+
+
+def front(inputs, firsts, q, k, v, o, d, cosine, sine, line):
+    slots, tok, depth = inputs.shape
+    span = slots * tok
+    wide = depth // 2
+    rows, down_rows = q.shape[0], d.shape[0]
+    anywhere = pl.BlockSpec(memory_space=pl.ANY)
+    weights = lambda columns: pltpu.VMEM((line, 2, rows, columns), BF16)
+    return pl.pallas_call(
+        functools.partial(front_kernel, line, tok),
+        grid=(6,),
+        in_specs=[anywhere] * 7 + [whole_block((HALF, span))] * 2,
+        out_specs=[
+            anywhere,
+            anywhere,
+            pl.BlockSpec((1, wide, span), lambda s: (jnp.minimum(s, 2), 0, 0)),
+            anywhere,
+            whole_block((span, depth)),
+            anywhere,
+            whole_block((8, depth)),
+            anywhere,
+            anywhere,
+            anywhere,
+        ],
+        out_shape=[
+            jax.ShapeDtypeStruct((tok, depth), BF16),
+            jax.ShapeDtypeStruct((tok, depth), BF16),
+            jax.ShapeDtypeStruct((3, wide, span), BF16),
+            jax.ShapeDtypeStruct((3, wide, span), BF16),
+            jax.ShapeDtypeStruct((span, depth), BF16),
+            jax.ShapeDtypeStruct((2, 3, line, 2, rows, wide), BF16),
+            jax.ShapeDtypeStruct((8, depth), F32),
+            jax.ShapeDtypeStruct((line, 2, rows, wide), BF16),
+            jax.ShapeDtypeStruct((line, 2, rows, wide), BF16),
+            jax.ShapeDtypeStruct((line, 2, down_rows, wide), BF16),
+        ],
+        scratch_shapes=[
+            pltpu.VMEM((span, depth), BF16),
+            pltpu.VMEM((span, depth), BF16),
+            weights(wide),
+            weights(wide),
+            weights(wide),
+            weights(wide),
+            weights(v.shape[1]),
+            weights(v.shape[1]),
+            pltpu.VMEM((3, wide, span), BF16),
+        ]
+        + [gather_sems(line)] * 5
+        + [
+            pltpu.SemaphoreType.DMA((2, 2)),
+            pltpu.SemaphoreType.DMA((2, 3)),
+            pltpu.SemaphoreType.DMA((10,)),
+        ],
+        compiler_params=pltpu.CompilerParams(
+            dimension_semantics=("arbitrary",),
+            vmem_limit_bytes=56 * MIB,
+            collective_id=1,
+            has_side_effects=True,
+        ),
+        cost_estimate=pl.CostEstimate(
+            flops=6 * span * depth * depth,
+            bytes_accessed=2 * (8 * span * depth + 6 * depth * depth),
+            transcendentals=0,
+        ),
+        name="front",
+    )(inputs, firsts, q, k, v, o, d, cosine, sine)
+
+
+def block_of(source, slot, tok):
+    _, _, side, core = seats()
+    rank = 1 - core if source == 0 else core
+    group = lax.rem(side + slot, 2)
+    return pl.ds(pl.multiple_of((group * 2 + rank) * tok, tok), tok)
+
+
+def attend_carry_kernel(line, tok, tile_k, *refs):
+    (
+        received,
+        own,
+        grad_in,
+        d_in,
+        g_shard,
+        u_shard,
+        mix_received,
+        mix_own,
+        lse_ref,
+        att_other,
+        grad_received,
+        d_own,
+        d_other,
+        g_own,
+        g_other,
+        u_own,
+        u_other,
+        qz,
+        kn,
+        vt,
+        ot,
+        outgoing,
+        d_sems,
+        g_sems,
+        u_sems,
+        swap_sems,
+        att_sems,
+    ) = refs
+    step = pl.program_id(0)
+    pairs = pl.num_programs(0)
+    _, _, side, _ = seats()
+    down = Gather(line, d_in, d_own, d_other, d_sems, split=True)
+    gate = Gather(line, g_shard, g_own, g_other, g_sems, split=True)
+    up = Gather(line, u_shard, u_own, u_other, u_sems)
+    swap = send(grad_in.at[1 - side], grad_received, swap_sems, 0, to_x_partner())
+    pieces = (received, own)
+
+    def hand_over(number):
+        rows = pl.ds(number * PAIR, PAIR)
+        return send(
+            outgoing.at[rows, :], att_other.at[rows, :], att_sems, number, to_core_partner()
+        )
+
+    @pl.when(step == 0)
+    def _():
+        meet(line, ("z", "y", "x", "core"))
+        down.along_y().start()
+        gate.start_z()
+        swap.start()
+
+    @pl.when(step == 2)
+    def _():
+        gate.wait_z()
+        gate.along_y().start()
+        up.start_z()
+
+    @pl.when(step == 3)
+    def _():
+        down.along_y().wait()
+        down.along_x().start()
+
+    for source in range(2):
+        for slot in range(2):
+            cols = block_of(source, slot, tok)
+            take = slice(slot * tok, (slot + 1) * tok)
+            query = pieces[source][0, :, take] * jnp.asarray(HEAD_DIM**-0.5, BF16)
+            for head in range(2):
+                qz[head, :, cols] = head_rows(query, head)
+            kn[cols, :] = pieces[source][1, :, take].T
+            vt[:, cols] = pieces[source][2, :, take]
+    attend_body(4 * tok, tile_k, qz, kn, vt, ot, lse_ref)
+    for slot in range(2):
+        take = slice(slot * tok, (slot + 1) * tok)
+        theirs = ot[:, block_of(0, slot, tok)]
+        mix_received[:, take] = theirs
+        for number in range(4):
+
+            @pl.when(step == number)
+            def _(number=number, theirs=theirs, take=take):
+                outgoing[number * PAIR : (number + 1) * PAIR, take] = theirs
+
+        mix_own[:, take] = ot[:, block_of(1, slot, tok)]
+    for number in range(4):
+
+        @pl.when(step == number)
+        def _(number=number):
+            hand_over(number).start()
+
+    @pl.when(step == pairs - 1)
+    def _():
+        gate.along_y().wait()
+        up.wait_z()
+        up.along_y().start()
+        down.along_x().wait()
+        swap.wait()
+        gate.along_x().start()
+        down.along_core().start()
+        up.along_y().wait()
+        up.along_core().start()
+        gate.along_x().wait()
+        gate.along_core().start()
+        for number in range(4):
+            hand_over(number).wait()
+        down.along_core().wait()
+        up.along_core().wait()
+        gate.along_core().wait()
+
+
+def attend_carry(received, own, grads, d_own, gate, up, line):
+    _, width, span = own.shape
+    tok = span // 2
+    length = 2 * span
+    pairs = width // PAIR
+    rows, down_rows = gate.shape[0], d_own.shape[2]
+    depth = grads.shape[2]
+    anywhere = pl.BlockSpec(memory_space=pl.ANY)
+    triple = pl.BlockSpec((3, PAIR, span), lambda p: (0, p, 0))
+    single = pl.BlockSpec((PAIR, span), lambda p: (p, 0))
+    whole_gate = jax.ShapeDtypeStruct((line, 2, rows, gate.shape[1]), BF16)
+    whole_down = jax.ShapeDtypeStruct((line, 2, down_rows, d_own.shape[3]), BF16)
+    area = pairs * 2 * length * length // 2
+    return pl.pallas_call(
+        functools.partial(attend_carry_kernel, line, tok, min(256, length)),
+        grid=(pairs,),
+        in_specs=[triple, triple] + [anywhere] * 4,
+        out_specs=[single, single, pl.BlockSpec((1, 8, length), lambda p: (p, 0, 0))]
+        + [anywhere] * 8,
+        out_shape=[
+            jax.ShapeDtypeStruct((width, span), BF16),
+            jax.ShapeDtypeStruct((width, span), BF16),
+            jax.ShapeDtypeStruct((pairs, 8, length), F32),
+            jax.ShapeDtypeStruct((width, span), BF16),
+            jax.ShapeDtypeStruct((tok, depth), BF16),
+            whole_down,
+            whole_down,
+            whole_gate,
+            whole_gate,
+            whole_gate,
+            whole_gate,
+        ],
+        scratch_shapes=[
+            pltpu.VMEM((2, PAIR, length), BF16),
+            pltpu.VMEM((length, PAIR), BF16),
+            pltpu.VMEM((PAIR, length), BF16),
+            pltpu.VMEM((PAIR, length), BF16),
+            pltpu.VMEM((width, span), BF16),
+        ]
+        + [gather_sems(line)] * 3
+        + [pltpu.SemaphoreType.DMA((2, 1)), pltpu.SemaphoreType.DMA((2, 4))],
+        input_output_aliases={3: 5},
+        compiler_params=pltpu.CompilerParams(
+            dimension_semantics=("arbitrary",),
+            vmem_limit_bytes=48 * MIB,
+            collective_id=2,
+            has_side_effects=True,
+        ),
+        cost_estimate=pl.CostEstimate(
+            flops=area * 1024, bytes_accessed=8 * width * length, transcendentals=area
+        ),
+        name="attend_carry",
+    )(received, own, grads, d_own, gate, up)
+
+
 def shards(
     inputs,
     first_values,
@@ -1094,34 +1651,87 @@
     order = order.astype(jnp.int32)
 
     gains = jnp.pad(jnp.stack([attn_gain, mlp_gain], axis=1), ((0, 0), (0, 126)))
-    qkv = [
-        jnp.concatenate(half + [gains], axis=1)
-        for half in split(query_weight, key_weight, value_weight)
-    ]
-    gate_up = [jnp.concatenate(half, axis=1) for half in split(gate_weight, up_weight)]
-    out_halves = [half[0] for half in split(output_weight)]
-    down_halves = [half[0] for half in split(down_weight)]
-
-    tokens = to_sequence(inputs)
-    qkv_z = gather_z(qkv[0])
-    firsts = to_sequence(after(first_values, *tokens))
-    qkv_own, qkv_other = gather_rest(qkv_z, qkv[1])
-    out_z = gather_z(after(out_halves[0], *qkv_z))
-    gate_up_z = gather_z(after(gate_up[0], *qkv_z))
-    down_z = gather_z(after(down_halves[0], *qkv_z))
-    grads = to_sequence(after(out_grad, *firsts))
-    out_own, out_other = gather_rest(out_z, out_halves[1])
-    gate_up_pieces = gather_rest(gate_up_z, gate_up[1])
-    down_pieces = gather_rest(down_z, down_halves[1])
-
-    heads_other, heads_own, normed, qkv_full, gains_full = project(
-        inputs, tokens, first_values, firsts, qkv_own, qkv_other, cosine, sine, place
+    gate_halves, up_halves, out_halves, down_halves = (
+        [half[0] for half in split(weight)]
+        for weight in (gate_weight, up_weight, output_weight, down_weight)
     )
-    pieces = exchange(halves_to_ranks(heads_other, heads_own, 1))
-    mixes, lse = attend(pieces, order, slots)
-    att_other, att_own = ranks_to_halves(exchange_back(mixes), 0)
+
+    if (slots, count) == (2, 2):
+        parts_of = lambda ref: [ref.reshape(-1, ref.shape[-1])]
+        (q_half,), (k_half,), (v_half,) = (
+            split(weight)[:1] for weight in (query_weight, key_weight, value_weight)
+        )
+        (
+            tokens,
+            firsts,
+            heads_own,
+            heads_received,
+            normed,
+            qkv_full,
+            gains_full,
+            out_own,
+            out_other,
+            down_own,
+        ) = front(
+            inputs,
+            first_values,
+            q_half[0],
+            k_half[0],
+            jnp.concatenate([v_half[0], gains], axis=1),
+            out_halves[0],
+            down_halves[0],
+            cosine,
+            sine,
+            line,
+        )
+        qkv_full = qkv_full.reshape(2, 3, D, wide)
+        tokens = [tokens]
+        pieces = [heads_received, heads_own]
+        (
+            mix_received,
+            att_own,
+            lse,
+            att_other,
+            grads,
+            down_own,
+            down_other,
+            gate_own,
+            gate_other,
+            up_own,
+            up_other,
+        ) = attend_carry(
+            heads_received, heads_own, out_grad, down_own, gate_halves[0], up_halves[0], line
+        )
+        mixes = [mix_received, att_own]
+        grads = [grads]
+        layout = jnp.stack([side, core, 0 * core]).astype(jnp.int32)
+        out_own, out_other = parts_of(out_own), parts_of(out_other)
+        gate_pieces = parts_of(gate_own), parts_of(gate_other)
+        up_pieces = parts_of(up_own), parts_of(up_other)
+        down_pieces = parts_of(down_own), parts_of(down_other)
+    else:
+        qkv = [
+            jnp.concatenate(half + [gains], axis=1)
+            for half in split(query_weight, key_weight, value_weight)
+        ]
+        layout = place
+        tokens = to_sequence(inputs)
+        firsts = to_sequence(first_values)
+        grads = to_sequence(out_grad)
+        qkv_own, qkv_other = gather_rest(gather_z(qkv[0]), qkv[1])
+        out_own, out_other = gather_rest(gather_z(out_halves[0]), out_halves[1])
+        gate_pieces = gather_rest(gather_z(gate_halves[0]), gate_halves[1])
+        up_pieces = gather_rest(gather_z(up_halves[0]), up_halves[1])
+        down_pieces = gather_rest(gather_z(down_halves[0]), down_halves[1])
+        heads_other, heads_own, normed, qkv_full, gains_full = project(
+            inputs, tokens, first_values, firsts, qkv_own, qkv_other, cosine, sine, place
+        )
+        pieces = exchange(halves_to_ranks(heads_other, heads_own, 1))
+        mixes, lse = attend(pieces, order, slots)
+        att_other, att_own = ranks_to_halves(exchange_back(mixes), 0)
+
     middle, normed2, out_full = output_projection(
-        inputs, tokens, out_own, out_other, att_other, att_own, gains_full, place
+        inputs, tokens, out_own, out_other, att_other, att_own, gains_full, layout
     )
     (
         outputs,
@@ -1133,7 +1743,7 @@
         gu_kept,
         down_sent,
         down_kept,
-    ) = mlp(out_grad, grads, middle, normed2, gains_full, gate_up_pieces, down_pieces, place)
+    ) = mlp(out_grad, grads, middle, normed2, gains_full, gate_pieces, up_pieces, down_pieces, layout)
     ga_other, ga_own, out_sent, out_kept = grad_attended(
         low_grad, out_full, att_other, att_own, place
     )

time: 843 us -> 738 us (0.88)
  waiting for transfers between devices: 431 us -> 254 us
  Pallas kernels: 246 us -> 374 us
  starting transfers between devices: 98.5 us -> 48.7 us
    ppermute x48 -> x20, waiting for transfers between devices: 359 us -> 199 us  [along_fsdp(): return lax.ppermute(value, 'fsdp', [(i, partner(i)) for i in range(parts)])]
    pallas_call x2, Pallas kernels: 51.4 us -> 179 us  [the longest x1 99.6 us: attend_carry(): pl.pallas_call(functools.partial(attend_carry_kernel, line, tok, min(256,...]
    ppermute x52 -> x19, starting transfers between devices: 63.4 us -> 29.3 us  [along_seq(): return lax.ppermute(value, 'seq', [(i, partner(i)) for i in range(groups)])]
    ppermute x52 -> x19, waiting for transfers between devices: 71.4 us -> 55 us  [along_seq(): return lax.ppermute(value, 'seq', [(i, partner(i)) for i in range(groups)])]
    ppermute x48 -> x20, starting transfers between devices: 35 us -> 19.4 us  [along_fsdp(): return lax.ppermute(value, 'fsdp', [(i, partner(i)) for i in range(parts)])]
  transfers between devices with their start and end apart: 100 -> 39, of which waited for: 35 -> 15; matrix products, arithmetic and copies ran while one was open for 6% -> 5% of each run, Pallas kernels for 8% -> 4%
where the time goes in v3:
time: 738 us; the launch traced here: 731 us
  Pallas kernels  374 us (51%)
  waiting for transfers between devices  254 us (34%)
  starting transfers between devices  48.7 us (7%)
  other arithmetic  37.5 us (5%)
  local copies, waits for them, and re-layouts  15.3 us (2%)
    ppermute x20, waiting for transfers between devices, along_fsdp(): return lax.ppermute(value, 'fsdp', [(i, partner(i)) for i in range(parts)])  199 us
    pallas_call x1, Pallas kernels, attend_carry(): pl.pallas_call(functools.partial(attend_carry_kernel, line, tok, min(256,...  99.6 us
    pallas_call x1, Pallas kernels, front(): pl.pallas_call(functools.partial(front_kernel, line, tok), grid=(6,), in_...  79.7 us
    pallas_call x1, Pallas kernels, mlp(): pl.pallas_call(functools.partial(mlp_kernel, slots, tok, count, rows, dow...  75.7 us
    pallas_call x1, Pallas kernels, attend_back(): pl.pallas_call(functools.partial(attend_back_kernel, count, slots, tok, t...  69.9 us
    ppermute x19, waiting for transfers between devices, along_seq(): return lax.ppermute(value, 'seq', [(i, partner(i)) for i in range(groups)])  55 us
    convert_element_type x16, other arithmetic, low(): return value.astype(BF16)  29.3 us
    ppermute x19, starting transfers between devices, along_seq(): return lax.ppermute(value, 'seq', [(i, partner(i)) for i in range(groups)])  29.3 us
  transfers between devices with their start and end apart: 39, of which 15 were waited for; matrix products, arithmetic and copies ran while one was open for 5% of the time, Pallas kernels for 4%

profile of v3, /device:TPU:25, one launch (start us, length us, event | category | flops | bytes accessed | tf_op | source)
XLA Modules:
  0.0 731.0 jit_solution(6881147394418564993)
XLA Ops:
  8.7 79.7 %front.1 = (bf16[512,1024]{1,0:T(8,128)(2,1)}, bf16[512,1024]{1,0:T(8,128)(2,1)}, bf16[3,512,1024]{2,1,0:T(8,128)(2,1)}, bf16[3,512,1024]{2,1,0:T(8,128)(2,1)}, ...) custom-call(bf16[2,512,1024]{2,1,0:T(8,128)(2,1)} %refs_0_.7, ...), custom_call_target="tpu_custom_call" | custom-call | flops 6442450944 | bytes 29360128 | tf_op jit(solution)/shard_map/front/pallas_call | solution.py:1221
  88.4 99.6 %attend_carry.1 = (bf16[512,1024]{1,0:T(8,128)(2,1)S(1)}, bf16[512,1024]{1,0:T(8,128)(2,1)S(1)}, f32[4,8,2048]{2,1,0:T(8,128)S(1)}, bf16[512,1024]{1,0:T(8,128)(...) custom-call(bf16[3,512,1024]{2,1,0:T(8,128)(2,1)} %get-tuple-element, ...), custom_call_target="tpu_custom_call", output_to_operand_aliasing={{5}: (3, {})} | custom-call | flops 17179869184 | bytes 8388608 | tf_op jit(solution)/shard_map/attend_carry/pallas_call | solution.py:1411
  192.6 9.1 %output_projection.1 = (f32[1024,1024]{1,0:T(8,128)}, bf16[1024,1024]{1,0:T(8,128)(2,1)}, bf16[1024,1024]{1,0:T(8,128)(2,1)}) custom-call(s32[3]{0:T(128)} %pad_add_fusion.place, bf16[2,512,1024]{2,1,0:T(8,128)(2,1)} %refs_0_.7, bf16[512,1024]{1,0:T(8,128)(2,1)} %get-tuple-element.61.refs_1_, bf16[1024,512]{1,0:T(8,128)(2,1)} %bitcast.203, ...), custom_call_target="tpu_custom_call" | custom-call | flops 2147483648 | bytes 16777216 | tf_op jit(solution)/shard_map/output_projection/pallas_call | solution.py:456
  201.8 75.7 %mlp.1 = (f32[2,512,1024]{2,1,0:T(8,128)}, bf16[512,1024]{1,0:T(8,128)(2,1)}, f32[1024,1024]{1,0:T(8,128)}, bf16[1024,1024]{1,0:T(8,128)(2,1)}, f32[8,1024]{1,0:...) custom-call(s32[3]{0:T(128)} %pad_add_fusion.place, ...), custom_call_target="tpu_custom_call" | custom-call | flops 47244640256 | bytes 55574528 | tf_op jit(solution)/shard_map/mlp/pallas_call | solution.py:649
  278.7 8.5 %grad_attended.1 = (bf16[512,1024]{1,0:T(8,128)(2,1)}, bf16[512,1024]{1,0:T(8,128)(2,1)S(1)}, bf16[1024,512]{1,0:T(8,128)(2,1)S(1)}, bf16[1024,512]{1,0:T(8,128)(2,1)S(1)}) custom-call(s32[10]{0:T(128)S(1)} %stack.61.place, bf16[1024,1024]{1,0:T(8,128)(2,1)} %get-tuple-element.78.low_ref, bf16[1024,1024]{1,0:T(8,128)(2,1)} %get-tuple-element.79.full_ref, ...), custom_call_target="tpu_custom_call" | custom-call | flops 4294967296 | bytes 10485760 | tf_op jit(solution)/shard_map/grad_attended/pallas_call | solution.py:720
  291.2 69.9 %attend_back.1 = (bf16[3,512,1024]{2,1,0:T(8,128)(2,1)}, bf16[3,512,1024]{2,1,0:T(8,128)(2,1)}) custom-call(s32[4]{0:T(128)} %add.667.order, bf16[3,512,1024]{2,1,0:T(8,128)(2,1)} %get-tuple-element.57.refs_0_, bf16[3,512,1024]{2,1,0:T(8,128)(2,1)} %get-tuple-element.58.refs_1_, bf16[512,1024]{1,0:T(8,128)(2,1)} %copy-done.7, bf16[512,1024]{1,0:T(8,128)(2,1)} %copy-done.3, ...), custom_call_target="tpu_custom_call" | custom-call | flops 42949672960 | bytes 16777216 | tf_op jit(solution)/shard_map/attend_back/pallas_call | solution.py:269
  361.7 5.4 collective-permute-done.2.refs_2_
  367.1 27.6 %tail.1 = (f32[2,512,1024]{2,1,0:T(8,128)}, bf16[512,1024]{1,0:T(8,128)(2,1)}, f32[2,512,1024]{2,1,0:T(8,128)}, bf16[512,1024]{1,0:T(8,128)(2,1)}, f32[8,1024]{1...) custom-call(s32[10]{0:T(128)} %copy-done.2, bf16[2,512,1024]{2,1,0:T(8,128)(2,1)} %refs_0_.7, ...), custom_call_target="tpu_custom_call" | custom-call | flops 12884901888 | bytes 37748736 | tf_op jit(solution)/shard_map/tail/pallas_call | solution.py:861
  395.3 5.1 fusion
  409.8 66.8 %collective-permute-done.19 = bf16[4,128,512]{2,1,0:T(8,128)(2,1)S(1)} collective-permute-done((bf16[4,128,512]{2,1,0:T(8,128)(2,1)S(1)}, bf16[4,128,512]{2,1,0:T(8,128)(2,1)S(1)}, u32[]{:S(2)}, u32[]{:S(2)}) %collective-permute-start.19) | collective-permute-done | bytes 524320 | tf_op jit(solution)/shard_map/ppermute | solution.py:1487
  483.5 4.0 collective-permute-done.21
  488.4 5.5 collective-permute-done.22
  503.4 4.2 collective-permute-done.33
  512.9 29.0 %collective-permute-done.6 = f32[8,1024]{1,0:T(8,128)S(1)} collective-permute-done((f32[8,1024]{1,0:T(8,128)S(1)}, f32[8,1024]{1,0:T(8,128)S(1)}, u32[]{:S(2)}, u32[]{:S(2)}) %collective-permute-start.6) | collective-permute-done | bytes 32800 | tf_op jit(solution)/shard_map/ppermute | solution.py:1487
  546.6 6.3 collective-permute-done.36
  562.0 3.8 fusion.5
  570.7 82.9 %collective-permute-done.14 = bf16[3,128,512]{2,1,0:T(8,128)(2,1)S(1)} collective-permute-done((bf16[3,128,512]{2,1,0:T(8,128)(2,1)S(1)}, bf16[3,128,512]{2,1,0:T(8,128)(2,1)S(1)}, u32[]{:S(2)}, u32[]{:S(2)}) %collective-permute-start.14) | collective-permute-done | bytes 393248 | tf_op jit(solution)/shard_map/ppermute | solution.py:1487
  656.5 3.9 collective-permute-start.38
  664.6 10.3 %collective-permute-done.4.part_ref = bf16[512,1024]{1,0:T(8,128)(2,1)S(1)} collective-permute-done((bf16[512,1024]{1,0:T(8,128)(2,1)S(1)}, bf16[512,1024]{1,0:T(8,128)(2,1)S(1)}, u32[]{:S(2)}, u32[]{:S(2)}) %collective-permute-start.4) | collective-permute-done | bytes 1048608 | tf_op jit(solution)/shard_map/ppermute | solution.py:1484
  676.3 21.1 %collective-permute-done.3.part_ref = bf16[512,1024]{1,0:T(8,128)(2,1)S(1)} collective-permute-done((bf16[512,1024]{1,0:T(8,128)(2,1)S(1)}, bf16[512,1024]{1,0:T(8,128)(2,1)S(1)}, u32[]{:S(2)}, u32[]{:S(2)}) %collective-permute-start.3) | collective-permute-done | bytes 1048608 | tf_op jit(solution)/shard_map/ppermute | solution.py:1484
  698.9 7.0 collective-permute-done.16
  706.0 8.1 %collective-permute-start.17 = (bf16[3,128,512]{2,1,0:T(8,128)(2,1)S(1)}, bf16[3,128,512]{2,1,0:T(8,128)(2,1)S(1)}, u32[]{:S(2)}, u32[]{:S(2)}) collective-permute-start(bf16[3,128,512]{2,1,0:T(8,128)(2,1)S(1)} %add_convert_fusion.5), channel_id=1, source_target_pairs={{0,1},{1,0},{2,3},{3,2},{4,5},{5,4},{6,7},{7,6},{8,9},{9,8},{10,11... | collective-permute-start | bytes 1179656 | tf_op jit(solution)/shard_map/ppermute | solution.py:1484
  714.1 7.2 collective-permute-done.30
  721.4 4.3 collective-permute-start.31
  (148 shorter events, 84.6 us)
Async XLA Ops:
  361.2 34.0 %collective-permute-start.25 = (bf16[2,1024,1408]{2,1,0:T(8,128)(2,1)}, bf16[2,1024,1408]{2,1,0:T(8,128)(2,1)}, u32[]{:S(2)}, u32[]{:S(2)}) collective-permute-start(bf16[2,1024,1408]{2,1,0:T(8,128)(2,1)} %get-tuple-element.99), channel_id=1, source_target_pairs={{0,1},{1,0},{2,3},{3,2},{4,5},{5,4},{6,7},{7,6},{8,9},{9,8},{10,11... | collective-permute-start | bytes 17301512 | tf_op jit(solution)/shard_map/ppermute | solution.py:1484
  361.6 43.4 %collective-permute-start.32 = (bf16[2816,512]{1,0:T(8,128)(2,1)}, bf16[2816,512]{1,0:T(8,128)(2,1)}, u32[]{:S(2)}, u32[]{:S(2)}) collective-permute-start(bf16[2816,512]{1,0:T(8,128)(2,1)} %bitcast.64), channel_id=1, source_target_pairs={{0,1},{1,0},{2,3},{3,2},{4,5},{5,4},{6,7},{7,6},{8,9},{9,8},{10,11... | collective-permute-start | bytes 8650760 | tf_op jit(solution)/shard_map/ppermute | solution.py:1484
  394.7 83.7 %collective-permute-start.11 = (bf16[3,1024,512]{2,1,0:T(8,128)(2,1)}, bf16[3,1024,512]{2,1,0:T(8,128)(2,1)}, u32[]{:S(2)}, u32[]{:S(2)}) collective-permute-start(bf16[3,1024,512]{2,1,0:T(8,128)(2,1)} %get-tuple-element.95), channel_id=1, source_target_pairs={{0,1},{1,0},{2,3},{3,2},{4,5},{5,4},{6,7},{7,6},{8,9},{9,8},{10,11... | collective-permute-start | bytes 9437192 | tf_op jit(solution)/shard_map/ppermute | solution.py:1484
  400.4 161.6 %collective-permute-start.26 = (bf16[2,4,128,1408]{3,2,0,1:T(8,128)(2,1)}, bf16[2,4,128,1408]{3,2,0,1:T(8,128)(2,1)}, u32[]{:S(2)}, u32[]{:S(2)}) collective-permute-start(bf16[2,4,128,1408]{3,2,0,1:T(8,128)(2,1)} %fusion), channel_id=1, source_target_pairs={{0,4},{4,0},{8,12},{12,8},{16,20},{20,16},{24,28},{28,24},{1,5},{5... | collective-permute-start | bytes 8650760 | tf_op jit(solution)/shard_map/ppermute | solution.py:1487
  403.6 73.0 %collective-permute-start.19 = (bf16[4,128,512]{2,1,0:T(8,128)(2,1)S(1)}, bf16[4,128,512]{2,1,0:T(8,128)(2,1)S(1)}, u32[]{:S(2)}, u32[]{:S(2)}) collective-permute-start(bf16[4,128,512]{2,1,0:T(8,128)(2,1)S(1)} %fusion.21), channel_id=1, source_target_pairs={{0,4},{4,0},{8,12},{12,8},{16,20},{20,16},{24,28},{28,24},{1,5},{5... | collective-permute-start | bytes 1572872 | tf_op jit(solution)/shard_map/ppermute | solution.py:1487
  407.9 99.7 %collective-permute-start.33 = (bf16[4,352,512]{2,1,0:T(8,128)(2,1)}, bf16[4,352,512]{2,1,0:T(8,128)(2,1)}, u32[]{:S(2)}, u32[]{:S(2)}) collective-permute-start(bf16[4,352,512]{2,1,0:T(8,128)(2,1)} %fusion.2), channel_id=1, source_target_pairs={{0,4},{4,0},{8,12},{12,8},{16,20},{20,16},{24,28},{28,24},{1,5},{5... | collective-permute-start | bytes 4325384 | tf_op jit(solution)/shard_map/ppermute | solution.py:1487
  408.0 103.9 %collective-permute-start = (bf16[512,1024]{1,0:T(8,128)(2,1)}, bf16[512,1024]{1,0:T(8,128)(2,1)S(1)}, u32[]{:S(2)}, u32[]{:S(2)}) collective-permute-start(bf16[512,1024]{1,0:T(8,128)(2,1)} %get-tuple-element.76), channel_id=1, source_target_pairs={{0,2},{1,3},{2,0},{3,1},{4,6},{5,7},{6,4},{7,5},{8,10},{9,11},{10,... | collective-permute-start | bytes 3145736 | tf_op jit(solution)/shard_map/ppermute | solution.py:1484
  482.3 72.2 %collective-permute-start.12 = (bf16[3,4,128,512]{3,2,0,1:T(8,128)(2,1)}, bf16[3,4,128,512]{3,2,0,1:T(8,128)(2,1)}, u32[]{:S(2)}, u32[]{:S(2)}) collective-permute-start(bf16[3,4,128,512]{3,2,0,1:T(8,128)(2,1)} %fusion.1), channel_id=1, source_target_pairs={{0,4},{4,0},{8,12},{12,8},{16,20},{20,16},{24,28},{28,24},{1,5},{5... | collective-permute-start | bytes 4718600 | tf_op jit(solution)/shard_map/ppermute | solution.py:1487
  507.6 34.3 %collective-permute-start.6 = (f32[8,1024]{1,0:T(8,128)S(1)}, f32[8,1024]{1,0:T(8,128)S(1)}, u32[]{:S(2)}, u32[]{:S(2)}) collective-permute-start(f32[8,1024]{1,0:T(8,128)S(1)} %add.668), channel_id=1, source_target_pairs={{0,4},{4,0},{8,12},{12,8},{16,20},{20,16},{24,28},{28,24},{1,5},{5... | collective-permute-start | bytes 98312 | tf_op jit(solution)/shard_map/ppermute | solution.py:1487
  511.9 31.4 %collective-permute-start.34 = (bf16[352,512]{1,0:T(8,128)(2,1)}, bf16[352,512]{1,0:T(8,128)(2,1)S(1)}, u32[]{:S(2)}, u32[]{:S(2)}) collective-permute-start(bf16[352,512]{1,0:T(8,128)(2,1)} %get-tuple-element.116), channel_id=1, source_target_pairs={{0,8},{4,12},{8,16},{12,20},{16,24},{20,28},{24,0},{28,4},{1,9},{5... | collective-permute-start | bytes 1081352 | tf_op jit(solution)/shard_map/ppermute | solution.py:1487
  512.5 34.2 %collective-permute-start.35 = (bf16[352,512]{1,0:T(8,128)(2,1)}, bf16[352,512]{1,0:T(8,128)(2,1)S(1)}, u32[]{:S(2)}, u32[]{:S(2)}) collective-permute-start(bf16[352,512]{1,0:T(8,128)(2,1)} %get-tuple-element.118), channel_id=1, source_target_pairs={{0,16},{4,20},{8,24},{12,28},{16,0},{20,4},{24,8},{28,12},{1,17},{... | collective-permute-start | bytes 1081352 | tf_op jit(solution)/shard_map/ppermute | solution.py:1487
  543.3 15.2 %collective-permute-start.7 = (f32[8,1024]{1,0:T(8,128)S(1)}, f32[8,1024]{1,0:T(8,128)S(1)}, u32[]{:S(2)}, u32[]{:S(2)}) collective-permute-start(f32[8,1024]{1,0:T(8,128)S(1)} %add.669), channel_id=1, source_target_pairs={{0,8},{4,12},{8,16},{12,20},{16,24},{20,28},{24,0},{28,4},{1,9},{5... | collective-permute-start | bytes 98312 | tf_op jit(solution)/shard_map/ppermute | solution.py:1487
  546.6 15.2 %collective-permute-start.8 = (f32[8,1024]{1,0:T(8,128)S(1)}, f32[8,1024]{1,0:T(8,128)S(1)}, u32[]{:S(2)}, u32[]{:S(2)}) collective-permute-start(f32[8,1024]{1,0:T(8,128)S(1)} %add.669), channel_id=1, source_target_pairs={{0,16},{4,20},{8,24},{12,28},{16,0},{20,4},{24,8},{28,12},{1,17},{... | collective-permute-start | bytes 98312 | tf_op jit(solution)/shard_map/ppermute | solution.py:1487
  565.8 90.7 %collective-permute-start.27 = (bf16[2,128,1408]{2,1,0:T(8,128)(2,1)S(1)}, bf16[2,128,1408]{2,1,0:T(8,128)(2,1)S(1)}, u32[]{:S(2)}, u32[]{:S(2)}) collective-permute-start(bf16[2,128,1408]{2,1,0:T(8,128)(2,1)S(1)} %get-tuple-element.110), channel_id=1, source_target_pairs={{0,8},{4,12},{8,16},{12,20},{16,24},{20,28},{24,0},{28,4},{1,9},{5... | collective-permute-start | bytes 2162696 | tf_op jit(solution)/shard_map/ppermute | solution.py:1487
  565.9 94.6 %collective-permute-start.28 = (bf16[2,128,1408]{2,1,0:T(8,128)(2,1)S(1)}, bf16[2,128,1408]{2,1,0:T(8,128)(2,1)S(1)}, u32[]{:S(2)}, u32[]{:S(2)}) collective-permute-start(bf16[2,128,1408]{2,1,0:T(8,128)(2,1)S(1)} %get-tuple-element.112), channel_id=1, source_target_pairs={{0,16},{4,20},{8,24},{12,28},{16,0},{20,4},{24,8},{28,12},{1,17},{... | collective-permute-start | bytes 2162696 | tf_op jit(solution)/shard_map/ppermute | solution.py:1487
  565.9 94.7 %collective-permute-start.29 = (bf16[2,128,1408]{2,1,0:T(8,128)(2,1)S(1)}, bf16[2,128,1408]{2,1,0:T(8,128)(2,1)S(1)}, u32[]{:S(2)}, u32[]{:S(2)}) collective-permute-start(bf16[2,128,1408]{2,1,0:T(8,128)(2,1)S(1)} %get-tuple-element.111), channel_id=1, source_target_pairs={{0,24},{4,28},{8,0},{12,4},{16,8},{20,12},{24,16},{28,20},{1,25},{... | collective-permute-start | bytes 2162696 | tf_op jit(solution)/shard_map/ppermute | solution.py:1487
  567.3 86.3 %collective-permute-start.14 = (bf16[3,128,512]{2,1,0:T(8,128)(2,1)S(1)}, bf16[3,128,512]{2,1,0:T(8,128)(2,1)S(1)}, u32[]{:S(2)}, u32[]{:S(2)}) collective-permute-start(bf16[3,128,512]{2,1,0:T(8,128)(2,1)S(1)} %get-tuple-element.115), channel_id=1, source_target_pairs={{0,16},{4,20},{8,24},{12,28},{16,0},{20,4},{24,8},{28,12},{1,17},{... | collective-permute-start | bytes 1179656 | tf_op jit(solution)/shard_map/ppermute | solution.py:1487
  569.7 85.1 %collective-permute-start.15 = (bf16[3,128,512]{2,1,0:T(8,128)(2,1)S(1)}, bf16[3,128,512]{2,1,0:T(8,128)(2,1)S(1)}, u32[]{:S(2)}, u32[]{:S(2)}) collective-permute-start(bf16[3,128,512]{2,1,0:T(8,128)(2,1)S(1)} %get-tuple-element.114), channel_id=1, source_target_pairs={{0,24},{4,28},{8,0},{12,4},{16,8},{20,12},{24,16},{28,20},{1,25},{... | collective-permute-start | bytes 1179656 | tf_op jit(solution)/shard_map/ppermute | solution.py:1487
  653.6 21.4 %collective-permute-start.4 = (bf16[512,1024]{1,0:T(8,128)(2,1)S(1)}, bf16[512,1024]{1,0:T(8,128)(2,1)S(1)}, u32[]{:S(2)}, u32[]{:S(2)}) collective-permute-start(bf16[512,1024]{1,0:T(8,128)(2,1)S(1)} %copy-done.16), channel_id=1, source_target_pairs={{0,2},{1,3},{2,0},{3,1},{4,6},{5,7},{6,4},{7,5},{8,10},{9,11},{10,... | collective-permute-start | bytes 3145736 | tf_op jit(solution)/shard_map/ppermute | solution.py:1484
  654.8 42.7 %collective-permute-start.3 = (bf16[512,1024]{1,0:T(8,128)(2,1)S(1)}, bf16[512,1024]{1,0:T(8,128)(2,1)S(1)}, u32[]{:S(2)}, u32[]{:S(2)}) collective-permute-start(bf16[512,1024]{1,0:T(8,128)(2,1)S(1)} %copy-done.15), channel_id=1, source_target_pairs={{0,2},{1,3},{2,0},{3,1},{4,6},{5,7},{6,4},{7,5},{8,10},{9,11},{10,... | collective-permute-start | bytes 3145736 | tf_op jit(solution)/shard_map/ppermute | solution.py:1484
  656.5 42.3 %collective-permute-start.38 = (bf16[352,512]{1,0:T(8,128)(2,1)S(1)}, bf16[352,512]{1,0:T(8,128)(2,1)S(1)}, u32[]{:S(2)}, u32[]{:S(2)}) collective-permute-start(bf16[352,512]{1,0:T(8,128)(2,1)S(1)} %add_convert_fusion.6), channel_id=1, source_target_pairs={{0,1},{1,0},{2,3},{3,2},{4,5},{5,4},{6,7},{7,6},{8,9},{9,8},{10,11... | collective-permute-start | bytes 1081352 | tf_op jit(solution)/shard_map/ppermute | solution.py:1484
  660.4 45.4 %collective-permute-start.16 = (bf16[3,128,512]{2,1,0:T(8,128)(2,1)S(1)}, bf16[3,128,512]{2,1,0:T(8,128)(2,1)S(1)}, u32[]{:S(2)}, u32[]{:S(2)}) collective-permute-start(bf16[3,128,512]{2,1,0:T(8,128)(2,1)S(1)} %get-tuple-element.108), channel_id=1, source_target_pairs={{0,2},{1,3},{2,0},{3,1},{4,6},{5,7},{6,4},{7,5},{8,10},{9,11},{10,... | collective-permute-start | bytes 1179656 | tf_op jit(solution)/shard_map/ppermute | solution.py:1484
  662.8 58.5 %collective-permute-start.30 = (bf16[2,128,1408]{2,1,0:T(8,128)(2,1)S(1)}, bf16[2,128,1408]{2,1,0:T(8,128)(2,1)S(1)}, u32[]{:S(2)}, u32[]{:S(2)}) collective-permute-start(bf16[2,128,1408]{2,1,0:T(8,128)(2,1)S(1)} %get-tuple-element.104), channel_id=1, source_target_pairs={{0,2},{1,3},{2,0},{3,1},{4,6},{5,7},{6,4},{7,5},{8,10},{9,11},{10,... | collective-permute-start | bytes 2162696 | tf_op jit(solution)/shard_map/ppermute | solution.py:1484
  706.0 21.0 %collective-permute-start.17 = (bf16[3,128,512]{2,1,0:T(8,128)(2,1)S(1)}, bf16[3,128,512]{2,1,0:T(8,128)(2,1)S(1)}, u32[]{:S(2)}, u32[]{:S(2)}) collective-permute-start(bf16[3,128,512]{2,1,0:T(8,128)(2,1)S(1)} %add_convert_fusion.5), channel_id=1, source_target_pairs={{0,1},{1,0},{2,3},{3,2},{4,5},{5,4},{6,7},{7,6},{8,9},{9,8},{10,11... | collective-permute-start | bytes 1179656 | tf_op jit(solution)/shard_map/ppermute | solution.py:1484
  (32 other events, 441.4 us)

commit v4 on v3

--- a/solution.py
+++ b/solution.py
@@ -142,17 +142,32 @@
     return (results[:count], results[count])
 
 
-def attend_back_kernel(count, slots, tok, tile_q, tile_k, order, *refs):
-    pieces = refs[:count]
-    mixes = refs[count : 2 * count]
-    grads = refs[2 * count : 3 * count]
-    lse_ref, cos_ref, sin_ref = refs[3 * count : 3 * count + 3]
-    outs = refs[3 * count + 3 : 4 * count + 3]
-    qz, gz, qn, gn, kn, vn, kt, inner, dq, dk, dv = refs[4 * count + 3 :]
-    length = count * slots * tok
-    for source in range(count):
+def attend_back_body(
+    pieces,
+    mixes,
+    grads,
+    columns,
+    tok,
+    length,
+    tile_q,
+    tile_k,
+    lse_ref,
+    qz,
+    gz,
+    qn,
+    gn,
+    kn,
+    vn,
+    kt,
+    inner,
+    dq,
+    dk,
+    dv,
+):
+    slots = pieces[0].shape[2] // tok
+    for source in range(len(pieces)):
         for slot in range(slots):
-            cols = pl.ds(pl.multiple_of(order[source * slots + slot] * tok, tok), tok)
+            cols = columns(source, slot)
             take = slice(slot * tok, (slot + 1) * tok)
             query = pieces[source][0, :, take] * jnp.asarray(HEAD_DIM**-0.5, BF16)
             grad = grads[source][:, take]
@@ -212,25 +227,53 @@
         return 0
 
     lax.fori_loop(0, length // tile_q, one, 0)
+
+
+def turn_back(dq, dk, dv, cols, cosine, sine):
     half = HEAD_DIM // 2
+    results = []
+    for grad in (dq[:, cols] * (HEAD_DIM**-0.5), dk[cols, :].T):
+        turned = []
+        for head in range(2):
+            low = head * HEAD_DIM
+            first = grad[low : low + half]
+            second = grad[low + half : low + 2 * half]
+            turned += [first * cosine + second * sine, second * cosine - first * sine]
+        results.append(jnp.concatenate(turned, axis=0).astype(BF16))
+    results.append(dv[cols, :].T.astype(BF16))
+    return results
+
+
+def attend_back_kernel(count, slots, tok, tile_q, tile_k, order, *refs):
+    pieces = refs[:count]
+    mixes = refs[count : 2 * count]
+    grads = refs[2 * count : 3 * count]
+    lse_ref, cos_ref, sin_ref = refs[3 * count : 3 * count + 3]
+    outs = refs[3 * count + 3 : 4 * count + 3]
+    scratch = refs[4 * count + 3 :]
+    dq, dk, dv = scratch[-3:]
+
+    def columns(source, slot):
+        return pl.ds(pl.multiple_of(order[source * slots + slot] * tok, tok), tok)
+
+    attend_back_body(
+        pieces,
+        mixes,
+        grads,
+        columns,
+        tok,
+        count * slots * tok,
+        tile_q,
+        tile_k,
+        lse_ref,
+        *scratch,
+    )
     for source in range(count):
         for slot in range(slots):
-            cols = pl.ds(pl.multiple_of(order[source * slots + slot] * tok, tok), tok)
-            take = slice(slot * tok, (slot + 1) * tok)
-            cosine = cos_ref[:, cols]
-            sine = sin_ref[:, cols]
-            for which, grad in enumerate((dq[:, cols] * (HEAD_DIM**-0.5), dk[cols, :].T)):
-                for head in range(2):
-                    low = head * HEAD_DIM
-                    first = grad[low : low + half]
-                    second = grad[low + half : low + 2 * half]
-                    outs[source][which, low : low + half, take] = (
-                        first * cosine + second * sine
-                    ).astype(BF16)
-                    outs[source][which, low + half : low + 2 * half, take] = (
-                        second * cosine - first * sine
-                    ).astype(BF16)
-            outs[source][2, :, take] = dv[cols, :].T.astype(BF16)
+            cols = columns(source, slot)
+            results = turn_back(dq, dk, dv, cols, cos_ref[:, cols], sin_ref[:, cols])
+            for which, result in enumerate(results):
+                outs[source][which, :, slot * tok : (slot + 1) * tok] = result
 
 
 def attend_back(pieces, mixes, grads, lse, cosine, sine, order, slots):
@@ -1450,6 +1493,625 @@
     )(received, own, grads, d_own, gate, up)
 
 
+def mlp_carry_kernel(line, tok, blocks, *refs):
+    (
+        grads,
+        grads_received,
+        middle_ref,
+        normed_ref,
+        gains_ref,
+        g_own,
+        g_other,
+        u_own,
+        u_other,
+        d_own_own,
+        d_own_other,
+        d_other_own,
+        d_other_other,
+        out_ref,
+        send_ref,
+        grad_ref,
+        low_ref,
+        gain_ref,
+        gu_ref,
+        d_ref,
+        gu_y,
+        og,
+        normed_t,
+        acc,
+        back,
+        gu_kept,
+        d_kept,
+        gu_sent,
+        d_sent,
+        gu_landed,
+        d_landed,
+        gu_outgoing,
+        down_full,
+        local_sems,
+        gu_sends,
+        gu_recvs,
+        d_sends,
+        d_recvs,
+        y_sems,
+    ) = refs
+    step = pl.program_id(0)
+    _, y, side, core = seats()
+    depth = og.shape[1]
+    wide = depth // 2
+    strip = 128
+    rows = gu_kept.shape[4]
+    mine = pl.ds(pl.multiple_of(core * wide, wide), wide)
+    others = pl.ds(pl.multiple_of((1 - core) * wide, wide), wide)
+
+    def core_copies(number):
+        slot = lax.rem(number, 2)
+        return [
+            pltpu.make_async_remote_copy(
+                src_ref=source.at[slot],
+                dst_ref=target.at[number],
+                send_sem=sends.at[slot],
+                recv_sem=recvs.at[number],
+                device_id=to_core_partner(),
+                device_id_type=MESH,
+            )
+            for source, target, sends, recvs in (
+                (gu_sent, gu_landed, gu_sends, gu_recvs),
+                (d_sent, d_landed, d_sends, d_recvs),
+            )
+        ]
+
+    def y_copy(number):
+        columns = pl.ds(pl.multiple_of(number * strip, strip), strip)
+        return send(
+            gu_outgoing.at[number], gu_y.at[:, :, :, columns], y_sems, number, to_y_partner()
+        )
+
+    @pl.when(step == 0)
+    def _():
+        meet(line, ("y", "core"))
+        loads = [
+            pltpu.make_async_copy(grads.at[side], og.at[pl.ds(0, tok), :], local_sems.at[0]),
+            pltpu.make_async_copy(grads_received, og.at[pl.ds(tok, tok), :], local_sems.at[1]),
+        ]
+        for load in loads:
+            load.start()
+        normed_t[...] = normed_ref[...].T
+        acc[...] = jnp.zeros_like(acc)
+        back[...] = jnp.zeros_like(back)
+        for load in loads:
+            load.wait()
+
+    @pl.when(step < blocks)
+    def _():
+        slot = lax.rem(step, 2)
+        gate_w = jnp.concatenate([g_own[...], g_other[...]], axis=1)
+        up_w = jnp.concatenate([u_own[...], u_other[...]], axis=1)
+        for number, pair in enumerate(
+            ((d_own_own, d_own_other), (d_other_own, d_other_other))
+        ):
+            at = pl.ds(number * strip, strip)
+            down_full[at, mine] = pair[0][...]
+            down_full[at, others] = pair[1][...]
+        down_w = down_full[...]
+        normed = normed_ref[...]
+        gate = dot(normed, gate_w)
+        up = dot(normed, up_w)
+        grad_active = nt(og[...], down_w)
+        sigma = jax.nn.sigmoid(gate)
+        silu = gate * sigma
+        active = (silu * up).astype(BF16)
+        grad_up = (grad_active * silu).astype(BF16)
+        grad_gate = (grad_active * up * sigma * (1.0 + gate * (1.0 - sigma))).astype(BF16)
+
+        @pl.when(step >= 2)
+        def _():
+            for copy in core_copies(step - 2):
+                copy.wait_send()
+
+        for number, grad in enumerate((grad_gate, grad_up)):
+            result = dot(normed_t[...], grad).astype(BF16)
+            shaped = result.reshape(line, 2, rows, 2 * strip)
+            gu_kept[slot, number] = shaped[..., :strip]
+            gu_sent[slot, number] = shaped[..., strip:]
+        active_t = active.T
+        kept = dot(active_t, og[:, mine]).astype(BF16)
+        d_kept[slot, core] = kept[:strip]
+        d_kept[slot, 1 - core] = kept[strip:]
+        sent = dot(active_t, og[:, others]).astype(BF16)
+        d_sent[slot, core] = sent[:strip]
+        d_sent[slot, 1 - core] = sent[strip:]
+        for copy in core_copies(step):
+            copy.start()
+        acc[...] += dot(active, down_w)
+        back[...] += nt(grad_gate, gate_w) + nt(grad_up, up_w)
+
+    @pl.when(step > 0)
+    def _():
+        number = step - 1
+        slot = lax.rem(number, 2)
+        for copy in core_copies(number):
+            copy.wait_recv()
+        for which in range(2):
+            theirs = gu_kept[slot, which, :, 1 - y].astype(F32)
+            theirs = theirs + gu_landed[number, which, :, 1 - y].astype(F32)
+            gu_outgoing[number, which] = theirs.astype(BF16)
+            ours = gu_kept[slot, which, :, y].astype(F32)
+            ours = ours + gu_landed[number, which, :, y].astype(F32)
+            gu_ref[which] = ours.astype(BF16)
+        y_copy(number).start()
+        d_ref[...] = (d_kept[slot].astype(F32) + d_landed[number].astype(F32)).astype(BF16)
+
+    @pl.when(step == blocks)
+    def _():
+        gain = gains_ref[1:2, :]
+        chunk = min(128, tok)
+        gain_ref[...] = jnp.zeros_like(gain_ref)
+        for slot in range(2):
+
+            def finish(number, _, slot=slot):
+                local = pl.ds(pl.multiple_of(number * chunk, chunk), chunk)
+                some = pl.ds(pl.multiple_of(slot * tok + number * chunk, chunk), chunk)
+                middle = middle_ref[some, :]
+                scale = lax.rsqrt(jnp.mean(middle * middle, axis=1, keepdims=True) + epsilon)
+                result = middle + acc[some, :]
+                if slot == 0:
+                    out_ref[0, local, :] = result
+                else:
+                    send_ref[local, :] = result.astype(BF16)
+                grad = back[some, :]
+                gain_ref[0:1, :] += jnp.sum(grad * middle * scale, axis=0, keepdims=True)
+                weighted = grad * gain
+                inner = jnp.mean(weighted * middle, axis=1, keepdims=True)
+                grad_middle = (
+                    scale * weighted
+                    - middle * (scale * scale * scale) * inner
+                    + og[some, :].astype(F32)
+                )
+                grad_ref[some, :] = grad_middle
+                low_ref[some, :] = grad_middle.astype(BF16)
+                return 0
+
+            lax.fori_loop(0, tok // chunk, finish, 0)
+        for number in (blocks - 2, blocks - 1):
+            for copy in core_copies(number):
+                copy.wait_send()
+        for number in range(blocks):
+            y_copy(number).wait()
+
+
+def mlp_carry(grads, grads_received, middle, normed, gains, gate, up, down, line):
+    slots, tok, depth = grads.shape
+    half_width = gate[0].shape[1]
+    wide = depth // 2
+    span = slots * tok
+    blocks = half_width // 128
+    rows = depth // (2 * line)
+    once = pl.Buffered(1)
+    anywhere = pl.BlockSpec(memory_space=pl.ANY)
+
+    def now(s):
+        return jnp.minimum(s, blocks - 1)
+
+    def done(s):
+        return jnp.maximum(s - 1, 0)
+
+    def core():
+        return lax.axis_index("seq") % 2
+
+    column = pl.BlockSpec((depth, 128), lambda s: (0, now(s)))
+    own_rows = pl.BlockSpec((128, wide), lambda s: (core() * blocks + now(s), 0))
+    other_rows = pl.BlockSpec((128, wide), lambda s: ((1 - core()) * blocks + now(s), 0))
+    full = pl.BlockSpec((span, depth), lambda s: (0, 0), pipeline_mode=once)
+    return pl.pallas_call(
+        functools.partial(mlp_carry_kernel, line, tok, blocks),
+        grid=(blocks + 1,),
+        in_specs=[anywhere, anywhere, full, full, whole_block((8, depth))]
+        + [column] * 4
+        + [own_rows, own_rows, other_rows, other_rows],
+        out_specs=[
+            pl.BlockSpec(
+                (1, tok, depth), lambda s: (lax.axis_index("seq") // 2, 0, 0), pipeline_mode=once
+            ),
+            pl.BlockSpec((tok, depth), lambda s: (0, 0), pipeline_mode=once),
+            full,
+            full,
+            whole_block((8, depth)),
+            pl.BlockSpec((2, line, rows, 128), lambda s: (0, 0, 0, done(s))),
+            pl.BlockSpec((2, 128, wide), lambda s: (0, done(s), 0)),
+            anywhere,
+        ],
+        out_shape=[
+            jax.ShapeDtypeStruct((slots, tok, depth), F32),
+            jax.ShapeDtypeStruct((tok, depth), BF16),
+            jax.ShapeDtypeStruct((span, depth), F32),
+            jax.ShapeDtypeStruct((span, depth), BF16),
+            jax.ShapeDtypeStruct((8, depth), F32),
+            jax.ShapeDtypeStruct((2, line, rows, half_width), BF16),
+            jax.ShapeDtypeStruct((2, half_width, wide), BF16),
+            jax.ShapeDtypeStruct((2, line, rows, half_width), BF16),
+        ],
+        scratch_shapes=[
+            pltpu.VMEM((span, depth), BF16),
+            pltpu.VMEM((depth, span), BF16),
+            pltpu.VMEM((span, depth), F32),
+            pltpu.VMEM((span, depth), F32),
+            pltpu.VMEM((2, 2, line, 2, rows, 128), BF16),
+            pltpu.VMEM((2, 2, 128, wide), BF16),
+            pltpu.VMEM((2, 2, line, 2, rows, 128), BF16),
+            pltpu.VMEM((2, 2, 128, wide), BF16),
+            pltpu.VMEM((blocks, 2, line, 2, rows, 128), BF16),
+            pltpu.VMEM((blocks, 2, 128, wide), BF16),
+            pltpu.VMEM((blocks, 2, line, rows, 128), BF16),
+            pltpu.VMEM((256, depth), BF16),
+            pltpu.SemaphoreType.DMA((2,)),
+            pltpu.SemaphoreType.DMA((2,)),
+            pltpu.SemaphoreType.DMA((blocks,)),
+            pltpu.SemaphoreType.DMA((2,)),
+            pltpu.SemaphoreType.DMA((blocks,)),
+            pltpu.SemaphoreType.DMA((2, blocks)),
+        ],
+        compiler_params=pltpu.CompilerParams(
+            dimension_semantics=("arbitrary",),
+            vmem_limit_bytes=63 * MIB,
+            collective_id=3,
+            has_side_effects=True,
+        ),
+        cost_estimate=pl.CostEstimate(
+            flops=16 * span * depth * 2 * half_width,
+            bytes_accessed=24 * depth * half_width + 20 * span * depth,
+            transcendentals=2 * span * half_width,
+        ),
+        name="mlp_carry",
+    )(
+        grads,
+        grads_received,
+        middle,
+        normed,
+        gains,
+        *gate,
+        *up,
+        down[0],
+        down[1],
+        down[0],
+        down[1],
+    )
+
+
+def grad_attended_carry_kernel(
+    line,
+    low_ref,
+    full_ref,
+    att_other,
+    att_own,
+    ga_own,
+    ga_received,
+    o_ref,
+    o_landed,
+    outgoing,
+    o_sent,
+    sems,
+):
+    step = pl.program_id(0)
+    _, _, _, core = seats()
+    wide = att_own.shape[0]
+    mine = pl.ds(pl.multiple_of(core * wide, wide), wide)
+    others = pl.ds(pl.multiple_of((1 - core) * wide, wide), wide)
+    heads = send(outgoing, ga_received, sems, 0, to_core_partner())
+
+    def sums(number):
+        half = 1 - core if number == 0 else core
+        at = pl.ds(pl.multiple_of(half * wide, wide), wide)
+        return send(o_sent.at[number], o_landed.at[at, :], sems, 1 + number, to_core_partner())
+
+    @pl.when(step == 0)
+    def _():
+        meet(line, ("core",))
+        outgoing[...] = nt(full_ref[...], low_ref[...]).astype(BF16)
+        heads.start()
+
+    @pl.when(step == 1)
+    def _():
+        ga_own[...] = nt(full_ref[...], low_ref[...]).astype(BF16)
+
+    for number, att in enumerate((att_other, att_own)):
+
+        @pl.when(step == number)
+        def _(number=number, att=att):
+            o_sent[number] = dot(att[...], low_ref[:, others]).astype(BF16)
+            sums(number).start()
+            o_ref[...] = dot(att[...], low_ref[:, mine]).astype(BF16)
+
+    @pl.when(step == 1)
+    def _():
+        heads.wait()
+        for number in range(2):
+            sums(number).wait()
+
+
+def grad_attended_carry(low, full, att_other, att_own, line):
+    span, depth = low.shape
+    wide = depth // 2
+
+    def half(s):
+        core = lax.axis_index("seq") % 2
+        return jnp.where(s == 0, 1 - core, core)
+
+    anywhere = pl.BlockSpec(memory_space=pl.ANY)
+    return pl.pallas_call(
+        functools.partial(grad_attended_carry_kernel, line),
+        grid=(2,),
+        in_specs=[
+            whole_block((span, depth)),
+            pl.BlockSpec((wide, depth), lambda s: (half(s), 0)),
+            whole_block((wide, span)),
+            whole_block((wide, span)),
+        ],
+        out_specs=[
+            whole_block((wide, span)),
+            anywhere,
+            pl.BlockSpec((wide, wide), lambda s: (half(s), 0)),
+            anywhere,
+        ],
+        out_shape=[
+            jax.ShapeDtypeStruct((wide, span), BF16),
+            jax.ShapeDtypeStruct((wide, span), BF16),
+            jax.ShapeDtypeStruct((depth, wide), BF16),
+            jax.ShapeDtypeStruct((depth, wide), BF16),
+        ],
+        scratch_shapes=[
+            pltpu.VMEM((wide, span), BF16),
+            pltpu.VMEM((2, wide, wide), BF16),
+            pltpu.SemaphoreType.DMA((2, 3)),
+        ],
+        compiler_params=pltpu.CompilerParams(
+            dimension_semantics=("arbitrary",),
+            vmem_limit_bytes=48 * MIB,
+            collective_id=4,
+            has_side_effects=True,
+        ),
+        cost_estimate=pl.CostEstimate(
+            flops=4 * span * depth * depth,
+            bytes_accessed=6 * span * depth + 4 * depth * depth,
+            transcendentals=0,
+        ),
+        name="grad_attended_carry",
+    )(low, full, att_other, att_own)
+
+
+def attend_back_carry_kernel(line, tok, tile_q, tile_k, *refs):
+    (
+        received,
+        own,
+        mix_received,
+        mix_own,
+        grad_received,
+        grad_own,
+        lse_ref,
+        cos_ref,
+        sin_ref,
+        outputs_sent,
+        gu_in,
+        gu_y,
+        d_in,
+        o_in,
+        o_landed,
+        back_own,
+        back_other,
+        outputs_received,
+        gu_mine,
+        gu_z,
+        d_y,
+        o_kept,
+        o_y,
+    ) = refs[:23]
+    (
+        qz,
+        gz,
+        qn,
+        gn,
+        kn,
+        vn,
+        kt,
+        inner,
+        dq,
+        dk,
+        dv,
+        outgoing,
+        gu_a,
+        gu_b,
+        o_a,
+        o_b,
+        local_sems,
+        back_sems,
+        z_sems,
+        other_sems,
+    ) = refs[23:]
+    step = pl.program_id(0)
+    pairs = pl.num_programs(0)
+    z, y, _, _ = seats()
+    length = 4 * tok
+    swap = send(outputs_sent, outputs_received, other_sems, 0, to_x_partner())
+    d_send = send(d_in.at[:, 1 - y], d_y, other_sems, 1, to_y_partner())
+    o_send = send(o_a.at[:, 1 - y], o_y, other_sems, 2, to_y_partner())
+
+    def z_send(jump):
+        target = lax.rem(z + jump, line)
+        return send(
+            gu_a.at[:, target], gu_z.at[jump - 1], z_sems, jump - 1, to_z_partner(line, jump)
+        )
+
+    stays = [
+        pltpu.make_async_copy(gu_a.at[:, z], gu_mine, local_sems.at[4]),
+        pltpu.make_async_copy(o_a.at[:, y], o_kept, local_sems.at[5]),
+    ]
+
+    def hand_over(number):
+        rows = pl.ds(number * PAIR, PAIR)
+        return send(
+            outgoing.at[:, rows, :],
+            back_other.at[:, rows, :],
+            back_sems,
+            number,
+            to_core_partner(),
+        )
+
+    @pl.when(step == 0)
+    def _():
+        meet(line, ("z", "y", "x", "core"))
+        swap.start()
+        loads = [
+            pltpu.make_async_copy(source, target, local_sems.at[number])
+            for number, (source, target) in enumerate(
+                ((o_in, o_a), (o_landed, o_b), (gu_in, gu_a), (gu_y, gu_b))
+            )
+        ]
+        for load in loads:
+            load.start()
+        loads[0].wait()
+        loads[1].wait()
+        o_a[...] = (o_a[...].astype(F32) + o_b[...].astype(F32)).astype(BF16)
+        o_send.start()
+        d_send.start()
+        loads[2].wait()
+        loads[3].wait()
+
+        def add(number, _):
+            which, index = number // line, lax.rem(number, line)
+            total = gu_a[which, index].astype(F32) + gu_b[which, index].astype(F32)
+            gu_a[which, index] = total.astype(BF16)
+            return 0
+
+        lax.fori_loop(0, 2 * line, add, 0)
+        for jump in range(1, line):
+            z_send(jump).start()
+        for copy in stays:
+            copy.start()
+
+    attend_back_body(
+        (received, own),
+        (mix_received, mix_own),
+        (grad_received, grad_own),
+        lambda source, slot: block_of(source, slot, tok),
+        tok,
+        length,
+        tile_q,
+        tile_k,
+        lse_ref,
+        qz,
+        gz,
+        qn,
+        gn,
+        kn,
+        vn,
+        kt,
+        inner,
+        dq,
+        dk,
+        dv,
+    )
+    for slot in range(2):
+        take = slice(slot * tok, (slot + 1) * tok)
+        for source in range(2):
+            cols = block_of(source, slot, tok)
+            results = turn_back(dq, dk, dv, cols, cos_ref[:, cols], sin_ref[:, cols])
+            for which, result in enumerate(results):
+                if source == 1:
+                    back_own[which, :, take] = result
+                else:
+                    at = pl.ds(pl.multiple_of(step * PAIR, PAIR), PAIR)
+                    outgoing[which, at, take] = result
+
+    for number in range(4):
+
+        @pl.when(step == number)
+        def _(number=number):
+            hand_over(number).start()
+
+    @pl.when(step == pairs - 1)
+    def _():
+        swap.wait()
+        d_send.wait()
+        o_send.wait()
+        for copy in stays:
+            copy.wait()
+        for jump in range(1, line):
+            z_send(jump).wait()
+        for number in range(4):
+            hand_over(number).wait()
+
+
+def attend_back_carry(
+    pieces, mixes, grads, lse, cosine, sine, outputs_sent, gu, gu_y, d, o, o_landed, line
+):
+    _, width, span = pieces[0].shape
+    tok = span // 2
+    length = 2 * span
+    pairs = width // PAIR
+    tile_q = min(512, length)
+    tile_k = min(256, length)
+    anywhere = pl.BlockSpec(memory_space=pl.ANY)
+    triple = pl.BlockSpec((3, PAIR, span), lambda p: (0, p, 0))
+    single = pl.BlockSpec((PAIR, span), lambda p: (p, 0))
+    table = pl.BlockSpec((HALF, length), lambda p: (0, 0))
+    rows, half_width = gu.shape[2:]
+    down_rows, wide = d.shape[2:]
+    area = pairs * 2 * length * length // 2
+    return pl.pallas_call(
+        functools.partial(attend_back_carry_kernel, line, tok, tile_q, tile_k),
+        grid=(pairs,),
+        in_specs=[triple] * 2
+        + [single] * 4
+        + [pl.BlockSpec((1, 8, length), lambda p: (p, 0, 0)), table, table]
+        + [anywhere] * 6,
+        out_specs=[triple] + [anywhere] * 7,
+        out_shape=[
+            jax.ShapeDtypeStruct((3, width, span), BF16),
+            jax.ShapeDtypeStruct((3, width, span), BF16),
+            jax.ShapeDtypeStruct(outputs_sent.shape, BF16),
+            jax.ShapeDtypeStruct((2, rows, half_width), BF16),
+            jax.ShapeDtypeStruct((line - 1, 2, rows, half_width), BF16),
+            jax.ShapeDtypeStruct((line, down_rows, wide), BF16),
+            jax.ShapeDtypeStruct((line, rows, wide), BF16),
+            jax.ShapeDtypeStruct((line, rows, wide), BF16),
+        ],
+        scratch_shapes=[
+            pltpu.VMEM((2, PAIR, length), BF16),
+            pltpu.VMEM((2, PAIR, length), BF16),
+            pltpu.VMEM((2, length, PAIR), BF16),
+            pltpu.VMEM((2, length, PAIR), BF16),
+            pltpu.VMEM((length, PAIR), BF16),
+            pltpu.VMEM((length, PAIR), BF16),
+            pltpu.VMEM((PAIR, length), BF16),
+            pltpu.VMEM((8, length), F32),
+            pltpu.VMEM((PAIR, length), F32),
+            pltpu.VMEM((length, PAIR), F32),
+            pltpu.VMEM((length, PAIR), F32),
+            pltpu.VMEM((3, width, span), BF16),
+            pltpu.VMEM((2, line, rows, half_width), BF16),
+            pltpu.VMEM((2, line, rows, half_width), BF16),
+            pltpu.VMEM((line, 2, rows, wide), BF16),
+            pltpu.VMEM((line, 2, rows, wide), BF16),
+            pltpu.SemaphoreType.DMA((6,)),
+            pltpu.SemaphoreType.DMA((2, 4)),
+            pltpu.SemaphoreType.DMA((2, line - 1)),
+            pltpu.SemaphoreType.DMA((2, 3)),
+        ],
+        compiler_params=pltpu.CompilerParams(
+            dimension_semantics=("arbitrary",),
+            vmem_limit_bytes=60 * MIB,
+            collective_id=5,
+            has_side_effects=True,
+        ),
+        cost_estimate=pl.CostEstimate(
+            flops=area * 2560, bytes_accessed=16 * width * length, transcendentals=area
+        ),
+        name="attend_back_carry",
+    )(
+        *pieces, *mixes, *grads, lse, cosine, sine, outputs_sent, gu, gu_y, d, o, o_landed
+    )
+
+
 def shards(
     inputs,
     first_values,
@@ -1593,6 +2255,19 @@
     def pick(value, index, axis):
         return lax.dynamic_index_in_dim(value, index, axis, keepdims=False)
 
+    def along_x_and_core(total):
+        mine = low(total)
+        for jump in range(1, groups // 2):
+            total = total + along_seq(mine, lambda i: (i + 2 * jump) % groups).astype(F32)
+        mine = low(total)
+        return (mine, to_core(mine))
+
+    def along_z_and_on(partial):
+        total = partial(z)
+        for jump in range(1, line):
+            total = total + to_z(low(partial((z + jump) % line)), jump).astype(F32)
+        return along_x_and_core(total)
+
     def scatter(sent, kept, rows_axis):
         shape = kept.shape
         rows = shape[rows_axis] // parts
@@ -1608,14 +2283,7 @@
             total = total + pick(kept_y[1], index, rows_axis).astype(F32)
             return total + pick(received_y, index, rows_axis).astype(F32)
 
-        total = partial(z)
-        for jump in range(1, line):
-            total = total + to_z(low(partial((z + jump) % line)), jump).astype(F32)
-        mine = low(total)
-        for jump in range(1, groups // 2):
-            total = total + along_seq(mine, lambda i: (i + 2 * jump) % groups).astype(F32)
-        mine = low(total)
-        return (mine, to_core(mine))
+        return along_z_and_on(partial)
 
     def columns(mine, others):
         first = jnp.where(core == 0, mine, others)
@@ -1733,28 +2401,91 @@
     middle, normed2, out_full = output_projection(
         inputs, tokens, out_own, out_other, att_other, att_own, gains_full, layout
     )
-    (
-        outputs,
-        outputs_sent,
-        grad_middle,
-        low_grad,
-        mlp_gain_grad,
-        gu_sent,
-        gu_kept,
-        down_sent,
-        down_kept,
-    ) = mlp(out_grad, grads, middle, normed2, gains_full, gate_pieces, up_pieces, down_pieces, layout)
-    ga_other, ga_own, out_sent, out_kept = grad_attended(
-        low_grad, out_full, att_other, att_own, place
-    )
-    gate_up_grad = scatter(gu_sent, gu_kept, 1)
-    down_grad = scatter(
-        down_sent.reshape(-1, wide), down_kept.reshape(-1, wide), 0
-    )
-    output_grad = scatter(out_sent, out_kept, 0)
-    grad_heads = exchange(halves_to_ranks(ga_other, ga_own, 0))
-    back = attend_back(pieces, mixes, grad_heads, lse, full_cos, full_sin, order, slots)
-    back_other, back_own = ranks_to_halves(exchange_back(back), 1)
+    if (slots, count) == (2, 2):
+        (
+            outputs,
+            outputs_sent,
+            grad_middle,
+            low_grad,
+            mlp_gain_grad,
+            gu_reduced,
+            down_reduced,
+            gu_y,
+        ) = mlp_carry(
+            out_grad,
+            grads[0],
+            middle,
+            normed2,
+            gains_full,
+            (gate_pieces[0][0], gate_pieces[1][0]),
+            (up_pieces[0][0], up_pieces[1][0]),
+            (down_pieces[0][0], down_pieces[1][0]),
+            line,
+        )
+        ga_own, ga_received, out_kept, out_landed = grad_attended_carry(
+            low_grad, out_full, att_other, att_own, line
+        )
+        down_reduced = down_reduced.reshape(line, 2, -1, wide)
+        out_kept = out_kept.reshape(line, 2, -1, wide)
+        out_landed = out_landed.reshape(line, 2, -1, wide)
+        (
+            back_own,
+            back_other,
+            outputs_received,
+            gu_mine,
+            gu_z,
+            down_y,
+            out_mine,
+            out_y,
+        ) = attend_back_carry(
+            pieces,
+            mixes,
+            [ga_received, ga_own],
+            lse,
+            full_cos,
+            full_sin,
+            outputs_sent,
+            gu_reduced,
+            gu_y,
+            down_reduced,
+            out_kept,
+            out_landed,
+            line,
+        )
+        outputs = land(outputs, outputs_received, (1 - side)[None])
+        gate_up_grad = gu_mine.astype(F32)
+        for jump in range(line - 1):
+            gate_up_grad = gate_up_grad + gu_z[jump].astype(F32)
+        gate_up_grad = along_x_and_core(gate_up_grad)
+        down_grad = along_z_and_on(
+            lambda index: pick(pick(down_reduced, y, 1), index, 0).astype(F32)
+            + pick(down_y, index, 0).astype(F32)
+        )
+        output_grad = along_z_and_on(
+            lambda index: pick(out_mine, index, 0).astype(F32) + pick(out_y, index, 0).astype(F32)
+        )
+    else:
+        (
+            outputs,
+            outputs_sent,
+            grad_middle,
+            low_grad,
+            mlp_gain_grad,
+            gu_sent,
+            gu_kept,
+            down_sent,
+            down_kept,
+        ) = mlp(out_grad, grads, middle, normed2, gains_full, gate_pieces, up_pieces, down_pieces, layout)
+        ga_other, ga_own, out_sent, out_kept = grad_attended(
+            low_grad, out_full, att_other, att_own, place
+        )
+        gate_up_grad = scatter(gu_sent, gu_kept, 1)
+        down_grad = scatter(down_sent.reshape(-1, wide), down_kept.reshape(-1, wide), 0)
+        output_grad = scatter(out_sent, out_kept, 0)
+        grad_heads = exchange(halves_to_ranks(ga_other, ga_own, 0))
+        back = attend_back(pieces, mixes, grad_heads, lse, full_cos, full_sin, order, slots)
+        back_other, back_own = ranks_to_halves(exchange_back(back), 1)
+        outputs = to_home(outputs, outputs_sent)
     input_grad, input_sent, first_grad, first_sent, gain_grads, qkv_sent, qkv_kept = tail(
         inputs,
         tokens,
@@ -1772,7 +2503,7 @@
     gain_grads = everywhere(gain_grads)
     gain_grads = lax.dynamic_slice_in_dim(gain_grads, shard * (D // parts), D // parts, 1)
     return (
-        to_home(outputs, outputs_sent),
+        outputs,
         to_home(input_grad, input_sent),
         to_home(first_grad, first_sent),
         gain_grads[0],

time: 738 us -> 654 us (0.89)
  waiting for transfers between devices: 254 us -> 144 us
  Pallas kernels: 374 us -> 406 us
  other arithmetic: 37.5 us -> 24.2 us
  local copies, waits for them, and re-layouts: 15.3 us -> 24.7 us
    ppermute x20 -> x14, waiting for transfers between devices: 199 us -> 78.6 us  [along_fsdp(): return lax.ppermute(value, 'fsdp', [(i, partner(i)) for i in range(parts)])]
    pallas_call x3, Pallas kernels: 154 us -> 188 us  [the longest x1 101 us: mlp_carry(): pl.pallas_call(functools.partial(mlp_carry_kernel, line, tok, blocks), gr...]
    convert_element_type x16 -> x12, other arithmetic: 29.3 us -> 15.4 us  [low(): return value.astype(BF16)]
    unnamed x35 -> x54, local copies, waits for them, and re-layouts: 6.84 us -> 17.4 us
    ppermute x19 -> x13, waiting for transfers between devices: 55 us -> 65.5 us  [along_seq(): return lax.ppermute(value, 'seq', [(i, partner(i)) for i in range(groups)])]
    ppermute x19 -> x13, starting transfers between devices: 29.3 us -> 19.7 us  [along_seq(): return lax.ppermute(value, 'seq', [(i, partner(i)) for i in range(groups)])]
    ppermute x20 -> x14, starting transfers between devices: 19.4 us -> 25.9 us  [along_fsdp(): return lax.ppermute(value, 'fsdp', [(i, partner(i)) for i in range(parts)])]
  transfers between devices with their start and end apart: 39 -> 27, of which waited for: 15 -> 10; matrix products, arithmetic and copies ran while one was open for 5% -> 3% of each run, Pallas kernels for 4% -> 0%
where the time goes in v4:
time: 654 us; the launch traced here: 646 us
  Pallas kernels  406 us (62%)
  waiting for transfers between devices  144 us (22%)
  starting transfers between devices  45.6 us (7%)
  local copies, waits for them, and re-layouts  24.7 us (4%)
  other arithmetic  24.2 us (4%)
    pallas_call x1, Pallas kernels, mlp_carry(): pl.pallas_call(functools.partial(mlp_carry_kernel, line, tok, blocks), gr...  101 us
    pallas_call x1, Pallas kernels, attend_carry(): pl.pallas_call(functools.partial(attend_carry_kernel, line, tok, min(256,...  99.3 us
    pallas_call x1, Pallas kernels, front(): pl.pallas_call(functools.partial(front_kernel, line, tok), grid=(6,), in_...  79.6 us
    ppermute x14, waiting for transfers between devices, along_fsdp(): return lax.ppermute(value, 'fsdp', [(i, partner(i)) for i in range(parts)])  78.6 us
    pallas_call x1, Pallas kernels, attend_back_carry(): pl.pallas_call(functools.partial(attend_back_carry_kernel, line, tok, til...  77.9 us
    ppermute x13, waiting for transfers between devices, along_seq(): return lax.ppermute(value, 'seq', [(i, partner(i)) for i in range(groups)])  65.5 us
    pallas_call x1, Pallas kernels, tail(): pl.pallas_call(functools.partial(tail_kernel, slots, tok), out_shape=[jax...  27.3 us
    ppermute x14, starting transfers between devices, along_fsdp(): return lax.ppermute(value, 'fsdp', [(i, partner(i)) for i in range(parts)])  25.9 us
  transfers between devices with their start and end apart: 27, of which 10 were waited for; matrix products, arithmetic and copies ran while one was open for 3% of the time, Pallas kernels for 0%

profile of v4, /device:TPU:25, one launch (start us, length us, event | category | flops | bytes accessed | tf_op | source)
XLA Modules:
  0.0 646.5 jit_solution(7965566009096277147)
XLA Ops:
  9.4 79.6 %front.1 = (bf16[512,1024]{1,0:T(8,128)(2,1)}, bf16[512,1024]{1,0:T(8,128)(2,1)}, bf16[3,512,1024]{2,1,0:T(8,128)(2,1)}, bf16[3,512,1024]{2,1,0:T(8,128)(2,1)}, ...) custom-call(bf16[2,512,1024]{2,1,0:T(8,128)(2,1)} %refs_0_.7, ...), custom_call_target="tpu_custom_call" | custom-call | flops 6442450944 | bytes 29360128 | tf_op jit(solution)/shard_map/front/pallas_call | solution.py:1264
  89.1 99.3 %attend_carry.1 = (bf16[512,1024]{1,0:T(8,128)(2,1)S(1)}, bf16[512,1024]{1,0:T(8,128)(2,1)S(1)}, f32[4,8,2048]{2,1,0:T(8,128)S(1)}, bf16[512,1024]{1,0:T(8,128)(...) custom-call(bf16[3,512,1024]{2,1,0:T(8,128)(2,1)} %get-tuple-element, ...), custom_call_target="tpu_custom_call", output_to_operand_aliasing={{5}: (3, {})} | custom-call | flops 17179869184 | bytes 8388608 | tf_op jit(solution)/shard_map/attend_carry/pallas_call | solution.py:1454
  193.1 9.1 %output_projection.1 = (f32[1024,1024]{1,0:T(8,128)}, bf16[1024,1024]{1,0:T(8,128)(2,1)}, bf16[1024,1024]{1,0:T(8,128)(2,1)}) custom-call(s32[3]{0:T(128)} %pad_add_fusion.place, bf16[2,512,1024]{2,1,0:T(8,128)(2,1)} %refs_0_.7, bf16[512,1024]{1,0:T(8,128)(2,1)} %get-tuple-element.66.refs_1_, bf16[1024,512]{1,0:T(8,128)(2,1)} %bitcast.177, ...), custom_call_target="tpu_custom_call" | custom-call | flops 2147483648 | bytes 16777216 | tf_op jit(solution)/shard_map/output_projection/pallas_call | solution.py:499
  202.1 101.0 %mlp_carry.1 = (f32[2,512,1024]{2,1,0:T(8,128)}, bf16[512,1024]{1,0:T(8,128)(2,1)}, f32[1024,1024]{1,0:T(8,128)}, bf16[1024,1024]{1,0:T(8,128)(2,1)}, f32[8,1024...) custom-call(bf16[2,512,1024]{2,1,0:T(8,128)(2,1)} %refs_0_.6, ...), custom_call_target="tpu_custom_call" | custom-call | flops 47244640256 | bytes 55574528 | tf_op jit(solution)/shard_map/mlp_carry/pallas_call | solution.py:1706
  304.3 9.3 %grad_attended_carry.1 = (bf16[512,1024]{1,0:T(8,128)(2,1)S(1)}, bf16[512,1024]{1,0:T(8,128)(2,1)S(1)}, bf16[1024,512]{1,0:T(8,128)(2,1)S(1)}, bf16[1024,512]{1,0:T(8,128)(2,1)S(1)}) custom-call(bf16[1024,1024]{1,0:T(8,128)(2,1)} %get-tuple-element.82.low_ref, bf16[1024,1024]{1,0:T(8,128)(2,1)} %get-tuple-element.83.full_ref, ...), custom_call_target="tpu_custom_call" | custom-call | flops 4294967296 | bytes 10485760 | tf_op jit(solution)/shard_map/grad_attended_carry/pallas_call | solution.py:1841
  318.1 77.9 %attend_back_carry.1 = (bf16[3,512,1024]{2,1,0:T(8,128)(2,1)}, bf16[3,512,1024]{2,1,0:T(8,128)(2,1)}, bf16[512,1024]{1,0:T(8,128)(2,1)}, bf16[2,128,1408]{2,1,0:...) custom-call(bf16[3,512,1024]{2,1,0:T(8,128)(2,1)} %get-tuple-element, ...), custom_call_target="tpu_custom_call" | custom-call | flops 42949672960 | bytes 16777216 | tf_op jit(solution)/shard_map/attend_back_carry/pallas_call | solution.py:2060
  396.0 27.3 %tail.1 = (f32[2,512,1024]{2,1,0:T(8,128)}, bf16[512,1024]{1,0:T(8,128)(2,1)}, f32[2,512,1024]{2,1,0:T(8,128)}, bf16[512,1024]{1,0:T(8,128)(2,1)}, f32[8,1024]{1...) custom-call(s32[10]{0:T(128)} %stack.61.place, bf16[2,512,1024]{2,1,0:T(8,128)(2,1)} %refs_0_.7, ...), custom_call_target="tpu_custom_call" | custom-call | flops 12884901888 | bytes 37748736 | tf_op jit(solution)/shard_map/tail/pallas_call | solution.py:904
  423.9 4.4 collective-permute-done.2
  430.4 2.8 fusion.9
  436.9 6.5 %collective-permute-done.4 = f32[8,1024]{1,0:T(8,128)S(1)} collective-permute-done((f32[8,1024]{1,0:T(8,128)S(1)}, f32[8,1024]{1,0:T(8,128)S(1)}, u32[]{:S(2)}, u32[]{:S(2)}) %collective-permute-start.4) | collective-permute-done | bytes 32800 | tf_op jit(solution)/shard_map/ppermute | solution.py:2149
  443.5 3.5 collective-permute-start.15
  450.1 2.2 copy-done.2
  454.5 2.4 collective-permute-start.23
  457.9 19.2 %collective-permute-done.17 = bf16[128,512]{1,0:T(8,128)(2,1)S(1)} collective-permute-done((bf16[128,512]{1,0:T(8,128)(2,1)}, bf16[128,512]{1,0:T(8,128)(2,1)S(1)}, u32[]{:S(2)}, u32[]{:S(2)}) %collective-permute-start.17) | collective-permute-done | bytes 131104 | tf_op jit(solution)/shard_map/ppermute | solution.py:2149
  479.7 2.4 collective-permute-done.23
  485.0 55.6 %collective-permute-done.18 = bf16[128,512]{1,0:T(8,128)(2,1)S(1)} collective-permute-done((bf16[128,512]{1,0:T(8,128)(2,1)S(1)}, bf16[128,512]{1,0:T(8,128)(2,1)S(1)}, u32[]{:S(2)}, u32[]{:S(2)}) %collective-permute-start.18) | collective-permute-done | bytes 131104 | tf_op jit(solution)/shard_map/ppermute | solution.py:2146
  542.3 3.0 collective-permute-start.19
  549.2 4.3 collective-permute-start.26
  559.0 20.5 %collective-permute-done.9 = bf16[3,4,128,512]{3,2,0,1:T(8,128)(2,1)S(1)} collective-permute-done((bf16[3,4,128,512]{3,2,0,1:T(8,128)(2,1)S(1)}, bf16[3,4,128,512]{3,2,0,1:T(8,128)(2,1)S(1)}, u32[]{:S(2)}, u32[]{:S(2)}) %collective-permute-start.9) | collective-permute-done | bytes 1572896 | tf_op jit(solution)/shard_map/ppermute | solution.py:2149
  583.3 11.7 %collective-permute-start.11 = (bf16[3,128,512]{2,1,0:T(8,128)(2,1)S(1)}, bf16[3,128,512]{2,1,0:T(8,128)(2,1)S(1)}, u32[]{:S(2)}, u32[]{:S(2)}) collective-permute-start(bf16[3,128,512]{2,1,0:T(8,128)(2,1)S(1)} %get-tuple-element.116), channel_id=1, source_target_pairs={{0,16},{4,20},{8,24},{12,28},{16,0},{20,4},{24,8},{28,12},{1,17},{... | collective-permute-start | bytes 1179656 | tf_op jit(solution)/shard_map/ppermute | solution.py:2149
  596.5 2.9 collective-permute-done.10
  599.4 27.1 %collective-permute-done.11 = bf16[3,128,512]{2,1,0:T(8,128)(2,1)S(1)} collective-permute-done((bf16[3,128,512]{2,1,0:T(8,128)(2,1)S(1)}, bf16[3,128,512]{2,1,0:T(8,128)(2,1)S(1)}, u32[]{:S(2)}, u32[]{:S(2)}) %collective-permute-start.11) | collective-permute-done | bytes 393248 | tf_op jit(solution)/shard_map/ppermute | solution.py:2149
  629.3 5.3 collective-permute-done.13
  634.7 5.0 collective-permute-start.14
  (136 shorter events, 62.9 us)
Async XLA Ops:
  423.4 119.0 %collective-permute-start.8 = (bf16[3,1024,512]{2,1,0:T(8,128)(2,1)}, bf16[3,1024,512]{2,1,0:T(8,128)(2,1)}, u32[]{:S(2)}, u32[]{:S(2)}) collective-permute-start(bf16[3,1024,512]{2,1,0:T(8,128)(2,1)} %get-tuple-element.106), channel_id=1, source_target_pairs={{0,1},{1,0},{2,3},{3,2},{4,5},{5,4},{6,7},{7,6},{8,9},{9,8},{10,11... | collective-permute-start | bytes 9437192 | tf_op jit(solution)/shard_map/ppermute | solution.py:2146
  433.2 45.3 %collective-permute-start.22 = (bf16[352,512]{1,0:T(8,128)(2,1)}, bf16[352,512]{1,0:T(8,128)(2,1)}, u32[]{:S(2)}, u32[]{:S(2)}) collective-permute-start(bf16[352,512]{1,0:T(8,128)(2,1)} %get-tuple-element.117), channel_id=1, source_target_pairs={{0,8},{4,12},{8,16},{12,20},{16,24},{20,28},{24,0},{28,4},{1,9},{5... | collective-permute-start | bytes 1081352 | tf_op jit(solution)/shard_map/ppermute | solution.py:2149
  434.6 8.9 %collective-permute-start.4 = (f32[8,1024]{1,0:T(8,128)S(1)}, f32[8,1024]{1,0:T(8,128)S(1)}, u32[]{:S(2)}, u32[]{:S(2)}) collective-permute-start(f32[8,1024]{1,0:T(8,128)S(1)} %add.417), channel_id=1, source_target_pairs={{0,8},{4,12},{8,16},{12,20},{16,24},{20,28},{24,0},{28,4},{1,9},{5... | collective-permute-start | bytes 98312 | tf_op jit(solution)/shard_map/ppermute | solution.py:2149
  435.7 11.3 %collective-permute-start.5 = (f32[8,1024]{1,0:T(8,128)S(1)}, f32[8,1024]{1,0:T(8,128)S(1)}, u32[]{:S(2)}, u32[]{:S(2)}) collective-permute-start(f32[8,1024]{1,0:T(8,128)S(1)} %add.417), channel_id=1, source_target_pairs={{0,16},{4,20},{8,24},{12,28},{16,0},{20,4},{24,8},{28,12},{1,17},{... | collective-permute-start | bytes 98312 | tf_op jit(solution)/shard_map/ppermute | solution.py:2149
  435.9 11.1 %collective-permute-start.6 = (f32[8,1024]{1,0:T(8,128)S(1)}, f32[8,1024]{1,0:T(8,128)S(1)}, u32[]{:S(2)}, u32[]{:S(2)}) collective-permute-start(f32[8,1024]{1,0:T(8,128)S(1)} %add.417), channel_id=1, source_target_pairs={{0,24},{4,28},{8,0},{12,4},{16,8},{20,12},{24,16},{28,20},{1,25},{... | collective-permute-start | bytes 98312 | tf_op jit(solution)/shard_map/ppermute | solution.py:2149
  443.5 13.4 %collective-permute-start.15 = (bf16[128,512]{1,0:T(8,128)(2,1)}, bf16[128,512]{1,0:T(8,128)(2,1)S(1)}, u32[]{:S(2)}, u32[]{:S(2)}) collective-permute-start(bf16[128,512]{1,0:T(8,128)(2,1)} %get-tuple-element.127), channel_id=1, source_target_pairs={{0,8},{4,12},{8,16},{12,20},{16,24},{20,28},{24,0},{28,4},{1,9},{5... | collective-permute-start | bytes 393224 | tf_op jit(solution)/shard_map/ppermute | solution.py:2149
  447.0 10.0 %collective-permute-start.16 = (bf16[128,512]{1,0:T(8,128)(2,1)}, bf16[128,512]{1,0:T(8,128)(2,1)S(1)}, u32[]{:S(2)}, u32[]{:S(2)}) collective-permute-start(bf16[128,512]{1,0:T(8,128)(2,1)} %get-tuple-element.129), channel_id=1, source_target_pairs={{0,16},{4,20},{8,24},{12,28},{16,0},{20,4},{24,8},{28,12},{1,17},{... | collective-permute-start | bytes 393224 | tf_op jit(solution)/shard_map/ppermute | solution.py:2149
  447.0 7.5 %collective-permute-start.7 = (f32[8,1024]{1,0:T(8,128)S(1)}, f32[8,1024]{1,0:T(8,128)S(1)}, u32[]{:S(2)}, u32[]{:S(2)}) collective-permute-start(f32[8,1024]{1,0:T(8,128)S(1)} %add_add_fusion), channel_id=1, source_target_pairs={{0,2},{1,3},{2,0},{3,1},{4,6},{5,7},{6,4},{7,5},{8,10},{9,11},{10,... | collective-permute-start | bytes 98312 | tf_op jit(solution)/shard_map/ppermute | solution.py:2146
  454.5 27.6 %collective-permute-start.23 = (bf16[352,512]{1,0:T(8,128)(2,1)}, bf16[352,512]{1,0:T(8,128)(2,1)S(1)}, u32[]{:S(2)}, u32[]{:S(2)}) collective-permute-start(bf16[352,512]{1,0:T(8,128)(2,1)} %get-tuple-element.119), channel_id=1, source_target_pairs={{0,16},{4,20},{8,24},{12,28},{16,0},{20,4},{24,8},{28,12},{1,17},{... | collective-permute-start | bytes 1081352 | tf_op jit(solution)/shard_map/ppermute | solution.py:2149
  456.9 25.2 %collective-permute-start.24 = (bf16[352,512]{1,0:T(8,128)(2,1)}, bf16[352,512]{1,0:T(8,128)(2,1)S(1)}, u32[]{:S(2)}, u32[]{:S(2)}) collective-permute-start(bf16[352,512]{1,0:T(8,128)(2,1)} %get-tuple-element.118), channel_id=1, source_target_pairs={{0,24},{4,28},{8,0},{12,4},{16,8},{20,12},{24,16},{28,20},{1,25},{... | collective-permute-start | bytes 1081352 | tf_op jit(solution)/shard_map/ppermute | solution.py:2149
  457.0 20.1 %collective-permute-start.17 = (bf16[128,512]{1,0:T(8,128)(2,1)}, bf16[128,512]{1,0:T(8,128)(2,1)S(1)}, u32[]{:S(2)}, u32[]{:S(2)}) collective-permute-start(bf16[128,512]{1,0:T(8,128)(2,1)} %get-tuple-element.128), channel_id=1, source_target_pairs={{0,24},{4,28},{8,0},{12,4},{16,8},{20,12},{24,16},{28,20},{1,25},{... | collective-permute-start | bytes 393224 | tf_op jit(solution)/shard_map/ppermute | solution.py:2149
  477.1 72.1 %collective-permute-start.20 = (bf16[2,128,1408]{2,1,0:T(8,128)(2,1)}, bf16[2,128,1408]{2,1,0:T(8,128)(2,1)S(1)}, u32[]{:S(2)}, u32[]{:S(2)}) collective-permute-start(bf16[2,128,1408]{2,1,0:T(8,128)(2,1)} %fusion.16), channel_id=1, source_target_pairs={{0,2},{1,3},{2,0},{3,1},{4,6},{5,7},{6,4},{7,5},{8,10},{9,11},{10,... | collective-permute-start | bytes 2162696 | tf_op jit(solution)/shard_map/ppermute | solution.py:2146
  478.5 76.4 %collective-permute-start.1 = (bf16[512,1024]{1,0:T(8,128)(2,1)}, bf16[512,1024]{1,0:T(8,128)(2,1)S(1)}, u32[]{:S(2)}, u32[]{:S(2)}) collective-permute-start(bf16[512,1024]{1,0:T(8,128)(2,1)} %get-tuple-element.103), channel_id=1, source_target_pairs={{0,2},{1,3},{2,0},{3,1},{4,6},{5,7},{6,4},{7,5},{8,10},{9,11},{10,... | collective-permute-start | bytes 3145736 | tf_op jit(solution)/shard_map/ppermute | solution.py:2146
  482.1 74.2 %collective-permute-start = (bf16[512,1024]{1,0:T(8,128)(2,1)}, bf16[512,1024]{1,0:T(8,128)(2,1)S(1)}, u32[]{:S(2)}, u32[]{:S(2)}) collective-permute-start(bf16[512,1024]{1,0:T(8,128)(2,1)} %get-tuple-element.101), channel_id=1, source_target_pairs={{0,2},{1,3},{2,0},{3,1},{4,6},{5,7},{6,4},{7,5},{8,10},{9,11},{10,... | collective-permute-start | bytes 3145736 | tf_op jit(solution)/shard_map/ppermute | solution.py:2146
  482.1 58.5 %collective-permute-start.18 = (bf16[128,512]{1,0:T(8,128)(2,1)S(1)}, bf16[128,512]{1,0:T(8,128)(2,1)S(1)}, u32[]{:S(2)}, u32[]{:S(2)}) collective-permute-start(bf16[128,512]{1,0:T(8,128)(2,1)S(1)} %fusion.25), channel_id=1, source_target_pairs={{0,2},{1,3},{2,0},{3,1},{4,6},{5,7},{6,4},{7,5},{8,10},{9,11},{10,... | collective-permute-start | bytes 393224 | tf_op jit(solution)/shard_map/ppermute | solution.py:2146
  540.6 6.9 %collective-permute-start.25 = (bf16[352,512]{1,0:T(8,128)(2,1)S(1)}, bf16[352,512]{1,0:T(8,128)(2,1)S(1)}, u32[]{:S(2)}, u32[]{:S(2)}) collective-permute-start(bf16[352,512]{1,0:T(8,128)(2,1)S(1)} %fusion.26), channel_id=1, source_target_pairs={{0,2},{1,3},{2,0},{3,1},{4,6},{5,7},{6,4},{7,5},{8,10},{9,11},{10,... | collective-permute-start | bytes 1081352 | tf_op jit(solution)/shard_map/ppermute | solution.py:2146
  542.3 11.6 %collective-permute-start.19 = (bf16[128,512]{1,0:T(8,128)(2,1)S(1)}, bf16[128,512]{1,0:T(8,128)(2,1)S(1)}, u32[]{:S(2)}, u32[]{:S(2)}) collective-permute-start(bf16[128,512]{1,0:T(8,128)(2,1)S(1)} %add_convert_fusion.4), channel_id=1, source_target_pairs={{0,1},{1,0},{2,3},{3,2},{4,5},{5,4},{6,7},{7,6},{8,9},{9,8},{10,11... | collective-permute-start | bytes 393224 | tf_op jit(solution)/shard_map/ppermute | solution.py:2146
  547.5 32.0 %collective-permute-start.9 = (bf16[3,4,128,512]{3,2,0,1:T(8,128)(2,1)S(1)}, bf16[3,4,128,512]{3,2,0,1:T(8,128)(2,1)S(1)}, u32[]{:S(2)}, u32[]{:S(2)}) collective-permute-start(bf16[3,4,128,512]{3,2,0,1:T(8,128)(2,1)S(1)} %fusion), channel_id=1, source_target_pairs={{0,4},{4,0},{8,12},{12,8},{16,20},{20,16},{24,28},{28,24},{1,5},{5... | collective-permute-start | bytes 4718600 | tf_op jit(solution)/shard_map/ppermute | solution.py:2149
  549.2 8.5 %collective-permute-start.26 = (bf16[352,512]{1,0:T(8,128)(2,1)S(1)}, bf16[352,512]{1,0:T(8,128)(2,1)S(1)}, u32[]{:S(2)}, u32[]{:S(2)}) collective-permute-start(bf16[352,512]{1,0:T(8,128)(2,1)S(1)} %add_convert_fusion.3), channel_id=1, source_target_pairs={{0,1},{1,0},{2,3},{3,2},{4,5},{5,4},{6,7},{7,6},{8,9},{9,8},{10,11... | collective-permute-start | bytes 1081352 | tf_op jit(solution)/shard_map/ppermute | solution.py:2146
  553.9 42.5 %collective-permute-start.21 = (bf16[2,128,1408]{2,1,0:T(8,128)(2,1)S(1)}, bf16[2,128,1408]{2,1,0:T(8,128)(2,1)S(1)}, u32[]{:S(2)}, u32[]{:S(2)}) collective-permute-start(bf16[2,128,1408]{2,1,0:T(8,128)(2,1)S(1)} %add_convert_fusion.1), channel_id=1, source_target_pairs={{0,1},{1,0},{2,3},{3,2},{4,5},{5,4},{6,7},{7,6},{8,9},{9,8},{10,11... | collective-permute-start | bytes 2162696 | tf_op jit(solution)/shard_map/ppermute | solution.py:2146
  581.3 18.2 %collective-permute-start.10 = (bf16[3,128,512]{2,1,0:T(8,128)(2,1)S(1)}, bf16[3,128,512]{2,1,0:T(8,128)(2,1)S(1)}, u32[]{:S(2)}, u32[]{:S(2)}) collective-permute-start(bf16[3,128,512]{2,1,0:T(8,128)(2,1)S(1)} %get-tuple-element.114), channel_id=1, source_target_pairs={{0,8},{4,12},{8,16},{12,20},{16,24},{20,28},{24,0},{28,4},{1,9},{5... | collective-permute-start | bytes 1179656 | tf_op jit(solution)/shard_map/ppermute | solution.py:2149
  583.3 43.2 %collective-permute-start.11 = (bf16[3,128,512]{2,1,0:T(8,128)(2,1)S(1)}, bf16[3,128,512]{2,1,0:T(8,128)(2,1)S(1)}, u32[]{:S(2)}, u32[]{:S(2)}) collective-permute-start(bf16[3,128,512]{2,1,0:T(8,128)(2,1)S(1)} %get-tuple-element.116), channel_id=1, source_target_pairs={{0,16},{4,20},{8,24},{12,28},{16,0},{20,4},{24,8},{28,12},{1,17},{... | collective-permute-start | bytes 1179656 | tf_op jit(solution)/shard_map/ppermute | solution.py:2149
  595.0 31.5 %collective-permute-start.12 = (bf16[3,128,512]{2,1,0:T(8,128)(2,1)S(1)}, bf16[3,128,512]{2,1,0:T(8,128)(2,1)S(1)}, u32[]{:S(2)}, u32[]{:S(2)}) collective-permute-start(bf16[3,128,512]{2,1,0:T(8,128)(2,1)S(1)} %get-tuple-element.115), channel_id=1, source_target_pairs={{0,24},{4,28},{8,0},{12,4},{16,8},{20,12},{24,16},{28,20},{1,25},{... | collective-permute-start | bytes 1179656 | tf_op jit(solution)/shard_map/ppermute | solution.py:2149
  634.7 6.7 %collective-permute-start.14 = (bf16[3,128,512]{2,1,0:T(8,128)(2,1)S(1)}, bf16[3,128,512]{2,1,0:T(8,128)(2,1)S(1)}, u32[]{:S(2)}, u32[]{:S(2)}) collective-permute-start(bf16[3,128,512]{2,1,0:T(8,128)(2,1)S(1)} %add_convert_fusion.2), channel_id=1, source_target_pairs={{0,1},{1,0},{2,3},{3,2},{4,5},{5,4},{6,7},{7,6},{8,9},{9,8},{10,11... | collective-permute-start | bytes 1179656 | tf_op jit(solution)/shard_map/ppermute | solution.py:2146
  (29 other events, 243.8 us)

commit v5 on v4

--- a/solution.py
+++ b/solution.py
@@ -1562,10 +1562,7 @@
         ]
 
     def y_copy(number):
-        columns = pl.ds(pl.multiple_of(number * strip, strip), strip)
-        return send(
-            gu_outgoing.at[number], gu_y.at[:, :, :, columns], y_sems, number, to_y_partner()
-        )
+        return send(gu_outgoing.at[number], gu_y.at[number], y_sems, number, to_y_partner())
 
     @pl.when(step == 0)
     def _():
@@ -1638,7 +1635,7 @@
             gu_outgoing[number, which] = theirs.astype(BF16)
             ours = gu_kept[slot, which, :, y].astype(F32)
             ours = ours + gu_landed[number, which, :, y].astype(F32)
-            gu_ref[which] = ours.astype(BF16)
+            gu_ref[0, which] = ours.astype(BF16)
         y_copy(number).start()
         d_ref[...] = (d_kept[slot].astype(F32) + d_landed[number].astype(F32)).astype(BF16)
 
@@ -1717,7 +1714,7 @@
             full,
             full,
             whole_block((8, depth)),
-            pl.BlockSpec((2, line, rows, 128), lambda s: (0, 0, 0, done(s))),
+            pl.BlockSpec((1, 2, line, rows, 128), lambda s: (done(s), 0, 0, 0, 0)),
             pl.BlockSpec((2, 128, wide), lambda s: (0, done(s), 0)),
             anywhere,
         ],
@@ -1727,9 +1724,9 @@
             jax.ShapeDtypeStruct((span, depth), F32),
             jax.ShapeDtypeStruct((span, depth), BF16),
             jax.ShapeDtypeStruct((8, depth), F32),
-            jax.ShapeDtypeStruct((2, line, rows, half_width), BF16),
+            jax.ShapeDtypeStruct((blocks, 2, line, rows, 128), BF16),
             jax.ShapeDtypeStruct((2, half_width, wide), BF16),
-            jax.ShapeDtypeStruct((2, line, rows, half_width), BF16),
+            jax.ShapeDtypeStruct((blocks, 2, line, rows, 128), BF16),
         ],
         scratch_shapes=[
             pltpu.VMEM((span, depth), BF16),
@@ -1938,11 +1935,11 @@
     def z_send(jump):
         target = lax.rem(z + jump, line)
         return send(
-            gu_a.at[:, target], gu_z.at[jump - 1], z_sems, jump - 1, to_z_partner(line, jump)
+            gu_a.at[:, :, target], gu_z.at[jump - 1], z_sems, jump - 1, to_z_partner(line, jump)
         )
 
     stays = [
-        pltpu.make_async_copy(gu_a.at[:, z], gu_mine, local_sems.at[4]),
+        pltpu.make_async_copy(gu_a.at[:, :, z], gu_mine, local_sems.at[4]),
         pltpu.make_async_copy(o_a.at[:, y], o_kept, local_sems.at[5]),
     ]
 
@@ -1977,12 +1974,11 @@
         loads[3].wait()
 
         def add(number, _):
-            which, index = number // line, lax.rem(number, line)
-            total = gu_a[which, index].astype(F32) + gu_b[which, index].astype(F32)
-            gu_a[which, index] = total.astype(BF16)
+            total = gu_a[number].astype(F32) + gu_b[number].astype(F32)
+            gu_a[number] = total.astype(BF16)
             return 0
 
-        lax.fori_loop(0, 2 * line, add, 0)
+        lax.fori_loop(0, gu_a.shape[0], add, 0)
         for jump in range(1, line):
             z_send(jump).start()
         for copy in stays:
@@ -2054,7 +2050,7 @@
     triple = pl.BlockSpec((3, PAIR, span), lambda p: (0, p, 0))
     single = pl.BlockSpec((PAIR, span), lambda p: (p, 0))
     table = pl.BlockSpec((HALF, length), lambda p: (0, 0))
-    rows, half_width = gu.shape[2:]
+    blocks, _, _, rows, _ = gu.shape
     down_rows, wide = d.shape[2:]
     area = pairs * 2 * length * length // 2
     return pl.pallas_call(
@@ -2069,8 +2065,8 @@
             jax.ShapeDtypeStruct((3, width, span), BF16),
             jax.ShapeDtypeStruct((3, width, span), BF16),
             jax.ShapeDtypeStruct(outputs_sent.shape, BF16),
-            jax.ShapeDtypeStruct((2, rows, half_width), BF16),
-            jax.ShapeDtypeStruct((line - 1, 2, rows, half_width), BF16),
+            jax.ShapeDtypeStruct((blocks, 2, rows, 128), BF16),
+            jax.ShapeDtypeStruct((line - 1, blocks, 2, rows, 128), BF16),
             jax.ShapeDtypeStruct((line, down_rows, wide), BF16),
             jax.ShapeDtypeStruct((line, rows, wide), BF16),
             jax.ShapeDtypeStruct((line, rows, wide), BF16),
@@ -2088,8 +2084,8 @@
             pltpu.VMEM((length, PAIR), F32),
             pltpu.VMEM((length, PAIR), F32),
             pltpu.VMEM((3, width, span), BF16),
-            pltpu.VMEM((2, line, rows, half_width), BF16),
-            pltpu.VMEM((2, line, rows, half_width), BF16),
+            pltpu.VMEM((blocks, 2, line, rows, 128), BF16),
+            pltpu.VMEM((blocks, 2, line, rows, 128), BF16),
             pltpu.VMEM((line, 2, rows, wide), BF16),
             pltpu.VMEM((line, 2, rows, wide), BF16),
             pltpu.SemaphoreType.DMA((6,)),
@@ -2109,6 +2105,527 @@
         name="attend_back_carry",
     )(
         *pieces, *mixes, *grads, lse, cosine, sine, outputs_sent, gu, gu_y, d, o, o_landed
+    )
+
+
+def tail_carry_kernel(line, tok, blocks, *refs):
+    (
+        inputs,
+        x_received,
+        back_other,
+        back_own,
+        full_ref,
+        normed_ref,
+        grad_in,
+        gains_ref,
+        mlp_gain_ref,
+        gu_mine,
+        gu_z,
+        d_in,
+        d_y,
+        o_in,
+        o_y,
+        input_grad,
+        first_grad,
+        gain_out,
+        q_out,
+        k_out,
+        v_out,
+        o_out,
+        g_out,
+        u_out,
+        d_out,
+        xs,
+        grad_middle,
+        normed_t,
+        acc,
+        grad,
+        sent,
+        landed,
+        y_landed,
+        z_landed,
+        d_a,
+        d_b,
+        d_landed,
+        o_a,
+        o_b,
+        o_landed,
+        gu_a,
+        gu_b,
+        gu_x,
+        gu_c,
+        d_low,
+        d_x,
+        d_c,
+        s_low,
+        s_x,
+        s_c,
+        first_stage,
+        first_send,
+        first_landed,
+        input_send,
+        input_landed,
+        gain,
+        gain_landed,
+        local_sems,
+        core_sems,
+        y_sems,
+        z_sems,
+        dz_sems,
+        oz_sems,
+        x_sems,
+        c_sems,
+        token_sems,
+        gain_sems,
+    ) = refs
+    step = pl.program_id(0)
+    target, turn = step // 3, lax.rem(step, 3)
+    z, y, side, core = seats()
+    wide, span = grad.shape
+    depth = 2 * wide
+    half = jnp.where(target == 0, 1 - core, core)
+    columns = pl.ds(pl.multiple_of(half * wide, wide), wide)
+    mine = pl.ds(pl.multiple_of(core * wide, wide), wide)
+    others = pl.ds(pl.multiple_of((1 - core) * wide, wide), wide)
+
+    def load(source, place, number):
+        return pltpu.make_async_copy(source, place, local_sems.at[number])
+
+    load_tokens = [
+        load(inputs.at[side], xs.at[pl.ds(0, tok), :], 0),
+        load(x_received, xs.at[pl.ds(tok, tok), :], 1),
+        load(grad_in, grad_middle, 2),
+    ]
+    store_input = load(acc.at[pl.ds(0, tok), :], input_grad.at[side], 3)
+    store_input_other = load(acc.at[pl.ds(tok, tok), :], input_grad.at[1 - side], 4)
+    store_first = load(first_stage, first_grad.at[side], 5)
+    store_first_other = load(first_stage, first_grad.at[1 - side], 6)
+
+    def along_z(source, place, sems, base=0):
+        return [
+            send(
+                source(lax.rem(z + jump, line)),
+                place(jump - 1),
+                sems,
+                base + jump - 1,
+                to_z_partner(line, jump),
+            )
+            for jump in range(1, line)
+        ]
+
+    d_sends = along_z(lambda at: d_a.at[at], lambda jump: d_landed.at[jump], dz_sems)
+    o_sends = along_z(lambda at: o_a.at[at], lambda jump: o_landed.at[jump], oz_sems)
+
+    def core_send(number):
+        return send(sent.at[number], landed.at[number], core_sems, number, to_core_partner())
+
+    def y_send(number):
+        return send(
+            landed.at[number, :, 1 - y], y_landed.at[number], y_sems, number, to_y_partner()
+        )
+
+    def z_sends(number):
+        return along_z(
+            lambda at: landed.at[number, at, y],
+            lambda jump: z_landed.at[number, jump],
+            z_sems,
+            number * (line - 1),
+        )
+
+    def first_part(number):
+        which = 1 - core if number == 0 else core
+        at = pl.ds(pl.multiple_of(which * wide, wide), wide)
+        return send(
+            first_send.at[:, at], first_landed.at[:, at], token_sems, number, to_x_partner()
+        )
+
+    input_part = send(input_send, input_landed, token_sems, 2, to_x_partner())
+    gu_sides = (
+        send(gu_a, gu_x, x_sems, 0, to_x_partner()),
+        send(gu_a, gu_c, c_sems, 0, to_core_partner()),
+    )
+    d_sides = (
+        send(d_low, d_x, x_sems, 1, to_x_partner()),
+        send(d_low, d_c, c_sems, 1, to_core_partner()),
+    )
+
+    def square_x(number):
+        return send(s_low.at[number], s_x.at[number], x_sems, 2 + number, to_x_partner())
+
+    def square_core(number):
+        return send(s_low.at[number], s_c.at[number], c_sems, 2 + number, to_core_partner())
+
+    squares = (o_out, v_out, q_out, k_out)
+
+    def gain_send(number, partner):
+        return send(gain.at[number], gain_landed.at[number], gain_sems, number, partner)
+
+    @pl.when(step == 0)
+    def _():
+        meet(line, ("z", "y", "x", "core"))
+        sources = ((d_in.at[:, y], d_a), (d_y, d_b), (o_in, o_a), (o_y, o_b), (gu_mine, gu_a), (gu_z, gu_b))
+        loads = [load(source, place, 7 + n) for n, (source, place) in enumerate(sources)]
+        for copy in loads:
+            copy.start()
+        for copy in load_tokens:
+            copy.start()
+        for copy in loads[:4]:
+            copy.wait()
+        for at in range(line):
+            d_a[at] = (d_a[at].astype(F32) + d_b[at].astype(F32)).astype(BF16)
+            o_a[at] = (o_a[at].astype(F32) + o_b[at].astype(F32)).astype(BF16)
+        for copy in d_sends + o_sends:
+            copy.start()
+        for copy in loads[4:]:
+            copy.wait()
+
+        def total(number, _):
+            for which, out in enumerate((g_out, u_out)):
+                value = gu_a[number, which].astype(F32)
+                for jump in range(line - 1):
+                    value = value + gu_b[jump, number, which].astype(F32)
+                at = pl.ds(pl.multiple_of((core * blocks + number) * 128, 128), 128)
+                out[:, at] = value
+                gu_a[number, which] = value.astype(BF16)
+            return 0
+
+        lax.fori_loop(0, blocks, total, 0)
+        gu_sides[0].start()
+        normed_t[...] = normed_ref[...].T
+        acc[...] = jnp.zeros_like(acc)
+
+    def own_part(back):
+        @pl.when(turn == 0)
+        def _():
+            value = 0.5 * back[0].astype(F32)
+            rows = value.T
+            first_stage[:, columns] = rows[:tok]
+            first_send[:, columns] = rows[tok:].astype(BF16)
+            grad[...] = value.astype(BF16)
+
+        @pl.when(turn > 0)
+        def _():
+            grad[...] = back[0]
+
+    @pl.when(target == 0)
+    def _():
+        own_part(back_other)
+
+    @pl.when(target == 1)
+    def _():
+        own_part(back_own)
+
+    @pl.when(step == 0)
+    def _():
+        first_part(0).start()
+
+    @pl.when(step == 3)
+    def _():
+        first_part(1).start()
+        store_first.start()
+
+    @pl.when(target < 2)
+    def _():
+        value = grad[...]
+        result = nt(normed_t[...], value)
+
+        @pl.when(target == 0)
+        def _():
+            sent[turn] = result.astype(BF16).reshape(sent.shape[1:])
+            core_send(turn).start()
+
+        @pl.when(target == 1)
+        def _():
+            core_send(turn).wait()
+            theirs = landed[turn].reshape(result.shape).astype(F32)
+            landed[turn] = (result + theirs).astype(BF16).reshape(landed.shape[1:])
+            y_send(turn).start()
+
+        acc[...] += nt(value.T, full_ref[0, 0])
+
+    @pl.when(step == 6)
+    def _():
+        for copy in load_tokens:
+            copy.wait()
+        weight = gains_ref[0:1, :]
+        chunk = min(128, tok)
+        gain[...] = jnp.zeros_like(gain)
+        gain[0, 1:2, :] = mlp_gain_ref[0:1, :]
+        for slot in (1, 0):
+
+            def finish(number, _, slot=slot):
+                local = pl.ds(pl.multiple_of(number * chunk, chunk), chunk)
+                some = pl.ds(pl.multiple_of(slot * tok + number * chunk, chunk), chunk)
+                values = xs[some, :].astype(F32)
+                scale = lax.rsqrt(jnp.mean(values * values, axis=1, keepdims=True) + epsilon)
+                value = acc[some, :]
+                gain[0, 0:1, :] += jnp.sum(value * values * scale, axis=0, keepdims=True)
+                weighted = value * weight
+                inner = jnp.mean(weighted * values, axis=1, keepdims=True)
+                result = (
+                    scale * weighted
+                    - values * (scale * scale * scale) * inner
+                    + grad_middle[some, :]
+                )
+                if slot == 0:
+                    acc[some, :] = result
+                else:
+                    input_send[local, :] = result.astype(BF16)
+                return 0
+
+            lax.fori_loop(0, tok // chunk, finish, 0)
+            if slot == 1:
+                input_part.start()
+        gain_send(0, to_core_partner()).start()
+        store_input.start()
+        gu_sides[0].wait()
+
+        def gather_x(number, _):
+            for which, out in enumerate((g_out, u_out)):
+                at = pl.ds(pl.multiple_of((core * blocks + number) * 128, 128), 128)
+                value = out[:, at] + gu_x[number, which].astype(F32)
+                out[:, at] = value
+                gu_a[number, which] = value.astype(BF16)
+            return 0
+
+        lax.fori_loop(0, blocks, gather_x, 0)
+        gu_sides[1].start()
+        gain_send(0, to_core_partner()).wait()
+        gain[1] = gain[0] + gain_landed[0]
+        gain_send(1, to_y_partner()).start()
+        for number in range(3):
+            y_send(number).wait()
+
+            def add(at, _, number=number):
+                value = landed[number, at, y].astype(F32) + y_landed[number, at].astype(F32)
+                landed[number, at, y] = value.astype(BF16)
+                return 0
+
+            lax.fori_loop(0, line, add, 0)
+            for copy in z_sends(number):
+                copy.start()
+            if number == 0:
+                gain_send(1, to_y_partner()).wait()
+                gain[2] = gain[1] + gain_landed[1]
+                for jump in range(1, line):
+                    gain_z(jump, line, gain, gain_landed, gain_sems).start()
+        for copy in d_sends + o_sends:
+            copy.wait()
+
+        def sum_z(own, places):
+            value = own.astype(F32)
+            for place in places:
+                value = value + place.astype(F32)
+            return value
+
+        value = sum_z(d_a[z], [d_landed[jump] for jump in range(line - 1)])
+        d_out[:, mine] = value
+        d_low[...] = value.astype(BF16)
+        d_sides[0].start()
+        value = sum_z(o_a[z], [o_landed[jump] for jump in range(line - 1)])
+        o_out[:, mine] = value
+        s_low[0] = value.astype(BF16)
+        square_x(0).start()
+        for jump in range(1, line):
+            gain_z(jump, line, gain, gain_landed, gain_sems).wait()
+        value = gain[2]
+        for jump in range(1, line):
+            value = value + gain_landed[1 + jump]
+        gain[3] = value
+        last_gain = send(gain.at[3], gain_landed.at[line + 1], gain_sems, line + 1, to_x_partner())
+        last_gain.start()
+        for number in range(3):
+            for copy in z_sends(number):
+                copy.wait()
+            value = sum_z(
+                landed[number, z, y], [z_landed[number, jump] for jump in range(line - 1)]
+            )
+            squares[1 + number][:, mine] = value
+            s_low[1 + number] = value.astype(BF16)
+            square_x(1 + number).start()
+        last_gain.wait()
+        gain[4] = gain[3] + gain_landed[line + 1]
+        gain_out[...] = gain[4, :, pl.ds(pl.multiple_of((2 * z + y) * 128, 128), 128)]
+        store_first.wait()
+        for number in range(2):
+            first_part(number).wait()
+        first_stage[...] = first_landed[...].astype(F32)
+        store_first_other.start()
+        d_sides[0].wait()
+        value = d_out[:, mine] + d_x[...].astype(F32)
+        d_out[:, mine] = value
+        d_low[...] = value.astype(BF16)
+        d_sides[1].start()
+        input_part.wait()
+        acc[pl.ds(tok, tok), :] = input_landed[...].astype(F32)
+        store_input_other.start()
+        for number in range(4):
+            square_x(number).wait()
+            value = squares[number][:, mine] + s_x[number].astype(F32)
+            squares[number][:, mine] = value
+            s_low[number] = value.astype(BF16)
+            square_core(number).start()
+        gu_sides[1].wait()
+
+        def gather_core(number, _):
+            for which, out in enumerate((g_out, u_out)):
+                at = pl.ds(pl.multiple_of(((1 - core) * blocks + number) * 128, 128), 128)
+                out[:, at] = gu_c[number, which].astype(F32)
+            return 0
+
+        lax.fori_loop(0, blocks, gather_core, 0)
+        d_sides[1].wait()
+        d_out[:, others] = d_c[...].astype(F32)
+        for number in range(4):
+            square_core(number).wait()
+            squares[number][:, others] = s_c[number].astype(F32)
+        store_input.wait()
+        store_input_other.wait()
+        store_first_other.wait()
+
+
+def gain_z(jump, line, gain, gain_landed, gain_sems):
+    return send(
+        gain.at[2], gain_landed.at[1 + jump], gain_sems, 1 + jump, to_z_partner(line, jump)
+    )
+
+
+def tail_carry(
+    inputs,
+    x_received,
+    back_other,
+    back_own,
+    full,
+    normed,
+    grad_middle,
+    gains,
+    mlp_gain,
+    gu_mine,
+    gu_z,
+    d,
+    d_y,
+    o,
+    o_y,
+    line,
+):
+    slots, tok, depth = inputs.shape
+    span = slots * tok
+    wide = depth // 2
+    blocks, _, rows, _ = gu_mine.shape
+    down_rows = d.shape[2]
+    once = pl.Buffered(1)
+    anywhere = pl.BlockSpec(memory_space=pl.ANY)
+
+    def half(s):
+        core = lax.axis_index("seq") % 2
+        return jnp.where(s < 3, 1 - core, core)
+
+    def kind(s):
+        return (s + 2) % 3
+
+    def clear(shape):
+        zeros = (0,) * len(shape)
+        return pl.BlockSpec(shape, lambda s: zeros, pipeline_mode=once)
+
+    square = jax.ShapeDtypeStruct((rows, depth), F32)
+    broad = jax.ShapeDtypeStruct((rows, 2 * blocks * 128), F32)
+    tall = jax.ShapeDtypeStruct((down_rows, depth), F32)
+    tokens = jax.ShapeDtypeStruct((slots, tok, depth), F32)
+    finals = [square] * 4 + [broad] * 2 + [tall]
+    vmem = pltpu.VMEM
+    dma = pltpu.SemaphoreType.DMA
+    return pl.pallas_call(
+        functools.partial(tail_carry_kernel, line, tok, blocks),
+        grid=(7,),
+        in_specs=[
+            anywhere,
+            anywhere,
+            pl.BlockSpec((1, wide, span), lambda s: (kind(jnp.minimum(s, 2)), 0, 0)),
+            pl.BlockSpec((1, wide, span), lambda s: (kind(jnp.clip(s, 3, 5)), 0, 0)),
+            pl.BlockSpec(
+                (1, 1, depth, wide),
+                lambda s: (half(jnp.minimum(s, 5)), kind(jnp.minimum(s, 5)), 0, 0),
+            ),
+            clear((span, depth)),
+            anywhere,
+            clear((8, depth)),
+            clear((8, depth)),
+        ]
+        + [anywhere] * 6,
+        out_specs=[anywhere, anywhere, clear((8, 128))] + [clear(final.shape) for final in finals],
+        out_shape=[tokens, tokens, jax.ShapeDtypeStruct((8, 128), F32)] + finals,
+        scratch_shapes=[
+            vmem((span, depth), BF16),
+            vmem((span, depth), F32),
+            vmem((depth, span), BF16),
+            vmem((span, depth), F32),
+            vmem((wide, span), BF16),
+            vmem((3, line, 2, rows, wide), BF16),
+            vmem((3, line, 2, rows, wide), BF16),
+            vmem((3, line, rows, wide), BF16),
+            vmem((3, line - 1, rows, wide), BF16),
+            vmem((line, down_rows, wide), BF16),
+            vmem((line, down_rows, wide), BF16),
+            vmem((line - 1, down_rows, wide), BF16),
+            vmem((line, rows, wide), BF16),
+            vmem((line, rows, wide), BF16),
+            vmem((line - 1, rows, wide), BF16),
+            vmem((blocks, 2, rows, 128), BF16),
+            vmem((line - 1, blocks, 2, rows, 128), BF16),
+            vmem((blocks, 2, rows, 128), BF16),
+            vmem((blocks, 2, rows, 128), BF16),
+            vmem((down_rows, wide), BF16),
+            vmem((down_rows, wide), BF16),
+            vmem((down_rows, wide), BF16),
+            vmem((4, rows, wide), BF16),
+            vmem((4, rows, wide), BF16),
+            vmem((4, rows, wide), BF16),
+            vmem((tok, depth), F32),
+            vmem((tok, depth), BF16),
+            vmem((tok, depth), BF16),
+            vmem((tok, depth), BF16),
+            vmem((tok, depth), BF16),
+            vmem((5, 8, depth), F32),
+            vmem((line + 2, 8, depth), F32),
+            dma((13,)),
+            dma((2, 3)),
+            dma((2, 3)),
+            dma((2, 3 * (line - 1))),
+            dma((2, line - 1)),
+            dma((2, line - 1)),
+            dma((2, 6)),
+            dma((2, 6)),
+            dma((2, 3)),
+            dma((2, line + 2)),
+        ],
+        compiler_params=pltpu.CompilerParams(
+            dimension_semantics=("arbitrary",),
+            vmem_limit_bytes=63 * MIB,
+            collective_id=6,
+            has_side_effects=True,
+        ),
+        cost_estimate=pl.CostEstimate(
+            flops=12 * span * depth * depth,
+            bytes_accessed=24 * span * depth + 12 * depth * depth,
+            transcendentals=0,
+        ),
+        name="tail_carry",
+    )(
+        inputs,
+        x_received,
+        back_other,
+        back_own,
+        full,
+        normed,
+        grad_middle,
+        gains,
+        mlp_gain,
+        gu_mine,
+        gu_z,
+        d,
+        d_y,
+        o,
+        o_y,
     )
 
 
@@ -2324,7 +2841,8 @@
         for weight in (gate_weight, up_weight, output_weight, down_weight)
     )
 
-    if (slots, count) == (2, 2):
+    whole_lanes = (slots, count) == (2, 2) and (D // parts) % 128 == 0
+    if whole_lanes:
         parts_of = lambda ref: [ref.reshape(-1, ref.shape[-1])]
         (q_half,), (k_half,), (v_half,) = (
             split(weight)[:1] for weight in (query_weight, key_weight, value_weight)
@@ -2401,7 +2919,7 @@
     middle, normed2, out_full = output_projection(
         inputs, tokens, out_own, out_other, att_other, att_own, gains_full, layout
     )
-    if (slots, count) == (2, 2):
+    if whole_lanes:
         (
             outputs,
             outputs_sent,
@@ -2453,16 +2971,34 @@
             line,
         )
         outputs = land(outputs, outputs_received, (1 - side)[None])
-        gate_up_grad = gu_mine.astype(F32)
-        for jump in range(line - 1):
-            gate_up_grad = gate_up_grad + gu_z[jump].astype(F32)
-        gate_up_grad = along_x_and_core(gate_up_grad)
-        down_grad = along_z_and_on(
-            lambda index: pick(pick(down_reduced, y, 1), index, 0).astype(F32)
-            + pick(down_y, index, 0).astype(F32)
-        )
-        output_grad = along_z_and_on(
-            lambda index: pick(out_mine, index, 0).astype(F32) + pick(out_y, index, 0).astype(F32)
+        (
+            input_grad,
+            first_grad,
+            gain_grads,
+            query_grad,
+            key_grad,
+            value_grad,
+            output_grad,
+            gate_grad,
+            up_grad,
+            down_grad,
+        ) = tail_carry(
+            inputs,
+            tokens[0],
+            back_other,
+            back_own,
+            qkv_full,
+            normed,
+            grad_middle,
+            gains_full,
+            mlp_gain_grad,
+            gu_mine,
+            gu_z,
+            down_reduced,
+            down_y,
+            out_mine,
+            out_y,
+            line,
         )
     else:
         (
@@ -2486,35 +3022,40 @@
         back = attend_back(pieces, mixes, grad_heads, lse, full_cos, full_sin, order, slots)
         back_other, back_own = ranks_to_halves(exchange_back(back), 1)
         outputs = to_home(outputs, outputs_sent)
-    input_grad, input_sent, first_grad, first_sent, gain_grads, qkv_sent, qkv_kept = tail(
-        inputs,
-        tokens,
-        back_other,
-        back_own,
-        qkv_full,
-        normed,
-        grad_middle,
-        gains_full,
-        mlp_gain_grad,
-        place,
-    )
-    qkv_grad = columns(*scatter(qkv_sent, qkv_kept, 1))
-    gate_up_grad = columns(*gate_up_grad)
-    gain_grads = everywhere(gain_grads)
-    gain_grads = lax.dynamic_slice_in_dim(gain_grads, shard * (D // parts), D // parts, 1)
+        input_grad, input_sent, first_grad, first_sent, gain_grads, qkv_sent, qkv_kept = tail(
+            inputs,
+            tokens,
+            back_other,
+            back_own,
+            qkv_full,
+            normed,
+            grad_middle,
+            gains_full,
+            mlp_gain_grad,
+            place,
+        )
+        query_grad, key_grad, value_grad = columns(*scatter(qkv_sent, qkv_kept, 1))
+        gate_grad, up_grad = columns(*gate_up_grad)
+        output_grad = columns(*output_grad)
+        down_grad = columns(*down_grad)
+        gain_grads = everywhere(gain_grads)
+        gain_grads = lax.dynamic_slice_in_dim(gain_grads, shard * (D // parts), D // parts, 1)
+        input_grad = to_home(input_grad, input_sent)
+        first_grad = to_home(first_grad, first_sent)
+
     return (
         outputs,
-        to_home(input_grad, input_sent),
-        to_home(first_grad, first_sent),
+        input_grad,
+        first_grad,
         gain_grads[0],
         gain_grads[1],
-        qkv_grad[0],
-        qkv_grad[1],
-        qkv_grad[2],
-        columns(*output_grad),
-        gate_up_grad[0],
-        gate_up_grad[1],
-        columns(*down_grad),
+        query_grad,
+        key_grad,
+        value_grad,
+        output_grad,
+        gate_grad,
+        up_grad,
+        down_grad,
     )
 
 

time: 654 us -> 525 us (0.80)
  waiting for transfers between devices: 144 us -> 0 us
  Pallas kernels: 406 us -> 473 us
  starting transfers between devices: 45.6 us -> 0 us
  other arithmetic: 24.2 us -> 5.08 us
  local copies, waits for them, and re-layouts: 24.7 us -> 37.9 us
    ppermute x27 -> x0, waiting for transfers between devices: 144 us -> none  [the longest x14 78.6 us: along_fsdp(): return lax.ppermute(value, 'fsdp', [(i, partner(i)) for i in range(parts)])]
    pallas_call x1, Pallas kernels: 27.3 us -> 97.2 us  [tail_carry(): pl.pallas_call(functools.partial(tail_carry_kernel, line, tok, blocks), g...]
    ppermute x27 -> x0, starting transfers between devices: 45.6 us -> none  [the longest x14 25.9 us: along_fsdp(): return lax.ppermute(value, 'fsdp', [(i, partner(i)) for i in range(parts)])]
    convert_element_type x16 -> x0, other arithmetic: 17.9 us -> none  [the longest x12 15.4 us: low(): return value.astype(BF16)]
    unnamed x54 -> x63, local copies, waits for them, and re-layouts: 17.4 us -> 32.3 us
  transfers between devices with their start and end apart: 27 -> 0, of which waited for: 10 -> 0; matrix products, arithmetic and copies ran while one was open for 3% -> 0% of each run, Pallas kernels for 0% -> 0%
where the time goes in v5:
time: 525 us; the launch traced here: 518 us
  Pallas kernels  473 us (90%)
  local copies, waits for them, and re-layouts  37.9 us (7%)
    pallas_call x1, Pallas kernels, mlp_carry(): pl.pallas_call(functools.partial(mlp_carry_kernel, line, tok, blocks), gr...  101 us
    pallas_call x1, Pallas kernels, attend_carry(): pl.pallas_call(functools.partial(attend_carry_kernel, line, tok, min(256,...  99.3 us
    pallas_call x1, Pallas kernels, tail_carry(): pl.pallas_call(functools.partial(tail_carry_kernel, line, tok, blocks), g...  97.2 us
    pallas_call x1, Pallas kernels, front(): pl.pallas_call(functools.partial(front_kernel, line, tok), grid=(6,), in_...  79.7 us
    pallas_call x1, Pallas kernels, attend_back_carry(): pl.pallas_call(functools.partial(attend_back_carry_kernel, line, tok, til...  77.8 us
    unnamed x63, local copies, waits for them, and re-layouts  32.3 us

profile of v5, /device:TPU:25, one launch (start us, length us, event | category | flops | bytes accessed | tf_op | source)
XLA Modules:
  0.0 517.6 jit_solution(2553248968604677235)
XLA Ops:
  0.7 1.7 constant_dynamic-slice_fusion.3
  4.8 1.2 multiply_sine_fusion.1
  6.0 1.7 constant_dynamic-slice_fusion.5
  7.7 79.7 %front.1 = (bf16[512,1024]{1,0:T(8,128)(2,1)}, bf16[512,1024]{1,0:T(8,128)(2,1)}, bf16[3,512,1024]{2,1,0:T(8,128)(2,1)}, bf16[3,512,1024]{2,1,0:T(8,128)(2,1)}, ...) custom-call(bf16[2,512,1024]{2,1,0:T(8,128)(2,1)} %refs_0_.7, ...), custom_call_target="tpu_custom_call" | custom-call | flops 6442450944 | bytes 29360128 | tf_op jit(solution)/shard_map/front/pallas_call | solution.py:1264
  87.5 99.3 %attend_carry.1 = (bf16[512,1024]{1,0:T(8,128)(2,1)S(1)}, bf16[512,1024]{1,0:T(8,128)(2,1)S(1)}, f32[4,8,2048]{2,1,0:T(8,128)S(1)}, bf16[512,1024]{1,0:T(8,128)(...) custom-call(bf16[3,512,1024]{2,1,0:T(8,128)(2,1)} %get-tuple-element, ...), custom_call_target="tpu_custom_call", output_to_operand_aliasing={{5}: (3, {})} | custom-call | flops 17179869184 | bytes 8388608 | tf_op jit(solution)/shard_map/attend_carry/pallas_call | solution.py:1454
  188.8 1.0 copy-done.12
  192.0 9.1 %output_projection.1 = (f32[1024,1024]{1,0:T(8,128)}, bf16[1024,1024]{1,0:T(8,128)(2,1)}, bf16[1024,1024]{1,0:T(8,128)(2,1)}) custom-call(s32[3]{0:T(128)} %pad_add_fusion.place, bf16[2,512,1024]{2,1,0:T(8,128)(2,1)} %refs_0_.7, bf16[512,1024]{1,0:T(8,128)(2,1)} %get-tuple-element.69.refs_1_, bf16[1024,512]{1,0:T(8,128)(2,1)} %bitcast.40, ...), custom_call_target="tpu_custom_call" | custom-call | flops 2147483648 | bytes 16777216 | tf_op jit(solution)/shard_map/output_projection/pallas_call | solution.py:499
  201.1 100.8 %mlp_carry.1 = (f32[2,512,1024]{2,1,0:T(8,128)}, bf16[512,1024]{1,0:T(8,128)(2,1)}, f32[1024,1024]{1,0:T(8,128)}, bf16[1024,1024]{1,0:T(8,128)(2,1)}, f32[8,1024...) custom-call(bf16[2,512,1024]{2,1,0:T(8,128)(2,1)} %refs_0_.6, ...), custom_call_target="tpu_custom_call" | custom-call | flops 47244640256 | bytes 55574528 | tf_op jit(solution)/shard_map/mlp_carry/pallas_call | solution.py:1703
  301.9 1.2 copy-done.9
  303.1 9.3 %grad_attended_carry.1 = (bf16[512,1024]{1,0:T(8,128)(2,1)S(1)}, bf16[512,1024]{1,0:T(8,128)(2,1)S(1)}, bf16[1024,512]{1,0:T(8,128)(2,1)S(1)}, bf16[1024,512]{1,0:T(8,128)(2,1)S(1)}) custom-call(bf16[1024,1024]{1,0:T(8,128)(2,1)} %get-tuple-element.85.low_ref, bf16[1024,1024]{1,0:T(8,128)(2,1)} %get-tuple-element.86.full_ref, ...), custom_call_target="tpu_custom_call" | custom-call | flops 4294967296 | bytes 10485760 | tf_op jit(solution)/shard_map/grad_attended_carry/pallas_call | solution.py:1838
  316.3 1.8 multiply_sine_fusion
  318.1 77.8 %attend_back_carry.1 = (bf16[3,512,1024]{2,1,0:T(8,128)(2,1)}, bf16[3,512,1024]{2,1,0:T(8,128)(2,1)}, bf16[512,1024]{1,0:T(8,128)(2,1)}, bf16[11,2,128,128]{3,2,...) custom-call(bf16[3,512,1024]{2,1,0:T(8,128)(2,1)} %get-tuple-element, ...), custom_call_target="tpu_custom_call" | custom-call | flops 42949672960 | bytes 16777216 | tf_op jit(solution)/shard_map/attend_back_carry/pallas_call | solution.py:2056
  395.9 97.2 %tail_carry.1 = (f32[2,512,1024]{2,1,0:T(8,128)}, f32[2,512,1024]{2,1,0:T(8,128)}, f32[8,128]{1,0:T(8,128)}, f32[128,1024]{1,0:T(8,128)}, f32[128,1024]{1,0:T(8,...) custom-call(bf16[2,512,1024]{2,1,0:T(8,128)(2,1)} %refs_0_.7, ...), custom_call_target="tpu_custom_call" | custom-call | flops 12884901888 | bytes 37748736 | tf_op jit(solution)/shard_map/tail_carry/pallas_call | solution.py:2537
  493.1 1.3 slice_bitcast_fusion
  494.4 2.2 copy-done.2
  496.6 1.2 copy-done.4
  498.0 2.0 copy-done.3
  500.0 4.9 copy.42
  505.0 2.1 copy.43
  507.1 1.6 copy-done.15
  508.7 2.0 copy.44
  513.9 1.1 copy.49
  515.0 1.1 copy.50
  516.1 1.1 copy.51
  (62 shorter events, 13.9 us)
Async XLA Ops:
  0.6 3.3 copy-start
  7.7 79.7 %copy-start.24 = (bf16[128,2816]{1,0:T(8,128)(2,1)S(1)}, bf16[128,2816]{1,0:T(8,128)(2,1)}, u32[]{:S(2)}) copy-start(bf16[128,2816]{1,0:T(8,128)(2,1)} %param.22) | copy-start | bytes 2162692
  7.7 79.8 %copy-start.25 = (bf16[128,2816]{1,0:T(8,128)(2,1)S(1)}, bf16[128,2816]{1,0:T(8,128)(2,1)}, u32[]{:S(2)}) copy-start(bf16[128,2816]{1,0:T(8,128)(2,1)} %param.21) | copy-start | bytes 2162692
  186.8 1.0 copy-start.7
  187.8 1.0 copy-start.8
  188.8 1.0 copy-start.12
  189.8 1.0 copy-start.13
  301.9 1.2 copy-start.9
  312.4 1.0 copy-start.5
  313.4 1.0 copy-start.6
  314.4 1.0 copy-start.10
  494.4 2.2 copy-start.2
  496.6 1.2 copy-start.4
  498.0 2.0 copy-start.3
  500.0 4.9 copy-start.16
  505.0 3.7 copy-start.15
  508.7 2.0 copy-start.23
  508.7 2.8 copy-start.22
  508.7 3.6 copy-start.21
  510.7 2.4 copy-start.20
  510.7 3.2 copy-start.19
  511.5 3.5 copy-start.18
  513.9 2.2 copy-start.17
  513.9 3.3 copy-start.1
  (2 other events, 1.7 us)

commit v6 on v5

--- a/solution.py
+++ b/solution.py
@@ -1,4 +1,5 @@
 import functools
+import math
 
 import jax
 import jax.numpy as jnp
@@ -1011,29 +1012,33 @@
 
 
 class Gather:
-    def __init__(self, line, shard, own, other, sems, split=False):
+    def __init__(self, line, shard, own, other, sems, share=0, columns=None):
         self.line, self.shard, self.own, self.other = line, shard, own, other
         self.sems = sems
         z, y, x, _ = seats()
-        self.z, self.y = z, y
+        self.z, self.y, self.share = z, y, share
         rows = own.shape[2]
-        if split:
-            self.rows = pl.ds(pl.multiple_of(x * (rows // 2), rows // 2), rows // 2)
+        self.columns = slice(None) if columns is None else pl.ds(*columns)
+        if share:
+            step = math.gcd(share, rows)
+            self.rows = pl.ds(pl.multiple_of(x * share, step), rows - share)
+            self.given = pl.ds(pl.multiple_of(x * (rows - share), step), share)
+            self.taken = pl.ds(pl.multiple_of((1 - x) * (rows - share), step), share)
         else:
-            self.rows = pl.ds(0, rows)
+            self.rows = slice(None)
 
     def here(self):
         return pltpu.make_async_copy(
-            self.shard.at[self.rows, :],
-            self.own.at[self.z, self.y, self.rows, :],
-            self.sems.at[0, self.line + 2],
+            self.shard.at[self.rows, self.columns],
+            self.own.at[self.z, self.y, self.rows, self.columns],
+            self.sems.at[0, self.line + 3],
         )
 
     def along_z(self):
         return [
             send(
-                self.shard.at[self.rows, :],
-                self.own.at[self.z, self.y, self.rows, :],
+                self.shard.at[self.rows, self.columns],
+                self.own.at[self.z, self.y, self.rows, self.columns],
                 self.sems,
                 jump - 1,
                 to_z_partner(self.line, jump),
@@ -1042,15 +1047,25 @@
         ]
 
     def along_y(self):
-        part = self.own.at[:, self.y, self.rows, :]
+        part = self.own.at[:, self.y, self.rows, self.columns]
         return send(part, part, self.sems, self.line - 1, to_y_partner())
 
     def along_x(self):
-        part = self.own.at[:, :, self.rows, :]
+        part = self.own.at[:, :, self.given, self.columns]
         return send(part, part, self.sems, self.line, to_x_partner())
 
-    def along_core(self):
-        return send(self.own, self.other, self.sems, self.line + 1, to_core_partner())
+    def to_core(self, late):
+        if self.share:
+            at = (slice(None), slice(None), self.taken if late else self.rows, self.columns)
+        else:
+            at = (slice(None), 1 - self.y if late else self.y, slice(None), self.columns)
+        return send(
+            self.own.at[at],
+            self.other.at[at],
+            self.sems,
+            self.line + 1 + late,
+            to_core_partner(),
+        )
 
     def start_z(self):
         self.here().start()
@@ -1062,15 +1077,20 @@
         for copy in self.along_z():
             copy.wait()
 
+    def wait_core(self):
+        self.to_core(0).wait()
+        self.to_core(1).wait()
+
 
 def gather_sems(line):
-    return pltpu.SemaphoreType.DMA((2, line + 3))
+    return pltpu.SemaphoreType.DMA((2, line + 4))
 
 
 def front_kernel(line, tok, *refs):
     (
         inputs,
         firsts,
+        grads,
         q_shard,
         k_shard,
         v_shard,
@@ -1080,6 +1100,7 @@
         sin_ref,
         x_received,
         f_received,
+        g_received,
         heads_own,
         heads_received,
         normed_ref,
@@ -1117,9 +1138,13 @@
     ]
     query, key, value = gathers
     out = Gather(line, o_shard, o_own, o_other, o_sems)
-    down = Gather(line, d_shard, d_own, d_own, d_sems, split=True)
+    down = Gather(line, d_shard, d_own, d_own, d_sems, d_own.shape[2] // 2)
     swap_x = send(inputs.at[1 - side], x_received, swap_sems, 0, to_x_partner())
     swap_f = send(firsts.at[1 - side], f_received, swap_sems, 1, to_x_partner())
+    early = pl.ds(0, tok // 2)
+    swap_g = send(
+        grads.at[1 - side, early], g_received.at[early], swap_sems, 2, to_x_partner()
+    )
     load_x = pltpu.make_async_copy(inputs.at[side], xs.at[pl.ds(0, tok), :], local_sems.at[0])
     load_f = pltpu.make_async_copy(firsts.at[side], fs.at[pl.ds(0, tok), :], local_sems.at[1])
     more_x = pltpu.make_async_copy(x_received, xs.at[pl.ds(tok, tok), :], local_sems.at[2])
@@ -1154,28 +1179,23 @@
         query.start_z()
         query.wait_z()
         query.along_y().start()
+        query.to_core(0).start()
         key.start_z()
         key.wait_z()
         key.along_y().start()
+        key.to_core(0).start()
         value.start_z()
-        query.along_y().wait()
-        query.along_core().start()
         swap_x.wait()
         more_x.start()
         swap_f.start()
-        value.wait_z()
-        value.along_y().start()
-        out.start_z()
-        key.along_y().wait()
-        key.along_core().start()
-        load_x.wait()
-        more_x.wait()
-        value.along_y().wait()
-        value.along_core().start()
-        columns = v_own[:, :, :, wide:].reshape(depth, 128)
+        query.along_y().wait()
+        query.to_core(1).start()
+        columns = q_own[:, :, :, wide:].reshape(depth, 128)
         gains_ref[...] = columns.astype(F32).T[:8]
         gain = gains_ref[0:1, :]
         chunk = min(256, 2 * tok)
+        load_x.wait()
+        more_x.wait()
 
         def norm(number, _):
             at = pl.ds(pl.multiple_of(number * chunk, chunk), chunk)
@@ -1186,28 +1206,43 @@
 
         lax.fori_loop(0, 2 * tok // chunk, norm, 0)
 
+    @pl.when(step == 1)
+    def _():
+        value.wait_z()
+        value.along_y().start()
+        value.to_core(0).start()
+        out.start_z()
+        key.along_y().wait()
+        key.to_core(1).start()
+
     @pl.when(step == 2)
     def _():
+        swap_f.wait()
+        more_f.start()
+        swap_g.start()
         out.wait_z()
         out.along_y().start()
+        out.to_core(0).start()
         down.start_z()
-        swap_f.wait()
-        more_f.start()
+        value.along_y().wait()
+        value.to_core(1).start()
         load_f.wait()
         more_f.wait()
 
     @pl.when(step == 3)
     def _():
-        query.along_core().wait()
-        key.along_core().wait()
-        value.along_core().wait()
-        for save in saves:
+        query.wait_core()
+        key.wait_core()
+        for save in saves[:4]:
             save.start()
 
     @pl.when(step == 5)
     def _():
+        value.wait_core()
+        for save in saves[4:]:
+            save.start()
         out.along_y().wait()
-        out.along_core().start()
+        out.to_core(1).start()
 
     def project_one(halves, kind, mine):
         raw = nt(weight(halves, slice(0, wide)).T, normed_ref[...])
@@ -1250,11 +1285,12 @@
             heads(number).wait()
         for save in saves:
             save.wait()
-        out.along_core().wait()
+        out.wait_core()
         down.wait_z()
-
-
-def front(inputs, firsts, q, k, v, o, d, cosine, sine, line):
+        swap_g.wait()
+
+
+def front(inputs, firsts, grads, q, k, v, o, d, cosine, sine, line):
     slots, tok, depth = inputs.shape
     span = slots * tok
     wide = depth // 2
@@ -1264,8 +1300,9 @@
     return pl.pallas_call(
         functools.partial(front_kernel, line, tok),
         grid=(6,),
-        in_specs=[anywhere] * 7 + [whole_block((HALF, span))] * 2,
+        in_specs=[anywhere] * 8 + [whole_block((HALF, span))] * 2,
         out_specs=[
+            anywhere,
             anywhere,
             anywhere,
             pl.BlockSpec((1, wide, span), lambda s: (jnp.minimum(s, 2), 0, 0)),
@@ -1280,6 +1317,7 @@
         out_shape=[
             jax.ShapeDtypeStruct((tok, depth), BF16),
             jax.ShapeDtypeStruct((tok, depth), BF16),
+            jax.ShapeDtypeStruct((tok, depth), BF16),
             jax.ShapeDtypeStruct((3, wide, span), BF16),
             jax.ShapeDtypeStruct((3, wide, span), BF16),
             jax.ShapeDtypeStruct((span, depth), BF16),
@@ -1292,23 +1330,23 @@
         scratch_shapes=[
             pltpu.VMEM((span, depth), BF16),
             pltpu.VMEM((span, depth), BF16),
+            weights(q.shape[1]),
+            weights(q.shape[1]),
             weights(wide),
             weights(wide),
             weights(wide),
             weights(wide),
-            weights(v.shape[1]),
-            weights(v.shape[1]),
             pltpu.VMEM((3, wide, span), BF16),
         ]
         + [gather_sems(line)] * 5
         + [
-            pltpu.SemaphoreType.DMA((2, 2)),
+            pltpu.SemaphoreType.DMA((2, 3)),
             pltpu.SemaphoreType.DMA((2, 3)),
             pltpu.SemaphoreType.DMA((10,)),
         ],
         compiler_params=pltpu.CompilerParams(
             dimension_semantics=("arbitrary",),
-            vmem_limit_bytes=56 * MIB,
+            vmem_limit_bytes=63 * MIB,
             collective_id=1,
             has_side_effects=True,
         ),
@@ -1318,7 +1356,7 @@
             transcendentals=0,
         ),
         name="front",
-    )(inputs, firsts, q, k, v, o, d, cosine, sine)
+    )(inputs, firsts, grads, q, k, v, o, d, cosine, sine)
 
 
 def block_of(source, slot, tok):
@@ -1332,13 +1370,22 @@
     (
         received,
         own,
+        inputs,
+        x_received,
+        gains_ref,
+        o_own,
+        o_other,
         grad_in,
+        _,
         d_in,
         g_shard,
         u_shard,
         mix_received,
         mix_own,
         lse_ref,
+        middle_ref,
+        normed_ref,
+        full_ref,
         att_other,
         grad_received,
         d_own,
@@ -1352,25 +1399,50 @@
         vt,
         ot,
         outgoing,
+        att_mine,
+        att_theirs,
+        xs,
         d_sems,
         g_sems,
         u_sems,
+        v_sems,
         swap_sems,
         att_sems,
+        local_sems,
     ) = refs
     step = pl.program_id(0)
     pairs = pl.num_programs(0)
-    _, _, side, _ = seats()
-    down = Gather(line, d_in, d_own, d_other, d_sems, split=True)
-    gate = Gather(line, g_shard, g_own, g_other, g_sems, split=True)
-    up = Gather(line, u_shard, u_own, u_other, u_sems)
-    swap = send(grad_in.at[1 - side], grad_received, swap_sems, 0, to_x_partner())
+    _, _, side, core = seats()
+    rows, columns = g_own.shape[2:]
+    first = columns // 256 * 128
+    down = Gather(line, d_in, d_own, d_other, d_sems, d_own.shape[2] // 2)
+    gate = Gather(line, g_shard, g_own, g_other, g_sems, rows * 3 // 8)
+    up = Gather(line, u_shard, u_own, u_other, u_sems, columns=(0, first))
+    up_more = Gather(line, u_shard, u_own, u_other, v_sems, columns=(first, columns - first))
+    late = pl.ds(tok // 2, tok - tok // 2)
+    swap = send(grad_in.at[1 - side, late], grad_received.at[late], swap_sems, 0, to_x_partner())
+    depth = xs.shape[1]
+    wide = depth // 2
+    mine = pl.ds(pl.multiple_of(core * wide, wide), wide)
+    others = pl.ds(pl.multiple_of((1 - core) * wide, wide), wide)
+    loads = [
+        pltpu.make_async_copy(source, place, local_sems.at[number])
+        for number, (source, place) in enumerate(
+            (
+                (inputs.at[side], xs.at[pl.ds(0, tok), :]),
+                (x_received, xs.at[pl.ds(tok, tok), :]),
+                (o_own, full_ref.at[:, mine]),
+                (o_other, full_ref.at[:, others]),
+            )
+        )
+    ]
+    save_att = pltpu.make_async_copy(att_theirs, att_other, local_sems.at[4])
     pieces = (received, own)
 
     def hand_over(number):
         rows = pl.ds(number * PAIR, PAIR)
         return send(
-            outgoing.at[rows, :], att_other.at[rows, :], att_sems, number, to_core_partner()
+            outgoing.at[rows, :], att_theirs.at[rows, :], att_sems, number, to_core_partner()
         )
 
     @pl.when(step == 0)
@@ -1382,14 +1454,14 @@
 
     @pl.when(step == 2)
     def _():
+        down.along_y().wait()
+        down.along_x().start()
+        down.to_core(0).start()
         gate.wait_z()
         gate.along_y().start()
         up.start_z()
-
-    @pl.when(step == 3)
-    def _():
-        down.along_y().wait()
-        down.along_x().start()
+        for load in loads:
+            load.start()
 
     for source in range(2):
         for slot in range(2):
@@ -1411,7 +1483,14 @@
             def _(number=number, theirs=theirs, take=take):
                 outgoing[number * PAIR : (number + 1) * PAIR, take] = theirs
 
-        mix_own[:, take] = ot[:, block_of(1, slot, tok)]
+        ours = ot[:, block_of(1, slot, tok)]
+        mix_own[:, take] = ours
+        for number in range(4):
+
+            @pl.when(step == number)
+            def _(number=number, ours=ours, take=take):
+                att_mine[number * PAIR : (number + 1) * PAIR, take] = ours
+
     for number in range(4):
 
         @pl.when(step == number)
@@ -1420,25 +1499,46 @@
 
     @pl.when(step == pairs - 1)
     def _():
-        gate.along_y().wait()
         up.wait_z()
         up.along_y().start()
+        up.to_core(0).start()
+        up_more.start_z()
+        gate.along_y().wait()
+        gate.to_core(0).start()
         down.along_x().wait()
-        swap.wait()
         gate.along_x().start()
-        down.along_core().start()
-        up.along_y().wait()
-        up.along_core().start()
-        gate.along_x().wait()
-        gate.along_core().start()
+        down.to_core(1).start()
+        up_more.wait_z()
+        up_more.along_y().start()
+        up_more.to_core(0).start()
         for number in range(4):
             hand_over(number).wait()
-        down.along_core().wait()
-        up.along_core().wait()
-        gate.along_core().wait()
-
-
-def attend_carry(received, own, grads, d_own, gate, up, line):
+        save_att.start()
+        for load in loads:
+            load.wait()
+        for slot in range(2):
+            take = slice(slot * tok, (slot + 1) * tok)
+            total = dot(att_mine[:, take].T, full_ref[mine, :])
+            total = total + dot(att_theirs[:, take].T, full_ref[others, :])
+            middle = xs[take, :].astype(F32) + total
+            middle_ref[take, :] = middle
+            scale = lax.rsqrt(jnp.mean(middle * middle, axis=1, keepdims=True) + epsilon)
+            normed_ref[take, :] = (middle * scale * gains_ref[1:2, :]).astype(BF16)
+        up.along_y().wait()
+        up.to_core(1).start()
+        up_more.along_y().wait()
+        up_more.to_core(1).start()
+        gate.along_x().wait()
+        gate.to_core(1).start()
+        swap.wait()
+        for gather in (down, up, up_more, gate):
+            gather.wait_core()
+        save_att.wait()
+
+
+def attend_carry(
+    received, own, inputs, x_received, gains, o_own, o_other, grads, g_received, d_own, gate, up, line
+):
     _, width, span = own.shape
     tok = span // 2
     length = 2 * span
@@ -1454,13 +1554,23 @@
     return pl.pallas_call(
         functools.partial(attend_carry_kernel, line, tok, min(256, length)),
         grid=(pairs,),
-        in_specs=[triple, triple] + [anywhere] * 4,
+        in_specs=[triple, triple]
+        + [anywhere] * 2
+        + [whole_block((8, depth))]
+        + [anywhere] * 7,
         out_specs=[single, single, pl.BlockSpec((1, 8, length), lambda p: (p, 0, 0))]
+        + [
+            pl.BlockSpec(shape, lambda p: (0, 0), pipeline_mode=pl.Buffered(1))
+            for shape in ((span, depth), (span, depth), (depth, depth))
+        ]
         + [anywhere] * 8,
         out_shape=[
             jax.ShapeDtypeStruct((width, span), BF16),
             jax.ShapeDtypeStruct((width, span), BF16),
             jax.ShapeDtypeStruct((pairs, 8, length), F32),
+            jax.ShapeDtypeStruct((span, depth), F32),
+            jax.ShapeDtypeStruct((span, depth), BF16),
+            jax.ShapeDtypeStruct((depth, depth), BF16),
             jax.ShapeDtypeStruct((width, span), BF16),
             jax.ShapeDtypeStruct((tok, depth), BF16),
             whole_down,
@@ -1476,13 +1586,20 @@
             pltpu.VMEM((PAIR, length), BF16),
             pltpu.VMEM((PAIR, length), BF16),
             pltpu.VMEM((width, span), BF16),
+            pltpu.VMEM((width, span), BF16),
+            pltpu.VMEM((width, span), BF16),
+            pltpu.VMEM((span, depth), BF16),
         ]
-        + [gather_sems(line)] * 3
-        + [pltpu.SemaphoreType.DMA((2, 1)), pltpu.SemaphoreType.DMA((2, 4))],
-        input_output_aliases={3: 5},
+        + [gather_sems(line)] * 4
+        + [
+            pltpu.SemaphoreType.DMA((2, 1)),
+            pltpu.SemaphoreType.DMA((2, 4)),
+            pltpu.SemaphoreType.DMA((5,)),
+        ],
+        input_output_aliases={8: 7, 9: 8},
         compiler_params=pltpu.CompilerParams(
             dimension_semantics=("arbitrary",),
-            vmem_limit_bytes=48 * MIB,
+            vmem_limit_bytes=63 * MIB,
             collective_id=2,
             has_side_effects=True,
         ),
@@ -1490,7 +1607,20 @@
             flops=area * 1024, bytes_accessed=8 * width * length, transcendentals=area
         ),
         name="attend_carry",
-    )(received, own, grads, d_own, gate, up)
+    )(
+        received,
+        own,
+        inputs,
+        x_received,
+        gains,
+        o_own,
+        o_other,
+        grads,
+        g_received,
+        d_own,
+        gate,
+        up,
+    )
 
 
 def mlp_carry_kernel(line, tok, blocks, *refs):
@@ -1863,7 +1993,7 @@
         ],
         compiler_params=pltpu.CompilerParams(
             dimension_semantics=("arbitrary",),
-            vmem_limit_bytes=48 * MIB,
+            vmem_limit_bytes=63 * MIB,
             collective_id=4,
             has_side_effects=True,
         ),
@@ -2095,7 +2225,7 @@
         ],
         compiler_params=pltpu.CompilerParams(
             dimension_semantics=("arbitrary",),
-            vmem_limit_bytes=60 * MIB,
+            vmem_limit_bytes=63 * MIB,
             collective_id=5,
             has_side_effects=True,
         ),
@@ -2126,7 +2256,9 @@
         o_in,
         o_y,
         input_grad,
+        input_landed,
         first_grad,
+        first_landed,
         gain_out,
         q_out,
         k_out,
@@ -2162,9 +2294,7 @@
         s_c,
         first_stage,
         first_send,
-        first_landed,
         input_send,
-        input_landed,
         gain,
         gain_landed,
         local_sems,
@@ -2196,10 +2326,8 @@
         load(x_received, xs.at[pl.ds(tok, tok), :], 1),
         load(grad_in, grad_middle, 2),
     ]
-    store_input = load(acc.at[pl.ds(0, tok), :], input_grad.at[side], 3)
-    store_input_other = load(acc.at[pl.ds(tok, tok), :], input_grad.at[1 - side], 4)
-    store_first = load(first_stage, first_grad.at[side], 5)
-    store_first_other = load(first_stage, first_grad.at[1 - side], 6)
+    store_input = load(acc.at[pl.ds(0, tok), :], input_grad, 3)
+    store_first = load(first_stage, first_grad, 4)
 
     def along_z(source, place, sems, base=0):
         return [
@@ -2449,16 +2577,12 @@
         store_first.wait()
         for number in range(2):
             first_part(number).wait()
-        first_stage[...] = first_landed[...].astype(F32)
-        store_first_other.start()
         d_sides[0].wait()
         value = d_out[:, mine] + d_x[...].astype(F32)
         d_out[:, mine] = value
         d_low[...] = value.astype(BF16)
         d_sides[1].start()
         input_part.wait()
-        acc[pl.ds(tok, tok), :] = input_landed[...].astype(F32)
-        store_input_other.start()
         for number in range(4):
             square_x(number).wait()
             value = squares[number][:, mine] + s_x[number].astype(F32)
@@ -2480,8 +2604,6 @@
             square_core(number).wait()
             squares[number][:, others] = s_c[number].astype(F32)
         store_input.wait()
-        store_input_other.wait()
-        store_first_other.wait()
 
 
 def gain_z(jump, line, gain, gain_landed, gain_sems):
@@ -2530,7 +2652,7 @@
     square = jax.ShapeDtypeStruct((rows, depth), F32)
     broad = jax.ShapeDtypeStruct((rows, 2 * blocks * 128), F32)
     tall = jax.ShapeDtypeStruct((down_rows, depth), F32)
-    tokens = jax.ShapeDtypeStruct((slots, tok, depth), F32)
+    tokens = [jax.ShapeDtypeStruct((tok, depth), dtype) for dtype in (F32, BF16)] * 2
     finals = [square] * 4 + [broad] * 2 + [tall]
     vmem = pltpu.VMEM
     dma = pltpu.SemaphoreType.DMA
@@ -2552,8 +2674,8 @@
             clear((8, depth)),
         ]
         + [anywhere] * 6,
-        out_specs=[anywhere, anywhere, clear((8, 128))] + [clear(final.shape) for final in finals],
-        out_shape=[tokens, tokens, jax.ShapeDtypeStruct((8, 128), F32)] + finals,
+        out_specs=[anywhere] * 4 + [clear((8, 128))] + [clear(final.shape) for final in finals],
+        out_shape=tokens + [jax.ShapeDtypeStruct((8, 128), F32)] + finals,
         scratch_shapes=[
             vmem((span, depth), BF16),
             vmem((span, depth), F32),
@@ -2581,8 +2703,6 @@
             vmem((4, rows, wide), BF16),
             vmem((4, rows, wide), BF16),
             vmem((tok, depth), F32),
-            vmem((tok, depth), BF16),
-            vmem((tok, depth), BF16),
             vmem((tok, depth), BF16),
             vmem((tok, depth), BF16),
             vmem((5, 8, depth), F32),
@@ -2629,6 +2749,46 @@
     )
 
 
+def finish_kernel(place, *refs):
+    count = (len(refs) - 2 * 3 - 3) // 2
+    tokens, plain = refs[:6], refs[6 : 6 + count]
+    outs = refs[6 + count :]
+    side = place[0]
+    for number in range(3):
+        outs[number][side] = tokens[2 * number][...].reshape(tokens[2 * number + 1].shape)
+        outs[number][1 - side] = tokens[2 * number + 1][...].astype(F32)
+    for number in range(count):
+        outs[3 + number][...] = plain[number][...]
+
+
+def finish(outputs, tokens, plain, side):
+    _, tok, depth = outputs[0].shape
+    steps = 4
+    tile = tok // steps
+    row = pl.BlockSpec((tile, depth), lambda s, p: (s, 0))
+    tiles = [
+        pl.BlockSpec((value.shape[0] // steps, value.shape[1]), lambda s, p: (s, 0))
+        for value in plain
+    ]
+    grid_spec = pltpu.PrefetchScalarGridSpec(
+        num_scalar_prefetch=1,
+        grid=(steps,),
+        in_specs=[pl.BlockSpec((1, tile, depth), lambda s, p: (p[0], s, 0))] + [row] * 5 + tiles,
+        out_specs=[pl.BlockSpec((2, tile, depth), lambda s, p: (0, s, 0))] * 3 + tiles,
+    )
+    return pl.pallas_call(
+        finish_kernel,
+        out_shape=[jax.ShapeDtypeStruct((2, tok, depth), F32)] * 3
+        + [jax.ShapeDtypeStruct(value.shape, value.dtype) for value in plain],
+        grid_spec=grid_spec,
+        compiler_params=parameters(60),
+        cost_estimate=pl.CostEstimate(
+            flops=tok * depth, bytes_accessed=60 * tok * depth, transcendentals=0
+        ),
+        name="finish",
+    )(side, *outputs, *tokens, *plain)
+
+
 def shards(
     inputs,
     first_values,
@@ -2849,7 +3009,8 @@
         )
         (
             tokens,
-            firsts,
+            _,
+            grads_early,
             heads_own,
             heads_received,
             normed,
@@ -2861,9 +3022,10 @@
         ) = front(
             inputs,
             first_values,
-            q_half[0],
+            out_grad,
+            jnp.concatenate([q_half[0], gains], axis=1),
             k_half[0],
-            jnp.concatenate([v_half[0], gains], axis=1),
+            v_half[0],
             out_halves[0],
             down_halves[0],
             cosine,
@@ -2877,6 +3039,9 @@
             mix_received,
             att_own,
             lse,
+            middle,
+            normed2,
+            out_full,
             att_other,
             grads,
             down_own,
@@ -2886,12 +3051,22 @@
             up_own,
             up_other,
         ) = attend_carry(
-            heads_received, heads_own, out_grad, down_own, gate_halves[0], up_halves[0], line
+            heads_received,
+            heads_own,
+            inputs,
+            tokens[0],
+            gains_full,
+            out_own.reshape(D, wide),
+            out_other.reshape(D, wide),
+            out_grad,
+            grads_early,
+            down_own,
+            gate_halves[0],
+            up_halves[0],
+            line,
         )
         mixes = [mix_received, att_own]
         grads = [grads]
-        layout = jnp.stack([side, core, 0 * core]).astype(jnp.int32)
-        out_own, out_other = parts_of(out_own), parts_of(out_other)
         gate_pieces = parts_of(gate_own), parts_of(gate_other)
         up_pieces = parts_of(up_own), parts_of(up_other)
         down_pieces = parts_of(down_own), parts_of(down_other)
@@ -2900,7 +3075,6 @@
             jnp.concatenate(half + [gains], axis=1)
             for half in split(query_weight, key_weight, value_weight)
         ]
-        layout = place
         tokens = to_sequence(inputs)
         firsts = to_sequence(first_values)
         grads = to_sequence(out_grad)
@@ -2915,10 +3089,10 @@
         pieces = exchange(halves_to_ranks(heads_other, heads_own, 1))
         mixes, lse = attend(pieces, order, slots)
         att_other, att_own = ranks_to_halves(exchange_back(mixes), 0)
-
-    middle, normed2, out_full = output_projection(
-        inputs, tokens, out_own, out_other, att_other, att_own, gains_full, layout
-    )
+        middle, normed2, out_full = output_projection(
+            inputs, tokens, out_own, out_other, att_other, att_own, gains_full, place
+        )
+
     if whole_lanes:
         (
             outputs,
@@ -2970,19 +3144,7 @@
             out_landed,
             line,
         )
-        outputs = land(outputs, outputs_received, (1 - side)[None])
-        (
-            input_grad,
-            first_grad,
-            gain_grads,
-            query_grad,
-            key_grad,
-            value_grad,
-            output_grad,
-            gate_grad,
-            up_grad,
-            down_grad,
-        ) = tail_carry(
+        input_own, input_received, first_own, first_received, *rest = tail_carry(
             inputs,
             tokens[0],
             back_other,
@@ -3000,6 +3162,14 @@
             out_y,
             line,
         )
+        gain_grads = rest[0]
+        outputs, input_grad, first_grad, *rest = finish(
+            (outputs,),
+            (outputs_received, input_own, input_received, first_own, first_received),
+            rest[1:],
+            side[None],
+        )
+        query_grad, key_grad, value_grad, output_grad, gate_grad, up_grad, down_grad = rest
     else:
         (
             outputs,
@@ -3011,7 +3181,7 @@
             gu_kept,
             down_sent,
             down_kept,
-        ) = mlp(out_grad, grads, middle, normed2, gains_full, gate_pieces, up_pieces, down_pieces, layout)
+        ) = mlp(out_grad, grads, middle, normed2, gains_full, gate_pieces, up_pieces, down_pieces, place)
         ga_other, ga_own, out_sent, out_kept = grad_attended(
             low_grad, out_full, att_other, att_own, place
         )

time: 525 us -> 478 us (0.910)
  local copies, waits for them, and re-layouts: 37.9 us -> 7.49 us
  Pallas kernels: 473 us -> 458 us
    unnamed x63 -> x7, local copies, waits for them, and re-layouts: 32.3 us -> 0.03 us
    pallas_call x1, Pallas kernels: 99.3 us -> 85.9 us  [attend_carry(): pl.pallas_call(functools.partial(attend_carry_kernel, line, tok, min(256,...]
    pallas_call x2 -> x1, Pallas kernels: 9.25 us -> 11.8 us  [finish(): pl.pallas_call(finish_kernel, out_shape=[jax.ShapeDtypeStruct((2, tok, de...]
where the time goes in v6:
time: 478 us; the launch traced here: 471 us
  Pallas kernels  458 us (96%)
  local copies, waits for them, and re-layouts  7.49 us (2%)
    pallas_call x1, Pallas kernels, mlp_carry(): pl.pallas_call(functools.partial(mlp_carry_kernel, line, tok, blocks), gr...  100 us
    pallas_call x1, Pallas kernels, tail_carry(): pl.pallas_call(functools.partial(tail_carry_kernel, line, tok, blocks), g...  96 us
    pallas_call x1, Pallas kernels, attend_carry(): pl.pallas_call(functools.partial(attend_carry_kernel, line, tok, min(256,...  85.9 us
    pallas_call x1, Pallas kernels, attend_back_carry(): pl.pallas_call(functools.partial(attend_back_carry_kernel, line, tok, til...  77.7 us
    pallas_call x1, Pallas kernels, front(): pl.pallas_call(functools.partial(front_kernel, line, tok), grid=(6,), in_...  75.2 us
    pallas_call x1, Pallas kernels, finish(): pl.pallas_call(finish_kernel, out_shape=[jax.ShapeDtypeStruct((2, tok, de...  11.8 us
    pallas_call x1, Pallas kernels, grad_attended_carry(): pl.pallas_call(functools.partial(grad_attended_carry_kernel, line), grid=...  11.1 us

profile of v6, /device:TPU:25, one launch (start us, length us, event | category | flops | bytes accessed | tf_op | source)
XLA Modules:
  0.0 470.8 jit_solution(16825675987682063712)
XLA Ops:
  0.6 0.0 copy-start
  0.7 1.7 constant_dynamic-slice_fusion.5
  2.4 0.7 pad_maximum_fusion
  3.1 0.1 copy.28
  3.2 0.7 fusion.1.refs_3_
  3.9 0.0 copy-done
  3.9 0.8 constant_dynamic-slice_fusion.2.refs_7_
  4.7 1.7 constant_dynamic-slice_fusion.3
  6.4 0.1 convert_bitcast_fusion
  6.4 1.2 multiply_sine_fusion.1
  7.7 0.0 copy-start.2
  7.7 75.2 %front.1 = (bf16[512,1024]{1,0:T(8,128)(2,1)}, bf16[512,1024]{1,0:T(8,128)(2,1)}, bf16[512,1024]{1,0:T(8,128)(2,1)}, bf16[3,512,1024]{2,1,0:T(8,128)(2,1)}, bf16...) custom-call(bf16[2,512,1024]{2,1,0:T(8,128)(2,1)} %refs_0_.5, ...), custom_call_target="tpu_custom_call" | custom-call | flops 6442450944 | bytes 29360128 | tf_op jit(solution)/shard_map/front/pallas_call | solution.py:1300
  82.9 0.0 copy-done.2
  82.9 1.9 constant_dynamic-slice_fusion
  84.8 85.9 %attend_carry.1 = (bf16[512,1024]{1,0:T(8,128)(2,1)}, bf16[512,1024]{1,0:T(8,128)(2,1)}, f32[4,8,2048]{2,1,0:T(8,128)}, f32[1024,1024]{1,0:T(8,128)}, bf16[1024,...) custom-call(bf16[3,512,1024]{2,1,0:T(8,128)(2,1)} %get-tuple-element, ...), custom_call_target="tpu_custom_call", output_to_operand_aliasing={{7}: (8, {}), {8}: (9, {})} | custom-call | flops 17179869184 | bytes 8388608 | tf_op jit(solution)/shard_map/attend_carry/pallas_call | solution.py:1554
  170.7 100.0 %mlp_carry.1 = (f32[2,512,1024]{2,1,0:T(8,128)}, bf16[512,1024]{1,0:T(8,128)(2,1)}, f32[1024,1024]{1,0:T(8,128)}, bf16[1024,1024]{1,0:T(8,128)(2,1)}, f32[8,1024...) custom-call(bf16[2,512,1024]{2,1,0:T(8,128)(2,1)} %refs_0_.4, ...), custom_call_target="tpu_custom_call" | custom-call | flops 47244640256 | bytes 55574528 | tf_op jit(solution)/shard_map/mlp_carry/pallas_call | solution.py:1833
  270.7 11.1 %grad_attended_carry.1 = (bf16[512,1024]{1,0:T(8,128)(2,1)}, bf16[512,1024]{1,0:T(8,128)(2,1)}, bf16[1024,512]{1,0:T(8,128)(2,1)}, bf16[1024,512]{1,0:T(8,128)(2,1)}) custom-call(bf16[1024,1024]{1,0:T(8,128)(2,1)} %get-tuple-element.98.low_ref, bf16[1024,1024]{1,0:T(8,128)(2,1)} %get-tuple-element.99.full_ref, ...), custom_call_target="tpu_custom_call" | custom-call | flops 4294967296 | bytes 10485760 | tf_op jit(solution)/shard_map/grad_attended_carry/pallas_call | solution.py:1968
  281.8 1.8 multiply_sine_fusion
  283.6 77.7 %attend_back_carry.1 = (bf16[3,512,1024]{2,1,0:T(8,128)(2,1)}, bf16[3,512,1024]{2,1,0:T(8,128)(2,1)}, bf16[512,1024]{1,0:T(8,128)(2,1)}, bf16[11,2,128,128]{3,2,...) custom-call(bf16[3,512,1024]{2,1,0:T(8,128)(2,1)} %get-tuple-element, ...), custom_call_target="tpu_custom_call" | custom-call | flops 42949672960 | bytes 16777216 | tf_op jit(solution)/shard_map/attend_back_carry/pallas_call | solution.py:2186
  361.3 96.0 %tail_carry.1 = (f32[512,1024]{1,0:T(8,128)}, bf16[512,1024]{1,0:T(8,128)(2,1)}, f32[512,1024]{1,0:T(8,128)}, bf16[512,1024]{1,0:T(8,128)(2,1)}, f32[8,128]{1,0:...) custom-call(bf16[2,512,1024]{2,1,0:T(8,128)(2,1)} %refs_0_.5, ...), custom_call_target="tpu_custom_call" | custom-call | flops 12884901888 | bytes 37748736 | tf_op jit(solution)/shard_map/tail_carry/pallas_call | solution.py:2659
  457.3 0.0 copy-start.1
  457.3 11.8 %finish.1 = (f32[2,512,1024]{2,1,0:T(8,128)}, f32[2,512,1024]{2,1,0:T(8,128)}, f32[2,512,1024]{2,1,0:T(8,128)}, f32[128,1024]{1,0:T(8,128)}, f32[128,1024]{1,0:T...) custom-call(s32[1]{0:T(128)} %bitcast.place, ...), custom_call_target="tpu_custom_call" | custom-call | flops 524288 | bytes 31457280 | tf_op jit(solution)/shard_map/finish/pallas_call | solution.py:2779
  469.1 1.3 slice_bitcast_fusion
  470.3 0.0 copy-done.1
  (4 shorter events, 0.0 us)
Async XLA Ops:
  0.6 3.3 copy-start
  7.7 75.2 %copy-start.2 = (bf16[128,2816]{1,0:T(8,128)(2,1)S(1)}, bf16[128,2816]{1,0:T(8,128)(2,1)}, u32[]{:S(2)}) copy-start(bf16[128,2816]{1,0:T(8,128)(2,1)} %param.22) | copy-start | bytes 2162692
  457.3 13.0 %copy-start.1 = (bf16[352,1024]{1,0:T(8,128)(2,1)S(1)}, bf16[352,1024]{1,0:T(8,128)(2,1)}, u32[]{:S(2)}) copy-start(bf16[352,1024]{1,0:T(8,128)(2,1)} %param.23) | copy-start | bytes 2162692

commit v7 on v6

--- a/solution.py
+++ b/solution.py
@@ -1015,10 +1015,15 @@
     def __init__(self, line, shard, own, other, sems, share=0, columns=None):
         self.line, self.shard, self.own, self.other = line, shard, own, other
         self.sems = sems
-        z, y, x, _ = seats()
+        z, y, x, core = seats()
         self.z, self.y, self.share = z, y, share
-        rows = own.shape[2]
-        self.columns = slice(None) if columns is None else pl.ds(*columns)
+        rows, width = own.shape[2:]
+        first, size = columns or (0, width)
+        self.columns = pl.ds(first, size)
+        if shard.shape[1] == width:
+            self.source = self.columns
+        else:
+            self.source = pl.ds(pl.multiple_of(core * width + first, 128), size)
         if share:
             step = math.gcd(share, rows)
             self.rows = pl.ds(pl.multiple_of(x * share, step), rows - share)
@@ -1029,7 +1034,7 @@
 
     def here(self):
         return pltpu.make_async_copy(
-            self.shard.at[self.rows, self.columns],
+            self.shard.at[self.rows, self.source],
             self.own.at[self.z, self.y, self.rows, self.columns],
             self.sems.at[0, self.line + 3],
         )
@@ -1037,7 +1042,7 @@
     def along_z(self):
         return [
             send(
-                self.shard.at[self.rows, self.columns],
+                self.shard.at[self.rows, self.source],
                 self.own.at[self.z, self.y, self.rows, self.columns],
                 self.sems,
                 jump - 1,
@@ -1096,6 +1101,7 @@
         v_shard,
         o_shard,
         d_shard,
+        gains_shard,
         cos_ref,
         sin_ref,
         x_received,
@@ -1118,11 +1124,14 @@
         v_own,
         v_other,
         outgoing,
+        all_gains,
         q_sems,
         k_sems,
         v_sems,
+        w_sems,
         o_sems,
         d_sems,
+        gain_sems,
         swap_sems,
         head_sems,
         local_sems,
@@ -1134,9 +1143,11 @@
     gathers = [
         Gather(line, q_shard, q_own, q_other, q_sems),
         Gather(line, k_shard, k_own, k_other, k_sems),
-        Gather(line, v_shard, v_own, v_other, v_sems),
+        Gather(line, v_shard, v_own, v_other, v_sems, columns=(0, wide // 2)),
+        Gather(line, v_shard, v_own, v_other, w_sems, columns=(wide // 2, wide // 2)),
     ]
-    query, key, value = gathers
+    query, key, value, value_more = gathers
+    gains = Gather(line, gains_shard, all_gains, all_gains, gain_sems)
     out = Gather(line, o_shard, o_own, o_other, o_sems)
     down = Gather(line, d_shard, d_own, d_own, d_sems, d_own.shape[2] // 2)
     swap_x = send(inputs.at[1 - side], x_received, swap_sems, 0, to_x_partner())
@@ -1176,7 +1187,10 @@
         swap_x.start()
         load_x.start()
         load_f.start()
+        gains.start_z()
         query.start_z()
+        gains.wait_z()
+        gains.along_y().start()
         query.wait_z()
         query.along_y().start()
         query.to_core(0).start()
@@ -1188,10 +1202,12 @@
         swap_x.wait()
         more_x.start()
         swap_f.start()
+        gains.along_y().wait()
         query.along_y().wait()
         query.to_core(1).start()
-        columns = q_own[:, :, :, wide:].reshape(depth, 128)
-        gains_ref[...] = columns.astype(F32).T[:8]
+        for number in range(2 * line):
+            columns = slice(number * 128, (number + 1) * 128)
+            gains_ref[:, columns] = all_gains[number // 2, number % 2]
         gain = gains_ref[0:1, :]
         chunk = min(256, 2 * tok)
         load_x.wait()
@@ -1205,27 +1221,33 @@
             return 0
 
         lax.fori_loop(0, 2 * tok // chunk, norm, 0)
-
-    @pl.when(step == 1)
-    def _():
         value.wait_z()
         value.along_y().start()
         value.to_core(0).start()
-        out.start_z()
+        value_more.start_z()
+
+    @pl.when(step == 1)
+    def _():
         key.along_y().wait()
         key.to_core(1).start()
+        value_more.wait_z()
+        value_more.along_y().start()
+        value_more.to_core(0).start()
+        out.start_z()
 
     @pl.when(step == 2)
     def _():
         swap_f.wait()
         more_f.start()
         swap_g.start()
+        value.along_y().wait()
+        value.to_core(1).start()
+        value_more.along_y().wait()
+        value_more.to_core(1).start()
         out.wait_z()
         out.along_y().start()
         out.to_core(0).start()
         down.start_z()
-        value.along_y().wait()
-        value.to_core(1).start()
         load_f.wait()
         more_f.wait()
 
@@ -1239,6 +1261,7 @@
     @pl.when(step == 5)
     def _():
         value.wait_core()
+        value_more.wait_core()
         for save in saves[4:]:
             save.start()
         out.along_y().wait()
@@ -1249,7 +1272,10 @@
         if kind < 2:
             parts = raw.reshape(wide // HEAD_DIM, 2, HALF, raw.shape[1])
             first, second = parts[:, 0], parts[:, 1]
-            cosine, sine = cos_ref[...][None], sin_ref[...][None]
+            cosine, sine = (
+                jnp.concatenate([ref[:, block_of(1, slot, tok)] for slot in range(2)], axis=1)[None]
+                for ref in (cos_ref, sin_ref)
+            )
             turned = jnp.stack(
                 [first * cosine - second * sine, first * sine + second * cosine], axis=1
             )
@@ -1290,7 +1316,7 @@
         swap_g.wait()
 
 
-def front(inputs, firsts, grads, q, k, v, o, d, cosine, sine, line):
+def front(inputs, firsts, grads, q, k, v, o, d, gains, cosine, sine, line):
     slots, tok, depth = inputs.shape
     span = slots * tok
     wide = depth // 2
@@ -1300,7 +1326,7 @@
     return pl.pallas_call(
         functools.partial(front_kernel, line, tok),
         grid=(6,),
-        in_specs=[anywhere] * 8 + [whole_block((HALF, span))] * 2,
+        in_specs=[anywhere] * 9 + [whole_block(cosine.shape)] * 2,
         out_specs=[
             anywhere,
             anywhere,
@@ -1330,15 +1356,16 @@
         scratch_shapes=[
             pltpu.VMEM((span, depth), BF16),
             pltpu.VMEM((span, depth), BF16),
-            weights(q.shape[1]),
-            weights(q.shape[1]),
+            weights(wide),
+            weights(wide),
             weights(wide),
             weights(wide),
             weights(wide),
             weights(wide),
             pltpu.VMEM((3, wide, span), BF16),
+            pltpu.VMEM((line, 2, 8, 128), F32),
         ]
-        + [gather_sems(line)] * 5
+        + [gather_sems(line)] * 7
         + [
             pltpu.SemaphoreType.DMA((2, 3)),
             pltpu.SemaphoreType.DMA((2, 3)),
@@ -1356,7 +1383,7 @@
             transcendentals=0,
         ),
         name="front",
-    )(inputs, firsts, grads, q, k, v, o, d, cosine, sine)
+    )(inputs, firsts, grads, q, k, v, o, d, gains, cosine, sine)
 
 
 def block_of(source, slot, tok):
@@ -1548,7 +1575,7 @@
     anywhere = pl.BlockSpec(memory_space=pl.ANY)
     triple = pl.BlockSpec((3, PAIR, span), lambda p: (0, p, 0))
     single = pl.BlockSpec((PAIR, span), lambda p: (p, 0))
-    whole_gate = jax.ShapeDtypeStruct((line, 2, rows, gate.shape[1]), BF16)
+    whole_gate = jax.ShapeDtypeStruct((line, 2, rows, gate.shape[1] // 2), BF16)
     whole_down = jax.ShapeDtypeStruct((line, 2, down_rows, d_own.shape[3]), BF16)
     area = pairs * 2 * length * length // 2
     return pl.pallas_call(
@@ -1623,6 +1650,9 @@
     )
 
 
+LATE = 2
+
+
 def mlp_carry_kernel(line, tok, blocks, *refs):
     (
         grads,
@@ -1646,6 +1676,7 @@
         gu_ref,
         d_ref,
         gu_y,
+        gu_late,
         og,
         normed_t,
         acc,
@@ -1694,6 +1725,11 @@
     def y_copy(number):
         return send(gu_outgoing.at[number], gu_y.at[number], y_sems, number, to_y_partner())
 
+    def leave(late):
+        return pltpu.make_async_copy(
+            gu_outgoing.at[blocks - LATE + late], gu_late.at[late], local_sems.at[2 + late]
+        )
+
     @pl.when(step == 0)
     def _():
         meet(line, ("y", "core"))
@@ -1721,26 +1757,49 @@
             down_full[at, mine] = pair[0][...]
             down_full[at, others] = pair[1][...]
         down_w = down_full[...]
-        normed = normed_ref[...]
-        gate = dot(normed, gate_w)
-        up = dot(normed, up_w)
-        grad_active = nt(og[...], down_w)
-        sigma = jax.nn.sigmoid(gate)
-        silu = gate * sigma
-        active = (silu * up).astype(BF16)
-        grad_up = (grad_active * silu).astype(BF16)
-        grad_gate = (grad_active * up * sigma * (1.0 + gate * (1.0 - sigma))).astype(BF16)
+        both_w = jnp.concatenate([gate_w, up_w], axis=1)
+        span = og.shape[0]
+        size = span // 2
+
+        def products(at):
+            both = dot(normed_ref[at, :], both_w)
+            return (both[:, : 2 * strip], both[:, 2 * strip :], nt(og[at, :], down_w))
+
+        def bend(gate, up, grad_active):
+            sigma = jax.nn.sigmoid(gate)
+            silu = gate * sigma
+            turned = grad_active * up * sigma * (1.0 + gate * (1.0 - sigma))
+            grad_both = jnp.concatenate([turned.astype(BF16), (grad_active * silu).astype(BF16)], axis=1)
+            return ((silu * up).astype(BF16), grad_both)
+
+        def spread(at, active, grad_both):
+            acc[at, :] += dot(active, down_w)
+            back[at, :] += nt(grad_both, both_w)
+
+        pieces = [slice(n * size, (n + 1) * size) for n in range(2)]
+        bent = []
+        ahead = products(pieces[0])
+        for number, at in enumerate(pieces):
+            now = ahead
+            if number + 1 < len(pieces):
+                ahead = products(pieces[number + 1])
+            bent.append(bend(*now))
+            if number:
+                spread(pieces[number - 1], *bent[number - 1])
+        spread(pieces[-1], *bent[-1])
+        active = jnp.concatenate([one for one, _ in bent], axis=0)
+        grad_both = jnp.concatenate([one for _, one in bent], axis=0)
 
         @pl.when(step >= 2)
         def _():
             for copy in core_copies(step - 2):
                 copy.wait_send()
 
-        for number, grad in enumerate((grad_gate, grad_up)):
-            result = dot(normed_t[...], grad).astype(BF16)
-            shaped = result.reshape(line, 2, rows, 2 * strip)
-            gu_kept[slot, number] = shaped[..., :strip]
-            gu_sent[slot, number] = shaped[..., strip:]
+        shaped = dot(normed_t[...], grad_both).astype(BF16).reshape(line, 2, rows, 4 * strip)
+        for number in range(2):
+            base = 2 * number * strip
+            gu_kept[slot, number] = shaped[..., base : base + strip]
+            gu_sent[slot, number] = shaped[..., base + strip : base + 2 * strip]
         active_t = active.T
         kept = dot(active_t, og[:, mine]).astype(BF16)
         d_kept[slot, core] = kept[:strip]
@@ -1750,8 +1809,6 @@
         d_sent[slot, 1 - core] = sent[strip:]
         for copy in core_copies(step):
             copy.start()
-        acc[...] += dot(active, down_w)
-        back[...] += nt(grad_gate, gate_w) + nt(grad_up, up_w)
 
     @pl.when(step > 0)
     def _():
@@ -1766,7 +1823,16 @@
             ours = gu_kept[slot, which, :, y].astype(F32)
             ours = ours + gu_landed[number, which, :, y].astype(F32)
             gu_ref[0, which] = ours.astype(BF16)
-        y_copy(number).start()
+        @pl.when(number < blocks - LATE)
+        def _():
+            y_copy(number).start()
+
+        for late in range(LATE):
+
+            @pl.when(number == blocks - LATE + late)
+            def _(late=late):
+                leave(late).start()
+
         d_ref[...] = (d_kept[slot].astype(F32) + d_landed[number].astype(F32)).astype(BF16)
 
     @pl.when(step == blocks)
@@ -1803,7 +1869,9 @@
         for number in (blocks - 2, blocks - 1):
             for copy in core_copies(number):
                 copy.wait_send()
-        for number in range(blocks):
+        for late in range(LATE):
+            leave(late).wait()
+        for number in range(blocks - LATE):
             y_copy(number).wait()
 
 
@@ -1847,6 +1915,7 @@
             pl.BlockSpec((1, 2, line, rows, 128), lambda s: (done(s), 0, 0, 0, 0)),
             pl.BlockSpec((2, 128, wide), lambda s: (0, done(s), 0)),
             anywhere,
+            anywhere,
         ],
         out_shape=[
             jax.ShapeDtypeStruct((slots, tok, depth), F32),
@@ -1856,7 +1925,8 @@
             jax.ShapeDtypeStruct((8, depth), F32),
             jax.ShapeDtypeStruct((blocks, 2, line, rows, 128), BF16),
             jax.ShapeDtypeStruct((2, half_width, wide), BF16),
-            jax.ShapeDtypeStruct((blocks, 2, line, rows, 128), BF16),
+            jax.ShapeDtypeStruct((blocks - LATE, 2, line, rows, 128), BF16),
+            jax.ShapeDtypeStruct((LATE, 2, line, rows, 128), BF16),
         ],
         scratch_shapes=[
             pltpu.VMEM((span, depth), BF16),
@@ -1871,12 +1941,12 @@
             pltpu.VMEM((blocks, 2, 128, wide), BF16),
             pltpu.VMEM((blocks, 2, line, rows, 128), BF16),
             pltpu.VMEM((256, depth), BF16),
-            pltpu.SemaphoreType.DMA((2,)),
+            pltpu.SemaphoreType.DMA((2 + LATE,)),
             pltpu.SemaphoreType.DMA((2,)),
             pltpu.SemaphoreType.DMA((blocks,)),
             pltpu.SemaphoreType.DMA((2,)),
             pltpu.SemaphoreType.DMA((blocks,)),
-            pltpu.SemaphoreType.DMA((2, blocks)),
+            pltpu.SemaphoreType.DMA((2, blocks - LATE)),
         ],
         compiler_params=pltpu.CompilerParams(
             dimension_semantics=("arbitrary",),
@@ -1993,7 +2063,7 @@
         ],
         compiler_params=pltpu.CompilerParams(
             dimension_semantics=("arbitrary",),
-            vmem_limit_bytes=63 * MIB,
+            vmem_limit_bytes=48 * MIB,
             collective_id=4,
             has_side_effects=True,
         ),
@@ -2020,6 +2090,7 @@
         outputs_sent,
         gu_in,
         gu_y,
+        gu_late,
         d_in,
         o_in,
         o_landed,
@@ -2028,10 +2099,11 @@
         outputs_received,
         gu_mine,
         gu_z,
+        d_kept,
         d_y,
         o_kept,
         o_y,
-    ) = refs[:23]
+    ) = refs[:25]
     (
         qz,
         gz,
@@ -2049,29 +2121,52 @@
         gu_b,
         o_a,
         o_b,
+        o_x,
+        d_a,
+        d_x,
         local_sems,
         back_sems,
         z_sems,
         other_sems,
-    ) = refs[23:]
+    ) = refs[25:]
     step = pl.program_id(0)
     pairs = pl.num_programs(0)
-    z, y, _, _ = seats()
+    z, y, x, _ = seats()
     length = 4 * tok
+    blocks = gu_a.shape[0]
+    o_half, d_half = o_x.shape[2], d_x.shape[2]
+    o_mine = pl.ds(pl.multiple_of(x * o_half, o_half), o_half)
+    o_theirs = pl.ds(pl.multiple_of((1 - x) * o_half, o_half), o_half)
+    d_mine = pl.ds(pl.multiple_of(x * d_half, d_half), d_half)
+    d_theirs = pl.ds(pl.multiple_of((1 - x) * d_half, d_half), d_half)
     swap = send(outputs_sent, outputs_received, other_sems, 0, to_x_partner())
-    d_send = send(d_in.at[:, 1 - y], d_y, other_sems, 1, to_y_partner())
-    o_send = send(o_a.at[:, 1 - y], o_y, other_sems, 2, to_y_partner())
-
-    def z_send(jump):
+    o_over = send(o_a.at[:, :, o_theirs, :], o_x, other_sems, 1, to_x_partner())
+    d_over = send(d_in.at[:, :, d_theirs, :], d_x, other_sems, 2, to_x_partner())
+    o_send = send(o_a.at[:, 1 - y, o_mine, :], o_y, other_sems, 3, to_y_partner())
+    d_send = send(d_a.at[:, 1 - y], d_y, other_sems, 4, to_y_partner())
+    late = pl.ds(blocks - LATE, LATE)
+    late_send = send(gu_late, gu_b.at[late], other_sems, 5, to_y_partner())
+
+    def z_send(jump, number):
         target = lax.rem(z + jump, line)
+        at = late if number else pl.ds(0, blocks - LATE)
         return send(
-            gu_a.at[:, :, target], gu_z.at[jump - 1], z_sems, jump - 1, to_z_partner(line, jump)
+            gu_a.at[at, :, target],
+            gu_z.at[jump - 1, at],
+            z_sems,
+            number * (line - 1) + jump - 1,
+            to_z_partner(line, jump),
         )
 
-    stays = [
-        pltpu.make_async_copy(gu_a.at[:, :, z], gu_mine, local_sems.at[4]),
-        pltpu.make_async_copy(o_a.at[:, y], o_kept, local_sems.at[5]),
-    ]
+    def add(number, _):
+        total = gu_a[number].astype(F32) + gu_b[number].astype(F32)
+        gu_a[number] = total.astype(BF16)
+        return 0
+
+    gu_stays = pltpu.make_async_copy(gu_a.at[:, :, z], gu_mine, local_sems.at[5])
+    o_stays = pltpu.make_async_copy(o_a.at[:, y, o_mine, :], o_kept, local_sems.at[6])
+    d_stays = pltpu.make_async_copy(d_a.at[:, y], d_kept, local_sems.at[7])
+    load_d = pltpu.make_async_copy(d_in.at[:, :, d_mine, :], d_a, local_sems.at[4])
 
     def hand_over(number):
         rows = pl.ds(number * PAIR, PAIR)
@@ -2086,33 +2181,57 @@
     @pl.when(step == 0)
     def _():
         meet(line, ("z", "y", "x", "core"))
-        swap.start()
+        late_send.start()
         loads = [
             pltpu.make_async_copy(source, target, local_sems.at[number])
             for number, (source, target) in enumerate(
-                ((o_in, o_a), (o_landed, o_b), (gu_in, gu_a), (gu_y, gu_b))
+                (
+                    (o_in, o_a),
+                    (o_landed, o_b),
+                    (gu_in, gu_a),
+                    (gu_y, gu_b.at[pl.ds(0, blocks - LATE)]),
+                )
             )
         ]
         for load in loads:
             load.start()
+        load_d.start()
         loads[0].wait()
         loads[1].wait()
         o_a[...] = (o_a[...].astype(F32) + o_b[...].astype(F32)).astype(BF16)
-        o_send.start()
-        d_send.start()
+        o_over.start()
+        d_over.start()
         loads[2].wait()
         loads[3].wait()
-
-        def add(number, _):
-            total = gu_a[number].astype(F32) + gu_b[number].astype(F32)
-            gu_a[number] = total.astype(BF16)
-            return 0
-
-        lax.fori_loop(0, gu_a.shape[0], add, 0)
+        lax.fori_loop(0, blocks - LATE, add, 0)
         for jump in range(1, line):
-            z_send(jump).start()
-        for copy in stays:
-            copy.start()
+            z_send(jump, 0).start()
+
+    @pl.when(step == 1)
+    def _():
+        late_send.wait()
+        lax.fori_loop(blocks - LATE, blocks, add, 0)
+        for jump in range(1, line):
+            z_send(jump, 1).start()
+        gu_stays.start()
+        o_over.wait()
+        summed = o_a[:, :, o_mine, :].astype(F32) + o_x[...].astype(F32)
+        o_a[:, :, o_mine, :] = summed.astype(BF16)
+        o_send.start()
+        o_stays.start()
+
+    @pl.when(step == 2)
+    def _():
+        swap.start()
+
+    @pl.when(step == 3)
+    def _():
+        load_d.wait()
+        d_over.wait()
+        for at in range(line):
+            d_a[at] = (d_a[at].astype(F32) + d_x[at].astype(F32)).astype(BF16)
+        d_send.start()
+        d_stays.start()
 
     attend_back_body(
         (received, own),
@@ -2159,16 +2278,17 @@
         swap.wait()
         d_send.wait()
         o_send.wait()
-        for copy in stays:
+        for copy in (gu_stays, o_stays, d_stays):
             copy.wait()
-        for jump in range(1, line):
-            z_send(jump).wait()
+        for number in range(2):
+            for jump in range(1, line):
+                z_send(jump, number).wait()
         for number in range(4):
             hand_over(number).wait()
 
 
 def attend_back_carry(
-    pieces, mixes, grads, lse, cosine, sine, outputs_sent, gu, gu_y, d, o, o_landed, line
+    pieces, mixes, grads, lse, cosine, sine, outputs_sent, gu, gu_y, gu_late, d, o, o_landed, line
 ):
     _, width, span = pieces[0].shape
     tok = span // 2
@@ -2189,17 +2309,18 @@
         in_specs=[triple] * 2
         + [single] * 4
         + [pl.BlockSpec((1, 8, length), lambda p: (p, 0, 0)), table, table]
-        + [anywhere] * 6,
-        out_specs=[triple] + [anywhere] * 7,
+        + [anywhere] * 7,
+        out_specs=[triple] + [anywhere] * 8,
         out_shape=[
             jax.ShapeDtypeStruct((3, width, span), BF16),
             jax.ShapeDtypeStruct((3, width, span), BF16),
             jax.ShapeDtypeStruct(outputs_sent.shape, BF16),
             jax.ShapeDtypeStruct((blocks, 2, rows, 128), BF16),
             jax.ShapeDtypeStruct((line - 1, blocks, 2, rows, 128), BF16),
-            jax.ShapeDtypeStruct((line, down_rows, wide), BF16),
-            jax.ShapeDtypeStruct((line, rows, wide), BF16),
-            jax.ShapeDtypeStruct((line, rows, wide), BF16),
+            jax.ShapeDtypeStruct((line, down_rows // 2, wide), BF16),
+            jax.ShapeDtypeStruct((line, down_rows // 2, wide), BF16),
+            jax.ShapeDtypeStruct((line, rows // 2, wide), BF16),
+            jax.ShapeDtypeStruct((line, rows // 2, wide), BF16),
         ],
         scratch_shapes=[
             pltpu.VMEM((2, PAIR, length), BF16),
@@ -2218,14 +2339,17 @@
             pltpu.VMEM((blocks, 2, line, rows, 128), BF16),
             pltpu.VMEM((line, 2, rows, wide), BF16),
             pltpu.VMEM((line, 2, rows, wide), BF16),
-            pltpu.SemaphoreType.DMA((6,)),
+            pltpu.VMEM((line, 2, rows // 2, wide), BF16),
+            pltpu.VMEM((line, 2, down_rows // 2, wide), BF16),
+            pltpu.VMEM((line, 2, down_rows // 2, wide), BF16),
+            pltpu.SemaphoreType.DMA((8,)),
             pltpu.SemaphoreType.DMA((2, 4)),
-            pltpu.SemaphoreType.DMA((2, line - 1)),
-            pltpu.SemaphoreType.DMA((2, 3)),
+            pltpu.SemaphoreType.DMA((2, 2 * (line - 1))),
+            pltpu.SemaphoreType.DMA((2, 6)),
         ],
         compiler_params=pltpu.CompilerParams(
             dimension_semantics=("arbitrary",),
-            vmem_limit_bytes=63 * MIB,
+            vmem_limit_bytes=60 * MIB,
             collective_id=5,
             has_side_effects=True,
         ),
@@ -2234,7 +2358,7 @@
         ),
         name="attend_back_carry",
     )(
-        *pieces, *mixes, *grads, lse, cosine, sine, outputs_sent, gu, gu_y, d, o, o_landed
+        *pieces, *mixes, *grads, lse, cosine, sine, outputs_sent, gu, gu_y, gu_late, d, o, o_landed
     )
 
 
@@ -2287,7 +2411,6 @@
         gu_x,
         gu_c,
         d_low,
-        d_x,
         d_c,
         s_low,
         s_x,
@@ -2310,7 +2433,8 @@
     ) = refs
     step = pl.program_id(0)
     target, turn = step // 3, lax.rem(step, 3)
-    z, y, side, core = seats()
+    z, y, x, core = seats()
+    side = x
     wide, span = grad.shape
     depth = 2 * wide
     half = jnp.where(target == 0, 1 - core, core)
@@ -2372,10 +2496,16 @@
         send(gu_a, gu_x, x_sems, 0, to_x_partner()),
         send(gu_a, gu_c, c_sems, 0, to_core_partner()),
     )
+    d_half, o_half = d_a.shape[1], o_a.shape[1]
+    d_mine = pl.ds(pl.multiple_of(x * d_half, d_half), d_half)
+    d_theirs = pl.ds(pl.multiple_of((1 - x) * d_half, d_half), d_half)
+    o_mine = pl.ds(pl.multiple_of(x * o_half, o_half), o_half)
+    o_theirs = pl.ds(pl.multiple_of((1 - x) * o_half, o_half), o_half)
     d_sides = (
-        send(d_low, d_x, x_sems, 1, to_x_partner()),
+        send(d_low.at[d_mine, :], d_low.at[d_mine, :], x_sems, 1, to_x_partner()),
         send(d_low, d_c, c_sems, 1, to_core_partner()),
     )
+    o_side = send(s_low.at[0, o_mine, :], s_low.at[0, o_mine, :], x_sems, 2, to_x_partner())
 
     def square_x(number):
         return send(s_low.at[number], s_x.at[number], x_sems, 2 + number, to_x_partner())
@@ -2391,7 +2521,7 @@
     @pl.when(step == 0)
     def _():
         meet(line, ("z", "y", "x", "core"))
-        sources = ((d_in.at[:, y], d_a), (d_y, d_b), (o_in, o_a), (o_y, o_b), (gu_mine, gu_a), (gu_z, gu_b))
+        sources = ((d_in, d_a), (d_y, d_b), (o_in, o_a), (o_y, o_b), (gu_mine, gu_a), (gu_z, gu_b))
         loads = [load(source, place, 7 + n) for n, (source, place) in enumerate(sources)]
         for copy in loads:
             copy.start()
@@ -2547,13 +2677,13 @@
             return value
 
         value = sum_z(d_a[z], [d_landed[jump] for jump in range(line - 1)])
-        d_out[:, mine] = value
-        d_low[...] = value.astype(BF16)
+        d_out[d_mine, mine] = value
+        d_low[d_mine, :] = value.astype(BF16)
         d_sides[0].start()
         value = sum_z(o_a[z], [o_landed[jump] for jump in range(line - 1)])
-        o_out[:, mine] = value
-        s_low[0] = value.astype(BF16)
-        square_x(0).start()
+        o_out[o_mine, mine] = value
+        s_low[0, o_mine, :] = value.astype(BF16)
+        o_side.start()
         for jump in range(1, line):
             gain_z(jump, line, gain, gain_landed, gain_sems).wait()
         value = gain[2]
@@ -2578,12 +2708,13 @@
         for number in range(2):
             first_part(number).wait()
         d_sides[0].wait()
-        value = d_out[:, mine] + d_x[...].astype(F32)
-        d_out[:, mine] = value
-        d_low[...] = value.astype(BF16)
+        d_out[d_theirs, mine] = d_low[d_theirs, :].astype(F32)
         d_sides[1].start()
+        o_side.wait()
+        o_out[o_theirs, mine] = s_low[0, o_theirs, :].astype(F32)
+        square_core(0).start()
         input_part.wait()
-        for number in range(4):
+        for number in range(1, 4):
             square_x(number).wait()
             value = squares[number][:, mine] + s_x[number].astype(F32)
             squares[number][:, mine] = value
@@ -2634,7 +2765,7 @@
     span = slots * tok
     wide = depth // 2
     blocks, _, rows, _ = gu_mine.shape
-    down_rows = d.shape[2]
+    down_rows = 2 * d.shape[1]
     once = pl.Buffered(1)
     anywhere = pl.BlockSpec(memory_space=pl.ANY)
 
@@ -2686,17 +2817,16 @@
             vmem((3, line, 2, rows, wide), BF16),
             vmem((3, line, rows, wide), BF16),
             vmem((3, line - 1, rows, wide), BF16),
-            vmem((line, down_rows, wide), BF16),
-            vmem((line, down_rows, wide), BF16),
-            vmem((line - 1, down_rows, wide), BF16),
-            vmem((line, rows, wide), BF16),
-            vmem((line, rows, wide), BF16),
-            vmem((line - 1, rows, wide), BF16),
+            vmem((line, down_rows // 2, wide), BF16),
+            vmem((line, down_rows // 2, wide), BF16),
+            vmem((line - 1, down_rows // 2, wide), BF16),
+            vmem((line, rows // 2, wide), BF16),
+            vmem((line, rows // 2, wide), BF16),
+            vmem((line - 1, rows // 2, wide), BF16),
             vmem((blocks, 2, rows, 128), BF16),
             vmem((line - 1, blocks, 2, rows, 128), BF16),
             vmem((blocks, 2, rows, 128), BF16),
             vmem((blocks, 2, rows, 128), BF16),
-            vmem((down_rows, wide), BF16),
             vmem((down_rows, wide), BF16),
             vmem((down_rows, wide), BF16),
             vmem((4, rows, wide), BF16),
@@ -2987,7 +3117,6 @@
         angles = freqs[:, None] * positions.astype(F32)[None, :]
         return (jnp.cos(angles), jnp.sin(angles))
 
-    cosine, sine = tables(positions)
     full_cos, full_sin = tables(jnp.arange(length, dtype=jnp.int32))
     sources = jnp.concatenate(
         [(rank - 1 - jnp.arange(count - 1, dtype=jnp.int32)) % count, rank[None]]
@@ -2995,18 +3124,10 @@
     order = (((side - steps) % slots)[None, :] * count + sources[:, None]).reshape(-1)
     order = order.astype(jnp.int32)
 
-    gains = jnp.pad(jnp.stack([attn_gain, mlp_gain], axis=1), ((0, 0), (0, 126)))
-    gate_halves, up_halves, out_halves, down_halves = (
-        [half[0] for half in split(weight)]
-        for weight in (gate_weight, up_weight, output_weight, down_weight)
-    )
-
     whole_lanes = (slots, count) == (2, 2) and (D // parts) % 128 == 0
     if whole_lanes:
+        gains = jnp.pad(jnp.stack([attn_gain, mlp_gain]).astype(F32), ((0, 6), (0, 0)))
         parts_of = lambda ref: [ref.reshape(-1, ref.shape[-1])]
-        (q_half,), (k_half,), (v_half,) = (
-            split(weight)[:1] for weight in (query_weight, key_weight, value_weight)
-        )
         (
             tokens,
             _,
@@ -3023,13 +3144,14 @@
             inputs,
             first_values,
             out_grad,
-            jnp.concatenate([q_half[0], gains], axis=1),
-            k_half[0],
-            v_half[0],
-            out_halves[0],
-            down_halves[0],
-            cosine,
-            sine,
+            query_weight,
+            key_weight,
+            value_weight,
+            output_weight,
+            down_weight,
+            gains,
+            full_cos,
+            full_sin,
             line,
         )
         qkv_full = qkv_full.reshape(2, 3, D, wide)
@@ -3061,8 +3183,8 @@
             out_grad,
             grads_early,
             down_own,
-            gate_halves[0],
-            up_halves[0],
+            gate_weight,
+            up_weight,
             line,
         )
         mixes = [mix_received, att_own]
@@ -3071,6 +3193,12 @@
         up_pieces = parts_of(up_own), parts_of(up_other)
         down_pieces = parts_of(down_own), parts_of(down_other)
     else:
+        gains = jnp.pad(jnp.stack([attn_gain, mlp_gain], axis=1), ((0, 0), (0, 126)))
+        gate_halves, up_halves, out_halves, down_halves = (
+            [half[0] for half in split(weight)]
+            for weight in (gate_weight, up_weight, output_weight, down_weight)
+        )
+        cosine, sine = tables(positions)
         qkv = [
             jnp.concatenate(half + [gains], axis=1)
             for half in split(query_weight, key_weight, value_weight)
@@ -3103,6 +3231,7 @@
             gu_reduced,
             down_reduced,
             gu_y,
+            gu_late,
         ) = mlp_carry(
             out_grad,
             grads[0],
@@ -3126,6 +3255,7 @@
             outputs_received,
             gu_mine,
             gu_z,
+            down_mine,
             down_y,
             out_mine,
             out_y,
@@ -3139,6 +3269,7 @@
             outputs_sent,
             gu_reduced,
             gu_y,
+            gu_late,
             down_reduced,
             out_kept,
             out_landed,
@@ -3156,7 +3287,7 @@
             mlp_gain_grad,
             gu_mine,
             gu_z,
-            down_reduced,
+            down_mine,
             down_y,
             out_mine,
             out_y,

time: 478 us -> 447 us (0.935)
  Pallas kernels: 458 us -> 429 us
    pallas_call x1, Pallas kernels: 100 us -> 79.2 us  [mlp_carry(): pl.pallas_call(functools.partial(mlp_carry_kernel, line, tok, blocks), gr...]
    dynamic_slice x4 -> x0, local copies, waits for them, and re-layouts: 6.06 us -> none  [split(): columns.append(lax.dynamic_slice_in_dim(weight, which * size, size, 1))]
    pallas_call x1, Pallas kernels: 96 us -> 90.7 us  [tail_carry(): pl.pallas_call(functools.partial(tail_carry_kernel, line, tok, blocks), g...]
    unnamed x7 -> x10, local copies, waits for them, and re-layouts: 0.03 us -> 5.09 us
where the time goes in v7:
time: 447 us; the launch traced here: 439 us
  Pallas kernels  429 us (96%)
  local copies, waits for them, and re-layouts  6.36 us (1%)
    pallas_call x1, Pallas kernels, tail_carry(): pl.pallas_call(functools.partial(tail_carry_kernel, line, tok, blocks), g...  90.7 us
    pallas_call x1, Pallas kernels, attend_carry(): pl.pallas_call(functools.partial(attend_carry_kernel, line, tok, min(256,...  84.6 us
    pallas_call x1, Pallas kernels, mlp_carry(): pl.pallas_call(functools.partial(mlp_carry_kernel, line, tok, blocks), gr...  79.2 us
    pallas_call x1, Pallas kernels, attend_back_carry(): pl.pallas_call(functools.partial(attend_back_carry_kernel, line, tok, til...  78.1 us
    pallas_call x1, Pallas kernels, front(): pl.pallas_call(functools.partial(front_kernel, line, tok), grid=(6,), in_...  75.2 us
    pallas_call x1, Pallas kernels, finish(): pl.pallas_call(finish_kernel, out_shape=[jax.ShapeDtypeStruct((2, tok, de...  11.8 us

profile of v7, /device:TPU:25, one launch (start us, length us, event | category | flops | bytes accessed | tf_op | source)
XLA Modules:
  0.0 439.2 jit_solution(9398137925500589995)
XLA Ops:
  0.7 1.8 multiply_sine_fusion
  2.5 1.3 fusion.3.refs_8_
  3.7 75.2 %front.1 = (bf16[512,1024]{1,0:T(8,128)(2,1)}, bf16[512,1024]{1,0:T(8,128)(2,1)}, bf16[512,1024]{1,0:T(8,128)(2,1)}, bf16[3,512,1024]{2,1,0:T(8,128)(2,1)}, bf16...) custom-call(bf16[2,512,1024]{2,1,0:T(8,128)(2,1)} %refs_0_.5, ...), custom_call_target="tpu_custom_call" | custom-call | flops 6442450944 | bytes 29360128 | tf_op jit(solution)/shard_map/front/pallas_call | solution.py:1326
  79.0 84.6 %attend_carry.1 = (bf16[512,1024]{1,0:T(8,128)(2,1)}, bf16[512,1024]{1,0:T(8,128)(2,1)}, f32[4,8,2048]{2,1,0:T(8,128)}, f32[1024,1024]{1,0:T(8,128)}, bf16[1024,...) custom-call(bf16[3,512,1024]{2,1,0:T(8,128)(2,1)} %get-tuple-element, ...), custom_call_target="tpu_custom_call", output_to_operand_aliasing={{7}: (8, {}), {8}: (9, {})} | custom-call | flops 17179869184 | bytes 8388608 | tf_op jit(solution)/shard_map/attend_carry/pallas_call | solution.py:1581
  163.6 79.2 %mlp_carry.1 = (f32[2,512,1024]{2,1,0:T(8,128)}, bf16[512,1024]{1,0:T(8,128)(2,1)}, f32[1024,1024]{1,0:T(8,128)}, bf16[1024,1024]{1,0:T(8,128)(2,1)}, f32[8,1024...) custom-call(bf16[2,512,1024]{2,1,0:T(8,128)(2,1)} %refs_0_.4, ...), custom_call_target="tpu_custom_call" | custom-call | flops 47244640256 | bytes 55574528 | tf_op jit(solution)/shard_map/mlp_carry/pallas_call | solution.py:1901
  242.8 0.0 copy-start.2
  242.8 1.2 copy-done.2
  244.0 8.9 %grad_attended_carry.1 = (bf16[512,1024]{1,0:T(8,128)(2,1)S(1)}, bf16[512,1024]{1,0:T(8,128)(2,1)S(1)}, bf16[1024,512]{1,0:T(8,128)(2,1)S(1)}, bf16[1024,512]{1,0:T(8,128)(2,1)S(1)}) custom-call(bf16[1024,1024]{1,0:T(8,128)(2,1)} %get-tuple-element.100.low_ref, bf16[1024,1024]{1,0:T(8,128)(2,1)} %get-tuple-element.101.full_ref, ...), custom_call_target="tpu_custom_call" | custom-call | flops 4294967296 | bytes 10485760 | tf_op jit(solution)/shard_map/grad_attended_carry/pallas_call | solution.py:2038
  252.9 0.0 copy-start
  253.0 1.0 copy-done
  253.9 0.0 copy-start.1
  253.9 1.0 copy-done.1
  254.9 0.0 copy-start.3
  254.9 1.0 copy-done.3
  255.9 0.0 copy-start.4
  255.9 1.0 copy-done.4
  256.8 78.1 %attend_back_carry.1 = (bf16[3,512,1024]{2,1,0:T(8,128)(2,1)}, bf16[3,512,1024]{2,1,0:T(8,128)(2,1)}, bf16[512,1024]{1,0:T(8,128)(2,1)}, bf16[11,2,128,128]{3,2,...) custom-call(bf16[3,512,1024]{2,1,0:T(8,128)(2,1)} %get-tuple-element, ...), custom_call_target="tpu_custom_call" | custom-call | flops 42949672960 | bytes 16777216 | tf_op jit(solution)/shard_map/attend_back_carry/pallas_call | solution.py:2306
  334.9 90.7 %tail_carry.1 = (f32[512,1024]{1,0:T(8,128)}, bf16[512,1024]{1,0:T(8,128)(2,1)}, f32[512,1024]{1,0:T(8,128)}, bf16[512,1024]{1,0:T(8,128)(2,1)}, f32[8,128]{1,0:...) custom-call(bf16[2,512,1024]{2,1,0:T(8,128)(2,1)} %refs_0_.5, ...), custom_call_target="tpu_custom_call" | custom-call | flops 12884901888 | bytes 37748736 | tf_op jit(solution)/shard_map/tail_carry/pallas_call | solution.py:2790
  425.6 11.8 %finish.1 = (f32[2,512,1024]{2,1,0:T(8,128)}, f32[2,512,1024]{2,1,0:T(8,128)}, f32[2,512,1024]{2,1,0:T(8,128)}, f32[128,1024]{1,0:T(8,128)}, f32[128,1024]{1,0:T...) custom-call(s32[1]{0:T(128)} %bitcast.place, ...), custom_call_target="tpu_custom_call" | custom-call | flops 524288 | bytes 31457280 | tf_op jit(solution)/shard_map/finish/pallas_call | solution.py:2909
  437.5 1.3 slice_bitcast_fusion
  (2 shorter events, 0.0 us)
Async XLA Ops:
  242.8 1.2 copy-start.2
  252.9 1.0 copy-start
  253.9 1.0 copy-start.1
  254.9 1.0 copy-start.3
  255.9 1.0 copy-start.4

commit v8 on v7

--- a/solution.py
+++ b/solution.py
@@ -974,6 +974,8 @@
         partners.append({"fsdp": shard + 1 - 2 * (shard % 2)})
     if "x" in keys:
         partners.append({"seq": lax.rem(seat + 2, 4)})
+    if "diagonal" in keys:
+        partners.append({"seq": 3 - seat})
     if "core" in keys:
         partners.append({"seq": seat + 1 - 2 * (seat % 2)})
     barrier = pltpu.get_barrier_semaphore()
@@ -1975,16 +1977,26 @@
     )
 
 
+def early_rows(rows):
+    return pl.ds(0, rows // 8)
+
+
+def late_rows(rows):
+    return pl.ds(rows // 8, rows - rows // 8)
+
+
 def grad_attended_carry_kernel(
     line,
     low_ref,
     full_ref,
     att_other,
     att_own,
+    outputs_sent,
     ga_own,
     ga_received,
     o_ref,
     o_landed,
+    outputs_received,
     outgoing,
     o_sent,
     sems,
@@ -1995,6 +2007,10 @@
     mine = pl.ds(pl.multiple_of(core * wide, wide), wide)
     others = pl.ds(pl.multiple_of((1 - core) * wide, wide), wide)
     heads = send(outgoing, ga_received, sems, 0, to_core_partner())
+    early = early_rows(outputs_sent.shape[0])
+    swap = send(
+        outputs_sent.at[early], outputs_received.at[early], sems, 3, to_x_partner()
+    )
 
     def sums(number):
         half = 1 - core if number == 0 else core
@@ -2003,7 +2019,8 @@
 
     @pl.when(step == 0)
     def _():
-        meet(line, ("core",))
+        meet(line, ("x", "core"))
+        swap.start()
         outgoing[...] = nt(full_ref[...], low_ref[...]).astype(BF16)
         heads.start()
 
@@ -2021,12 +2038,13 @@
 
     @pl.when(step == 1)
     def _():
+        swap.wait()
         heads.wait()
         for number in range(2):
             sums(number).wait()
 
 
-def grad_attended_carry(low, full, att_other, att_own, line):
+def grad_attended_carry(low, full, att_other, att_own, outputs_sent, line):
     span, depth = low.shape
     wide = depth // 2
 
@@ -2043,11 +2061,13 @@
             pl.BlockSpec((wide, depth), lambda s: (half(s), 0)),
             whole_block((wide, span)),
             whole_block((wide, span)),
+            anywhere,
         ],
         out_specs=[
             whole_block((wide, span)),
             anywhere,
             pl.BlockSpec((wide, wide), lambda s: (half(s), 0)),
+            anywhere,
             anywhere,
         ],
         out_shape=[
@@ -2055,11 +2075,12 @@
             jax.ShapeDtypeStruct((wide, span), BF16),
             jax.ShapeDtypeStruct((depth, wide), BF16),
             jax.ShapeDtypeStruct((depth, wide), BF16),
+            jax.ShapeDtypeStruct(outputs_sent.shape, BF16),
         ],
         scratch_shapes=[
             pltpu.VMEM((wide, span), BF16),
             pltpu.VMEM((2, wide, wide), BF16),
-            pltpu.SemaphoreType.DMA((2, 3)),
+            pltpu.SemaphoreType.DMA((2, 4)),
         ],
         compiler_params=pltpu.CompilerParams(
             dimension_semantics=("arbitrary",),
@@ -2073,7 +2094,7 @@
             transcendentals=0,
         ),
         name="grad_attended_carry",
-    )(low, full, att_other, att_own)
+    )(low, full, att_other, att_own, outputs_sent)
 
 
 def attend_back_carry_kernel(line, tok, tile_q, tile_k, *refs):
@@ -2088,6 +2109,7 @@
         cos_ref,
         sin_ref,
         outputs_sent,
+        _,
         gu_in,
         gu_y,
         gu_late,
@@ -2103,7 +2125,8 @@
         d_y,
         o_kept,
         o_y,
-    ) = refs[:25]
+        first_received,
+    ) = refs[:27]
     (
         qz,
         gz,
@@ -2124,14 +2147,18 @@
         o_x,
         d_a,
         d_x,
+        first_out,
         local_sems,
         back_sems,
         z_sems,
         other_sems,
-    ) = refs[25:]
+        first_sems,
+    ) = refs[27:]
     step = pl.program_id(0)
     pairs = pl.num_programs(0)
-    z, y, x, _ = seats()
+    z, y, x, core = seats()
+    wide = d_a.shape[3]
+    late_part = late_rows(tok)
     length = 4 * tok
     blocks = gu_a.shape[0]
     o_half, d_half = o_x.shape[2], d_x.shape[2]
@@ -2139,7 +2166,13 @@
     o_theirs = pl.ds(pl.multiple_of((1 - x) * o_half, o_half), o_half)
     d_mine = pl.ds(pl.multiple_of(x * d_half, d_half), d_half)
     d_theirs = pl.ds(pl.multiple_of((1 - x) * d_half, d_half), d_half)
-    swap = send(outputs_sent, outputs_received, other_sems, 0, to_x_partner())
+    swap = send(
+        outputs_sent.at[late_part],
+        outputs_received.at[late_part],
+        other_sems,
+        0,
+        to_x_partner(),
+    )
     o_over = send(o_a.at[:, :, o_theirs, :], o_x, other_sems, 1, to_x_partner())
     d_over = send(d_in.at[:, :, d_theirs, :], d_x, other_sems, 2, to_x_partner())
     o_send = send(o_a.at[:, 1 - y, o_mine, :], o_y, other_sems, 3, to_y_partner())
@@ -2168,6 +2201,13 @@
     d_stays = pltpu.make_async_copy(d_a.at[:, y], d_kept, local_sems.at[7])
     load_d = pltpu.make_async_copy(d_in.at[:, :, d_mine, :], d_a, local_sems.at[4])
 
+    def first_send(source):
+        columns = pl.ds(pl.multiple_of(core * wide, wide), PAIR)
+        partner = to_x_partner() if source else {"seq": 3 - lax.axis_index("seq")}
+        return send(
+            first_out.at[source], first_received.at[:, columns], first_sems, source, partner
+        )
+
     def hand_over(number):
         rows = pl.ds(number * PAIR, PAIR)
         return send(
@@ -2180,7 +2220,7 @@
 
     @pl.when(step == 0)
     def _():
-        meet(line, ("z", "y", "x", "core"))
+        meet(line, ("z", "y", "x", "core", "diagonal"))
         late_send.start()
         loads = [
             pltpu.make_async_copy(source, target, local_sems.at[number])
@@ -2267,6 +2307,13 @@
                     at = pl.ds(pl.multiple_of(step * PAIR, PAIR), PAIR)
                     outgoing[which, at, take] = result
 
+    @pl.when(step == 0)
+    def _():
+        for source in range(2):
+            rows = dv[block_of(source, 1, tok), :]
+            first_out[source] = (0.5 * rows).astype(BF16)
+            first_send(source).start()
+
     for number in range(4):
 
         @pl.when(step == number)
@@ -2276,6 +2323,8 @@
     @pl.when(step == pairs - 1)
     def _():
         swap.wait()
+        for source in range(2):
+            first_send(source).wait()
         d_send.wait()
         o_send.wait()
         for copy in (gu_stays, o_stays, d_stays):
@@ -2288,7 +2337,21 @@
 
 
 def attend_back_carry(
-    pieces, mixes, grads, lse, cosine, sine, outputs_sent, gu, gu_y, gu_late, d, o, o_landed, line
+    pieces,
+    mixes,
+    grads,
+    lse,
+    cosine,
+    sine,
+    outputs_sent,
+    outputs_received,
+    gu,
+    gu_y,
+    gu_late,
+    d,
+    o,
+    o_landed,
+    line,
 ):
     _, width, span = pieces[0].shape
     tok = span // 2
@@ -2309,8 +2372,8 @@
         in_specs=[triple] * 2
         + [single] * 4
         + [pl.BlockSpec((1, 8, length), lambda p: (p, 0, 0)), table, table]
-        + [anywhere] * 7,
-        out_specs=[triple] + [anywhere] * 8,
+        + [anywhere] * 8,
+        out_specs=[triple] + [anywhere] * 9,
         out_shape=[
             jax.ShapeDtypeStruct((3, width, span), BF16),
             jax.ShapeDtypeStruct((3, width, span), BF16),
@@ -2321,7 +2384,9 @@
             jax.ShapeDtypeStruct((line, down_rows // 2, wide), BF16),
             jax.ShapeDtypeStruct((line, rows // 2, wide), BF16),
             jax.ShapeDtypeStruct((line, rows // 2, wide), BF16),
+            jax.ShapeDtypeStruct(outputs_sent.shape, BF16),
         ],
+        input_output_aliases={10: 2},
         scratch_shapes=[
             pltpu.VMEM((2, PAIR, length), BF16),
             pltpu.VMEM((2, PAIR, length), BF16),
@@ -2342,10 +2407,12 @@
             pltpu.VMEM((line, 2, rows // 2, wide), BF16),
             pltpu.VMEM((line, 2, down_rows // 2, wide), BF16),
             pltpu.VMEM((line, 2, down_rows // 2, wide), BF16),
+            pltpu.VMEM((2, tok, PAIR), BF16),
             pltpu.SemaphoreType.DMA((8,)),
             pltpu.SemaphoreType.DMA((2, 4)),
             pltpu.SemaphoreType.DMA((2, 2 * (line - 1))),
             pltpu.SemaphoreType.DMA((2, 6)),
+            pltpu.SemaphoreType.DMA((2, 2)),
         ],
         compiler_params=pltpu.CompilerParams(
             dimension_semantics=("arbitrary",),
@@ -2358,7 +2425,20 @@
         ),
         name="attend_back_carry",
     )(
-        *pieces, *mixes, *grads, lse, cosine, sine, outputs_sent, gu, gu_y, gu_late, d, o, o_landed
+        *pieces,
+        *mixes,
+        *grads,
+        lse,
+        cosine,
+        sine,
+        outputs_sent,
+        outputs_received,
+        gu,
+        gu_y,
+        gu_late,
+        d,
+        o,
+        o_landed,
     )
 
 
@@ -2379,6 +2459,7 @@
         d_y,
         o_in,
         o_y,
+        _,
         input_grad,
         input_landed,
         first_grad,
@@ -2432,7 +2513,8 @@
         gain_sems,
     ) = refs
     step = pl.program_id(0)
-    target, turn = step // 3, lax.rem(step, 3)
+    target = jnp.where(step < 6, lax.rem(step, 2), 2)
+    turn = lax.rem(step // 2, 3)
     z, y, x, core = seats()
     side = x
     wide, span = grad.shape
@@ -2486,7 +2568,7 @@
 
     def first_part(number):
         which = 1 - core if number == 0 else core
-        at = pl.ds(pl.multiple_of(which * wide, wide), wide)
+        at = pl.ds(pl.multiple_of(which * wide + PAIR, PAIR), wide - PAIR)
         return send(
             first_send.at[:, at], first_landed.at[:, at], token_sems, number, to_x_partner()
         )
@@ -2577,7 +2659,7 @@
     def _():
         first_part(0).start()
 
-    @pl.when(step == 3)
+    @pl.when(step == 1)
     def _():
         first_part(1).start()
         store_first.start()
@@ -2759,6 +2841,7 @@
     d_y,
     o,
     o_y,
+    first_received,
     line,
 ):
     slots, tok, depth = inputs.shape
@@ -2771,10 +2854,10 @@
 
     def half(s):
         core = lax.axis_index("seq") % 2
-        return jnp.where(s < 3, 1 - core, core)
+        return jnp.where(s % 2 == 0, 1 - core, core)
 
     def kind(s):
-        return (s + 2) % 3
+        return (jnp.minimum(s // 2, 2) + 2) % 3
 
     def clear(shape):
         zeros = (0,) * len(shape)
@@ -2793,18 +2876,19 @@
         in_specs=[
             anywhere,
             anywhere,
-            pl.BlockSpec((1, wide, span), lambda s: (kind(jnp.minimum(s, 2)), 0, 0)),
-            pl.BlockSpec((1, wide, span), lambda s: (kind(jnp.clip(s, 3, 5)), 0, 0)),
+            pl.BlockSpec((1, wide, span), lambda s: (kind(s), 0, 0)),
+            pl.BlockSpec((1, wide, span), lambda s: (kind(s), 0, 0)),
             pl.BlockSpec(
                 (1, 1, depth, wide),
-                lambda s: (half(jnp.minimum(s, 5)), kind(jnp.minimum(s, 5)), 0, 0),
+                lambda s: (half(jnp.minimum(s, 5)), kind(s), 0, 0),
             ),
             clear((span, depth)),
             anywhere,
             clear((8, depth)),
             clear((8, depth)),
         ]
-        + [anywhere] * 6,
+        + [anywhere] * 7,
+        input_output_aliases={15: 3},
         out_specs=[anywhere] * 4 + [clear((8, 128))] + [clear(final.shape) for final in finals],
         out_shape=tokens + [jax.ShapeDtypeStruct((8, 128), F32)] + finals,
         scratch_shapes=[
@@ -2876,6 +2960,7 @@
         d_y,
         o,
         o_y,
+        first_received,
     )
 
 
@@ -3243,8 +3328,8 @@
             (down_pieces[0][0], down_pieces[1][0]),
             line,
         )
-        ga_own, ga_received, out_kept, out_landed = grad_attended_carry(
-            low_grad, out_full, att_other, att_own, line
+        ga_own, ga_received, out_kept, out_landed, outputs_received = grad_attended_carry(
+            low_grad, out_full, att_other, att_own, outputs_sent, line
         )
         down_reduced = down_reduced.reshape(line, 2, -1, wide)
         out_kept = out_kept.reshape(line, 2, -1, wide)
@@ -3259,6 +3344,7 @@
             down_y,
             out_mine,
             out_y,
+            first_received,
         ) = attend_back_carry(
             pieces,
             mixes,
@@ -3267,6 +3353,7 @@
             full_cos,
             full_sin,
             outputs_sent,
+            outputs_received,
             gu_reduced,
             gu_y,
             gu_late,
@@ -3291,6 +3378,7 @@
             down_y,
             out_mine,
             out_y,
+            first_received,
             line,
         )
         gain_grads = rest[0]

time: 447 us -> 441 us (0.987)
  Pallas kernels: 429 us -> 424 us
    pallas_call x1, Pallas kernels: 90.7 us -> 85.5 us  [tail_carry(): pl.pallas_call(functools.partial(tail_carry_kernel, line, tok, blocks), g...]
where the time goes in v8:
time: 441 us; the launch traced here: 434 us
  Pallas kernels  424 us (96%)
  local copies, waits for them, and re-layouts  6.12 us (1%)
    pallas_call x1, Pallas kernels, tail_carry(): pl.pallas_call(functools.partial(tail_carry_kernel, line, tok, blocks), g...  85.5 us
    pallas_call x1, Pallas kernels, attend_carry(): pl.pallas_call(functools.partial(attend_carry_kernel, line, tok, min(256,...  84.4 us
    pallas_call x1, Pallas kernels, mlp_carry(): pl.pallas_call(functools.partial(mlp_carry_kernel, line, tok, blocks), gr...  79.2 us
    pallas_call x1, Pallas kernels, attend_back_carry(): pl.pallas_call(functools.partial(attend_back_carry_kernel, line, tok, til...  78.2 us
    pallas_call x1, Pallas kernels, front(): pl.pallas_call(functools.partial(front_kernel, line, tok), grid=(6,), in_...  75.2 us
    pallas_call x1, Pallas kernels, finish(): pl.pallas_call(finish_kernel, out_shape=[jax.ShapeDtypeStruct((2, tok, de...  11.8 us
    pallas_call x1, Pallas kernels, grad_attended_carry(): pl.pallas_call(functools.partial(grad_attended_carry_kernel, line), grid=...  9.28 us

profile of v8, /device:TPU:25, one launch (start us, length us, event | category | flops | bytes accessed | tf_op | source)
XLA Modules:
  0.0 434.0 jit_solution(11790476314831508584)
XLA Ops:
  0.7 1.8 multiply_sine_fusion
  2.5 1.3 fusion.3.refs_8_
  3.7 75.2 %front.1 = (bf16[512,1024]{1,0:T(8,128)(2,1)}, bf16[512,1024]{1,0:T(8,128)(2,1)}, bf16[512,1024]{1,0:T(8,128)(2,1)}, bf16[3,512,1024]{2,1,0:T(8,128)(2,1)}, bf16...) custom-call(bf16[2,512,1024]{2,1,0:T(8,128)(2,1)} %refs_0_.5, ...), custom_call_target="tpu_custom_call" | custom-call | flops 6442450944 | bytes 29360128 | tf_op jit(solution)/shard_map/front/pallas_call | solution.py:1328
  79.0 84.4 %attend_carry.1 = (bf16[512,1024]{1,0:T(8,128)(2,1)}, bf16[512,1024]{1,0:T(8,128)(2,1)}, f32[4,8,2048]{2,1,0:T(8,128)}, f32[1024,1024]{1,0:T(8,128)}, bf16[1024,...) custom-call(bf16[3,512,1024]{2,1,0:T(8,128)(2,1)} %get-tuple-element, ...), custom_call_target="tpu_custom_call", output_to_operand_aliasing={{7}: (8, {}), {8}: (9, {})} | custom-call | flops 17179869184 | bytes 8388608 | tf_op jit(solution)/shard_map/attend_carry/pallas_call | solution.py:1583
  163.4 79.2 %mlp_carry.1 = (f32[2,512,1024]{2,1,0:T(8,128)}, bf16[512,1024]{1,0:T(8,128)(2,1)}, f32[1024,1024]{1,0:T(8,128)}, bf16[1024,1024]{1,0:T(8,128)(2,1)}, f32[8,1024...) custom-call(bf16[2,512,1024]{2,1,0:T(8,128)(2,1)} %refs_0_.4, ...), custom_call_target="tpu_custom_call" | custom-call | flops 47244640256 | bytes 55574528 | tf_op jit(solution)/shard_map/mlp_carry/pallas_call | solution.py:1903
  242.6 9.3 %grad_attended_carry.1 = (bf16[512,1024]{1,0:T(8,128)(2,1)S(1)}, bf16[512,1024]{1,0:T(8,128)(2,1)S(1)}, bf16[1024,512]{1,0:T(8,128)(2,1)S(1)}, bf16[1024,512]{1,0:T(8,128)(2,1)S(1)}, bf16[512,1024]{1,0:T(8,128)(2,1)S(1)}) custom-call(bf16[1024,1024]{1,0:T(8,128)(2,1)} %get-tuple-element.102.low_ref, bf16[1024,1024]{1,0:T(8,128)(2,1)} %get-tuple-element.103.full_ref, ...), custom_call_target="tpu_custom_call" | custom-call | flops 4294967296 | bytes 10485760 | tf_op jit(solution)/shard_map/grad_attended_carry/pallas_call | solution.py:2056
  251.9 0.0 copy-start
  251.9 1.0 copy-done
  252.9 0.0 copy-start.1
  252.9 1.0 copy-done.1
  253.9 0.0 copy-start.2
  253.9 1.0 copy-done.2
  254.8 0.0 copy-start.3
  254.8 1.0 copy-done.3
  255.8 0.0 copy-start.4
  255.8 1.0 copy-done.4
  256.8 78.2 %attend_back_carry.1 = (bf16[3,512,1024]{2,1,0:T(8,128)(2,1)}, bf16[3,512,1024]{2,1,0:T(8,128)(2,1)}, bf16[512,1024]{1,0:T(8,128)(2,1)}, bf16[11,2,128,128]{3,2,...) custom-call(bf16[3,512,1024]{2,1,0:T(8,128)(2,1)} %get-tuple-element, ...), custom_call_target="tpu_custom_call", output_to_operand_aliasing={{2}: (10, {})} | custom-call | flops 42949672960 | bytes 16777216 | tf_op jit(solution)/shard_map/attend_back_carry/pallas_call | solution.py:2369
  334.9 85.5 %tail_carry.1 = (f32[512,1024]{1,0:T(8,128)}, bf16[512,1024]{1,0:T(8,128)(2,1)}, f32[512,1024]{1,0:T(8,128)}, bf16[512,1024]{1,0:T(8,128)(2,1)}, f32[8,128]{1,0:...) custom-call(bf16[2,512,1024]{2,1,0:T(8,128)(2,1)} %refs_0_.5, ...), custom_call_target="tpu_custom_call", output_to_operand_aliasing={{3}: (15, {})} | custom-call | flops 12884901888 | bytes 37748736 | tf_op jit(solution)/shard_map/tail_carry/pallas_call | solution.py:2873
  420.5 11.8 %finish.1 = (f32[2,512,1024]{2,1,0:T(8,128)}, f32[2,512,1024]{2,1,0:T(8,128)}, f32[2,512,1024]{2,1,0:T(8,128)}, f32[128,1024]{1,0:T(8,128)}, f32[128,1024]{1,0:T...) custom-call(s32[1]{0:T(128)} %bitcast.place, ...), custom_call_target="tpu_custom_call" | custom-call | flops 524288 | bytes 31457280 | tf_op jit(solution)/shard_map/finish/pallas_call | solution.py:2994
  432.3 1.3 slice_bitcast_fusion
  (2 shorter events, 0.0 us)
Async XLA Ops:
  251.9 1.0 copy-start
  252.9 1.0 copy-start.1
  253.9 1.0 copy-start.2
  254.8 1.0 copy-start.3
  255.8 1.0 copy-start.4

commit v9 on v8

--- a/solution.py
+++ b/solution.py
@@ -2357,7 +2357,7 @@
     tok = span // 2
     length = 2 * span
     pairs = width // PAIR
-    tile_q = min(512, length)
+    tile_q = min(1024, length)
     tile_k = min(256, length)
     anywhere = pl.BlockSpec(memory_space=pl.ANY)
     triple = pl.BlockSpec((3, PAIR, span), lambda p: (0, p, 0))

time: 441 us -> 438 us (level)
  no operation moved by 1% of the time
where the time goes in v9:
time: 438 us; the launch traced here: 431 us
  Pallas kernels  421 us (96%)
  local copies, waits for them, and re-layouts  6.12 us (1%)
    pallas_call x1, Pallas kernels, attend_carry(): pl.pallas_call(functools.partial(attend_carry_kernel, line, tok, min(256,...  84.5 us
    pallas_call x1, Pallas kernels, tail_carry(): pl.pallas_call(functools.partial(tail_carry_kernel, line, tok, blocks), g...  84.1 us
    pallas_call x1, Pallas kernels, mlp_carry(): pl.pallas_call(functools.partial(mlp_carry_kernel, line, tok, blocks), gr...  79.5 us
    pallas_call x1, Pallas kernels, attend_back_carry(): pl.pallas_call(functools.partial(attend_back_carry_kernel, line, tok, til...  76.3 us
    pallas_call x1, Pallas kernels, front(): pl.pallas_call(functools.partial(front_kernel, line, tok), grid=(6,), in_...  75.2 us
    pallas_call x1, Pallas kernels, finish(): pl.pallas_call(finish_kernel, out_shape=[jax.ShapeDtypeStruct((2, tok, de...  11.8 us
    pallas_call x1, Pallas kernels, grad_attended_carry(): pl.pallas_call(functools.partial(grad_attended_carry_kernel, line), grid=...  9.28 us

profile of v9, /device:TPU:25, one launch (start us, length us, event | category | flops | bytes accessed | tf_op | source)
XLA Modules:
  0.0 430.9 jit_solution(11720433829961715174)
XLA Ops:
  0.7 1.8 multiply_sine_fusion
  2.5 1.3 fusion.3.refs_8_
  3.7 75.2 %front.1 = (bf16[512,1024]{1,0:T(8,128)(2,1)}, bf16[512,1024]{1,0:T(8,128)(2,1)}, bf16[512,1024]{1,0:T(8,128)(2,1)}, bf16[3,512,1024]{2,1,0:T(8,128)(2,1)}, bf16...) custom-call(bf16[2,512,1024]{2,1,0:T(8,128)(2,1)} %refs_0_.5, ...), custom_call_target="tpu_custom_call" | custom-call | flops 6442450944 | bytes 29360128 | tf_op jit(solution)/shard_map/front/pallas_call | solution.py:1328
  79.0 84.5 %attend_carry.1 = (bf16[512,1024]{1,0:T(8,128)(2,1)}, bf16[512,1024]{1,0:T(8,128)(2,1)}, f32[4,8,2048]{2,1,0:T(8,128)}, f32[1024,1024]{1,0:T(8,128)}, bf16[1024,...) custom-call(bf16[3,512,1024]{2,1,0:T(8,128)(2,1)} %get-tuple-element, ...), custom_call_target="tpu_custom_call", output_to_operand_aliasing={{7}: (8, {}), {8}: (9, {})} | custom-call | flops 17179869184 | bytes 8388608 | tf_op jit(solution)/shard_map/attend_carry/pallas_call | solution.py:1583
  163.5 79.5 %mlp_carry.1 = (f32[2,512,1024]{2,1,0:T(8,128)}, bf16[512,1024]{1,0:T(8,128)(2,1)}, f32[1024,1024]{1,0:T(8,128)}, bf16[1024,1024]{1,0:T(8,128)(2,1)}, f32[8,1024...) custom-call(bf16[2,512,1024]{2,1,0:T(8,128)(2,1)} %refs_0_.4, ...), custom_call_target="tpu_custom_call" | custom-call | flops 47244640256 | bytes 55574528 | tf_op jit(solution)/shard_map/mlp_carry/pallas_call | solution.py:1903
  243.1 9.3 %grad_attended_carry.1 = (bf16[512,1024]{1,0:T(8,128)(2,1)S(1)}, bf16[512,1024]{1,0:T(8,128)(2,1)S(1)}, bf16[1024,512]{1,0:T(8,128)(2,1)S(1)}, bf16[1024,512]{1,0:T(8,128)(2,1)S(1)}, bf16[512,1024]{1,0:T(8,128)(2,1)S(1)}) custom-call(bf16[1024,1024]{1,0:T(8,128)(2,1)} %get-tuple-element.102.low_ref, bf16[1024,1024]{1,0:T(8,128)(2,1)} %get-tuple-element.103.full_ref, ...), custom_call_target="tpu_custom_call" | custom-call | flops 4294967296 | bytes 10485760 | tf_op jit(solution)/shard_map/grad_attended_carry/pallas_call | solution.py:2056
  252.3 0.0 copy-start
  252.3 1.0 copy-done
  253.3 0.0 copy-start.1
  253.3 1.0 copy-done.1
  254.3 0.0 copy-start.2
  254.3 1.0 copy-done.2
  255.3 0.0 copy-start.3
  255.3 1.0 copy-done.3
  256.2 0.0 copy-start.4
  256.2 1.0 copy-done.4
  257.2 76.3 %attend_back_carry.1 = (bf16[3,512,1024]{2,1,0:T(8,128)(2,1)}, bf16[3,512,1024]{2,1,0:T(8,128)(2,1)}, bf16[512,1024]{1,0:T(8,128)(2,1)}, bf16[11,2,128,128]{3,2,...) custom-call(bf16[3,512,1024]{2,1,0:T(8,128)(2,1)} %get-tuple-element, ...), custom_call_target="tpu_custom_call", output_to_operand_aliasing={{2}: (10, {})} | custom-call | flops 42949672960 | bytes 16777216 | tf_op jit(solution)/shard_map/attend_back_carry/pallas_call | solution.py:2369
  333.5 84.1 %tail_carry.1 = (f32[512,1024]{1,0:T(8,128)}, bf16[512,1024]{1,0:T(8,128)(2,1)}, f32[512,1024]{1,0:T(8,128)}, bf16[512,1024]{1,0:T(8,128)(2,1)}, f32[8,128]{1,0:...) custom-call(bf16[2,512,1024]{2,1,0:T(8,128)(2,1)} %refs_0_.5, ...), custom_call_target="tpu_custom_call", output_to_operand_aliasing={{3}: (15, {})} | custom-call | flops 12884901888 | bytes 37748736 | tf_op jit(solution)/shard_map/tail_carry/pallas_call | solution.py:2873
  417.6 11.8 %finish.1 = (f32[2,512,1024]{2,1,0:T(8,128)}, f32[2,512,1024]{2,1,0:T(8,128)}, f32[2,512,1024]{2,1,0:T(8,128)}, f32[128,1024]{1,0:T(8,128)}, f32[128,1024]{1,0:T...) custom-call(s32[1]{0:T(128)} %bitcast.place, ...), custom_call_target="tpu_custom_call" | custom-call | flops 524288 | bytes 31457280 | tf_op jit(solution)/shard_map/finish/pallas_call | solution.py:2994
  429.4 1.3 slice_bitcast_fusion
  (2 shorter events, 0.0 us)
Async XLA Ops:
  252.3 1.0 copy-start
  253.3 1.0 copy-start.1
  254.3 1.0 copy-start.2
  255.3 1.0 copy-start.3
  256.2 1.0 copy-start.4

commit v10 on v9

--- a/solution.py
+++ b/solution.py
@@ -1761,7 +1761,7 @@
         down_w = down_full[...]
         both_w = jnp.concatenate([gate_w, up_w], axis=1)
         span = og.shape[0]
-        size = span // 2
+        size = span // 4
 
         def products(at):
             both = dot(normed_ref[at, :], both_w)
@@ -1778,7 +1778,7 @@
             acc[at, :] += dot(active, down_w)
             back[at, :] += nt(grad_both, both_w)
 
-        pieces = [slice(n * size, (n + 1) * size) for n in range(2)]
+        pieces = [slice(n * size, (n + 1) * size) for n in range(4)]
         bent = []
         ahead = products(pieces[0])
         for number, at in enumerate(pieces):
@@ -2573,7 +2573,12 @@
             first_send.at[:, at], first_landed.at[:, at], token_sems, number, to_x_partner()
         )
 
-    input_part = send(input_send, input_landed, token_sems, 2, to_x_partner())
+    def input_part(number):
+        at = pl.ds(number * (tok // 2), tok // 2)
+        return send(
+            input_send.at[at], input_landed.at[at], token_sems, 2 + number, to_x_partner()
+        )
+
     gu_sides = (
         send(gu_a, gu_x, x_sems, 0, to_x_partner()),
         send(gu_a, gu_c, c_sems, 0, to_core_partner()),
@@ -2713,9 +2718,11 @@
                     input_send[local, :] = result.astype(BF16)
                 return 0
 
-            lax.fori_loop(0, tok // chunk, finish, 0)
-            if slot == 1:
-                input_part.start()
+            for number in range(2):
+                turns = tok // chunk // 2
+                lax.fori_loop(number * turns, (number + 1) * turns, finish, 0)
+                if slot == 1:
+                    input_part(number).start()
         gain_send(0, to_core_partner()).start()
         store_input.start()
         gu_sides[0].wait()
@@ -2795,7 +2802,8 @@
         o_side.wait()
         o_out[o_theirs, mine] = s_low[0, o_theirs, :].astype(F32)
         square_core(0).start()
-        input_part.wait()
+        for number in range(2):
+            input_part(number).wait()
         for number in range(1, 4):
             square_x(number).wait()
             value = squares[number][:, mine] + s_x[number].astype(F32)
@@ -2929,7 +2937,7 @@
             dma((2, line - 1)),
             dma((2, 6)),
             dma((2, 6)),
-            dma((2, 3)),
+            dma((2, 4)),
             dma((2, line + 2)),
         ],
         compiler_params=pltpu.CompilerParams(

time: 438 us -> 438 us (level)
  no operation moved by 1% of the time
where the time goes in v10:
time: 438 us; the launch traced here: 430 us
  Pallas kernels  420 us (96%)
  local copies, waits for them, and re-layouts  6.12 us (1%)
    pallas_call x1, Pallas kernels, attend_carry(): pl.pallas_call(functools.partial(attend_carry_kernel, line, tok, min(256,...  84.5 us
    pallas_call x1, Pallas kernels, tail_carry(): pl.pallas_call(functools.partial(tail_carry_kernel, line, tok, blocks), g...  84.1 us
    pallas_call x1, Pallas kernels, mlp_carry(): pl.pallas_call(functools.partial(mlp_carry_kernel, line, tok, blocks), gr...  79 us
    pallas_call x1, Pallas kernels, attend_back_carry(): pl.pallas_call(functools.partial(attend_back_carry_kernel, line, tok, til...  76.3 us
    pallas_call x1, Pallas kernels, front(): pl.pallas_call(functools.partial(front_kernel, line, tok), grid=(6,), in_...  75.2 us
    pallas_call x1, Pallas kernels, finish(): pl.pallas_call(finish_kernel, out_shape=[jax.ShapeDtypeStruct((2, tok, de...  11.8 us
    pallas_call x1, Pallas kernels, grad_attended_carry(): pl.pallas_call(functools.partial(grad_attended_carry_kernel, line), grid=...  9.28 us

profile of v10, /device:TPU:25, one launch (start us, length us, event | category | flops | bytes accessed | tf_op | source)
XLA Modules:
  0.0 430.4 jit_solution(16407148731558674493)
XLA Ops:
  0.7 1.8 multiply_sine_fusion
  2.5 1.3 fusion.3.refs_8_
  3.7 75.2 %front.1 = (bf16[512,1024]{1,0:T(8,128)(2,1)}, bf16[512,1024]{1,0:T(8,128)(2,1)}, bf16[512,1024]{1,0:T(8,128)(2,1)}, bf16[3,512,1024]{2,1,0:T(8,128)(2,1)}, bf16...) custom-call(bf16[2,512,1024]{2,1,0:T(8,128)(2,1)} %refs_0_.5, ...), custom_call_target="tpu_custom_call" | custom-call | flops 6442450944 | bytes 29360128 | tf_op jit(solution)/shard_map/front/pallas_call | solution.py:1328
  79.0 84.5 %attend_carry.1 = (bf16[512,1024]{1,0:T(8,128)(2,1)}, bf16[512,1024]{1,0:T(8,128)(2,1)}, f32[4,8,2048]{2,1,0:T(8,128)}, f32[1024,1024]{1,0:T(8,128)}, bf16[1024,...) custom-call(bf16[3,512,1024]{2,1,0:T(8,128)(2,1)} %get-tuple-element, ...), custom_call_target="tpu_custom_call", output_to_operand_aliasing={{7}: (8, {}), {8}: (9, {})} | custom-call | flops 17179869184 | bytes 8388608 | tf_op jit(solution)/shard_map/attend_carry/pallas_call | solution.py:1583
  163.5 79.0 %mlp_carry.1 = (f32[2,512,1024]{2,1,0:T(8,128)}, bf16[512,1024]{1,0:T(8,128)(2,1)}, f32[1024,1024]{1,0:T(8,128)}, bf16[1024,1024]{1,0:T(8,128)(2,1)}, f32[8,1024...) custom-call(bf16[2,512,1024]{2,1,0:T(8,128)(2,1)} %refs_0_.4, ...), custom_call_target="tpu_custom_call" | custom-call | flops 47244640256 | bytes 55574528 | tf_op jit(solution)/shard_map/mlp_carry/pallas_call | solution.py:1903
  242.5 9.3 %grad_attended_carry.1 = (bf16[512,1024]{1,0:T(8,128)(2,1)S(1)}, bf16[512,1024]{1,0:T(8,128)(2,1)S(1)}, bf16[1024,512]{1,0:T(8,128)(2,1)S(1)}, bf16[1024,512]{1,0:T(8,128)(2,1)S(1)}, bf16[512,1024]{1,0:T(8,128)(2,1)S(1)}) custom-call(bf16[1024,1024]{1,0:T(8,128)(2,1)} %get-tuple-element.102.low_ref, bf16[1024,1024]{1,0:T(8,128)(2,1)} %get-tuple-element.103.full_ref, ...), custom_call_target="tpu_custom_call" | custom-call | flops 4294967296 | bytes 10485760 | tf_op jit(solution)/shard_map/grad_attended_carry/pallas_call | solution.py:2056
  251.8 0.0 copy-start
  251.8 1.0 copy-done
  252.8 0.0 copy-start.1
  252.8 1.0 copy-done.1
  253.7 0.0 copy-start.2
  253.7 1.0 copy-done.2
  254.7 0.0 copy-start.3
  254.7 1.0 copy-done.3
  255.7 0.0 copy-start.4
  255.7 1.0 copy-done.4
  256.6 76.3 %attend_back_carry.1 = (bf16[3,512,1024]{2,1,0:T(8,128)(2,1)}, bf16[3,512,1024]{2,1,0:T(8,128)(2,1)}, bf16[512,1024]{1,0:T(8,128)(2,1)}, bf16[11,2,128,128]{3,2,...) custom-call(bf16[3,512,1024]{2,1,0:T(8,128)(2,1)} %get-tuple-element, ...), custom_call_target="tpu_custom_call", output_to_operand_aliasing={{2}: (10, {})} | custom-call | flops 42949672960 | bytes 16777216 | tf_op jit(solution)/shard_map/attend_back_carry/pallas_call | solution.py:2369
  332.9 84.1 %tail_carry.1 = (f32[512,1024]{1,0:T(8,128)}, bf16[512,1024]{1,0:T(8,128)(2,1)}, f32[512,1024]{1,0:T(8,128)}, bf16[512,1024]{1,0:T(8,128)(2,1)}, f32[8,128]{1,0:...) custom-call(bf16[2,512,1024]{2,1,0:T(8,128)(2,1)} %refs_0_.5, ...), custom_call_target="tpu_custom_call", output_to_operand_aliasing={{3}: (15, {})} | custom-call | flops 12884901888 | bytes 37748736 | tf_op jit(solution)/shard_map/tail_carry/pallas_call | solution.py:2881
  417.0 11.8 %finish.1 = (f32[2,512,1024]{2,1,0:T(8,128)}, f32[2,512,1024]{2,1,0:T(8,128)}, f32[2,512,1024]{2,1,0:T(8,128)}, f32[128,1024]{1,0:T(8,128)}, f32[128,1024]{1,0:T...) custom-call(s32[1]{0:T(128)} %bitcast.place, ...), custom_call_target="tpu_custom_call" | custom-call | flops 524288 | bytes 31457280 | tf_op jit(solution)/shard_map/finish/pallas_call | solution.py:3002
  428.9 1.3 slice_bitcast_fusion
  (2 shorter events, 0.0 us)
Async XLA Ops:
  251.8 1.0 copy-start
  252.8 1.0 copy-start.1
  253.7 1.0 copy-start.2
  254.7 1.0 copy-start.3
  255.7 1.0 copy-start.4
